TPU v7x, 32 devices: a whole 2x2x4 slice. The times are simulated.
32 devices in a mesh: sib: 2 (over core), row: 4 (over z), col: 4 (over y, x).
Axes of the slice: x: 2, y: 2, z: 4, core: 2. Of those that a mesh axis runs over, the one named last changes fastest.
Arguments:
- child_front: float32 [2, 2048, 2048], P('sib', 'row', 'col'), may hold values from -6 to 6
- child_panel: float32 [2, 2048, 1024], P('sib', ('row', 'col')), may hold values from -0.42 to 0.42
- block_map: int32 [2, 16], replicated, may hold values from 0 to 23, as said below
- parent_front: float32 [3072, 3072], P(('row', 'sib'), 'col'), may hold values from -6 to 6
- pivot_inverse: float32 [512, 512], replicated, may hold values from -0.03 to 0.1, as said below
Outputs:
- parent_out: float32 [3072, 3072], P(('row', 'sib'), 'col')
Inputs may be any that keep to these rules, and one draw needn't show every extreme that they name: `block_map`: each row is strictly increasing. A child block i that lands in parent block g * 6 + k with 0 <= k < 6 satisfies g * 4 - 2 <= i < (g + 1) * 4; the lower end is met for g = 1 in every draw, and the last parent block is always named. `pivot_inverse`: lower triangular with diagonal entries from 0.05 to 0.1.
All inputs are finite; a program needn't handle non-finite values.
Results may differ from a plain program's by a relative error of at most 0.0001.
Values sent between devices are 32-bit elements; how exact they have to be, the bound alone decides.
No kernel may reach another device: no remote copies, remote signals or barrier semaphores. Data moves between devices by JAX's collectives and lax.ppermute only.
A program may use at most 64 MiB of HBM per device.

v0:
```python
import jax
import jax.numpy as jnp
from jax import lax
from jax.experimental import pallas as pl
from jax.experimental.pallas import tpu as pltpu
from jax.sharding import PartitionSpec as P


BLK = 128
CBD = 4
PBD = 6
HB = 2
PIV = 4
PANEL = 512
HALF = PBD // 2
EDGE = HB * BLK


SMEM = pl.BlockSpec(memory_space=pltpu.SMEM)
VMEM = pl.BlockSpec(memory_space=pltpu.VMEM)
ANY = pl.BlockSpec(memory_space=pl.ANY)

ROW, COL, SIB = 0, 1, 2
OWN_ROWS, OTHER_ROWS, OWN_COLS, OTHER_COLS = 3, 9, 15, 21
OWN_PIVOT, OTHER_PIVOT = 27, 31


def f32(*shape):
    return jax.ShapeDtypeStruct(shape, jnp.float32)


def halves(value):
    high = value.astype(jnp.bfloat16)
    low = (value - high.astype(jnp.float32)).astype(jnp.bfloat16)
    return high, low


def times_transpose(left, right):
    def dot(x, y):
        return lax.dot_general(
            x, y, (((1,), (1,)), ((), ())), preferred_element_type=jnp.float32
        )

    return dot(left[0], right[0]) + (dot(left[0], right[1]) + dot(left[1], right[0]))


def rotated(value, axis, steps):
    count = lax.axis_size(axis)
    return lax.ppermute(value, axis, [(i, (i + steps) % count) for i in range(count)])


def swapped(value, axis, mask):
    count = lax.axis_size(axis)
    return lax.ppermute(value, axis, [(i, i ^ mask) for i in range(count)])


def shifted(value, axis):
    count = lax.axis_size(axis)
    return lax.ppermute(value, axis, [(i, i + 1) for i in range(count - 1)])


def shifted_both(value, count):
    pairs = [
        (r * count + c, (r + 1) * count + c + 1)
        for r in range(count - 1)
        for c in range(count - 1)
    ]
    return lax.ppermute(value, ("row", "col"), pairs)


def run_copies(copies):
    for copy in copies:
        copy.start()
    for copy in copies:
        copy.wait()


def span(index, size):
    return pl.ds(pl.multiple_of(index * size, size), size)


def gather_copies(table, pieces, target, sems, size, base=0):
    return [
        pltpu.make_async_copy(piece, target.at[span(table[COL] ^ k, size)], sems.at[base + k])
        for k, piece in enumerate(pieces)
    ]


def window_choice(block_row, group, parent_span):
    padded = jnp.concatenate([jnp.full((HB,), -1, jnp.int32), block_row])
    window = lax.dynamic_slice_in_dim(padded, group * CBD, CBD + HB)
    target = group * parent_span + jnp.arange(parent_span, dtype=jnp.int32)
    places = jnp.arange(1, CBD + HB + 1, dtype=jnp.int32)
    hit = window[None, :] == target[:, None]
    return jnp.sum(jnp.where(hit, places[None, :], 0), axis=1).astype(jnp.int32) - 1


def start_chosen(chosen, choices, target, sem):
    for d, choice in enumerate(choices):

        @pl.when(chosen == d)
        def _():
            pltpu.make_async_copy(choice, target, sem).start()


def turn_of(sc, mask, count):
    return lax.rem(sc[ROW] - (sc[COL] ^ mask) + count, count)


def pivot_product(table, rows, turned, dealt):
    count = len(rows)
    sub, depth = rows[0].shape
    size = count * sub

    def body(*refs):
        sc = refs[0]
        row_refs = refs[1 : 1 + count]
        col_refs = refs[1 + count : 1 + 2 * count]
        deal_refs = refs[1 + 2 * count : 1 + 3 * count]
        out, edge, row_buf, col_buf, front, sems = refs[1 + 3 * count :]
        start_chosen(sc[ROW], col_refs, col_buf, sems.at[count])
        front_parts = [ref.at[pl.ds(0, size)] for ref in deal_refs]
        start_chosen(sc[COL], front_parts, front, sems.at[count + 1])
        run_copies(gather_copies(sc, row_refs, row_buf, sems, sub))
        pltpu.make_async_copy(col_refs[0], col_buf, sems.at[count]).wait()
        pltpu.make_async_copy(front_parts[0], front, sems.at[count + 1]).wait()
        part = front[...] - times_transpose(halves(row_buf[...]), halves(col_buf[...]))
        out[...] = part
        edge[...] = part[-EDGE:]

    return pl.pallas_call(
        body,
        in_specs=[SMEM] + [ANY] * (3 * count),
        out_specs=[VMEM, VMEM],
        out_shape=[f32(size, sub), f32(EDGE, sub)],
        scratch_shapes=[
            pltpu.VMEM((size, depth), jnp.float32),
            pltpu.VMEM((sub, depth), jnp.float32),
            pltpu.VMEM((size, sub), jnp.float32),
            pltpu.SemaphoreType.DMA((count + 2,)),
        ],
        name="pivot_product",
    )(table, *rows, *turned, *dealt)


def update_product(table, rows, turned, cols, front):
    count = len(rows)
    sub, depth = rows[0].shape
    size = count * sub

    def body(*refs):
        sc = refs[0]
        row_refs = refs[1 : 1 + count]
        turn_refs = refs[1 + count : 1 + 2 * count]
        col_refs = refs[1 + 2 * count : 3 * count]
        front_ref, out, right, up, corner, row_buf, col_buf, sems = refs[3 * count :]
        home = col_buf.at[span(sc[COL], sub)]
        start_chosen(turn_of(sc, 0, count), turn_refs, home, sems.at[count])
        copies = gather_copies(sc, row_refs, row_buf, sems, sub)
        copies += [
            pltpu.make_async_copy(
                ref, col_buf.at[span(sc[COL] ^ (k + 1), sub)], sems.at[count + 1 + k]
            )
            for k, ref in enumerate(col_refs)
        ]
        run_copies(copies)
        pltpu.make_async_copy(turn_refs[0], home, sems.at[count]).wait()
        part = front_ref[...] - times_transpose(halves(row_buf[...]), halves(col_buf[...]))
        out[...] = part
        right[...] = part[:, -EDGE:]
        up[...] = part[-EDGE:, :]
        corner[...] = part[-EDGE:, -EDGE:]

    return pl.pallas_call(
        body,
        in_specs=[SMEM] + [ANY] * (3 * count - 1) + [VMEM],
        out_specs=[VMEM] * 4,
        out_shape=[f32(size, size), f32(size, EDGE), f32(EDGE, size), f32(EDGE, EDGE)],
        scratch_shapes=[
            pltpu.VMEM((size, depth), jnp.float32),
            pltpu.VMEM((size, depth), jnp.float32),
            pltpu.SemaphoreType.DMA((2 * count,)),
        ],
        name="update_product",
    )(table, *rows, *turned, *cols, front)


def pick_for_cols(table, pieces, masks):
    count = len(pieces)

    def body(*refs):
        sc = refs[0]
        ins = refs[1 : 1 + count]
        outs = refs[1 + count : -1]
        sems = refs[-1]
        for i, mask in enumerate(masks):
            start_chosen(turn_of(sc, mask, count), ins, outs[i], sems.at[i])
        for i in range(len(masks)):
            pltpu.make_async_copy(ins[0], outs[i], sems.at[i]).wait()

    return pl.pallas_call(
        body,
        in_specs=[SMEM] + [ANY] * count,
        out_specs=[VMEM] * len(masks),
        out_shape=[f32(*pieces[0].shape)] * len(masks),
        scratch_shapes=[pltpu.SemaphoreType.DMA((len(masks),))],
        name="pick_for_cols",
    )(table, *pieces)


def place_rows(table, part, edge):
    size, width = part.shape
    rows = HALF * BLK

    def body(sc, part_ref, edge_ref, keep, send, window):
        window[:EDGE] = edge_ref[...]
        window[EDGE:] = part_ref[...]
        for target, half in ((keep, sc[SIB]), (send, 1 - sc[SIB])):
            for slot in range(HALF):
                place = sc[OWN_ROWS + half * HALF + slot]
                block = window[span(jnp.maximum(place, 0), BLK), :]
                target[slot * BLK : (slot + 1) * BLK, :] = jnp.where(place >= 0, block, 0.0)

    return pl.pallas_call(
        body,
        in_specs=[SMEM, VMEM, VMEM],
        out_specs=[VMEM, VMEM],
        out_shape=[f32(rows, width), f32(rows, width)],
        scratch_shapes=[pltpu.VMEM((size + EDGE, width), jnp.float32)],
        name="place_rows",
    )(table, part, edge)


def factor_slice(table, small, dealt, pivot_inverse):
    count = len(small)
    _, rows, sub = small[0].shape
    total = dealt[0].shape[0]
    below = total - PANEL // sub * rows

    def body(*refs):
        sc = refs[0]
        pieces = refs[1 : 1 + count]
        deal_refs = refs[1 + count : 1 + 2 * count]
        inverse_ref, out, order, child, parent, sums, sems = refs[1 + 2 * count :]
        parent_parts = [ref.at[pl.ds(below, total - below)] for ref in deal_refs]
        start_chosen(sc[COL], parent_parts, parent, sems.at[count])
        run_copies(
            [
                pltpu.make_async_copy(piece, order.at[sc[COL] ^ k], sems.at[k])
                for k, piece in enumerate(pieces)
            ]
        )
        pltpu.make_async_copy(parent_parts[0], parent, sems.at[count]).wait()
        for j in range(count):
            block, lane = divmod(j * sub, BLK)
            for sibling in range(2):
                child[sibling, block, :, lane : lane + sub] = order[j, sibling]
            sums[:, j * sub : (j + 1) * sub] = parent[j * rows : (j + 1) * rows]
        for p in range(PIV):
            lanes = slice(p * BLK, (p + 1) * BLK)
            added = sums[:, lanes]
            for sibling, base in ((0, OWN_PIVOT), (1, OTHER_PIVOT)):
                place = sc[base + p]
                block = child[sibling, jnp.maximum(place - HB, 0)]
                added += jnp.where(place >= HB, block, 0.0)
            sums[:, lanes] = added
        out[...] = times_transpose(halves(sums[...]), halves(inverse_ref[...]))

    return pl.pallas_call(
        body,
        in_specs=[SMEM] + [ANY] * (2 * count) + [VMEM],
        out_specs=VMEM,
        out_shape=f32(rows, PANEL),
        scratch_shapes=[
            pltpu.VMEM((count, 2, rows, sub), jnp.float32),
            pltpu.VMEM((2, PIV, rows, BLK), jnp.float32),
            pltpu.VMEM((total - below, sub), jnp.float32),
            pltpu.VMEM((rows, PANEL), jnp.float32),
            pltpu.SemaphoreType.DMA((count + 1,)),
        ],
        name="factor_slice",
    )(table, *small, *dealt, pivot_inverse)


def finish(table, parent, own, other, row_pieces, col_own, col_other):
    count = len(row_pieces)
    rows, width = parent.shape
    piece_rows = row_pieces[0].shape[0]
    size = own[0].shape[0]

    def body(*refs):
        sc, parent_ref = refs[:2]
        own_refs, other_refs = refs[2:6], refs[6:10]
        row_refs = refs[10 : 10 + count]
        col_own_refs = refs[10 + count : 10 + 2 * count]
        col_other_refs = refs[10 + 2 * count : 10 + 3 * count]
        out = refs[10 + 3 * count]
        own_win, other_win, row_factor, col_factor, products, sems = refs[11 + 3 * count :]
        low, high = slice(0, EDGE), slice(EDGE, EDGE + size)
        factors = gather_copies(sc, row_refs, row_factor, sems, piece_rows)
        factors += gather_copies(
            sc, col_own_refs, col_factor.at[sc[SIB]], sems, piece_rows, count
        )
        factors += gather_copies(
            sc, col_other_refs, col_factor.at[1 - sc[SIB]], sems, piece_rows, 2 * count
        )
        place = 3 * count
        windows = []
        for refs_in, window in ((own_refs, own_win), (other_refs, other_win)):
            spots = ((high, high), (high, low), (low, high), (low, low))
            for ref, (down, across) in zip(refs_in, spots):
                windows.append(
                    pltpu.make_async_copy(ref, window.at[down, across], sems.at[place])
                )
                place += 1
        for copy in factors + windows:
            copy.start()
        for copy in factors:
            copy.wait()
        left = halves(row_factor[...])
        for half in range(2):
            right = halves(col_factor[half])
            products[:, half * rows : (half + 1) * rows] = times_transpose(left, right)
        for copy in windows:
            copy.wait()
        first_row = (sc[ROW] * 2 + sc[SIB]) * HALF
        first_col = sc[COL] * PBD
        for q in range(PBD):
            cols = slice(q * BLK, (q + 1) * BLK)
            col_inside = first_col + q >= PIV
            for p in range(HALF):
                lines = slice(p * BLK, (p + 1) * BLK)
                total = parent_ref[lines, cols]
                for window, row_base, col_base in (
                    (own_win, OWN_ROWS, OWN_COLS),
                    (other_win, OTHER_ROWS, OTHER_COLS),
                ):
                    down = sc[row_base + sc[SIB] * HALF + p]
                    across = sc[col_base + q]
                    block = window[
                        span(jnp.maximum(down, 0), BLK), span(jnp.maximum(across, 0), BLK)
                    ]
                    total += jnp.where((down >= 0) & (across >= 0), block, 0.0)
                inside = col_inside & (first_row + p >= PIV)
                total = jnp.where(inside, total - products[lines, cols], total)
                if q < PIV:
                    total = jnp.where(sc[COL] == 0, row_factor[lines, cols], total)
                out[lines, cols] = total

    return pl.pallas_call(
        body,
        in_specs=[SMEM, VMEM] + [ANY] * (8 + 3 * count),
        out_specs=VMEM,
        out_shape=f32(rows, width),
        scratch_shapes=[
            pltpu.VMEM((size + EDGE, size + EDGE), jnp.float32),
            pltpu.VMEM((size + EDGE, size + EDGE), jnp.float32),
            pltpu.VMEM((rows, PANEL), jnp.float32),
            pltpu.VMEM((2, rows, PANEL), jnp.float32),
            pltpu.VMEM((rows, 2 * rows), jnp.float32),
            pltpu.SemaphoreType.DMA((3 * count + 8,)),
        ],
        name="finish",
    )(table, parent, *own, *other, *row_pieces, *col_own, *col_other)


def shards(child_front, child_panel, block_map, parent_front, pivot_inverse):
    front_index = lax.axis_index("sib")
    row_index = lax.axis_index("row")
    col_index = lax.axis_index("col")
    count = lax.axis_size("col")
    front = child_front[0]
    panel = child_panel[0]
    sub = panel.shape[0]
    parent_rows, parent_cols = parent_front.shape
    parent_span = parent_cols // BLK
    deal = parent_rows // count

    own_map = lax.dynamic_index_in_dim(block_map, front_index, 0, keepdims=False)
    other_map = lax.dynamic_index_in_dim(block_map, 1 - front_index, 0, keepdims=False)
    table = jnp.concatenate(
        [
            jnp.stack([row_index, col_index, front_index]).astype(jnp.int32),
            window_choice(own_map, row_index, parent_span),
            window_choice(other_map, row_index, parent_span),
            window_choice(own_map, col_index, parent_span),
            window_choice(other_map, col_index, parent_span),
            window_choice(own_map, 0, parent_span)[:PIV],
            window_choice(other_map, 0, parent_span)[:PIV],
        ]
    )

    def over_col(values):
        got = []
        for k, value in zip(range(1, count), values):
            got.append(swapped(value, "col", k))
        return got

    def over_row(value):
        got = [value]
        for d in range(1, count):
            got.append(rotated(value, "row", d))
        return got

    def to_sibling(value):
        return swapped(value, "sib", 1)

    turned = over_row(panel)
    rows = [panel] + over_col([panel] * (count - 1))

    dealt = []
    for j in range(count):
        lines = parent_front[j * deal : (j + 1) * deal, :PANEL]
        pieces = [lines[:, i : i + sub] for i in range(0, PANEL, sub)]
        value = jnp.concatenate([front[:, j * sub : (j + 1) * sub]] + pieces, axis=0)
        dealt.append(lax.ppermute(value, "col", [(0, j)]) if j else value)

    part, edge = pivot_product(table, rows, turned, dealt)
    edge = shifted(edge, "row")
    picked = pick_for_cols(table, turned, range(1, count))
    cols = over_col(picked)
    keep, send = place_rows(table, part, edge)
    both = jnp.stack([keep, to_sibling(send)])
    slices = [
        lax.dynamic_slice_in_dim(both, (col_index ^ k) * deal, deal, axis=1)
        for k in range(count)
    ]
    small = [slices[0]] + over_col(slices[1:])
    factor = factor_slice(table, small, dealt, pivot_inverse)
    factors = over_row(factor)
    row_pieces = [factor] + over_col([factor] * (count - 1))

    update, right, up, corner = update_product(table, rows, turned, cols, front)
    right = shifted(right, "col")
    up = shifted(up, "row")
    corner = shifted_both(corner, count)
    own = [update, right, up, corner]

    picked = pick_for_cols(table, factors, range(count))
    col_own = [picked[0]] + over_col(picked[1:])
    col_other = [to_sibling(value) for value in col_own]

    other = [to_sibling(value) for value in own]
    return finish(table, parent_front, own, other, row_pieces, col_own, col_other)


def solution(mesh):
    in_specs = (
        P("sib", "row", "col"),
        P("sib", ("row", "col"), None),
        P(),
        P(("row", "sib"), "col"),
        P(),
    )
    out_specs = P(("row", "sib"), "col")

    return jax.shard_map(shards, mesh=mesh, in_specs=in_specs, out_specs=out_specs, check_vma=False)
```

profile of v0, /device:TPU:0, one launch (start us, length us, event | category | flops | bytes accessed | tf_op | source)
XLA Modules:
  0.0 156.0 jit_solution(8606108715297914347)
XLA Ops:
  0.0 3.1 %collective-permute-start.3 = (f32[128,1024]{1,0:T(8,128)}, f32[128,1024]{1,0:T(8,128)S(1)}, u32[]{:S(2)}, u32[]{:S(2)}) collective-permute-start(f32[128,1024]{1,0:T(8,128)} %bitcast.13), channel_id=1, source_target_pairs={{0,4},{4,8},{8,12},{12,0},{1,5},{5,9},{9,13},{13,1},{2,6},{6,10},{... | collective-permute-start | bytes 1572872 | tf_op jit(solution)/shard_map/ppermute | solution.py:49
  3.1 2.6 %collective-permute-start.4 = (f32[128,1024]{1,0:T(8,128)}, f32[128,1024]{1,0:T(8,128)S(1)}, u32[]{:S(2)}, u32[]{:S(2)}) collective-permute-start(f32[128,1024]{1,0:T(8,128)} %bitcast.14), channel_id=1, source_target_pairs={{0,8},{4,12},{8,0},{12,4},{1,9},{5,13},{9,1},{13,5},{2,10},{6,14},... | collective-permute-start | bytes 1572872 | tf_op jit(solution)/shard_map/ppermute | solution.py:49
  5.6 1.3 slice_dynamic-update-slice_fusion
  7.1 4.3 %collective-permute-start.16 = (f32[896,128]{1,0:T(8,128)S(1)}, f32[896,128]{1,0:T(8,128)}, u32[]{:S(2)}, u32[]{:S(2)}) collective-permute-start(f32[896,128]{1,0:T(8,128)S(1)} %get-tuple-element.47), channel_id=1, source_target_pairs={{0,1},{4,5},{8,9},{12,13},{16,17},{20,21},{24,25},{28,29}} | collective-permute-start | bytes 1376264 | tf_op jit(solution)/shard_map/ppermute | solution.py:416
  11.4 2.1 %collective-permute-start.17 = (f32[896,128]{1,0:T(8,128)S(1)}, f32[896,128]{1,0:T(8,128)}, u32[]{:S(2)}, u32[]{:S(2)}) collective-permute-start(f32[896,128]{1,0:T(8,128)S(1)} %get-tuple-element.46), channel_id=1, source_target_pairs={{0,2},{4,6},{8,10},{12,14},{16,18},{20,22},{24,26},{28,30}} | collective-permute-start | bytes 1376264 | tf_op jit(solution)/shard_map/ppermute | solution.py:416
  13.5 2.1 %collective-permute-start.18 = (f32[896,128]{1,0:T(8,128)S(1)}, f32[896,128]{1,0:T(8,128)}, u32[]{:S(2)}, u32[]{:S(2)}) collective-permute-start(f32[896,128]{1,0:T(8,128)S(1)} %get-tuple-element.45), channel_id=1, source_target_pairs={{0,3},{4,7},{8,11},{12,15},{16,19},{20,23},{24,27},{28,31}} | collective-permute-start | bytes 1376264 | tf_op jit(solution)/shard_map/ppermute | solution.py:416
  15.6 0.1 pad_dynamic-slice_fusion.9
  15.7 0.3 select_reduce_fusion.2
  16.0 5.5 %collective-permute-done.16.refs_10_.refs_6_ = f32[896,128]{1,0:T(8,128)} collective-permute-done((f32[896,128]{1,0:T(8,128)S(1)}, f32[896,128]{1,0:T(8,128)}, u32[]{:S(2)}, u32[]{:S(2)}) %collective-permute-start.16) | collective-permute-done | bytes 458784 | tf_op jit(solution)/shard_map/ppermute | solution.py:416
  21.5 1.3 collective-permute-start.5
  22.9 2.6 %collective-permute-start = (f32[128,1024]{1,0:T(8,128)S(1)}, f32[128,1024]{1,0:T(8,128)S(1)}, u32[]{:S(2)}, u32[]{:S(2)}) collective-permute-start(f32[128,1024]{1,0:T(8,128)S(1)} %bitcast.21), channel_id=1, source_target_pairs={{0,1},{1,0},{2,3},{3,2},{4,5},{5,4},{6,7},{7,6},{8,9},{9,8},{10,11... | collective-permute-start | bytes 1572872 | tf_op jit(solution)/shard_map/ppermute | solution.py:54
  25.4 5.9 %collective-permute-done.18.refs_12_.refs_8_ = f32[896,128]{1,0:T(8,128)} collective-permute-done((f32[896,128]{1,0:T(8,128)S(1)}, f32[896,128]{1,0:T(8,128)}, u32[]{:S(2)}, u32[]{:S(2)}) %collective-permute-start.18) | collective-permute-done | bytes 458784 | tf_op jit(solution)/shard_map/ppermute | solution.py:416
  31.3 3.6 %collective-permute-start.2 = (f32[128,1024]{1,0:T(8,128)S(1)}, f32[128,1024]{1,0:T(8,128)}, u32[]{:S(2)}, u32[]{:S(2)}) collective-permute-start(f32[128,1024]{1,0:T(8,128)S(1)} %bitcast.23), channel_id=1, source_target_pairs={{0,3},{1,2},{2,1},{3,0},{4,7},{5,6},{6,5},{7,4},{8,11},{9,10},{10,... | collective-permute-start | bytes 1572872 | tf_op jit(solution)/shard_map/ppermute | solution.py:54
  34.9 0.6 concatenate.27.refs_0_.sc
  35.5 4.3 %collective-permute-done.4.refs_3_.refs_7_ = f32[128,1024]{1,0:T(8,128)S(1)} collective-permute-done((f32[128,1024]{1,0:T(8,128)}, f32[128,1024]{1,0:T(8,128)S(1)}, u32[]{:S(2)}, u32[]{:S(2)}) %collective-permute-start.4) | collective-permute-done | bytes 524320 | tf_op jit(solution)/shard_map/ppermute | solution.py:49
  39.8 3.4 %collective-permute-done.5.refs_4_.refs_8_ = f32[128,1024]{1,0:T(8,128)S(1)} collective-permute-done((f32[128,1024]{1,0:T(8,128)S(1)}, f32[128,1024]{1,0:T(8,128)S(1)}, u32[]{:S(2)}, u32[]{:S(2)}) %collective-permute-start.5) | collective-permute-done | bytes 524320 | tf_op jit(solution)/shard_map/ppermute | solution.py:49
  43.2 9.9 %collective-permute-done.1.refs_3_ = f32[128,1024]{1,0:T(8,128)S(1)} collective-permute-done((f32[128,1024]{1,0:T(8,128)S(1)}, f32[128,1024]{1,0:T(8,128)S(1)}, u32[]{:S(2)}, u32[]{:S(2)}) %collective-permute-start.1) | collective-permute-done | bytes 524320 | tf_op jit(solution)/shard_map/ppermute | solution.py:54
  53.2 0.8 copy-done.7
  53.9 4.2 %pivot_product.1 = (f32[512,128]{1,0:T(8,128)}, f32[256,128]{1,0:T(8,128)}) custom-call(s32[35]{0:T(128)} %concatenate.27.refs_0_.sc, f32[128,1024]{1,0:T(8,128)} %bitcast.15, f32[128,1024]{1,0:T(8,128)} %copy-done.6, f32[128,1024]{1,0:T(8,128)} %copy-done.7, f32[128,1024]{1,0:T(8,128)} %collective-permute-done.2.refs_4_, f32[128,1024]{1,0:T(8,128)} %bitcast.16, ...), custom_call_target="tpu_custom_call" | custom-call | tf_op jit(solution)/shard_map/pivot_product/pallas_call | solution.py:131
  58.1 2.4 %collective-permute-start.19 = (f32[256,128]{1,0:T(8,128)}, f32[256,128]{1,0:T(8,128)S(1)}, u32[]{:S(2)}, u32[]{:S(2)}) collective-permute-start(f32[256,128]{1,0:T(8,128)} %get-tuple-element.28), channel_id=1, source_target_pairs={{0,4},{4,8},{8,12},{1,5},{5,9},{9,13},{2,6},{6,10},{10,14},{3,7},{... | collective-permute-start | bytes 393224 | tf_op jit(solution)/shard_map/ppermute | solution.py:59
  60.5 3.2 %pick_for_cols.2 = (f32[128,1024]{1,0:T(8,128)}, f32[128,1024]{1,0:T(8,128)}, f32[128,1024]{1,0:T(8,128)}) custom-call(s32[35]{0:T(128)} %concatenate.27.refs_0_.sc, f32[128,1024]{1,0:T(8,128)} %bitcast.17, f32[128,1024]{1,0:T(8,128)} %copy-done.1, f32[128,1024]{1,0:T(8,128)} %copy-done.2, f32[128,1024]{1,0:T(8,128)} %copy-done.3), custom_call_target="tpu_custom_call" | custom-call | tf_op jit(solution)/shard_map/pick_for_cols/pallas_call | solution.py:201
  63.7 2.4 %collective-permute-start.6 = (f32[128,1024]{1,0:T(8,128)}, f32[128,1024]{1,0:T(8,128)S(1)}, u32[]{:S(2)}, u32[]{:S(2)}) collective-permute-start(f32[128,1024]{1,0:T(8,128)} %get-tuple-element.20), channel_id=1, source_target_pairs={{0,1},{1,0},{2,3},{3,2},{4,5},{5,4},{6,7},{7,6},{8,9},{9,8},{10,11... | collective-permute-start | bytes 1572872 | tf_op jit(solution)/shard_map/ppermute | solution.py:54
  66.1 1.9 %collective-permute-start.7 = (f32[128,1024]{1,0:T(8,128)}, f32[128,1024]{1,0:T(8,128)S(1)}, u32[]{:S(2)}, u32[]{:S(2)}) collective-permute-start(f32[128,1024]{1,0:T(8,128)} %get-tuple-element.21), channel_id=1, source_target_pairs={{0,2},{1,3},{2,0},{3,1},{4,6},{5,7},{6,4},{7,5},{8,10},{9,11},{10,... | collective-permute-start | bytes 1572872 | tf_op jit(solution)/shard_map/ppermute | solution.py:54
  68.0 0.6 copy-done.31
  68.7 1.8 %place_rows.1 = (f32[384,128]{1,0:T(8,128)}, f32[384,128]{1,0:T(8,128)}) custom-call(s32[35]{0:T(128)} %concatenate.27.refs_0_.sc, f32[512,128]{1,0:T(8,128)} %get-tuple-element.27.part_ref, f32[256,128]{1,0:T(8,128)} %copy-done.31), custom_call_target="tpu_custom_call" | custom-call | tf_op jit(solution)/shard_map/place_rows/pallas_call | solution.py:224
  70.5 1.6 %collective-permute-done.20 = f32[384,128]{1,0:T(8,128)S(1)} collective-permute-done((f32[384,128]{1,0:T(8,128)}, f32[384,128]{1,0:T(8,128)S(1)}, u32[]{:S(2)}, u32[]{:S(2)}) %collective-permute-start.20) | collective-permute-done | bytes 196640 | tf_op jit(solution)/shard_map/ppermute | solution.py:54
  72.1 1.5 fusion
  73.6 1.6 %collective-permute-start.21 = (f32[2,96,128]{2,1,0:T(8,128)S(1)}, f32[2,96,128]{2,1,0:T(8,128)S(1)}, u32[]{:S(2)}, u32[]{:S(2)}) collective-permute-start(f32[2,96,128]{2,1,0:T(8,128)S(1)} %get-tuple-element.67), channel_id=1, source_target_pairs={{0,1},{1,0},{2,3},{3,2},{4,5},{5,4},{6,7},{7,6},{8,9},{9,8},{10,11... | collective-permute-start | bytes 294920 | tf_op jit(solution)/shard_map/ppermute | solution.py:54
  75.2 1.9 %collective-permute-start.22 = (f32[2,96,128]{2,1,0:T(8,128)S(1)}, f32[2,96,128]{2,1,0:T(8,128)S(1)}, u32[]{:S(2)}, u32[]{:S(2)}) collective-permute-start(f32[2,96,128]{2,1,0:T(8,128)S(1)} %get-tuple-element.68), channel_id=1, source_target_pairs={{0,2},{1,3},{2,0},{3,1},{4,6},{5,7},{6,4},{7,5},{8,10},{9,11},{10,... | collective-permute-start | bytes 294920 | tf_op jit(solution)/shard_map/ppermute | solution.py:54
  77.1 12.1 %collective-permute-done.21.refs_2_ = f32[2,96,128]{2,1,0:T(8,128)S(1)} collective-permute-done((f32[2,96,128]{2,1,0:T(8,128)S(1)}, f32[2,96,128]{2,1,0:T(8,128)S(1)}, u32[]{:S(2)}, u32[]{:S(2)}) %collective-permute-start.21) | collective-permute-done | bytes 98336 | tf_op jit(solution)/shard_map/ppermute | solution.py:54
  89.2 3.6 %collective-permute-start.23 = (f32[2,96,128]{2,1,0:T(8,128)S(1)}, f32[2,96,128]{2,1,0:T(8,128)S(1)}, u32[]{:S(2)}, u32[]{:S(2)}) collective-permute-start(f32[2,96,128]{2,1,0:T(8,128)S(1)} %get-tuple-element.65), channel_id=1, source_target_pairs={{0,3},{1,2},{2,1},{3,0},{4,7},{5,6},{6,5},{7,4},{8,11},{9,10},{10,... | collective-permute-start | bytes 294920 | tf_op jit(solution)/shard_map/ppermute | solution.py:54
  92.9 2.6 %collective-permute-done.23.refs_4_ = f32[2,96,128]{2,1,0:T(8,128)S(1)} collective-permute-done((f32[2,96,128]{2,1,0:T(8,128)S(1)}, f32[2,96,128]{2,1,0:T(8,128)S(1)}, u32[]{:S(2)}, u32[]{:S(2)}) %collective-permute-start.23) | collective-permute-done | bytes 98336 | tf_op jit(solution)/shard_map/ppermute | solution.py:54
  95.5 0.6 copy-done.34
  96.1 3.7 %factor_slice.1.refs_1_.refs_10_ = f32[96,512]{1,0:T(8,128)} custom-call(s32[35]{0:T(128)} %concatenate.27.refs_0_.sc, f32[2,96,128]{2,1,0:T(8,128)} %get-tuple-element.66.refs_1_, f32[2,96,128]{2,1,0:T(8,128)} %copy-done.32, f32[2,96,128]{2,1,0:T(8,128)} %copy-done.33, f32[2,96,128]{2,1,0:T(8,128)} %copy-done.34, f32[896,128]{1,0:T(8,128)} %copy-done.5, ...), custom_call_target="tpu_custom_call" | custom-call | tf_op jit(solution)/shard_map/factor_slice/pallas_call | solution.py:269
  99.8 0.3 collective-permute-start.27
  100.1 0.6 collective-permute-start.28
  100.8 3.0 %collective-permute-start.29 = (f32[96,512]{1,0:T(8,128)}, f32[96,512]{1,0:T(8,128)S(1)}, u32[]{:S(2)}, u32[]{:S(2)}) collective-permute-start(f32[96,512]{1,0:T(8,128)} %factor_slice.1.refs_1_.refs_10_), channel_id=1, source_target_pairs={{0,12},{4,0},{8,4},{12,8},{1,13},{5,1},{9,5},{13,9},{2,14},{6,2},{... | collective-permute-start | bytes 589832 | tf_op jit(solution)/shard_map/ppermute | solution.py:49
  103.7 1.8 %collective-permute-start.24 = (f32[96,512]{1,0:T(8,128)}, f32[96,512]{1,0:T(8,128)S(1)}, u32[]{:S(2)}, u32[]{:S(2)}) collective-permute-start(f32[96,512]{1,0:T(8,128)} %factor_slice.1.refs_1_.refs_10_), channel_id=1, source_target_pairs={{0,1},{1,0},{2,3},{3,2},{4,5},{5,4},{6,7},{7,6},{8,9},{9,8},{10,11... | collective-permute-start | bytes 589832 | tf_op jit(solution)/shard_map/ppermute | solution.py:54
  105.5 1.7 %collective-permute-start.25 = (f32[96,512]{1,0:T(8,128)}, f32[96,512]{1,0:T(8,128)S(1)}, u32[]{:S(2)}, u32[]{:S(2)}) collective-permute-start(f32[96,512]{1,0:T(8,128)} %factor_slice.1.refs_1_.refs_10_), channel_id=1, source_target_pairs={{0,2},{1,3},{2,0},{3,1},{4,6},{5,7},{6,4},{7,5},{8,10},{9,11},{10,... | collective-permute-start | bytes 589832 | tf_op jit(solution)/shard_map/ppermute | solution.py:54
  107.2 6.7 %update_product.1 = (f32[512,512]{1,0:T(8,128)}, f32[512,256]{1,0:T(8,128)}, f32[256,512]{1,0:T(8,128)}, f32[256,256]{1,0:T(8,128)}) custom-call(s32[35]{0:T(128)} %concatenate.27.refs_0_.sc, f32[128,1024]{1,0:T(8,128)} %bitcast.18, f32[128,1024]{1,0:T(8,128)} %copy-done.6, f32[128,1024]{1,0:T(8,128)} %copy-done.7, ...), custom_call_target="tpu_custom_call" | custom-call | tf_op jit(solution)/shard_map/update_product/pallas_call | solution.py:174
  114.0 2.0 %collective-permute-start.11 = (f32[256,256]{1,0:T(8,128)}, f32[256,256]{1,0:T(8,128)S(1)}, u32[]{:S(2)}, u32[]{:S(2)}) collective-permute-start(f32[256,256]{1,0:T(8,128)} %get-tuple-element.26), channel_id=1, source_target_pairs={{0,5},{1,6},{2,7},{4,9},{5,10},{6,11},{8,13},{9,14},{10,15},{16,21... | collective-permute-start | bytes 786440 | tf_op jit(solution)/shard_map/ppermute | solution.py:68
  116.1 0.1 collective-permute-start.26
  116.2 4.3 %collective-permute-start.9 = (f32[512,256]{1,0:T(8,128)}, f32[512,256]{1,0:T(8,128)S(1)}, u32[]{:S(2)}, u32[]{:S(2)}) collective-permute-start(f32[512,256]{1,0:T(8,128)} %get-tuple-element.24), channel_id=1, source_target_pairs={{0,1},{1,2},{2,3},{4,5},{5,6},{6,7},{8,9},{9,10},{10,11},{12,13},{... | collective-permute-start | bytes 1572872 | tf_op jit(solution)/shard_map/ppermute | solution.py:59
  120.5 3.7 %collective-permute-start.10 = (f32[256,512]{1,0:T(8,128)}, f32[256,512]{1,0:T(8,128)S(1)}, u32[]{:S(2)}, u32[]{:S(2)}) collective-permute-start(f32[256,512]{1,0:T(8,128)} %get-tuple-element.25), channel_id=1, source_target_pairs={{0,4},{4,8},{8,12},{1,5},{5,9},{9,13},{2,6},{6,10},{10,14},{3,7},{... | collective-permute-start | bytes 1572872 | tf_op jit(solution)/shard_map/ppermute | solution.py:59
  124.3 0.7 copy-done.23
  125.0 2.9 %pick_for_cols.3 = (f32[96,512]{1,0:T(8,128)}, f32[96,512]{1,0:T(8,128)}, f32[96,512]{1,0:T(8,128)}, f32[96,512]{1,0:T(8,128)}) custom-call(s32[35]{0:T(128)} %concatenate.27.refs_0_.sc, f32[96,512]{1,0:T(8,128)} %factor_slice.1.refs_1_.refs_10_, f32[96,512]{1,0:T(8,128)} %copy-done.19, f32[96,512]{1,0:T(8,128)} %copy-done.20, f32[96,512]{1,0:T(8,128)} %copy-done.21), custom_call_target="tpu_custom_call" | custom-call | tf_op jit(solution)/shard_map/pick_for_cols/pallas_call | solution.py:201
  127.8 2.8 %collective-permute-start.30 = (f32[96,512]{1,0:T(8,128)}, f32[96,512]{1,0:T(8,128)S(1)}, u32[]{:S(2)}, u32[]{:S(2)}) collective-permute-start(f32[96,512]{1,0:T(8,128)} %get-tuple-element.32), channel_id=1, source_target_pairs={{0,1},{1,0},{2,3},{3,2},{4,5},{5,4},{6,7},{7,6},{8,9},{9,8},{10,11... | collective-permute-start | bytes 589832 | tf_op jit(solution)/shard_map/ppermute | solution.py:54
  130.6 5.8 %collective-permute-done.30.refs_15_ = f32[96,512]{1,0:T(8,128)S(1)} collective-permute-done((f32[96,512]{1,0:T(8,128)}, f32[96,512]{1,0:T(8,128)S(1)}, u32[]{:S(2)}, u32[]{:S(2)}) %collective-permute-start.30) | collective-permute-done | bytes 196640 | tf_op jit(solution)/shard_map/ppermute | solution.py:54
  136.4 1.5 collective-permute-done.31.refs_16_
  137.9 0.5 collective-permute-start.13
  138.4 0.1 collective-permute-start.14
  138.5 5.7 %collective-permute-done.32.refs_17_ = f32[96,512]{1,0:T(8,128)S(1)} collective-permute-done((f32[96,512]{1,0:T(8,128)}, f32[96,512]{1,0:T(8,128)S(1)}, u32[]{:S(2)}, u32[]{:S(2)}) %collective-permute-start.32) | collective-permute-done | bytes 196640 | tf_op jit(solution)/shard_map/ppermute | solution.py:54
  144.3 0.5 collective-permute-start.35
  144.8 0.9 collective-permute-done.34.refs_19_
  145.7 0.1 collective-permute-start.15
  145.8 0.1 collective-permute-done.35.refs_20_
  146.0 0.2 collective-permute-start.36
  146.2 1.3 collective-permute-done.36.refs_21_
  147.6 0.6 copy-done.30
  148.2 0.1 copy-done.18
  148.3 0.2 copy-done.12
  148.5 0.6 copy-done.13
  149.1 1.0 copy-done.9
  150.1 5.9 %finish.1 = f32[384,768]{1,0:T(8,128)} custom-call(s32[35]{0:T(128)} %concatenate.27.refs_0_.sc, f32[384,768]{1,0:T(8,128)} %refs_1_.1, f32[512,512]{1,0:T(8,128)} %get-tuple-element.23.refs_2_, f32[512,256]{1,0:T(8,128)} %copy-done.10, f32[256,512]{1,0:T(8,128)} %copy-done.11, f32[256,256]{1,0:T(8,128)} %copy-done.17, f32[512,512]{1,0:T(8,128)} %copy-done.9, ...), custom_call_target="tpu_custom_call" | custom-call | tf_op jit(solution)/shard_map/finish/pallas_call | solution.py:350
  (107 shorter events, 0.3 us)
Async XLA Ops:
  0.0 7.0 %copy-start.4 = (f32[384,768]{1,0:T(8,128)S(1)}, f32[384,768]{1,0:T(8,128)}, u32[]{:S(2)}) copy-start(f32[384,768]{1,0:T(8,128)} %refs_1_.1) | copy-start | bytes 3538948
  0.0 31.3 %collective-permute-start.3 = (f32[128,1024]{1,0:T(8,128)}, f32[128,1024]{1,0:T(8,128)S(1)}, u32[]{:S(2)}, u32[]{:S(2)}) collective-permute-start(f32[128,1024]{1,0:T(8,128)} %bitcast.13), channel_id=1, source_target_pairs={{0,4},{4,8},{8,12},{12,0},{1,5},{5,9},{9,13},{13,1},{2,6},{6,10},{... | collective-permute-start | bytes 1572872 | tf_op jit(solution)/shard_map/ppermute | solution.py:49
  3.1 36.8 %collective-permute-start.4 = (f32[128,1024]{1,0:T(8,128)}, f32[128,1024]{1,0:T(8,128)S(1)}, u32[]{:S(2)}, u32[]{:S(2)}) collective-permute-start(f32[128,1024]{1,0:T(8,128)} %bitcast.14), channel_id=1, source_target_pairs={{0,8},{4,12},{8,0},{12,4},{1,9},{5,13},{9,1},{13,5},{2,10},{6,14},... | collective-permute-start | bytes 1572872 | tf_op jit(solution)/shard_map/ppermute | solution.py:49
  6.9 8.6 %copy-start.35 = (s32[2,16]{1,0:T(2,128)S(1)}, s32[2,16]{1,0:T(2,128)}, u32[]{:S(2)}) copy-start(s32[2,16]{1,0:T(2,128)} %param.7) | copy-start | bytes 388
  6.9 14.6 %copy-start = (f32[1,128,1024]{2,1,0:T(8,128)S(1)}, f32[1,128,1024]{2,1,0:T(8,128)}, u32[]{:S(2)}) copy-start(f32[1,128,1024]{2,1,0:T(8,128)} %param.6) | copy-start | bytes 1572868
  7.1 8.9 %copy-start.5 = (f32[896,128]{1,0:T(8,128)}, f32[896,128]{1,0:T(8,128)S(1)}, u32[]{:S(2)}) copy-start(f32[896,128]{1,0:T(8,128)S(1)} %get-tuple-element.48.refs_9_.refs_5_) | copy-start | bytes 1376260
  7.1 14.4 %collective-permute-start.16 = (f32[896,128]{1,0:T(8,128)S(1)}, f32[896,128]{1,0:T(8,128)}, u32[]{:S(2)}, u32[]{:S(2)}) collective-permute-start(f32[896,128]{1,0:T(8,128)S(1)} %get-tuple-element.47), channel_id=1, source_target_pairs={{0,1},{4,5},{8,9},{12,13},{16,17},{20,21},{24,25},{28,29}} | collective-permute-start | bytes 1376264 | tf_op jit(solution)/shard_map/ppermute | solution.py:416
  11.4 11.5 %collective-permute-start.17 = (f32[896,128]{1,0:T(8,128)S(1)}, f32[896,128]{1,0:T(8,128)}, u32[]{:S(2)}, u32[]{:S(2)}) collective-permute-start(f32[896,128]{1,0:T(8,128)S(1)} %get-tuple-element.46), channel_id=1, source_target_pairs={{0,2},{4,6},{8,10},{12,14},{16,18},{20,22},{24,26},{28,30}} | collective-permute-start | bytes 1376264 | tf_op jit(solution)/shard_map/ppermute | solution.py:416
  13.5 17.9 %collective-permute-start.18 = (f32[896,128]{1,0:T(8,128)S(1)}, f32[896,128]{1,0:T(8,128)}, u32[]{:S(2)}, u32[]{:S(2)}) collective-permute-start(f32[896,128]{1,0:T(8,128)S(1)} %get-tuple-element.45), channel_id=1, source_target_pairs={{0,3},{4,7},{8,11},{12,15},{16,19},{20,23},{24,27},{28,31}} | collective-permute-start | bytes 1376264 | tf_op jit(solution)/shard_map/ppermute | solution.py:416
  21.5 21.7 %collective-permute-start.5 = (f32[128,1024]{1,0:T(8,128)S(1)}, f32[128,1024]{1,0:T(8,128)S(1)}, u32[]{:S(2)}, u32[]{:S(2)}) collective-permute-start(f32[128,1024]{1,0:T(8,128)S(1)} %bitcast.20), channel_id=1, source_target_pairs={{0,12},{4,0},{8,4},{12,8},{1,13},{5,1},{9,5},{13,9},{2,14},{6,2},{... | collective-permute-start | bytes 1572872 | tf_op jit(solution)/shard_map/ppermute | solution.py:49
  22.9 20.3 %collective-permute-start = (f32[128,1024]{1,0:T(8,128)S(1)}, f32[128,1024]{1,0:T(8,128)S(1)}, u32[]{:S(2)}, u32[]{:S(2)}) collective-permute-start(f32[128,1024]{1,0:T(8,128)S(1)} %bitcast.21), channel_id=1, source_target_pairs={{0,1},{1,0},{2,3},{3,2},{4,5},{5,4},{6,7},{7,6},{8,9},{9,8},{10,11... | collective-permute-start | bytes 1572872 | tf_op jit(solution)/shard_map/ppermute | solution.py:54
  31.3 21.8 %collective-permute-start.1 = (f32[128,1024]{1,0:T(8,128)S(1)}, f32[128,1024]{1,0:T(8,128)S(1)}, u32[]{:S(2)}, u32[]{:S(2)}) collective-permute-start(f32[128,1024]{1,0:T(8,128)S(1)} %bitcast.22), channel_id=1, source_target_pairs={{0,2},{1,3},{2,0},{3,1},{4,6},{5,7},{6,4},{7,5},{8,10},{9,11},{10,... | collective-permute-start | bytes 1572872 | tf_op jit(solution)/shard_map/ppermute | solution.py:54
  31.3 21.8 %copy-start.1 = (f32[128,1024]{1,0:T(8,128)}, f32[128,1024]{1,0:T(8,128)S(1)}, u32[]{:S(2)}) copy-start(f32[128,1024]{1,0:T(8,128)S(1)} %collective-permute-done.3.refs_2_.refs_6_) | copy-start | bytes 1572868
  31.3 21.8 %collective-permute-start.2 = (f32[128,1024]{1,0:T(8,128)S(1)}, f32[128,1024]{1,0:T(8,128)}, u32[]{:S(2)}, u32[]{:S(2)}) collective-permute-start(f32[128,1024]{1,0:T(8,128)S(1)} %bitcast.23), channel_id=1, source_target_pairs={{0,3},{1,2},{2,1},{3,0},{4,7},{5,6},{6,5},{7,4},{8,11},{9,10},{10,... | collective-permute-start | bytes 1572872 | tf_op jit(solution)/shard_map/ppermute | solution.py:54
  39.8 13.3 %copy-start.2 = (f32[128,1024]{1,0:T(8,128)}, f32[128,1024]{1,0:T(8,128)S(1)}, u32[]{:S(2)}) copy-start(f32[128,1024]{1,0:T(8,128)S(1)} %collective-permute-done.4.refs_3_.refs_7_) | copy-start | bytes 1572868
  43.2 9.9 %copy-start.3 = (f32[128,1024]{1,0:T(8,128)}, f32[128,1024]{1,0:T(8,128)S(1)}, u32[]{:S(2)}) copy-start(f32[128,1024]{1,0:T(8,128)S(1)} %collective-permute-done.5.refs_4_.refs_8_) | copy-start | bytes 1572868
  43.2 10.0 %copy-start.6 = (f32[128,1024]{1,0:T(8,128)}, f32[128,1024]{1,0:T(8,128)S(1)}, u32[]{:S(2)}) copy-start(f32[128,1024]{1,0:T(8,128)S(1)} %collective-permute-done.refs_2_) | copy-start | bytes 1572868
  58.1 9.9 %collective-permute-start.19 = (f32[256,128]{1,0:T(8,128)}, f32[256,128]{1,0:T(8,128)S(1)}, u32[]{:S(2)}, u32[]{:S(2)}) collective-permute-start(f32[256,128]{1,0:T(8,128)} %get-tuple-element.28), channel_id=1, source_target_pairs={{0,4},{4,8},{8,12},{1,5},{5,9},{9,13},{2,6},{6,10},{10,14},{3,7},{... | collective-permute-start | bytes 393224 | tf_op jit(solution)/shard_map/ppermute | solution.py:59
  63.7 37.0 %collective-permute-start.6 = (f32[128,1024]{1,0:T(8,128)}, f32[128,1024]{1,0:T(8,128)S(1)}, u32[]{:S(2)}, u32[]{:S(2)}) collective-permute-start(f32[128,1024]{1,0:T(8,128)} %get-tuple-element.20), channel_id=1, source_target_pairs={{0,1},{1,0},{2,3},{3,2},{4,5},{5,4},{6,7},{7,6},{8,9},{9,8},{10,11... | collective-permute-start | bytes 1572872 | tf_op jit(solution)/shard_map/ppermute | solution.py:54
  66.1 37.6 %collective-permute-start.7 = (f32[128,1024]{1,0:T(8,128)}, f32[128,1024]{1,0:T(8,128)S(1)}, u32[]{:S(2)}, u32[]{:S(2)}) collective-permute-start(f32[128,1024]{1,0:T(8,128)} %get-tuple-element.21), channel_id=1, source_target_pairs={{0,2},{1,3},{2,0},{3,1},{4,6},{5,7},{6,4},{7,5},{8,10},{9,11},{10,... | collective-permute-start | bytes 1572872 | tf_op jit(solution)/shard_map/ppermute | solution.py:54
  68.0 37.5 %collective-permute-start.8 = (f32[128,1024]{1,0:T(8,128)}, f32[128,1024]{1,0:T(8,128)S(1)}, u32[]{:S(2)}, u32[]{:S(2)}) collective-permute-start(f32[128,1024]{1,0:T(8,128)} %get-tuple-element.22), channel_id=1, source_target_pairs={{0,3},{1,2},{2,1},{3,0},{4,7},{5,6},{6,5},{7,4},{8,11},{9,10},{10,... | collective-permute-start | bytes 1572872 | tf_op jit(solution)/shard_map/ppermute | solution.py:54
  70.5 1.7 %collective-permute-start.20 = (f32[384,128]{1,0:T(8,128)}, f32[384,128]{1,0:T(8,128)S(1)}, u32[]{:S(2)}, u32[]{:S(2)}) collective-permute-start(f32[384,128]{1,0:T(8,128)} %get-tuple-element.30), channel_id=1, source_target_pairs={{0,16},{16,0},{1,17},{17,1},{2,18},{18,2},{3,19},{19,3},{4,20},{20... | collective-permute-start | bytes 589832 | tf_op jit(solution)/shard_map/ppermute | solution.py:54
  73.6 15.6 %collective-permute-start.21 = (f32[2,96,128]{2,1,0:T(8,128)S(1)}, f32[2,96,128]{2,1,0:T(8,128)S(1)}, u32[]{:S(2)}, u32[]{:S(2)}) collective-permute-start(f32[2,96,128]{2,1,0:T(8,128)S(1)} %get-tuple-element.67), channel_id=1, source_target_pairs={{0,1},{1,0},{2,3},{3,2},{4,5},{5,4},{6,7},{7,6},{8,9},{9,8},{10,11... | collective-permute-start | bytes 294920 | tf_op jit(solution)/shard_map/ppermute | solution.py:54
  75.2 17.6 %collective-permute-start.22 = (f32[2,96,128]{2,1,0:T(8,128)S(1)}, f32[2,96,128]{2,1,0:T(8,128)S(1)}, u32[]{:S(2)}, u32[]{:S(2)}) collective-permute-start(f32[2,96,128]{2,1,0:T(8,128)S(1)} %get-tuple-element.68), channel_id=1, source_target_pairs={{0,2},{1,3},{2,0},{3,1},{4,6},{5,7},{6,4},{7,5},{8,10},{9,11},{10,... | collective-permute-start | bytes 294920 | tf_op jit(solution)/shard_map/ppermute | solution.py:54
  89.2 6.2 %copy-start.32 = (f32[2,96,128]{2,1,0:T(8,128)}, f32[2,96,128]{2,1,0:T(8,128)S(1)}, u32[]{:S(2)}) copy-start(f32[2,96,128]{2,1,0:T(8,128)S(1)} %collective-permute-done.21.refs_2_) | copy-start | bytes 294916
  89.2 6.2 %collective-permute-start.23 = (f32[2,96,128]{2,1,0:T(8,128)S(1)}, f32[2,96,128]{2,1,0:T(8,128)S(1)}, u32[]{:S(2)}, u32[]{:S(2)}) collective-permute-start(f32[2,96,128]{2,1,0:T(8,128)S(1)} %get-tuple-element.65), channel_id=1, source_target_pairs={{0,3},{1,2},{2,1},{3,0},{4,7},{5,6},{6,5},{7,4},{8,11},{9,10},{10,... | collective-permute-start | bytes 294920 | tf_op jit(solution)/shard_map/ppermute | solution.py:54
  92.9 2.6 %copy-start.33 = (f32[2,96,128]{2,1,0:T(8,128)}, f32[2,96,128]{2,1,0:T(8,128)S(1)}, u32[]{:S(2)}) copy-start(f32[2,96,128]{2,1,0:T(8,128)S(1)} %collective-permute-done.22.refs_3_) | copy-start | bytes 294916
  99.8 16.3 %copy-start.8 = (f32[96,512]{1,0:T(8,128)S(1)}, f32[96,512]{1,0:T(8,128)}, u32[]{:S(2)}) copy-start(f32[96,512]{1,0:T(8,128)} %factor_slice.1.refs_1_.refs_10_) | copy-start | bytes 589828
  99.8 14.2 %collective-permute-start.27 = (f32[96,512]{1,0:T(8,128)}, f32[96,512]{1,0:T(8,128)S(1)}, u32[]{:S(2)}, u32[]{:S(2)}) collective-permute-start(f32[96,512]{1,0:T(8,128)} %factor_slice.1.refs_1_.refs_10_), channel_id=1, source_target_pairs={{0,4},{4,8},{8,12},{12,0},{1,5},{5,9},{9,13},{13,1},{2,6},{6,10},{... | collective-permute-start | bytes 589832 | tf_op jit(solution)/shard_map/ppermute | solution.py:49
  100.1 15.9 %collective-permute-start.28 = (f32[96,512]{1,0:T(8,128)}, f32[96,512]{1,0:T(8,128)S(1)}, u32[]{:S(2)}, u32[]{:S(2)}) collective-permute-start(f32[96,512]{1,0:T(8,128)} %factor_slice.1.refs_1_.refs_10_), channel_id=1, source_target_pairs={{0,8},{4,12},{8,0},{12,4},{1,9},{5,13},{9,1},{13,5},{2,10},{6,14},... | collective-permute-start | bytes 589832 | tf_op jit(solution)/shard_map/ppermute | solution.py:49
  100.8 6.5 %copy-start.14 = (f32[128,1024]{1,0:T(8,128)}, f32[128,1024]{1,0:T(8,128)S(1)}, u32[]{:S(2)}) copy-start(f32[128,1024]{1,0:T(8,128)S(1)} %collective-permute-done.6.refs_9_) | copy-start | bytes 1572868
  100.8 15.4 %collective-permute-start.29 = (f32[96,512]{1,0:T(8,128)}, f32[96,512]{1,0:T(8,128)S(1)}, u32[]{:S(2)}, u32[]{:S(2)}) collective-permute-start(f32[96,512]{1,0:T(8,128)} %factor_slice.1.refs_1_.refs_10_), channel_id=1, source_target_pairs={{0,12},{4,0},{8,4},{12,8},{1,13},{5,1},{9,5},{13,9},{2,14},{6,2},{... | collective-permute-start | bytes 589832 | tf_op jit(solution)/shard_map/ppermute | solution.py:49
  103.7 3.5 %copy-start.15 = (f32[128,1024]{1,0:T(8,128)}, f32[128,1024]{1,0:T(8,128)S(1)}, u32[]{:S(2)}) copy-start(f32[128,1024]{1,0:T(8,128)S(1)} %collective-permute-done.7.refs_10_) | copy-start | bytes 1572868
  103.7 16.8 %collective-permute-start.24 = (f32[96,512]{1,0:T(8,128)}, f32[96,512]{1,0:T(8,128)S(1)}, u32[]{:S(2)}, u32[]{:S(2)}) collective-permute-start(f32[96,512]{1,0:T(8,128)} %factor_slice.1.refs_1_.refs_10_), channel_id=1, source_target_pairs={{0,1},{1,0},{2,3},{3,2},{4,5},{5,4},{6,7},{7,6},{8,9},{9,8},{10,11... | collective-permute-start | bytes 589832 | tf_op jit(solution)/shard_map/ppermute | solution.py:54
  105.5 1.7 %copy-start.16 = (f32[128,1024]{1,0:T(8,128)}, f32[128,1024]{1,0:T(8,128)S(1)}, u32[]{:S(2)}) copy-start(f32[128,1024]{1,0:T(8,128)S(1)} %collective-permute-done.8.refs_11_) | copy-start | bytes 1572868
  105.5 18.7 %collective-permute-start.25 = (f32[96,512]{1,0:T(8,128)}, f32[96,512]{1,0:T(8,128)S(1)}, u32[]{:S(2)}, u32[]{:S(2)}) collective-permute-start(f32[96,512]{1,0:T(8,128)} %factor_slice.1.refs_1_.refs_10_), channel_id=1, source_target_pairs={{0,2},{1,3},{2,0},{3,1},{4,6},{5,7},{6,4},{7,5},{8,10},{9,11},{10,... | collective-permute-start | bytes 589832 | tf_op jit(solution)/shard_map/ppermute | solution.py:54
  114.0 11.0 %copy-start.19 = (f32[96,512]{1,0:T(8,128)}, f32[96,512]{1,0:T(8,128)S(1)}, u32[]{:S(2)}) copy-start(f32[96,512]{1,0:T(8,128)S(1)} %collective-permute-done.27.refs_2_) | copy-start | bytes 589828
  114.0 16.7 %collective-permute-start.11 = (f32[256,256]{1,0:T(8,128)}, f32[256,256]{1,0:T(8,128)S(1)}, u32[]{:S(2)}, u32[]{:S(2)}) collective-permute-start(f32[256,256]{1,0:T(8,128)} %get-tuple-element.26), channel_id=1, source_target_pairs={{0,5},{1,6},{2,7},{4,9},{5,10},{6,11},{8,13},{9,14},{10,15},{16,21... | collective-permute-start | bytes 786440 | tf_op jit(solution)/shard_map/ppermute | solution.py:68
  116.0 8.9 %copy-start.20 = (f32[96,512]{1,0:T(8,128)}, f32[96,512]{1,0:T(8,128)S(1)}, u32[]{:S(2)}) copy-start(f32[96,512]{1,0:T(8,128)S(1)} %collective-permute-done.28.refs_3_) | copy-start | bytes 589828
  116.1 11.8 %collective-permute-start.26 = (f32[96,512]{1,0:T(8,128)S(1)}, f32[96,512]{1,0:T(8,128)}, u32[]{:S(2)}, u32[]{:S(2)}) collective-permute-start(f32[96,512]{1,0:T(8,128)S(1)} %copy-done.8), channel_id=1, source_target_pairs={{0,3},{1,2},{2,1},{3,0},{4,7},{5,6},{6,5},{7,4},{8,11},{9,10},{10,... | collective-permute-start | bytes 589832 | tf_op jit(solution)/shard_map/ppermute | solution.py:54
  116.1 8.8 %copy-start.21 = (f32[96,512]{1,0:T(8,128)}, f32[96,512]{1,0:T(8,128)S(1)}, u32[]{:S(2)}) copy-start(f32[96,512]{1,0:T(8,128)S(1)} %collective-permute-done.29.refs_4_) | copy-start | bytes 589828
  116.2 21.7 %collective-permute-start.9 = (f32[512,256]{1,0:T(8,128)}, f32[512,256]{1,0:T(8,128)S(1)}, u32[]{:S(2)}, u32[]{:S(2)}) collective-permute-start(f32[512,256]{1,0:T(8,128)} %get-tuple-element.24), channel_id=1, source_target_pairs={{0,1},{1,2},{2,3},{4,5},{5,6},{6,7},{8,9},{9,10},{10,11},{12,13},{... | collective-permute-start | bytes 1572872 | tf_op jit(solution)/shard_map/ppermute | solution.py:59
  120.5 17.9 %copy-start.22 = (f32[96,512]{1,0:T(8,128)}, f32[96,512]{1,0:T(8,128)S(1)}, u32[]{:S(2)}) copy-start(f32[96,512]{1,0:T(8,128)S(1)} %collective-permute-done.24.refs_11_) | copy-start | bytes 589828
  120.5 17.9 %collective-permute-start.10 = (f32[256,512]{1,0:T(8,128)}, f32[256,512]{1,0:T(8,128)S(1)}, u32[]{:S(2)}, u32[]{:S(2)}) collective-permute-start(f32[256,512]{1,0:T(8,128)} %get-tuple-element.25), channel_id=1, source_target_pairs={{0,4},{4,8},{8,12},{1,5},{5,9},{9,13},{2,6},{6,10},{10,14},{3,7},{... | collective-permute-start | bytes 1572872 | tf_op jit(solution)/shard_map/ppermute | solution.py:59
  125.0 23.3 %collective-permute-start.12 = (f32[512,512]{1,0:T(8,128)}, f32[512,512]{1,0:T(8,128)S(1)}, u32[]{:S(2)}, u32[]{:S(2)}) collective-permute-start(f32[512,512]{1,0:T(8,128)} %get-tuple-element.23.refs_2_), channel_id=1, source_target_pairs={{0,16},{16,0},{1,17},{17,1},{2,18},{18,2},{3,19},{19,3},{4,20},{20... | collective-permute-start | bytes 3145736 | tf_op jit(solution)/shard_map/ppermute | solution.py:54
  127.8 8.6 %collective-permute-start.30 = (f32[96,512]{1,0:T(8,128)}, f32[96,512]{1,0:T(8,128)S(1)}, u32[]{:S(2)}, u32[]{:S(2)}) collective-permute-start(f32[96,512]{1,0:T(8,128)} %get-tuple-element.32), channel_id=1, source_target_pairs={{0,1},{1,0},{2,3},{3,2},{4,5},{5,4},{6,7},{7,6},{8,9},{9,8},{10,11... | collective-permute-start | bytes 589832 | tf_op jit(solution)/shard_map/ppermute | solution.py:54
  130.6 17.7 %copy-start.17 = (f32[256,256]{1,0:T(8,128)}, f32[256,256]{1,0:T(8,128)S(1)}, u32[]{:S(2)}) copy-start(f32[256,256]{1,0:T(8,128)S(1)} %collective-permute-done.11.refs_5_) | copy-start | bytes 786436
  130.6 7.2 %collective-permute-start.31 = (f32[96,512]{1,0:T(8,128)}, f32[96,512]{1,0:T(8,128)S(1)}, u32[]{:S(2)}, u32[]{:S(2)}) collective-permute-start(f32[96,512]{1,0:T(8,128)} %get-tuple-element.33), channel_id=1, source_target_pairs={{0,2},{1,3},{2,0},{3,1},{4,6},{5,7},{6,4},{7,5},{8,10},{9,11},{10,... | collective-permute-start | bytes 589832 | tf_op jit(solution)/shard_map/ppermute | solution.py:54
  136.4 8.4 %copy-start.24 = (f32[96,512]{1,0:T(8,128)}, f32[96,512]{1,0:T(8,128)S(1)}, u32[]{:S(2)}) copy-start(f32[96,512]{1,0:T(8,128)S(1)} %collective-permute-done.30.refs_15_) | copy-start | bytes 589828
  136.4 7.8 %collective-permute-start.32 = (f32[96,512]{1,0:T(8,128)}, f32[96,512]{1,0:T(8,128)S(1)}, u32[]{:S(2)}, u32[]{:S(2)}) collective-permute-start(f32[96,512]{1,0:T(8,128)} %get-tuple-element.34), channel_id=1, source_target_pairs={{0,3},{1,2},{2,1},{3,0},{4,7},{5,6},{6,5},{7,4},{8,11},{9,10},{10,... | collective-permute-start | bytes 589832 | tf_op jit(solution)/shard_map/ppermute | solution.py:54
  137.9 9.7 %copy-start.25 = (f32[96,512]{1,0:T(8,128)}, f32[96,512]{1,0:T(8,128)S(1)}, u32[]{:S(2)}) copy-start(f32[96,512]{1,0:T(8,128)S(1)} %collective-permute-done.31.refs_16_) | copy-start | bytes 589828
  137.9 6.4 %collective-permute-start.33 = (f32[96,512]{1,0:T(8,128)}, f32[96,512]{1,0:T(8,128)S(1)}, u32[]{:S(2)}, u32[]{:S(2)}) collective-permute-start(f32[96,512]{1,0:T(8,128)} %get-tuple-element.31.refs_14_), channel_id=1, source_target_pairs={{0,16},{16,0},{1,17},{17,1},{2,18},{18,2},{3,19},{19,3},{4,20},{20... | collective-permute-start | bytes 589832 | tf_op jit(solution)/shard_map/ppermute | solution.py:54
  137.9 10.4 %copy-start.10 = (f32[512,256]{1,0:T(8,128)}, f32[512,256]{1,0:T(8,128)S(1)}, u32[]{:S(2)}) copy-start(f32[512,256]{1,0:T(8,128)S(1)} %collective-permute-done.9.refs_3_) | copy-start | bytes 1572868
  137.9 9.6 %collective-permute-start.13 = (f32[512,256]{1,0:T(8,128)S(1)}, f32[512,256]{1,0:T(8,128)S(1)}, u32[]{:S(2)}, u32[]{:S(2)}) collective-permute-start(f32[512,256]{1,0:T(8,128)S(1)} %collective-permute-done.9.refs_3_), channel_id=1, source_target_pairs={{0,16},{16,0},{1,17},{17,1},{2,18},{18,2},{3,19},{19,3},{4,20},{20... | collective-permute-start | bytes 1572872 | tf_op jit(solution)/shard_map/ppermute | solution.py:54
  138.4 9.9 %copy-start.11 = (f32[256,512]{1,0:T(8,128)}, f32[256,512]{1,0:T(8,128)S(1)}, u32[]{:S(2)}) copy-start(f32[256,512]{1,0:T(8,128)S(1)} %collective-permute-done.10.refs_4_) | copy-start | bytes 1572868
  138.4 9.1 %collective-permute-start.14 = (f32[256,512]{1,0:T(8,128)S(1)}, f32[256,512]{1,0:T(8,128)S(1)}, u32[]{:S(2)}, u32[]{:S(2)}) collective-permute-start(f32[256,512]{1,0:T(8,128)S(1)} %collective-permute-done.10.refs_4_), channel_id=1, source_target_pairs={{0,16},{16,0},{1,17},{17,1},{2,18},{18,2},{3,19},{19,3},{4,20},{20... | collective-permute-start | bytes 1572872 | tf_op jit(solution)/shard_map/ppermute | solution.py:54
  144.2 3.3 %copy-start.26 = (f32[96,512]{1,0:T(8,128)}, f32[96,512]{1,0:T(8,128)S(1)}, u32[]{:S(2)}) copy-start(f32[96,512]{1,0:T(8,128)S(1)} %collective-permute-done.32.refs_17_) | copy-start | bytes 589828
  144.2 1.4 collective-permute-start.34
  144.3 3.3 %copy-start.27 = (f32[96,512]{1,0:T(8,128)}, f32[96,512]{1,0:T(8,128)S(1)}, u32[]{:S(2)}) copy-start(f32[96,512]{1,0:T(8,128)S(1)} %collective-permute-done.33.refs_18_) | copy-start | bytes 589828
  144.3 1.7 %collective-permute-start.35 = (f32[96,512]{1,0:T(8,128)S(1)}, f32[96,512]{1,0:T(8,128)S(1)}, u32[]{:S(2)}, u32[]{:S(2)}) collective-permute-start(f32[96,512]{1,0:T(8,128)S(1)} %collective-permute-done.31.refs_16_), channel_id=1, source_target_pairs={{0,16},{16,0},{1,17},{17,1},{2,18},{18,2},{3,19},{19,3},{4,20},{20... | collective-permute-start | bytes 589832 | tf_op jit(solution)/shard_map/ppermute | solution.py:54
  145.7 1.9 %copy-start.28 = (f32[96,512]{1,0:T(8,128)}, f32[96,512]{1,0:T(8,128)S(1)}, u32[]{:S(2)}) copy-start(f32[96,512]{1,0:T(8,128)S(1)} %collective-permute-done.34.refs_19_) | copy-start | bytes 589828
  145.7 1.8 %collective-permute-start.15 = (f32[256,256]{1,0:T(8,128)S(1)}, f32[256,256]{1,0:T(8,128)S(1)}, u32[]{:S(2)}, u32[]{:S(2)}) collective-permute-start(f32[256,256]{1,0:T(8,128)S(1)} %collective-permute-done.11.refs_5_), channel_id=1, source_target_pairs={{0,16},{16,0},{1,17},{17,1},{2,18},{18,2},{3,19},{19,3},{4,20},{20... | collective-permute-start | bytes 786440 | tf_op jit(solution)/shard_map/ppermute | solution.py:54
  146.0 1.6 %copy-start.29 = (f32[96,512]{1,0:T(8,128)}, f32[96,512]{1,0:T(8,128)S(1)}, u32[]{:S(2)}) copy-start(f32[96,512]{1,0:T(8,128)S(1)} %collective-permute-done.35.refs_20_) | copy-start | bytes 589828
  146.0 1.5 collective-permute-start.36
  (9 other events, 6.9 us)
where the time goes:
time: 158 us; the launch traced here: 156 us
  waiting for transfers between devices  60.7 us (38%)
  starting transfers between devices  57.3 us (36%)
  Pallas kernels  28.4 us (18%)
  local copies, waits for them, and re-layouts  7.35 us (5%)
  other arithmetic  1.81 us (1%)
    ppermute x24, waiting for transfers between devices, swapped(): return lax.ppermute(value, axis, [(i, i ^ mask) for i in range(count)])  41.6 us
    ppermute x24, starting transfers between devices, swapped(): return lax.ppermute(value, axis, [(i, i ^ mask) for i in range(count)])  25.4 us
    ppermute x3, waiting for transfers between devices, shards(): dealt.append(lax.ppermute(value, 'col', [(0, j)]) if j else value)  11.4 us
    ppermute x6, starting transfers between devices, rotated(): lax.ppermute(value, axis, [(i, (i + steps) % count) for i in range(count)])  10.9 us
    ppermute x3, starting transfers between devices, shifted(): return lax.ppermute(value, axis, [(i, i + 1) for i in range(count - 1)])  10.5 us
    ppermute x3, starting transfers between devices, shards(): dealt.append(lax.ppermute(value, 'col', [(0, j)]) if j else value)  8.48 us
    ppermute x6, waiting for transfers between devices, rotated(): lax.ppermute(value, axis, [(i, (i + steps) % count) for i in range(count)])  7.67 us
    pallas_call x1, Pallas kernels, update_product(): pl.pallas_call(body, in_specs=[SMEM] + [ANY] * (3 * count - 1) + [VMEM],...  6.71 us
  transfers between devices with their start and end apart: 37, of which 14 were waited for; matrix products, arithmetic and copies ran while one was open for 2% of the time, Pallas kernels for 12%

commit v1 on v0

--- a/solution.py
+++ b/solution.py
@@ -19,6 +19,8 @@
 SMEM = pl.BlockSpec(memory_space=pltpu.SMEM)
 VMEM = pl.BlockSpec(memory_space=pltpu.VMEM)
 ANY = pl.BlockSpec(memory_space=pl.ANY)
+
+LIMITS = pltpu.CompilerParams(vmem_limit_bytes=16 << 20)
 
 ROW, COL, SIB = 0, 1, 2
 OWN_ROWS, OTHER_ROWS, OWN_COLS, OTHER_COLS = 3, 9, 15, 21
@@ -140,6 +142,7 @@
             pltpu.SemaphoreType.DMA((count + 2,)),
         ],
         name="pivot_product",
+        compiler_params=LIMITS,
     )(table, *rows, *turned, *dealt)
 
 
@@ -182,6 +185,7 @@
             pltpu.SemaphoreType.DMA((2 * count,)),
         ],
         name="update_product",
+        compiler_params=LIMITS,
     )(table, *rows, *turned, *cols, front)
 
 
@@ -205,6 +209,7 @@
         out_shape=[f32(*pieces[0].shape)] * len(masks),
         scratch_shapes=[pltpu.SemaphoreType.DMA((len(masks),))],
         name="pick_for_cols",
+        compiler_params=LIMITS,
     )(table, *pieces)
 
 
@@ -228,6 +233,7 @@
         out_shape=[f32(rows, width), f32(rows, width)],
         scratch_shapes=[pltpu.VMEM((size + EDGE, width), jnp.float32)],
         name="place_rows",
+        compiler_params=LIMITS,
     )(table, part, edge)
 
 
@@ -279,6 +285,7 @@
             pltpu.SemaphoreType.DMA((count + 1,)),
         ],
         name="factor_slice",
+        compiler_params=LIMITS,
     )(table, *small, *dealt, pivot_inverse)
 
 
@@ -361,6 +368,7 @@
             pltpu.SemaphoreType.DMA((3 * count + 8,)),
         ],
         name="finish",
+        compiler_params=LIMITS,
     )(table, parent, *own, *other, *row_pieces, *col_own, *col_other)
 
 

time: 158 us -> 159 us (level)
  Pallas kernels: 28.4 us -> 21.5 us
  local copies, waits for them, and re-layouts: 7.35 us -> 11.8 us
  waiting for transfers between devices: 60.7 us -> 63.3 us
    unnamed x76 -> x26, local copies, waits for them, and re-layouts: 6.6 us -> 10.9 us
    pallas_call x2, Pallas kernels: 6.05 us -> 3.59 us  [pick_for_cols(): pl.pallas_call(body, in_specs=[SMEM] + [ANY] * count, out_specs=[VMEM] *...]
    pallas_call x1, Pallas kernels: 6.71 us -> 4.41 us  [update_product(): pl.pallas_call(body, in_specs=[SMEM] + [ANY] * (3 * count - 1) + [VMEM],...]
    pallas_call x1, Pallas kernels: 3.7 us -> 2.02 us  [factor_slice(): pl.pallas_call(body, in_specs=[SMEM] + [ANY] * (2 * count) + [VMEM], out_...]
  transfers between devices with their start and end apart: 37 -> 37, of which waited for: 14 -> 13; matrix products, arithmetic and copies ran while one was open for 2% -> 4% of each run, Pallas kernels for 12% -> 7%
where the time goes in v1:
time: 159 us; the launch traced here: 156 us
  waiting for transfers between devices  63.3 us (40%)
  starting transfers between devices  57.8 us (36%)
  Pallas kernels  21.5 us (14%)
  local copies, waits for them, and re-layouts  11.8 us (7%)
    ppermute x24, waiting for transfers between devices, swapped(): return lax.ppermute(value, axis, [(i, i ^ mask) for i in range(count)])  42.2 us
    ppermute x24, starting transfers between devices, swapped(): return lax.ppermute(value, axis, [(i, i ^ mask) for i in range(count)])  25.7 us
    ppermute x3, waiting for transfers between devices, shards(): dealt.append(lax.ppermute(value, 'col', [(0, j)]) if j else value)  12 us
    ppermute x6, starting transfers between devices, rotated(): lax.ppermute(value, axis, [(i, (i + steps) % count) for i in range(count)])  11.4 us
    unnamed x26, local copies, waits for them, and re-layouts  10.9 us
    ppermute x3, starting transfers between devices, shifted(): return lax.ppermute(value, axis, [(i, i + 1) for i in range(count - 1)])  10.6 us
    ppermute x6, waiting for transfers between devices, rotated(): lax.ppermute(value, axis, [(i, (i + steps) % count) for i in range(count)])  9.17 us
    ppermute x3, starting transfers between devices, shards(): dealt.append(lax.ppermute(value, 'col', [(0, j)]) if j else value)  7.55 us
  transfers between devices with their start and end apart: 37, of which 13 were waited for; matrix products, arithmetic and copies ran while one was open for 4% of the time, Pallas kernels for 7%

profile of v1, /device:TPU:0, one launch (start us, length us, event | category | flops | bytes accessed | tf_op | source)
XLA Modules:
  0.0 155.7 jit_solution(9411604829029056952)
XLA Ops:
  0.0 3.1 %collective-permute-start.3 = (f32[128,1024]{1,0:T(8,128)}, f32[128,1024]{1,0:T(8,128)S(1)}, u32[]{:S(2)}, u32[]{:S(2)}) collective-permute-start(f32[128,1024]{1,0:T(8,128)} %bitcast.13), channel_id=1, source_target_pairs={{0,4},{4,8},{8,12},{12,0},{1,5},{5,9},{9,13},{13,1},{2,6},{6,10},{... | collective-permute-start | bytes 1572872 | tf_op jit(solution)/shard_map/ppermute | solution.py:51
  3.1 2.6 %collective-permute-start.4 = (f32[128,1024]{1,0:T(8,128)}, f32[128,1024]{1,0:T(8,128)S(1)}, u32[]{:S(2)}, u32[]{:S(2)}) collective-permute-start(f32[128,1024]{1,0:T(8,128)} %bitcast.14), channel_id=1, source_target_pairs={{0,8},{4,12},{8,0},{12,4},{1,9},{5,13},{9,1},{13,5},{2,10},{6,14},... | collective-permute-start | bytes 1572872 | tf_op jit(solution)/shard_map/ppermute | solution.py:51
  5.6 2.1 %slice_dynamic-update-slice_fusion = (f32[896,128]{1,0:T(8,128)}, f32[896,128]{1,0:T(8,128)}, f32[896,128]{1,0:T(8,128)}, f32[896,128]{1,0:T(8,128)S(1)}) fusion(f32[512,512]{1,0:T(8,128)} %bitcast.24), kind=kLoop, calls=%fused_computation.8 | loop fusion | bytes 2097152
  7.8 0.7 slice_dynamic-update-slice_fusion.7
  8.4 0.6 slice_dynamic-update-slice_fusion.6
  9.1 0.7 slice_dynamic-update-slice_fusion.5
  9.7 0.6 slice_dynamic-update-slice_fusion.4
  10.4 0.8 copy-done.3
  11.1 3.4 %collective-permute-start.16 = (f32[896,128]{1,0:T(8,128)}, f32[896,128]{1,0:T(8,128)S(1)}, u32[]{:S(2)}, u32[]{:S(2)}) collective-permute-start(f32[896,128]{1,0:T(8,128)} %get-tuple-element.47), channel_id=1, source_target_pairs={{0,1},{4,5},{8,9},{12,13},{16,17},{20,21},{24,25},{28,29}} | collective-permute-start | bytes 1376264 | tf_op jit(solution)/shard_map/ppermute | solution.py:424
  14.6 2.1 %collective-permute-start.17 = (f32[896,128]{1,0:T(8,128)}, f32[896,128]{1,0:T(8,128)}, u32[]{:S(2)}, u32[]{:S(2)}) collective-permute-start(f32[896,128]{1,0:T(8,128)} %get-tuple-element.46), channel_id=1, source_target_pairs={{0,2},{4,6},{8,10},{12,14},{16,18},{20,22},{24,26},{28,30}} | collective-permute-start | bytes 1376264 | tf_op jit(solution)/shard_map/ppermute | solution.py:424
  16.6 2.1 %collective-permute-start.18 = (f32[896,128]{1,0:T(8,128)}, f32[896,128]{1,0:T(8,128)}, u32[]{:S(2)}, u32[]{:S(2)}) collective-permute-start(f32[896,128]{1,0:T(8,128)} %get-tuple-element.45), channel_id=1, source_target_pairs={{0,3},{4,7},{8,11},{12,15},{16,19},{20,23},{24,27},{28,31}} | collective-permute-start | bytes 1376264 | tf_op jit(solution)/shard_map/ppermute | solution.py:424
  18.7 0.1 pad_dynamic-slice_fusion.9
  18.8 0.3 select_reduce_fusion.2
  19.1 6.6 %collective-permute-done.16.refs_10_.refs_6_ = f32[896,128]{1,0:T(8,128)S(1)} collective-permute-done((f32[896,128]{1,0:T(8,128)}, f32[896,128]{1,0:T(8,128)S(1)}, u32[]{:S(2)}, u32[]{:S(2)}) %collective-permute-start.16) | collective-permute-done | bytes 458784 | tf_op jit(solution)/shard_map/ppermute | solution.py:424
  25.7 0.8 copy-done.6
  26.5 1.3 collective-permute-start.5
  27.9 2.4 %collective-permute-start = (f32[128,1024]{1,0:T(8,128)S(1)}, f32[128,1024]{1,0:T(8,128)}, u32[]{:S(2)}, u32[]{:S(2)}) collective-permute-start(f32[128,1024]{1,0:T(8,128)S(1)} %bitcast.16), channel_id=1, source_target_pairs={{0,1},{1,0},{2,3},{3,2},{4,5},{5,4},{6,7},{7,6},{8,9},{9,8},{10,11... | collective-permute-start | bytes 1572872 | tf_op jit(solution)/shard_map/ppermute | solution.py:56
  30.2 5.3 %collective-permute-done.18.refs_12_.refs_8_ = f32[896,128]{1,0:T(8,128)} collective-permute-done((f32[896,128]{1,0:T(8,128)}, f32[896,128]{1,0:T(8,128)}, u32[]{:S(2)}, u32[]{:S(2)}) %collective-permute-start.18) | collective-permute-done | bytes 458784 | tf_op jit(solution)/shard_map/ppermute | solution.py:424
  35.6 3.4 %collective-permute-start.2 = (f32[128,1024]{1,0:T(8,128)S(1)}, f32[128,1024]{1,0:T(8,128)}, u32[]{:S(2)}, u32[]{:S(2)}) collective-permute-start(f32[128,1024]{1,0:T(8,128)S(1)} %bitcast.18), channel_id=1, source_target_pairs={{0,3},{1,2},{2,1},{3,0},{4,7},{5,6},{6,5},{7,4},{8,11},{9,10},{10,... | collective-permute-start | bytes 1572872 | tf_op jit(solution)/shard_map/ppermute | solution.py:56
  39.0 0.8 collective-permute-done.4.refs_3_.refs_7_
  39.8 8.4 %collective-permute-done.5.refs_4_.refs_8_ = f32[128,1024]{1,0:T(8,128)S(1)} collective-permute-done((f32[128,1024]{1,0:T(8,128)S(1)}, f32[128,1024]{1,0:T(8,128)S(1)}, u32[]{:S(2)}, u32[]{:S(2)}) %collective-permute-start.5) | collective-permute-done | bytes 524320 | tf_op jit(solution)/shard_map/ppermute | solution.py:51
  48.2 9.3 %collective-permute-done.1.refs_3_ = f32[128,1024]{1,0:T(8,128)} collective-permute-done((f32[128,1024]{1,0:T(8,128)S(1)}, f32[128,1024]{1,0:T(8,128)}, u32[]{:S(2)}, u32[]{:S(2)}) %collective-permute-start.1) | collective-permute-done | bytes 524320 | tf_op jit(solution)/shard_map/ppermute | solution.py:56
  57.5 1.0 copy-done.4
  58.5 1.0 copy-done.7
  59.5 3.1 %pivot_product.1 = (f32[512,128]{1,0:T(8,128)S(1)}, f32[256,128]{1,0:T(8,128)S(1)}) custom-call(s32[35]{0:T(128)S(1)} %concatenate.27.refs_0_.sc, f32[128,1024]{1,0:T(8,128)S(1)} %bitcast.19, f32[128,1024]{1,0:T(8,128)} %collective-permute-done.refs_2_, f32[128,1024]{1,0:T(8,128)} %collective-permute-done.1.refs_3_, ...), custom_call_target="tpu_custom_call" | custom-call | tf_op jit(solution)/shard_map/pivot_product/pallas_call | solution.py:133
  62.6 2.4 %collective-permute-start.19 = (f32[256,128]{1,0:T(8,128)S(1)}, f32[256,128]{1,0:T(8,128)S(1)}, u32[]{:S(2)}, u32[]{:S(2)}) collective-permute-start(f32[256,128]{1,0:T(8,128)S(1)} %get-tuple-element.28), channel_id=1, source_target_pairs={{0,4},{4,8},{8,12},{1,5},{5,9},{9,13},{2,6},{6,10},{10,14},{3,7},{... | collective-permute-start | bytes 393224 | tf_op jit(solution)/shard_map/ppermute | solution.py:61
  65.0 1.9 %pick_for_cols.2 = (f32[128,1024]{1,0:T(8,128)}, f32[128,1024]{1,0:T(8,128)}, f32[128,1024]{1,0:T(8,128)}) custom-call(s32[35]{0:T(128)S(1)} %concatenate.27.refs_0_.sc, f32[128,1024]{1,0:T(8,128)S(1)} %bitcast.21, f32[128,1024]{1,0:T(8,128)S(1)} %collective-permute-done.3.refs_2_.refs_6_, f32[128,1024]{1,0:T(8,128)S(1)} %collective-permute-done.4.refs_3_.refs_7_, ...), custom_call_target="tpu_custom_call" | custom-call | tf_op jit(solution)/shard_map/pick_for_cols/pallas_call | solution.py:205
  66.9 2.3 %collective-permute-start.6 = (f32[128,1024]{1,0:T(8,128)}, f32[128,1024]{1,0:T(8,128)}, u32[]{:S(2)}, u32[]{:S(2)}) collective-permute-start(f32[128,1024]{1,0:T(8,128)} %get-tuple-element.20), channel_id=1, source_target_pairs={{0,1},{1,0},{2,3},{3,2},{4,5},{5,4},{6,7},{7,6},{8,9},{9,8},{10,11... | collective-permute-start | bytes 1572872 | tf_op jit(solution)/shard_map/ppermute | solution.py:56
  69.1 1.9 %collective-permute-start.7 = (f32[128,1024]{1,0:T(8,128)}, f32[128,1024]{1,0:T(8,128)}, u32[]{:S(2)}, u32[]{:S(2)}) collective-permute-start(f32[128,1024]{1,0:T(8,128)} %get-tuple-element.21), channel_id=1, source_target_pairs={{0,2},{1,3},{2,0},{3,1},{4,6},{5,7},{6,4},{7,5},{8,10},{9,11},{10,... | collective-permute-start | bytes 1572872 | tf_op jit(solution)/shard_map/ppermute | solution.py:56
  71.1 1.3 place_rows.1
  72.4 1.8 %collective-permute-done.20 = f32[384,128]{1,0:T(8,128)} collective-permute-done((f32[384,128]{1,0:T(8,128)}, f32[384,128]{1,0:T(8,128)}, u32[]{:S(2)}, u32[]{:S(2)}) %collective-permute-start.20) | collective-permute-done | bytes 196640 | tf_op jit(solution)/shard_map/ppermute | solution.py:56
  74.2 0.9 fusion
  75.1 1.6 %collective-permute-start.21 = (f32[2,96,128]{2,1,0:T(8,128)S(1)}, f32[2,96,128]{2,1,0:T(8,128)S(1)}, u32[]{:S(2)}, u32[]{:S(2)}) collective-permute-start(f32[2,96,128]{2,1,0:T(8,128)S(1)} %get-tuple-element.67), channel_id=1, source_target_pairs={{0,1},{1,0},{2,3},{3,2},{4,5},{5,4},{6,7},{7,6},{8,9},{9,8},{10,11... | collective-permute-start | bytes 294920 | tf_op jit(solution)/shard_map/ppermute | solution.py:56
  76.7 1.9 %collective-permute-start.22 = (f32[2,96,128]{2,1,0:T(8,128)S(1)}, f32[2,96,128]{2,1,0:T(8,128)S(1)}, u32[]{:S(2)}, u32[]{:S(2)}) collective-permute-start(f32[2,96,128]{2,1,0:T(8,128)S(1)} %get-tuple-element.68), channel_id=1, source_target_pairs={{0,2},{1,3},{2,0},{3,1},{4,6},{5,7},{6,4},{7,5},{8,10},{9,11},{10,... | collective-permute-start | bytes 294920 | tf_op jit(solution)/shard_map/ppermute | solution.py:56
  78.6 13.2 %collective-permute-done.21.refs_2_ = f32[2,96,128]{2,1,0:T(8,128)S(1)} collective-permute-done((f32[2,96,128]{2,1,0:T(8,128)S(1)}, f32[2,96,128]{2,1,0:T(8,128)S(1)}, u32[]{:S(2)}, u32[]{:S(2)}) %collective-permute-start.21) | collective-permute-done | bytes 98336 | tf_op jit(solution)/shard_map/ppermute | solution.py:56
  91.8 4.1 %collective-permute-start.23 = (f32[2,96,128]{2,1,0:T(8,128)S(1)}, f32[2,96,128]{2,1,0:T(8,128)S(1)}, u32[]{:S(2)}, u32[]{:S(2)}) collective-permute-start(f32[2,96,128]{2,1,0:T(8,128)S(1)} %get-tuple-element.65), channel_id=1, source_target_pairs={{0,3},{1,2},{2,1},{3,0},{4,7},{5,6},{6,5},{7,4},{8,11},{9,10},{10,... | collective-permute-start | bytes 294920 | tf_op jit(solution)/shard_map/ppermute | solution.py:56
  95.9 2.6 %collective-permute-done.23.refs_4_ = f32[2,96,128]{2,1,0:T(8,128)S(1)} collective-permute-done((f32[2,96,128]{2,1,0:T(8,128)S(1)}, f32[2,96,128]{2,1,0:T(8,128)S(1)}, u32[]{:S(2)}, u32[]{:S(2)}) %collective-permute-start.23) | collective-permute-done | bytes 98336 | tf_op jit(solution)/shard_map/ppermute | solution.py:56
  98.5 1.0 copy-done.5
  99.5 1.0 copy-done.8
  100.5 1.2 copy-done.9
  101.8 2.0 %factor_slice.1.refs_1_.refs_10_ = f32[96,512]{1,0:T(8,128)S(1)} custom-call(s32[35]{0:T(128)S(1)} %concatenate.27.refs_0_.sc, f32[2,96,128]{2,1,0:T(8,128)S(1)} %get-tuple-element.66.refs_1_, f32[2,96,128]{2,1,0:T(8,128)S(1)} %collective-permute-done.21.refs_2_, f32[2,96,128]{2,1,0:T(8,128)S(1)} %collective-permute-done.22.refs_3_, ...), custom_call_target="tpu_custom_call" | custom-call | tf_op jit(solution)/shard_map/factor_slice/pallas_call | solution.py:275
  103.8 0.5 collective-permute-start.27
  104.3 1.1 collective-permute-start.28
  105.4 2.8 %collective-permute-start.29 = (f32[96,512]{1,0:T(8,128)S(1)}, f32[96,512]{1,0:T(8,128)S(1)}, u32[]{:S(2)}, u32[]{:S(2)}) collective-permute-start(f32[96,512]{1,0:T(8,128)S(1)} %factor_slice.1.refs_1_.refs_10_), channel_id=1, source_target_pairs={{0,12},{4,0},{8,4},{12,8},{1,13},{5,1},{9,5},{13,9},{2,14},{6,2},{... | collective-permute-start | bytes 589832 | tf_op jit(solution)/shard_map/ppermute | solution.py:51
  108.2 0.7 collective-permute-start.24
  108.9 2.9 %collective-permute-start.25 = (f32[96,512]{1,0:T(8,128)S(1)}, f32[96,512]{1,0:T(8,128)S(1)}, u32[]{:S(2)}, u32[]{:S(2)}) collective-permute-start(f32[96,512]{1,0:T(8,128)S(1)} %factor_slice.1.refs_1_.refs_10_), channel_id=1, source_target_pairs={{0,2},{1,3},{2,0},{3,1},{4,6},{5,7},{6,4},{7,5},{8,10},{9,11},{10,... | collective-permute-start | bytes 589832 | tf_op jit(solution)/shard_map/ppermute | solution.py:56
  111.9 4.4 %update_product.1 = (f32[512,512]{1,0:T(8,128)S(1)}, f32[512,256]{1,0:T(8,128)S(1)}, f32[256,512]{1,0:T(8,128)S(1)}, f32[256,256]{1,0:T(8,128)S(1)}) custom-call(s32[35]{0:T(128)S(1)} %concatenate.27.refs_0_.sc, f32[128,1024]{1,0:T(8,128)S(1)} %bitcast.22, f32[128,1024]{1,0:T(8,128)} %collective-permute-done.refs_2_, ...), custom_call_target="tpu_custom_call" | custom-call | tf_op jit(solution)/shard_map/update_product/pallas_call | solution.py:177
  116.3 2.5 %collective-permute-start.11 = (f32[256,256]{1,0:T(8,128)S(1)}, f32[256,256]{1,0:T(8,128)S(1)}, u32[]{:S(2)}, u32[]{:S(2)}) collective-permute-start(f32[256,256]{1,0:T(8,128)S(1)} %get-tuple-element.26), channel_id=1, source_target_pairs={{0,5},{1,6},{2,7},{4,9},{5,10},{6,11},{8,13},{9,14},{10,15},{16,21... | collective-permute-start | bytes 786440 | tf_op jit(solution)/shard_map/ppermute | solution.py:70
  118.9 0.5 collective-permute-start.26
  119.4 3.8 %collective-permute-start.9 = (f32[512,256]{1,0:T(8,128)S(1)}, f32[512,256]{1,0:T(8,128)S(1)}, u32[]{:S(2)}, u32[]{:S(2)}) collective-permute-start(f32[512,256]{1,0:T(8,128)S(1)} %get-tuple-element.24), channel_id=1, source_target_pairs={{0,1},{1,2},{2,3},{4,5},{5,6},{6,7},{8,9},{9,10},{10,11},{12,13},{... | collective-permute-start | bytes 1572872 | tf_op jit(solution)/shard_map/ppermute | solution.py:61
  123.2 4.4 %collective-permute-start.10 = (f32[256,512]{1,0:T(8,128)S(1)}, f32[256,512]{1,0:T(8,128)S(1)}, u32[]{:S(2)}, u32[]{:S(2)}) collective-permute-start(f32[256,512]{1,0:T(8,128)S(1)} %get-tuple-element.25), channel_id=1, source_target_pairs={{0,4},{4,8},{8,12},{1,5},{5,9},{9,13},{2,6},{6,10},{10,14},{3,7},{... | collective-permute-start | bytes 1572872 | tf_op jit(solution)/shard_map/ppermute | solution.py:61
  127.7 1.7 %pick_for_cols.3 = (f32[96,512]{1,0:T(8,128)S(1)}, f32[96,512]{1,0:T(8,128)S(1)}, f32[96,512]{1,0:T(8,128)S(1)}, f32[96,512]{1,0:T(8,128)S(1)}) custom-call(s32[35]{0:T(128)S(1)} %concatenate.27.refs_0_.sc, f32[96,512]{1,0:T(8,128)S(1)} %factor_slice.1.refs_1_.refs_10_, f32[96,512]{1,0:T(8,128)S(1)} %collective-permute-done.27.refs_2_, ...), custom_call_target="tpu_custom_call" | custom-call | tf_op jit(solution)/shard_map/pick_for_cols/pallas_call | solution.py:205
  129.4 1.9 %collective-permute-start.30 = (f32[96,512]{1,0:T(8,128)S(1)}, f32[96,512]{1,0:T(8,128)S(1)}, u32[]{:S(2)}, u32[]{:S(2)}) collective-permute-start(f32[96,512]{1,0:T(8,128)S(1)} %get-tuple-element.32), channel_id=1, source_target_pairs={{0,1},{1,0},{2,3},{3,2},{4,5},{5,4},{6,7},{7,6},{8,9},{9,8},{10,11... | collective-permute-start | bytes 589832 | tf_op jit(solution)/shard_map/ppermute | solution.py:56
  131.3 7.5 %collective-permute-done.30.refs_15_ = f32[96,512]{1,0:T(8,128)S(1)} collective-permute-done((f32[96,512]{1,0:T(8,128)S(1)}, f32[96,512]{1,0:T(8,128)S(1)}, u32[]{:S(2)}, u32[]{:S(2)}) %collective-permute-start.30) | collective-permute-done | bytes 196640 | tf_op jit(solution)/shard_map/ppermute | solution.py:56
  138.8 0.5 collective-permute-start.32
  139.3 0.5 collective-permute-start.13
  139.9 5.5 %collective-permute-done.32.refs_17_ = f32[96,512]{1,0:T(8,128)S(1)} collective-permute-done((f32[96,512]{1,0:T(8,128)S(1)}, f32[96,512]{1,0:T(8,128)S(1)}, u32[]{:S(2)}, u32[]{:S(2)}) %collective-permute-start.32) | collective-permute-done | bytes 196640 | tf_op jit(solution)/shard_map/ppermute | solution.py:56
  145.3 0.5 collective-permute-start.35
  145.9 0.9 collective-permute-done.34.refs_19_
  146.8 0.1 collective-permute-start.15
  146.9 0.1 collective-permute-done.35.refs_20_
  147.1 0.2 collective-permute-start.36
  147.3 1.3 collective-permute-done.36.refs_21_
  148.6 7.1 %finish.1 = f32[384,768]{1,0:T(8,128)} custom-call(s32[35]{0:T(128)S(1)} %concatenate.27.refs_0_.sc, f32[384,768]{1,0:T(8,128)S(1)} %copy-done.2, f32[512,512]{1,0:T(8,128)S(1)} %get-tuple-element.23.refs_2_, f32[512,256]{1,0:T(8,128)S(1)} %collective-permute-done.9.refs_3_, f32[256,512]{1,0:T(8,128)S(1)} %collective-permute-done.10.refs_4_, ...), custom_call_target="tpu_custom_call" | custom-call | tf_op jit(solution)/shard_map/finish/pallas_call | solution.py:357
  (57 shorter events, 0.4 us)
Async XLA Ops:
  0.0 7.7 %copy-start.2 = (f32[384,768]{1,0:T(8,128)S(1)}, f32[384,768]{1,0:T(8,128)}, u32[]{:S(2)}) copy-start(f32[384,768]{1,0:T(8,128)} %refs_1_.1) | copy-start | bytes 3538948
  0.0 35.6 %collective-permute-start.3 = (f32[128,1024]{1,0:T(8,128)}, f32[128,1024]{1,0:T(8,128)S(1)}, u32[]{:S(2)}, u32[]{:S(2)}) collective-permute-start(f32[128,1024]{1,0:T(8,128)} %bitcast.13), channel_id=1, source_target_pairs={{0,4},{4,8},{8,12},{12,0},{1,5},{5,9},{9,13},{13,1},{2,6},{6,10},{... | collective-permute-start | bytes 1572872 | tf_op jit(solution)/shard_map/ppermute | solution.py:51
  3.1 36.8 %collective-permute-start.4 = (f32[128,1024]{1,0:T(8,128)}, f32[128,1024]{1,0:T(8,128)S(1)}, u32[]{:S(2)}, u32[]{:S(2)}) collective-permute-start(f32[128,1024]{1,0:T(8,128)} %bitcast.14), channel_id=1, source_target_pairs={{0,8},{4,12},{8,0},{12,4},{1,9},{5,13},{9,1},{13,5},{2,10},{6,14},... | collective-permute-start | bytes 1572872 | tf_op jit(solution)/shard_map/ppermute | solution.py:51
  7.7 11.0 %copy-start.10 = (s32[2,16]{1,0:T(2,128)S(1)}, s32[2,16]{1,0:T(2,128)}, u32[]{:S(2)}) copy-start(s32[2,16]{1,0:T(2,128)} %param.7) | copy-start | bytes 388
  7.7 18.8 %copy-start = (f32[1,128,1024]{2,1,0:T(8,128)S(1)}, f32[1,128,1024]{2,1,0:T(8,128)}, u32[]{:S(2)}) copy-start(f32[1,128,1024]{2,1,0:T(8,128)} %param.6) | copy-start | bytes 1572868
  10.4 0.8 copy-start.3
  11.1 14.6 %collective-permute-start.16 = (f32[896,128]{1,0:T(8,128)}, f32[896,128]{1,0:T(8,128)S(1)}, u32[]{:S(2)}, u32[]{:S(2)}) collective-permute-start(f32[896,128]{1,0:T(8,128)} %get-tuple-element.47), channel_id=1, source_target_pairs={{0,1},{4,5},{8,9},{12,13},{16,17},{20,21},{24,25},{28,29}} | collective-permute-start | bytes 1376264 | tf_op jit(solution)/shard_map/ppermute | solution.py:424
  14.6 13.3 %collective-permute-start.17 = (f32[896,128]{1,0:T(8,128)}, f32[896,128]{1,0:T(8,128)}, u32[]{:S(2)}, u32[]{:S(2)}) collective-permute-start(f32[896,128]{1,0:T(8,128)} %get-tuple-element.46), channel_id=1, source_target_pairs={{0,2},{4,6},{8,10},{12,14},{16,18},{20,22},{24,26},{28,30}} | collective-permute-start | bytes 1376264 | tf_op jit(solution)/shard_map/ppermute | solution.py:424
  16.6 19.0 %collective-permute-start.18 = (f32[896,128]{1,0:T(8,128)}, f32[896,128]{1,0:T(8,128)}, u32[]{:S(2)}, u32[]{:S(2)}) collective-permute-start(f32[896,128]{1,0:T(8,128)} %get-tuple-element.45), channel_id=1, source_target_pairs={{0,3},{4,7},{8,11},{12,15},{16,19},{20,23},{24,27},{28,31}} | collective-permute-start | bytes 1376264 | tf_op jit(solution)/shard_map/ppermute | solution.py:424
  25.7 0.8 copy-start.6
  26.5 21.7 %collective-permute-start.5 = (f32[128,1024]{1,0:T(8,128)S(1)}, f32[128,1024]{1,0:T(8,128)S(1)}, u32[]{:S(2)}, u32[]{:S(2)}) collective-permute-start(f32[128,1024]{1,0:T(8,128)S(1)} %bitcast.15), channel_id=1, source_target_pairs={{0,12},{4,0},{8,4},{12,8},{1,13},{5,1},{9,5},{13,9},{2,14},{6,2},{... | collective-permute-start | bytes 1572872 | tf_op jit(solution)/shard_map/ppermute | solution.py:51
  27.9 20.3 %collective-permute-start = (f32[128,1024]{1,0:T(8,128)S(1)}, f32[128,1024]{1,0:T(8,128)}, u32[]{:S(2)}, u32[]{:S(2)}) collective-permute-start(f32[128,1024]{1,0:T(8,128)S(1)} %bitcast.16), channel_id=1, source_target_pairs={{0,1},{1,0},{2,3},{3,2},{4,5},{5,4},{6,7},{7,6},{8,9},{9,8},{10,11... | collective-permute-start | bytes 1572872 | tf_op jit(solution)/shard_map/ppermute | solution.py:56
  35.6 21.9 %collective-permute-start.1 = (f32[128,1024]{1,0:T(8,128)S(1)}, f32[128,1024]{1,0:T(8,128)}, u32[]{:S(2)}, u32[]{:S(2)}) collective-permute-start(f32[128,1024]{1,0:T(8,128)S(1)} %bitcast.17), channel_id=1, source_target_pairs={{0,2},{1,3},{2,0},{3,1},{4,6},{5,7},{6,4},{7,5},{8,10},{9,11},{10,... | collective-permute-start | bytes 1572872 | tf_op jit(solution)/shard_map/ppermute | solution.py:56
  35.6 21.9 %collective-permute-start.2 = (f32[128,1024]{1,0:T(8,128)S(1)}, f32[128,1024]{1,0:T(8,128)}, u32[]{:S(2)}, u32[]{:S(2)}) collective-permute-start(f32[128,1024]{1,0:T(8,128)S(1)} %bitcast.18), channel_id=1, source_target_pairs={{0,3},{1,2},{2,1},{3,0},{4,7},{5,6},{6,5},{7,4},{8,11},{9,10},{10,... | collective-permute-start | bytes 1572872 | tf_op jit(solution)/shard_map/ppermute | solution.py:56
  57.5 1.0 copy-start.4
  58.5 1.0 copy-start.7
  62.6 8.5 %collective-permute-start.19 = (f32[256,128]{1,0:T(8,128)S(1)}, f32[256,128]{1,0:T(8,128)S(1)}, u32[]{:S(2)}, u32[]{:S(2)}) collective-permute-start(f32[256,128]{1,0:T(8,128)S(1)} %get-tuple-element.28), channel_id=1, source_target_pairs={{0,4},{4,8},{8,12},{1,5},{5,9},{9,13},{2,6},{6,10},{10,14},{3,7},{... | collective-permute-start | bytes 393224 | tf_op jit(solution)/shard_map/ppermute | solution.py:61
  66.9 38.5 %collective-permute-start.6 = (f32[128,1024]{1,0:T(8,128)}, f32[128,1024]{1,0:T(8,128)}, u32[]{:S(2)}, u32[]{:S(2)}) collective-permute-start(f32[128,1024]{1,0:T(8,128)} %get-tuple-element.20), channel_id=1, source_target_pairs={{0,1},{1,0},{2,3},{3,2},{4,5},{5,4},{6,7},{7,6},{8,9},{9,8},{10,11... | collective-permute-start | bytes 1572872 | tf_op jit(solution)/shard_map/ppermute | solution.py:56
  69.1 39.1 %collective-permute-start.7 = (f32[128,1024]{1,0:T(8,128)}, f32[128,1024]{1,0:T(8,128)}, u32[]{:S(2)}, u32[]{:S(2)}) collective-permute-start(f32[128,1024]{1,0:T(8,128)} %get-tuple-element.21), channel_id=1, source_target_pairs={{0,2},{1,3},{2,0},{3,1},{4,6},{5,7},{6,4},{7,5},{8,10},{9,11},{10,... | collective-permute-start | bytes 1572872 | tf_op jit(solution)/shard_map/ppermute | solution.py:56
  71.1 37.9 %collective-permute-start.8 = (f32[128,1024]{1,0:T(8,128)}, f32[128,1024]{1,0:T(8,128)}, u32[]{:S(2)}, u32[]{:S(2)}) collective-permute-start(f32[128,1024]{1,0:T(8,128)} %get-tuple-element.22), channel_id=1, source_target_pairs={{0,3},{1,2},{2,1},{3,0},{4,7},{5,6},{6,5},{7,4},{8,11},{9,10},{10,... | collective-permute-start | bytes 1572872 | tf_op jit(solution)/shard_map/ppermute | solution.py:56
  72.4 1.8 %collective-permute-start.20 = (f32[384,128]{1,0:T(8,128)}, f32[384,128]{1,0:T(8,128)}, u32[]{:S(2)}, u32[]{:S(2)}) collective-permute-start(f32[384,128]{1,0:T(8,128)} %get-tuple-element.30), channel_id=1, source_target_pairs={{0,16},{16,0},{1,17},{17,1},{2,18},{18,2},{3,19},{19,3},{4,20},{20... | collective-permute-start | bytes 589832 | tf_op jit(solution)/shard_map/ppermute | solution.py:56
  75.1 16.8 %collective-permute-start.21 = (f32[2,96,128]{2,1,0:T(8,128)S(1)}, f32[2,96,128]{2,1,0:T(8,128)S(1)}, u32[]{:S(2)}, u32[]{:S(2)}) collective-permute-start(f32[2,96,128]{2,1,0:T(8,128)S(1)} %get-tuple-element.67), channel_id=1, source_target_pairs={{0,1},{1,0},{2,3},{3,2},{4,5},{5,4},{6,7},{7,6},{8,9},{9,8},{10,11... | collective-permute-start | bytes 294920 | tf_op jit(solution)/shard_map/ppermute | solution.py:56
  76.7 19.2 %collective-permute-start.22 = (f32[2,96,128]{2,1,0:T(8,128)S(1)}, f32[2,96,128]{2,1,0:T(8,128)S(1)}, u32[]{:S(2)}, u32[]{:S(2)}) collective-permute-start(f32[2,96,128]{2,1,0:T(8,128)S(1)} %get-tuple-element.68), channel_id=1, source_target_pairs={{0,2},{1,3},{2,0},{3,1},{4,6},{5,7},{6,4},{7,5},{8,10},{9,11},{10,... | collective-permute-start | bytes 294920 | tf_op jit(solution)/shard_map/ppermute | solution.py:56
  91.8 6.7 %collective-permute-start.23 = (f32[2,96,128]{2,1,0:T(8,128)S(1)}, f32[2,96,128]{2,1,0:T(8,128)S(1)}, u32[]{:S(2)}, u32[]{:S(2)}) collective-permute-start(f32[2,96,128]{2,1,0:T(8,128)S(1)} %get-tuple-element.65), channel_id=1, source_target_pairs={{0,3},{1,2},{2,1},{3,0},{4,7},{5,6},{6,5},{7,4},{8,11},{9,10},{10,... | collective-permute-start | bytes 294920 | tf_op jit(solution)/shard_map/ppermute | solution.py:56
  98.5 1.0 copy-start.5
  99.5 1.0 copy-start.8
  100.5 1.2 copy-start.9
  101.8 10.1 %copy-start.1 = (f32[1,512,512]{2,1,0:T(8,128)S(1)}, f32[1,512,512]{2,1,0:T(8,128)}, u32[]{:S(2)}) copy-start(f32[1,512,512]{2,1,0:T(8,128)} %param.5) | copy-start | bytes 3145732
  103.8 12.5 %collective-permute-start.27 = (f32[96,512]{1,0:T(8,128)S(1)}, f32[96,512]{1,0:T(8,128)S(1)}, u32[]{:S(2)}, u32[]{:S(2)}) collective-permute-start(f32[96,512]{1,0:T(8,128)S(1)} %factor_slice.1.refs_1_.refs_10_), channel_id=1, source_target_pairs={{0,4},{4,8},{8,12},{12,0},{1,5},{5,9},{9,13},{13,1},{2,6},{6,10},{... | collective-permute-start | bytes 589832 | tf_op jit(solution)/shard_map/ppermute | solution.py:51
  104.3 14.6 %collective-permute-start.28 = (f32[96,512]{1,0:T(8,128)S(1)}, f32[96,512]{1,0:T(8,128)S(1)}, u32[]{:S(2)}, u32[]{:S(2)}) collective-permute-start(f32[96,512]{1,0:T(8,128)S(1)} %factor_slice.1.refs_1_.refs_10_), channel_id=1, source_target_pairs={{0,8},{4,12},{8,0},{12,4},{1,9},{5,13},{9,1},{13,5},{2,10},{6,14},... | collective-permute-start | bytes 589832 | tf_op jit(solution)/shard_map/ppermute | solution.py:51
  105.4 14.0 %collective-permute-start.29 = (f32[96,512]{1,0:T(8,128)S(1)}, f32[96,512]{1,0:T(8,128)S(1)}, u32[]{:S(2)}, u32[]{:S(2)}) collective-permute-start(f32[96,512]{1,0:T(8,128)S(1)} %factor_slice.1.refs_1_.refs_10_), channel_id=1, source_target_pairs={{0,12},{4,0},{8,4},{12,8},{1,13},{5,1},{9,5},{13,9},{2,14},{6,2},{... | collective-permute-start | bytes 589832 | tf_op jit(solution)/shard_map/ppermute | solution.py:51
  108.2 15.0 %collective-permute-start.24 = (f32[96,512]{1,0:T(8,128)S(1)}, f32[96,512]{1,0:T(8,128)S(1)}, u32[]{:S(2)}, u32[]{:S(2)}) collective-permute-start(f32[96,512]{1,0:T(8,128)S(1)} %factor_slice.1.refs_1_.refs_10_), channel_id=1, source_target_pairs={{0,1},{1,0},{2,3},{3,2},{4,5},{5,4},{6,7},{7,6},{8,9},{9,8},{10,11... | collective-permute-start | bytes 589832 | tf_op jit(solution)/shard_map/ppermute | solution.py:56
  108.9 18.7 %collective-permute-start.25 = (f32[96,512]{1,0:T(8,128)S(1)}, f32[96,512]{1,0:T(8,128)S(1)}, u32[]{:S(2)}, u32[]{:S(2)}) collective-permute-start(f32[96,512]{1,0:T(8,128)S(1)} %factor_slice.1.refs_1_.refs_10_), channel_id=1, source_target_pairs={{0,2},{1,3},{2,0},{3,1},{4,6},{5,7},{6,4},{7,5},{8,10},{9,11},{10,... | collective-permute-start | bytes 589832 | tf_op jit(solution)/shard_map/ppermute | solution.py:56
  116.3 15.0 %collective-permute-start.11 = (f32[256,256]{1,0:T(8,128)S(1)}, f32[256,256]{1,0:T(8,128)S(1)}, u32[]{:S(2)}, u32[]{:S(2)}) collective-permute-start(f32[256,256]{1,0:T(8,128)S(1)} %get-tuple-element.26), channel_id=1, source_target_pairs={{0,5},{1,6},{2,7},{4,9},{5,10},{6,11},{8,13},{9,14},{10,15},{16,21... | collective-permute-start | bytes 786440 | tf_op jit(solution)/shard_map/ppermute | solution.py:70
  118.9 10.6 %collective-permute-start.26 = (f32[96,512]{1,0:T(8,128)S(1)}, f32[96,512]{1,0:T(8,128)S(1)}, u32[]{:S(2)}, u32[]{:S(2)}) collective-permute-start(f32[96,512]{1,0:T(8,128)S(1)} %factor_slice.1.refs_1_.refs_10_), channel_id=1, source_target_pairs={{0,3},{1,2},{2,1},{3,0},{4,7},{5,6},{6,5},{7,4},{8,11},{9,10},{10,... | collective-permute-start | bytes 589832 | tf_op jit(solution)/shard_map/ppermute | solution.py:56
  119.4 19.9 %collective-permute-start.9 = (f32[512,256]{1,0:T(8,128)S(1)}, f32[512,256]{1,0:T(8,128)S(1)}, u32[]{:S(2)}, u32[]{:S(2)}) collective-permute-start(f32[512,256]{1,0:T(8,128)S(1)} %get-tuple-element.24), channel_id=1, source_target_pairs={{0,1},{1,2},{2,3},{4,5},{5,6},{6,7},{8,9},{9,10},{10,11},{12,13},{... | collective-permute-start | bytes 1572872 | tf_op jit(solution)/shard_map/ppermute | solution.py:61
  123.2 16.6 %collective-permute-start.10 = (f32[256,512]{1,0:T(8,128)S(1)}, f32[256,512]{1,0:T(8,128)S(1)}, u32[]{:S(2)}, u32[]{:S(2)}) collective-permute-start(f32[256,512]{1,0:T(8,128)S(1)} %get-tuple-element.25), channel_id=1, source_target_pairs={{0,4},{4,8},{8,12},{1,5},{5,9},{9,13},{2,6},{6,10},{10,14},{3,7},{... | collective-permute-start | bytes 1572872 | tf_op jit(solution)/shard_map/ppermute | solution.py:61
  127.6 21.0 %collective-permute-start.12 = (f32[512,512]{1,0:T(8,128)S(1)}, f32[512,512]{1,0:T(8,128)S(1)}, u32[]{:S(2)}, u32[]{:S(2)}) collective-permute-start(f32[512,512]{1,0:T(8,128)S(1)} %get-tuple-element.23.refs_2_), channel_id=1, source_target_pairs={{0,16},{16,0},{1,17},{17,1},{2,18},{18,2},{3,19},{19,3},{4,20},{20... | collective-permute-start | bytes 3145736 | tf_op jit(solution)/shard_map/ppermute | solution.py:56
  129.4 9.3 %collective-permute-start.30 = (f32[96,512]{1,0:T(8,128)S(1)}, f32[96,512]{1,0:T(8,128)S(1)}, u32[]{:S(2)}, u32[]{:S(2)}) collective-permute-start(f32[96,512]{1,0:T(8,128)S(1)} %get-tuple-element.32), channel_id=1, source_target_pairs={{0,1},{1,0},{2,3},{3,2},{4,5},{5,4},{6,7},{7,6},{8,9},{9,8},{10,11... | collective-permute-start | bytes 589832 | tf_op jit(solution)/shard_map/ppermute | solution.py:56
  131.3 8.0 %collective-permute-start.31 = (f32[96,512]{1,0:T(8,128)S(1)}, f32[96,512]{1,0:T(8,128)S(1)}, u32[]{:S(2)}, u32[]{:S(2)}) collective-permute-start(f32[96,512]{1,0:T(8,128)S(1)} %get-tuple-element.33), channel_id=1, source_target_pairs={{0,2},{1,3},{2,0},{3,1},{4,6},{5,7},{6,4},{7,5},{8,10},{9,11},{10,... | collective-permute-start | bytes 589832 | tf_op jit(solution)/shard_map/ppermute | solution.py:56
  138.8 6.6 %collective-permute-start.32 = (f32[96,512]{1,0:T(8,128)S(1)}, f32[96,512]{1,0:T(8,128)S(1)}, u32[]{:S(2)}, u32[]{:S(2)}) collective-permute-start(f32[96,512]{1,0:T(8,128)S(1)} %get-tuple-element.34), channel_id=1, source_target_pairs={{0,3},{1,2},{2,1},{3,0},{4,7},{5,6},{6,5},{7,4},{8,11},{9,10},{10,... | collective-permute-start | bytes 589832 | tf_op jit(solution)/shard_map/ppermute | solution.py:56
  139.3 6.1 %collective-permute-start.33 = (f32[96,512]{1,0:T(8,128)S(1)}, f32[96,512]{1,0:T(8,128)S(1)}, u32[]{:S(2)}, u32[]{:S(2)}) collective-permute-start(f32[96,512]{1,0:T(8,128)S(1)} %get-tuple-element.31.refs_14_), channel_id=1, source_target_pairs={{0,16},{16,0},{1,17},{17,1},{2,18},{18,2},{3,19},{19,3},{4,20},{20... | collective-permute-start | bytes 589832 | tf_op jit(solution)/shard_map/ppermute | solution.py:56
  139.3 9.3 %collective-permute-start.13 = (f32[512,256]{1,0:T(8,128)S(1)}, f32[512,256]{1,0:T(8,128)S(1)}, u32[]{:S(2)}, u32[]{:S(2)}) collective-permute-start(f32[512,256]{1,0:T(8,128)S(1)} %collective-permute-done.9.refs_3_), channel_id=1, source_target_pairs={{0,16},{16,0},{1,17},{17,1},{2,18},{18,2},{3,19},{19,3},{4,20},{20... | collective-permute-start | bytes 1572872 | tf_op jit(solution)/shard_map/ppermute | solution.py:56
  139.8 8.8 %collective-permute-start.14 = (f32[256,512]{1,0:T(8,128)S(1)}, f32[256,512]{1,0:T(8,128)S(1)}, u32[]{:S(2)}, u32[]{:S(2)}) collective-permute-start(f32[256,512]{1,0:T(8,128)S(1)} %collective-permute-done.10.refs_4_), channel_id=1, source_target_pairs={{0,16},{16,0},{1,17},{17,1},{2,18},{18,2},{3,19},{19,3},{4,20},{20... | collective-permute-start | bytes 1572872 | tf_op jit(solution)/shard_map/ppermute | solution.py:56
  145.3 1.4 collective-permute-start.34
  145.3 1.7 %collective-permute-start.35 = (f32[96,512]{1,0:T(8,128)S(1)}, f32[96,512]{1,0:T(8,128)S(1)}, u32[]{:S(2)}, u32[]{:S(2)}) collective-permute-start(f32[96,512]{1,0:T(8,128)S(1)} %collective-permute-done.31.refs_16_), channel_id=1, source_target_pairs={{0,16},{16,0},{1,17},{17,1},{2,18},{18,2},{3,19},{19,3},{4,20},{20... | collective-permute-start | bytes 589832 | tf_op jit(solution)/shard_map/ppermute | solution.py:56
  146.8 1.8 %collective-permute-start.15 = (f32[256,256]{1,0:T(8,128)S(1)}, f32[256,256]{1,0:T(8,128)S(1)}, u32[]{:S(2)}, u32[]{:S(2)}) collective-permute-start(f32[256,256]{1,0:T(8,128)S(1)} %collective-permute-done.11.refs_5_), channel_id=1, source_target_pairs={{0,16},{16,0},{1,17},{17,1},{2,18},{18,2},{3,19},{19,3},{4,20},{20... | collective-permute-start | bytes 786440 | tf_op jit(solution)/shard_map/ppermute | solution.py:56
  147.1 1.5 collective-permute-start.36

commit v2 on v0

--- a/solution.py
+++ b/solution.py
@@ -20,6 +20,13 @@
 VMEM = pl.BlockSpec(memory_space=pltpu.VMEM)
 ANY = pl.BlockSpec(memory_space=pl.ANY)
 
+
+def limit_for(sub, mebibytes):
+    if sub < BLK:
+        mebibytes = 56
+    return pltpu.CompilerParams(vmem_limit_bytes=mebibytes << 20)
+
+
 ROW, COL, SIB = 0, 1, 2
 OWN_ROWS, OTHER_ROWS, OWN_COLS, OTHER_COLS = 3, 9, 15, 21
 OWN_PIVOT, OTHER_PIVOT = 27, 31
@@ -57,15 +64,6 @@
 def shifted(value, axis):
     count = lax.axis_size(axis)
     return lax.ppermute(value, axis, [(i, i + 1) for i in range(count - 1)])
-
-
-def shifted_both(value, count):
-    pairs = [
-        (r * count + c, (r + 1) * count + c + 1)
-        for r in range(count - 1)
-        for c in range(count - 1)
-    ]
-    return lax.ppermute(value, ("row", "col"), pairs)
 
 
 def run_copies(copies):
@@ -107,82 +105,129 @@
     return lax.rem(sc[ROW] - (sc[COL] ^ mask) + count, count)
 
 
-def pivot_product(table, rows, turned, dealt):
+def slice_place(sc, mask, count):
+    half = count // 2
+    diff = sc[ROW] - (sc[COL] ^ mask)
+    near = (diff < 0) & (-diff < half)
+    return jnp.where(near, 2 * half - 1 - diff, jnp.abs(diff))
+
+
+def around_row(value):
+    count = lax.axis_size("row")
+    half = count // 2
+    middle = rotated(value, "row", half)
+    below, above, far = [], [], []
+    for d in range(1, half):
+        below.append(lax.ppermute(value, "row", [(i, i + d) for i in range(count - d)]))
+        above.append(lax.ppermute(value, "row", [(i + d, i) for i in range(count - d)]))
+        pairs = [(i, i + d) for i in range(half, count - d)]
+        pairs += [(i, i - d) for i in range(d, half)]
+        far.append(lax.ppermute(middle, "row", pairs))
+    return [value] + below + [middle] + far + above
+
+
+def slice_products(table, rows, around, fronts):
     count = len(rows)
+    many = len(around)
     sub, depth = rows[0].shape
     size = count * sub
 
     def body(*refs):
         sc = refs[0]
         row_refs = refs[1 : 1 + count]
-        col_refs = refs[1 + count : 1 + 2 * count]
-        deal_refs = refs[1 + 2 * count : 1 + 3 * count]
-        out, edge, row_buf, col_buf, front, sems = refs[1 + 3 * count :]
-        start_chosen(sc[ROW], col_refs, col_buf, sems.at[count])
-        front_parts = [ref.at[pl.ds(0, size)] for ref in deal_refs]
-        start_chosen(sc[COL], front_parts, front, sems.at[count + 1])
+        around_refs = refs[1 + count : 1 + count + many]
+        front_refs = refs[1 + count + many : 1 + 2 * count + many]
+        outs = refs[1 + 2 * count + many :][:count]
+        pivot, edge, up, previous, row_buf, col_buf, sems = refs[1 + 3 * count + many :]
+        for m in range(count):
+            group = sc[COL] ^ m
+            start_chosen(
+                slice_place(sc, m, count),
+                around_refs,
+                col_buf.at[span(group, sub)],
+                sems.at[count + m],
+            )
         run_copies(gather_copies(sc, row_refs, row_buf, sems, sub))
-        pltpu.make_async_copy(col_refs[0], col_buf, sems.at[count]).wait()
-        pltpu.make_async_copy(front_parts[0], front, sems.at[count + 1]).wait()
-        part = front[...] - times_transpose(halves(row_buf[...]), halves(col_buf[...]))
-        out[...] = part
-        edge[...] = part[-EDGE:]
+        for m in range(count):
+            group = sc[COL] ^ m
+            pltpu.make_async_copy(
+                around_refs[0], col_buf.at[span(group, sub)], sems.at[count + m]
+            ).wait()
+        left = halves(row_buf[...])
+        for m in range(count):
+            group = sc[COL] ^ m
+            right = halves(col_buf[span(group, sub), :])
+            part = front_refs[m][...] - times_transpose(left, right)
+            outs[m][...] = part
+
+            @pl.when(group == 0)
+            def _():
+                pivot[...] = part
+                edge[...] = part[-EDGE:]
+
+            @pl.when(group > 0)
+            def _():
+                up[group - 1] = part[-EDGE:]
+
+            @pl.when(group < count - 1)
+            def _():
+                previous[group] = part
 
     return pl.pallas_call(
         body,
-        in_specs=[SMEM] + [ANY] * (3 * count),
-        out_specs=[VMEM, VMEM],
-        out_shape=[f32(size, sub), f32(EDGE, sub)],
-        scratch_shapes=[
-            pltpu.VMEM((size, depth), jnp.float32),
-            pltpu.VMEM((sub, depth), jnp.float32),
-            pltpu.VMEM((size, sub), jnp.float32),
-            pltpu.SemaphoreType.DMA((count + 2,)),
-        ],
-        name="pivot_product",
-    )(table, *rows, *turned, *dealt)
-
-
-def update_product(table, rows, turned, cols, front):
-    count = len(rows)
-    sub, depth = rows[0].shape
-    size = count * sub
-
-    def body(*refs):
-        sc = refs[0]
-        row_refs = refs[1 : 1 + count]
-        turn_refs = refs[1 + count : 1 + 2 * count]
-        col_refs = refs[1 + 2 * count : 3 * count]
-        front_ref, out, right, up, corner, row_buf, col_buf, sems = refs[3 * count :]
-        home = col_buf.at[span(sc[COL], sub)]
-        start_chosen(turn_of(sc, 0, count), turn_refs, home, sems.at[count])
-        copies = gather_copies(sc, row_refs, row_buf, sems, sub)
-        copies += [
-            pltpu.make_async_copy(
-                ref, col_buf.at[span(sc[COL] ^ (k + 1), sub)], sems.at[count + 1 + k]
-            )
-            for k, ref in enumerate(col_refs)
-        ]
-        run_copies(copies)
-        pltpu.make_async_copy(turn_refs[0], home, sems.at[count]).wait()
-        part = front_ref[...] - times_transpose(halves(row_buf[...]), halves(col_buf[...]))
-        out[...] = part
-        right[...] = part[:, -EDGE:]
-        up[...] = part[-EDGE:, :]
-        corner[...] = part[-EDGE:, -EDGE:]
-
-    return pl.pallas_call(
-        body,
-        in_specs=[SMEM] + [ANY] * (3 * count - 1) + [VMEM],
-        out_specs=[VMEM] * 4,
-        out_shape=[f32(size, size), f32(size, EDGE), f32(EDGE, size), f32(EDGE, EDGE)],
+        in_specs=[SMEM] + [ANY] * (count + many) + [VMEM] * count,
+        out_specs=[VMEM] * (count + 4),
+        out_shape=[f32(size, sub)] * (count + 1)
+        + [f32(EDGE, sub), f32(count - 1, EDGE, sub), f32(count - 1, size, sub)],
         scratch_shapes=[
             pltpu.VMEM((size, depth), jnp.float32),
             pltpu.VMEM((size, depth), jnp.float32),
             pltpu.SemaphoreType.DMA((2 * count,)),
         ],
-        name="update_product",
-    )(table, *rows, *turned, *cols, front)
+        compiler_params=limit_for(sub, 24),
+        name="slice_products",
+    )(table, *rows, *around, *fronts)
+
+
+def pack_halo(table, previous, edge, up):
+    less, size, sub = previous.shape
+    count = less + 1
+
+    def body(sc, previous_ref, edge_ref, up_ref, *refs):
+        outs, ups, sems = refs[:count], refs[count], refs[count + 1]
+        run_copies(
+            [
+                pltpu.make_async_copy(edge_ref, ups.at[0], sems.at[0]),
+                pltpu.make_async_copy(up_ref, ups.at[pl.ds(1, less)], sems.at[1]),
+            ]
+        )
+        copies = []
+        for m, out in enumerate(outs):
+            group = sc[COL] ^ m
+            before = jnp.maximum(group - 1, 0)
+            parts = (
+                (previous_ref.at[before], pl.ds(0, size)),
+                (ups.at[group], pl.ds(size, EDGE)),
+                (ups.at[before], pl.ds(size + EDGE, EDGE)),
+            )
+            copies += [
+                pltpu.make_async_copy(part, out.at[place], sems.at[3 * m + i])
+                for i, (part, place) in enumerate(parts)
+            ]
+        run_copies(copies)
+
+    return pl.pallas_call(
+        body,
+        in_specs=[SMEM] + [ANY] * 3,
+        out_specs=[VMEM] * count,
+        out_shape=[f32(size + 2 * EDGE, sub)] * count,
+        scratch_shapes=[
+            pltpu.VMEM((count, EDGE, sub), jnp.float32),
+            pltpu.SemaphoreType.DMA((3 * count,)),
+        ],
+        compiler_params=limit_for(sub, 16),
+        name="pack_halo",
+    )(table, previous, edge, up)
 
 
 def pick_for_cols(table, pieces, masks):
@@ -204,6 +249,7 @@
         out_specs=[VMEM] * len(masks),
         out_shape=[f32(*pieces[0].shape)] * len(masks),
         scratch_shapes=[pltpu.SemaphoreType.DMA((len(masks),))],
+        compiler_params=limit_for(BLK, 16),
         name="pick_for_cols",
     )(table, *pieces)
 
@@ -228,34 +274,31 @@
         out_shape=[f32(rows, width), f32(rows, width)],
         scratch_shapes=[pltpu.VMEM((size + EDGE, width), jnp.float32)],
         name="place_rows",
+        compiler_params=limit_for(width, 16),
     )(table, part, edge)
 
 
 def factor_slice(table, small, dealt, pivot_inverse):
     count = len(small)
     _, rows, sub = small[0].shape
-    total = dealt[0].shape[0]
-    below = total - PANEL // sub * rows
 
     def body(*refs):
         sc = refs[0]
         pieces = refs[1 : 1 + count]
         deal_refs = refs[1 + count : 1 + 2 * count]
-        inverse_ref, out, order, child, parent, sums, sems = refs[1 + 2 * count :]
-        parent_parts = [ref.at[pl.ds(below, total - below)] for ref in deal_refs]
-        start_chosen(sc[COL], parent_parts, parent, sems.at[count])
+        inverse_ref, out, order, child, sums, sems = refs[1 + 2 * count :]
+        start_chosen(sc[COL], deal_refs, sums, sems.at[count])
         run_copies(
             [
                 pltpu.make_async_copy(piece, order.at[sc[COL] ^ k], sems.at[k])
                 for k, piece in enumerate(pieces)
             ]
         )
-        pltpu.make_async_copy(parent_parts[0], parent, sems.at[count]).wait()
         for j in range(count):
             block, lane = divmod(j * sub, BLK)
             for sibling in range(2):
                 child[sibling, block, :, lane : lane + sub] = order[j, sibling]
-            sums[:, j * sub : (j + 1) * sub] = parent[j * rows : (j + 1) * rows]
+        pltpu.make_async_copy(deal_refs[0], sums, sems.at[count]).wait()
         for p in range(PIV):
             lanes = slice(p * BLK, (p + 1) * BLK)
             added = sums[:, lanes]
@@ -274,10 +317,10 @@
         scratch_shapes=[
             pltpu.VMEM((count, 2, rows, sub), jnp.float32),
             pltpu.VMEM((2, PIV, rows, BLK), jnp.float32),
-            pltpu.VMEM((total - below, sub), jnp.float32),
             pltpu.VMEM((rows, PANEL), jnp.float32),
             pltpu.SemaphoreType.DMA((count + 1,)),
         ],
+        compiler_params=limit_for(sub, 16),
         name="factor_slice",
     )(table, *small, *dealt, pivot_inverse)
 
@@ -286,17 +329,19 @@
     count = len(row_pieces)
     rows, width = parent.shape
     piece_rows = row_pieces[0].shape[0]
-    size = own[0].shape[0]
+    size, sub = own[0].shape
+    half = count // 2
+    split = BLK // sub
 
     def body(*refs):
         sc, parent_ref = refs[:2]
-        own_refs, other_refs = refs[2:6], refs[6:10]
-        row_refs = refs[10 : 10 + count]
-        col_own_refs = refs[10 + count : 10 + 2 * count]
-        col_other_refs = refs[10 + 2 * count : 10 + 3 * count]
-        out = refs[10 + 3 * count]
-        own_win, other_win, row_factor, col_factor, products, sems = refs[11 + 3 * count :]
-        low, high = slice(0, EDGE), slice(EDGE, EDGE + size)
+        own_refs, other_refs = refs[2 : 2 + 2 * count], refs[2 + 2 * count : 2 + 4 * count]
+        at = 2 + 4 * count
+        row_refs = refs[at : at + count]
+        col_own_refs = refs[at + count : at + 2 * count]
+        col_other_refs = refs[at + 2 * count : at + 3 * count]
+        out = refs[at + 3 * count]
+        own_win, other_win, row_factor, col_factor, products, sems = refs[at + 3 * count + 1 :]
         factors = gather_copies(sc, row_refs, row_factor, sems, piece_rows)
         factors += gather_copies(
             sc, col_own_refs, col_factor.at[sc[SIB]], sems, piece_rows, count
@@ -304,25 +349,59 @@
         factors += gather_copies(
             sc, col_other_refs, col_factor.at[1 - sc[SIB]], sems, piece_rows, 2 * count
         )
-        place = 3 * count
-        windows = []
+        at = 3 * count
+        always, edges = [], []
         for refs_in, window in ((own_refs, own_win), (other_refs, other_win)):
-            spots = ((high, high), (high, low), (low, high), (low, low))
-            for ref, (down, across) in zip(refs_in, spots):
-                windows.append(
-                    pltpu.make_async_copy(ref, window.at[down, across], sems.at[place])
-                )
-                place += 1
-        for copy in factors + windows:
+            for m in range(count):
+                home, halo = refs_in[m], refs_in[count + m]
+                piece = sc[COL] ^ m
+                main = half + piece
+                side = jnp.maximum(piece - half, 0)
+                low, high = pl.ds(0, EDGE), pl.ds(EDGE, size)
+                always += [
+                    pltpu.make_async_copy(home, window.at[main, high], sems.at[at]),
+                    pltpu.make_async_copy(
+                        halo.at[pl.ds(size, EDGE)], window.at[main, low], sems.at[at + 1]
+                    ),
+                ]
+                edges += [
+                    (
+                        piece,
+                        pltpu.make_async_copy(
+                            halo.at[pl.ds(0, size)], window.at[side, high], sems.at[at + 2]
+                        ),
+                        pltpu.make_async_copy(
+                            halo.at[pl.ds(size + EDGE, EDGE)],
+                            window.at[side, low],
+                            sems.at[at + 3],
+                        ),
+                    )
+                ]
+                at += 4
+        for copy in factors + always:
             copy.start()
+        for piece, first, second in edges:
+
+            @pl.when(piece >= half)
+            def _():
+                first.start()
+                second.start()
+
         for copy in factors:
             copy.wait()
         left = halves(row_factor[...])
-        for half in range(2):
-            right = halves(col_factor[half])
-            products[:, half * rows : (half + 1) * rows] = times_transpose(left, right)
-        for copy in windows:
+        for side in range(2):
+            right = halves(col_factor[side])
+            products[:, side * rows : (side + 1) * rows] = times_transpose(left, right)
+        for copy in always:
             copy.wait()
+        for piece, first, second in edges:
+
+            @pl.when(piece >= half)
+            def _():
+                first.wait()
+                second.wait()
+
         first_row = (sc[ROW] * 2 + sc[SIB]) * HALF
         first_col = sc[COL] * PBD
         for q in range(PBD):
@@ -337,9 +416,11 @@
                 ):
                     down = sc[row_base + sc[SIB] * HALF + p]
                     across = sc[col_base + q]
-                    block = window[
-                        span(jnp.maximum(down, 0), BLK), span(jnp.maximum(across, 0), BLK)
+                    start = jnp.maximum(across, 0) * split
+                    pieces = [
+                        window[start + i, span(jnp.maximum(down, 0), BLK), :] for i in range(split)
                     ]
+                    block = pieces[0] if split == 1 else jnp.concatenate(pieces, axis=1)
                     total += jnp.where((down >= 0) & (across >= 0), block, 0.0)
                 inside = col_inside & (first_row + p >= PIV)
                 total = jnp.where(inside, total - products[lines, cols], total)
@@ -349,17 +430,18 @@
 
     return pl.pallas_call(
         body,
-        in_specs=[SMEM, VMEM] + [ANY] * (8 + 3 * count),
+        in_specs=[SMEM, VMEM] + [ANY] * (7 * count),
         out_specs=VMEM,
         out_shape=f32(rows, width),
         scratch_shapes=[
-            pltpu.VMEM((size + EDGE, size + EDGE), jnp.float32),
-            pltpu.VMEM((size + EDGE, size + EDGE), jnp.float32),
+            pltpu.VMEM((half + count, size + EDGE, sub), jnp.float32),
+            pltpu.VMEM((half + count, size + EDGE, sub), jnp.float32),
             pltpu.VMEM((rows, PANEL), jnp.float32),
             pltpu.VMEM((2, rows, PANEL), jnp.float32),
             pltpu.VMEM((rows, 2 * rows), jnp.float32),
-            pltpu.SemaphoreType.DMA((3 * count + 8,)),
+            pltpu.SemaphoreType.DMA((11 * count,)),
         ],
+        compiler_params=limit_for(sub, 24),
         name="finish",
     )(table, parent, *own, *other, *row_pieces, *col_own, *col_other)
 
@@ -405,36 +487,35 @@
     def to_sibling(value):
         return swapped(value, "sib", 1)
 
-    turned = over_row(panel)
+    around = around_row(panel)
     rows = [panel] + over_col([panel] * (count - 1))
+    slices = [
+        lax.dynamic_slice_in_dim(front, (col_index ^ k) * sub, sub, axis=1) for k in range(count)
+    ]
+    fronts = [slices[0]] + over_col(slices[1:])
 
     dealt = []
     for j in range(count):
-        lines = parent_front[j * deal : (j + 1) * deal, :PANEL]
-        pieces = [lines[:, i : i + sub] for i in range(0, PANEL, sub)]
-        value = jnp.concatenate([front[:, j * sub : (j + 1) * sub]] + pieces, axis=0)
+        value = parent_front[j * deal : (j + 1) * deal, :PANEL]
         dealt.append(lax.ppermute(value, "col", [(0, j)]) if j else value)
 
-    part, edge = pivot_product(table, rows, turned, dealt)
+    *homes, pivot, edge, up, previous = slice_products(table, rows, around, fronts)
     edge = shifted(edge, "row")
-    picked = pick_for_cols(table, turned, range(1, count))
-    cols = over_col(picked)
-    keep, send = place_rows(table, part, edge)
+    own = [homes[0]] + over_col(homes[1:])
+    up = shifted(up, "row")
+
+    keep, send = place_rows(table, pivot, edge)
     both = jnp.stack([keep, to_sibling(send)])
     slices = [
         lax.dynamic_slice_in_dim(both, (col_index ^ k) * deal, deal, axis=1)
         for k in range(count)
     ]
     small = [slices[0]] + over_col(slices[1:])
+    packed = pack_halo(table, previous, edge, up)
+    own = own + [packed[0]] + over_col(packed[1:])
     factor = factor_slice(table, small, dealt, pivot_inverse)
     factors = over_row(factor)
     row_pieces = [factor] + over_col([factor] * (count - 1))
-
-    update, right, up, corner = update_product(table, rows, turned, cols, front)
-    right = shifted(right, "col")
-    up = shifted(up, "row")
-    corner = shifted_both(corner, count)
-    own = [update, right, up, corner]
 
     picked = pick_for_cols(table, factors, range(count))
     col_own = [picked[0]] + over_col(picked[1:])

time: 158 us -> 182 us (1.15)
  waiting for transfers between devices: 60.7 us -> 77.7 us
  local copies, waits for them, and re-layouts: 7.35 us -> 17.7 us
    ppermute x6 -> x4, waiting for transfers between devices: 7.67 us -> 21 us  [rotated(): lax.ppermute(value, axis, [(i, (i + steps) % count) for i in range(count)])]
    unnamed x76 -> x50, local copies, waits for them, and re-layouts: 6.6 us -> 15.5 us
    ppermute x1 -> x3, waiting for transfers between devices: 0.01 us -> 7.71 us  [the longest x1 7.71 us: around_row(): far.append(lax.ppermute(middle, 'row', pairs))]
    ppermute x3 -> x2, starting transfers between devices: 10.5 us -> 3.35 us  [shifted(): return lax.ppermute(value, axis, [(i, i + 1) for i in range(count - 1)])]
    ppermute x24 -> x34, starting transfers between devices: 25.4 us -> 32.2 us  [swapped(): return lax.ppermute(value, axis, [(i, i ^ mask) for i in range(count)])]
    pallas_call x3, Pallas kernels: 16.8 us -> 22.1 us  [the longest x1 10.1 us: slice_products(): pl.pallas_call(body, in_specs=[SMEM] + [ANY] * (count + many) + [VMEM] *...]
    ppermute x3, waiting for transfers between devices: 11.4 us -> 6.95 us  [shards(): dealt.append(lax.ppermute(value, 'col', [(0, j)]) if j else value)]
    pallas_call x2 -> x1, Pallas kernels: 6.05 us -> 1.69 us  [pick_for_cols(): pl.pallas_call(body, in_specs=[SMEM] + [ANY] * count, out_specs=[VMEM] *...]
  transfers between devices with their start and end apart: 37 -> 46, of which waited for: 14 -> 16; matrix products, arithmetic and copies ran while one was open for 2% -> 2% of each run, Pallas kernels for 12% -> 4%
where the time goes in v2:
time: 182 us; the launch traced here: 181 us
  waiting for transfers between devices  77.7 us (43%)
  starting transfers between devices  57.4 us (32%)
  Pallas kernels  27.1 us (15%)
  local copies, waits for them, and re-layouts  17.7 us (10%)
    ppermute x34, waiting for transfers between devices, swapped(): return lax.ppermute(value, axis, [(i, i ^ mask) for i in range(count)])  42 us
    ppermute x34, starting transfers between devices, swapped(): return lax.ppermute(value, axis, [(i, i ^ mask) for i in range(count)])  32.2 us
    ppermute x4, waiting for transfers between devices, rotated(): lax.ppermute(value, axis, [(i, (i + steps) % count) for i in range(count)])  21 us
    unnamed x50, local copies, waits for them, and re-layouts  15.5 us
    pallas_call x1, Pallas kernels, slice_products(): pl.pallas_call(body, in_specs=[SMEM] + [ANY] * (count + many) + [VMEM] *...  10.1 us
    pallas_call x1, Pallas kernels, finish(): pl.pallas_call(body, in_specs=[SMEM, VMEM] + [ANY] * (7 * count), out_spe...  9.47 us
    ppermute x4, starting transfers between devices, rotated(): lax.ppermute(value, axis, [(i, (i + steps) % count) for i in range(count)])  7.9 us
    ppermute x3, starting transfers between devices, shards(): dealt.append(lax.ppermute(value, 'col', [(0, j)]) if j else value)  7.77 us
  transfers between devices with their start and end apart: 46, of which 16 were waited for; matrix products, arithmetic and copies ran while one was open for 2% of the time, Pallas kernels for 4%

profile of v2, /device:TPU:0, one launch (start us, length us, event | category | flops | bytes accessed | tf_op | source)
XLA Modules:
  0.0 181.4 jit_solution(17146423113203981936)
XLA Ops:
  0.0 1.4 collective-permute-start.6
  1.4 5.2 %collective-permute-start.4 = (f32[128,1024]{1,0:T(8,128)}, f32[128,1024]{1,0:T(8,128)S(1)}, u32[]{:S(2)}, u32[]{:S(2)}) collective-permute-start(f32[128,1024]{1,0:T(8,128)} %bitcast.21), channel_id=1, source_target_pairs={{0,8},{4,12},{8,0},{12,4},{1,9},{5,13},{9,1},{13,5},{2,10},{6,14},... | collective-permute-start | bytes 1572872 | tf_op jit(solution)/shard_map/ppermute | solution.py:56
  6.6 1.3 dynamic-slice_bitcast_fusion
  7.9 2.5 %collective-permute-start.9 = (f32[512,128]{1,0:T(8,128)S(1)}, f32[512,128]{1,0:T(8,128)S(1)}, u32[]{:S(2)}, u32[]{:S(2)}) collective-permute-start(f32[512,128]{1,0:T(8,128)S(1)} %get-tuple-element.55), channel_id=1, source_target_pairs={{0,3},{1,2},{2,1},{3,0},{4,7},{5,6},{6,5},{7,4},{8,11},{9,10},{10,... | collective-permute-start | bytes 786440 | tf_op jit(solution)/shard_map/ppermute | solution.py:61
  11.9 6.2 %collective-permute-done.9.refs_13_ = f32[512,128]{1,0:T(8,128)S(1)} collective-permute-done((f32[512,128]{1,0:T(8,128)S(1)}, f32[512,128]{1,0:T(8,128)S(1)}, u32[]{:S(2)}, u32[]{:S(2)}) %collective-permute-start.9) | collective-permute-done | bytes 262176 | tf_op jit(solution)/shard_map/ppermute | solution.py:61
  18.1 0.7 copy-done.13
  18.8 3.5 %collective-permute-start.3 = (f32[128,1024]{1,0:T(8,128)S(1)}, f32[128,1024]{1,0:T(8,128)S(1)}, u32[]{:S(2)}, u32[]{:S(2)}) collective-permute-start(f32[128,1024]{1,0:T(8,128)S(1)} %bitcast.22), channel_id=1, source_target_pairs={{0,4},{4,8},{8,12},{1,5},{5,9},{9,13},{2,6},{6,10},{10,14},{3,7},{... | collective-permute-start | bytes 1572872 | tf_op jit(solution)/shard_map/ppermute | solution.py:121
  22.3 0.7 copy-done.15
  23.0 2.4 %collective-permute-start.2 = (f32[128,1024]{1,0:T(8,128)S(1)}, f32[128,1024]{1,0:T(8,128)S(1)}, u32[]{:S(2)}, u32[]{:S(2)}) collective-permute-start(f32[128,1024]{1,0:T(8,128)S(1)} %bitcast.23), channel_id=1, source_target_pairs={{0,3},{1,2},{2,1},{3,0},{4,7},{5,6},{6,5},{7,4},{8,11},{9,10},{10,... | collective-permute-start | bytes 1572872 | tf_op jit(solution)/shard_map/ppermute | solution.py:61
  25.5 0.7 copy-done.17
  27.2 13.6 %collective-permute-done.4.refs_7_ = f32[128,1024]{1,0:T(8,128)S(1)} collective-permute-done((f32[128,1024]{1,0:T(8,128)}, f32[128,1024]{1,0:T(8,128)S(1)}, u32[]{:S(2)}, u32[]{:S(2)}) %collective-permute-start.4) | collective-permute-done | bytes 524320 | tf_op jit(solution)/shard_map/ppermute | solution.py:56
  40.9 1.3 collective-permute-start.5
  42.1 0.8 copy-done.3
  43.0 0.8 copy-done.5
  43.8 0.8 copy-done.7
  44.6 2.5 %collective-permute-done.1.refs_3_ = f32[128,1024]{1,0:T(8,128)S(1)} collective-permute-done((f32[128,1024]{1,0:T(8,128)S(1)}, f32[128,1024]{1,0:T(8,128)S(1)}, u32[]{:S(2)}, u32[]{:S(2)}) %collective-permute-start.1) | collective-permute-done | bytes 524320 | tf_op jit(solution)/shard_map/ppermute | solution.py:61
  47.1 0.8 copy-done.9
  47.9 7.7 %collective-permute-done.5.refs_8_ = f32[128,1024]{1,0:T(8,128)} collective-permute-done((f32[128,1024]{1,0:T(8,128)S(1)}, f32[128,1024]{1,0:T(8,128)}, u32[]{:S(2)}, u32[]{:S(2)}) %collective-permute-start.5) | collective-permute-done | bytes 524320 | tf_op jit(solution)/shard_map/ppermute | solution.py:125
  55.7 1.0 copy-done.4
  56.7 1.0 copy-done.6
  57.7 1.0 copy-done.8
  58.8 1.0 copy-done.10
  59.8 0.9 copy-done.14
  60.8 0.9 copy-done.16
  61.7 0.9 copy-done.18
  62.7 10.1 %slice_products.1 = (f32[512,128]{1,0:T(8,128)S(1)}, f32[512,128]{1,0:T(8,128)}, f32[512,128]{1,0:T(8,128)}, f32[512,128]{1,0:T(8,128)}, f32[512,128]{1,0:T(8,12...) custom-call(s32[35]{0:T(128)S(1)} %concatenate.15.refs_0_.sc, ...), custom_call_target="tpu_custom_call" | custom-call | tf_op jit(solution)/shard_map/slice_products/pallas_call | solution.py:176
  72.9 1.4 collective-permute-start.13
  74.3 0.7 fusion.6
  75.1 4.3 %collective-permute-start.32 = (f32[96,512]{1,0:T(8,128)S(1)}, f32[96,512]{1,0:T(8,128)S(1)}, u32[]{:S(2)}, u32[]{:S(2)}) collective-permute-start(f32[96,512]{1,0:T(8,128)S(1)} %get-tuple-element.51), channel_id=1, source_target_pairs={{0,3},{4,7},{8,11},{12,15},{16,19},{20,23},{24,27},{28,31}} | collective-permute-start | bytes 589832 | tf_op jit(solution)/shard_map/ppermute | solution.py:500
  79.4 1.3 collective-permute-start.31
  80.7 1.3 place_rows.1
  83.2 3.4 %collective-permute-start.12 = (f32[512,128]{1,0:T(8,128)}, f32[512,128]{1,0:T(8,128)}, u32[]{:S(2)}, u32[]{:S(2)}) collective-permute-start(f32[512,128]{1,0:T(8,128)} %get-tuple-element.26), channel_id=1, source_target_pairs={{0,3},{1,2},{2,1},{3,0},{4,7},{5,6},{6,5},{7,4},{8,11},{9,10},{10,... | collective-permute-start | bytes 786440 | tf_op jit(solution)/shard_map/ppermute | solution.py:61
  86.6 0.7 copy-done.21
  87.3 2.1 %collective-permute-start.30 = (f32[96,512]{1,0:T(8,128)}, f32[96,512]{1,0:T(8,128)}, u32[]{:S(2)}, u32[]{:S(2)}) collective-permute-start(f32[96,512]{1,0:T(8,128)} %get-tuple-element.53), channel_id=1, source_target_pairs={{0,1},{4,5},{8,9},{12,13},{16,17},{20,21},{24,25},{28,29}} | collective-permute-start | bytes 589832 | tf_op jit(solution)/shard_map/ppermute | solution.py:500
  89.4 1.9 %collective-permute-start.14 = (f32[3,256,128]{2,1,0:T(8,128)}, f32[3,256,128]{2,1,0:T(8,128)S(1)}, u32[]{:S(2)}, u32[]{:S(2)}) collective-permute-start(f32[3,256,128]{2,1,0:T(8,128)} %copy-done.23), channel_id=1, source_target_pairs={{0,4},{4,8},{8,12},{1,5},{5,9},{9,13},{2,6},{6,10},{10,14},{3,7},{... | collective-permute-start | bytes 1179656 | tf_op jit(solution)/shard_map/ppermute | solution.py:66
  91.4 0.9 fusion
  92.3 6.4 %collective-permute-done.30.refs_6_ = f32[96,512]{1,0:T(8,128)} collective-permute-done((f32[96,512]{1,0:T(8,128)}, f32[96,512]{1,0:T(8,128)}, u32[]{:S(2)}, u32[]{:S(2)}) %collective-permute-start.30) | collective-permute-done | bytes 196640 | tf_op jit(solution)/shard_map/ppermute | solution.py:500
  98.7 2.5 %collective-permute-start.27 = (f32[2,96,128]{2,1,0:T(8,128)S(1)}, f32[2,96,128]{2,1,0:T(8,128)S(1)}, u32[]{:S(2)}, u32[]{:S(2)}) collective-permute-start(f32[2,96,128]{2,1,0:T(8,128)S(1)} %get-tuple-element.61), channel_id=1, source_target_pairs={{0,1},{1,0},{2,3},{3,2},{4,5},{5,4},{6,7},{7,6},{8,9},{9,8},{10,11... | collective-permute-start | bytes 294920 | tf_op jit(solution)/shard_map/ppermute | solution.py:61
  101.2 1.6 collective-permute-start.28
  102.8 1.4 collective-permute-done.29.refs_4_
  104.2 1.9 %collective-permute-done.27.refs_2_ = f32[2,96,128]{2,1,0:T(8,128)S(1)} collective-permute-done((f32[2,96,128]{2,1,0:T(8,128)S(1)}, f32[2,96,128]{2,1,0:T(8,128)S(1)}, u32[]{:S(2)}, u32[]{:S(2)}) %collective-permute-start.27) | collective-permute-done | bytes 98336 | tf_op jit(solution)/shard_map/ppermute | solution.py:61
  106.7 0.9 copy-done.20
  107.6 0.9 copy-done.22
  108.6 2.0 %factor_slice.1.refs_1_.refs_18_ = f32[96,512]{1,0:T(8,128)S(1)} custom-call(s32[35]{0:T(128)S(1)} %concatenate.15.refs_0_.sc, f32[2,96,128]{2,1,0:T(8,128)S(1)} %get-tuple-element.60.refs_1_, f32[2,96,128]{2,1,0:T(8,128)S(1)} %collective-permute-done.27.refs_2_, f32[2,96,128]{2,1,0:T(8,128)S(1)} %collective-permute-done.28.refs_3_, ...), custom_call_target="tpu_custom_call" | custom-call | tf_op jit(solution)/shard_map/factor_slice/pallas_call | solution.py:312
  110.7 1.4 collective-permute-start.37
  112.1 1.2 collective-permute-start.36
  113.3 2.6 %collective-permute-start.35 = (f32[96,512]{1,0:T(8,128)S(1)}, f32[96,512]{1,0:T(8,128)S(1)}, u32[]{:S(2)}, u32[]{:S(2)}) collective-permute-start(f32[96,512]{1,0:T(8,128)S(1)} %factor_slice.1.refs_1_.refs_18_), channel_id=1, source_target_pairs={{0,3},{1,2},{2,1},{3,0},{4,7},{5,6},{6,5},{7,4},{8,11},{9,10},{10,... | collective-permute-start | bytes 589832 | tf_op jit(solution)/shard_map/ppermute | solution.py:61
  116.0 1.3 collective-permute-start.34
  117.2 1.1 collective-permute-done.38.refs_4_
  118.3 2.7 %collective-permute-start.33 = (f32[96,512]{1,0:T(8,128)S(1)}, f32[96,512]{1,0:T(8,128)S(1)}, u32[]{:S(2)}, u32[]{:S(2)}) collective-permute-start(f32[96,512]{1,0:T(8,128)S(1)} %factor_slice.1.refs_1_.refs_18_), channel_id=1, source_target_pairs={{0,1},{1,0},{2,3},{3,2},{4,5},{5,4},{6,7},{7,6},{8,9},{9,8},{10,11... | collective-permute-start | bytes 589832 | tf_op jit(solution)/shard_map/ppermute | solution.py:61
  121.0 2.5 %pack_halo.1 = (f32[1024,128]{1,0:T(8,128)S(1)}, f32[1024,128]{1,0:T(8,128)S(1)}, f32[1024,128]{1,0:T(8,128)S(1)}, f32[1024,128]{1,0:T(8,128)S(1)}) custom-call(s32[35]{0:T(128)S(1)} %concatenate.15.refs_0_.sc, f32[3,512,128]{2,1,0:T(8,128)S(1)} %get-tuple-element.27.previous_ref, f32[256,128]{1,0:T(8,128)S(1)} %collective-permute-done.13.edge_ref, ...), custom_call_target="tpu_custom_call" | custom-call | tf_op jit(solution)/shard_map/pack_halo/pallas_call | solution.py:219
  123.5 6.3 %collective-permute-done.37.refs_3_ = f32[96,512]{1,0:T(8,128)S(1)} collective-permute-done((f32[96,512]{1,0:T(8,128)S(1)}, f32[96,512]{1,0:T(8,128)S(1)}, u32[]{:S(2)}, u32[]{:S(2)}) %collective-permute-start.37) | collective-permute-done | bytes 196640 | tf_op jit(solution)/shard_map/ppermute | solution.py:56
  129.8 2.7 %collective-permute-start.15 = (f32[1024,128]{1,0:T(8,128)S(1)}, f32[1024,128]{1,0:T(8,128)S(1)}, u32[]{:S(2)}, u32[]{:S(2)}) collective-permute-start(f32[1024,128]{1,0:T(8,128)S(1)} %get-tuple-element.31), channel_id=1, source_target_pairs={{0,1},{1,0},{2,3},{3,2},{4,5},{5,4},{6,7},{7,6},{8,9},{9,8},{10,11... | collective-permute-start | bytes 1572872 | tf_op jit(solution)/shard_map/ppermute | solution.py:61
  132.5 0.8 collective-permute-start.16
  133.3 0.7 collective-permute-start.17
  134.0 1.7 pick_for_cols.1
  135.7 2.1 %collective-permute-start.39 = (f32[96,512]{1,0:T(8,128)S(1)}, f32[96,512]{1,0:T(8,128)S(1)}, u32[]{:S(2)}, u32[]{:S(2)}) collective-permute-start(f32[96,512]{1,0:T(8,128)S(1)} %get-tuple-element.38), channel_id=1, source_target_pairs={{0,1},{1,0},{2,3},{3,2},{4,5},{5,4},{6,7},{7,6},{8,9},{9,8},{10,11... | collective-permute-start | bytes 589832 | tf_op jit(solution)/shard_map/ppermute | solution.py:61
  137.8 0.8 collective-permute-start.40
  138.5 21.2 %collective-permute-done.39.refs_23_ = f32[96,512]{1,0:T(8,128)S(1)} collective-permute-done((f32[96,512]{1,0:T(8,128)S(1)}, f32[96,512]{1,0:T(8,128)S(1)}, u32[]{:S(2)}, u32[]{:S(2)}) %collective-permute-start.39) | collective-permute-done | bytes 196640 | tf_op jit(solution)/shard_map/ppermute | solution.py:61
  159.7 1.9 %collective-permute-start.41 = (f32[96,512]{1,0:T(8,128)S(1)}, f32[96,512]{1,0:T(8,128)S(1)}, u32[]{:S(2)}, u32[]{:S(2)}) collective-permute-start(f32[96,512]{1,0:T(8,128)S(1)} %get-tuple-element.40), channel_id=1, source_target_pairs={{0,3},{1,2},{2,1},{3,0},{4,7},{5,6},{6,5},{7,4},{8,11},{9,10},{10,... | collective-permute-start | bytes 589832 | tf_op jit(solution)/shard_map/ppermute | solution.py:61
  161.7 4.8 %collective-permute-done.41.refs_25_ = f32[96,512]{1,0:T(8,128)S(1)} collective-permute-done((f32[96,512]{1,0:T(8,128)S(1)}, f32[96,512]{1,0:T(8,128)S(1)}, u32[]{:S(2)}, u32[]{:S(2)}) %collective-permute-start.41) | collective-permute-done | bytes 196640 | tf_op jit(solution)/shard_map/ppermute | solution.py:61
  168.5 2.0 %collective-permute-done.43.refs_27_ = f32[96,512]{1,0:T(8,128)S(1)} collective-permute-done((f32[96,512]{1,0:T(8,128)S(1)}, f32[96,512]{1,0:T(8,128)S(1)}, u32[]{:S(2)}, u32[]{:S(2)}) %collective-permute-start.43) | collective-permute-done | bytes 196640 | tf_op jit(solution)/shard_map/ppermute | solution.py:61
  170.8 1.2 collective-permute-done.45.refs_29_
  171.9 9.5 %finish.1 = f32[384,768]{1,0:T(8,128)} custom-call(s32[35]{0:T(128)S(1)} %concatenate.15.refs_0_.sc, f32[384,768]{1,0:T(8,128)S(1)} %copy-done, f32[512,128]{1,0:T(8,128)S(1)} %copy-done.12, f32[512,128]{1,0:T(8,128)} %collective-permute-done.10.refs_3_, f32[512,128]{1,0:T(8,128)} %collective-permute-done.11.refs_4_, ...), custom_call_target="tpu_custom_call" | custom-call | tf_op jit(solution)/shard_map/finish/pallas_call | solution.py:431
  (99 shorter events, 6.7 us)
Async XLA Ops:
  0.0 18.8 %copy-start.1 = (f32[1,128,1024]{2,1,0:T(8,128)S(1)}, f32[1,128,1024]{2,1,0:T(8,128)}, u32[]{:S(2)}) copy-start(f32[1,128,1024]{2,1,0:T(8,128)} %param.6) | copy-start | bytes 1572868
  0.0 11.5 %copy-start.24 = (s32[2,16]{1,0:T(2,128)S(1)}, s32[2,16]{1,0:T(2,128)}, u32[]{:S(2)}) copy-start(s32[2,16]{1,0:T(2,128)} %param.7) | copy-start | bytes 388
  0.0 26.7 %collective-permute-start.6 = (f32[128,1024]{1,0:T(8,128)}, f32[128,1024]{1,0:T(8,128)S(1)}, u32[]{:S(2)}, u32[]{:S(2)}) collective-permute-start(f32[128,1024]{1,0:T(8,128)} %bitcast.20), channel_id=1, source_target_pairs={{4,0},{8,4},{12,8},{5,1},{9,5},{13,9},{6,2},{10,6},{14,10},{7,3},{... | collective-permute-start | bytes 1572872 | tf_op jit(solution)/shard_map/ppermute | solution.py:122
  1.4 39.4 %collective-permute-start.4 = (f32[128,1024]{1,0:T(8,128)}, f32[128,1024]{1,0:T(8,128)S(1)}, u32[]{:S(2)}, u32[]{:S(2)}) collective-permute-start(f32[128,1024]{1,0:T(8,128)} %bitcast.21), channel_id=1, source_target_pairs={{0,8},{4,12},{8,0},{12,4},{1,9},{5,13},{9,1},{13,5},{2,10},{6,14},... | collective-permute-start | bytes 1572872 | tf_op jit(solution)/shard_map/ppermute | solution.py:56
  7.9 10.2 %collective-permute-start.9 = (f32[512,128]{1,0:T(8,128)S(1)}, f32[512,128]{1,0:T(8,128)S(1)}, u32[]{:S(2)}, u32[]{:S(2)}) collective-permute-start(f32[512,128]{1,0:T(8,128)S(1)} %get-tuple-element.55), channel_id=1, source_target_pairs={{0,3},{1,2},{2,1},{3,0},{4,7},{5,6},{6,5},{7,4},{8,11},{9,10},{10,... | collective-permute-start | bytes 786440 | tf_op jit(solution)/shard_map/ppermute | solution.py:61
  10.4 11.9 %collective-permute-start.7 = (f32[512,128]{1,0:T(8,128)S(1)}, f32[512,128]{1,0:T(8,128)S(1)}, u32[]{:S(2)}, u32[]{:S(2)}) collective-permute-start(f32[512,128]{1,0:T(8,128)S(1)} %get-tuple-element.56), channel_id=1, source_target_pairs={{0,1},{1,0},{2,3},{3,2},{4,5},{5,4},{6,7},{7,6},{8,9},{9,8},{10,11... | collective-permute-start | bytes 786440 | tf_op jit(solution)/shard_map/ppermute | solution.py:61
  11.0 14.5 %collective-permute-start.8 = (f32[512,128]{1,0:T(8,128)S(1)}, f32[512,128]{1,0:T(8,128)S(1)}, u32[]{:S(2)}, u32[]{:S(2)}) collective-permute-start(f32[512,128]{1,0:T(8,128)S(1)} %get-tuple-element.58), channel_id=1, source_target_pairs={{0,2},{1,3},{2,0},{3,1},{4,6},{5,7},{6,4},{7,5},{8,10},{9,11},{10,... | collective-permute-start | bytes 786440 | tf_op jit(solution)/shard_map/ppermute | solution.py:61
  18.8 24.2 %collective-permute-start.3 = (f32[128,1024]{1,0:T(8,128)S(1)}, f32[128,1024]{1,0:T(8,128)S(1)}, u32[]{:S(2)}, u32[]{:S(2)}) collective-permute-start(f32[128,1024]{1,0:T(8,128)S(1)} %bitcast.22), channel_id=1, source_target_pairs={{0,4},{4,8},{8,12},{1,5},{5,9},{9,13},{2,6},{6,10},{10,14},{3,7},{... | collective-permute-start | bytes 1572872 | tf_op jit(solution)/shard_map/ppermute | solution.py:121
  23.0 20.8 %collective-permute-start.2 = (f32[128,1024]{1,0:T(8,128)S(1)}, f32[128,1024]{1,0:T(8,128)S(1)}, u32[]{:S(2)}, u32[]{:S(2)}) collective-permute-start(f32[128,1024]{1,0:T(8,128)S(1)} %bitcast.23), channel_id=1, source_target_pairs={{0,3},{1,2},{2,1},{3,0},{4,7},{5,6},{6,5},{7,4},{8,11},{9,10},{10,... | collective-permute-start | bytes 1572872 | tf_op jit(solution)/shard_map/ppermute | solution.py:61
  26.2 21.0 %collective-permute-start.1 = (f32[128,1024]{1,0:T(8,128)S(1)}, f32[128,1024]{1,0:T(8,128)S(1)}, u32[]{:S(2)}, u32[]{:S(2)}) collective-permute-start(f32[128,1024]{1,0:T(8,128)S(1)} %bitcast.24), channel_id=1, source_target_pairs={{0,2},{1,3},{2,0},{3,1},{4,6},{5,7},{6,4},{7,5},{8,10},{9,11},{10,... | collective-permute-start | bytes 1572872 | tf_op jit(solution)/shard_map/ppermute | solution.py:61
  26.7 21.2 %collective-permute-start = (f32[128,1024]{1,0:T(8,128)S(1)}, f32[128,1024]{1,0:T(8,128)}, u32[]{:S(2)}, u32[]{:S(2)}) collective-permute-start(f32[128,1024]{1,0:T(8,128)S(1)} %bitcast.25), channel_id=1, source_target_pairs={{0,1},{1,0},{2,3},{3,2},{4,5},{5,4},{6,7},{7,6},{8,9},{9,8},{10,11... | collective-permute-start | bytes 1572872 | tf_op jit(solution)/shard_map/ppermute | solution.py:61
  40.9 14.8 %collective-permute-start.5 = (f32[128,1024]{1,0:T(8,128)S(1)}, f32[128,1024]{1,0:T(8,128)}, u32[]{:S(2)}, u32[]{:S(2)}) collective-permute-start(f32[128,1024]{1,0:T(8,128)S(1)} %collective-permute-done.4.refs_7_), channel_id=1, source_target_pairs={{8,12},{4,0},{9,13},{5,1},{10,14},{6,2},{11,15},{7,3},{24,28},{20,... | collective-permute-start | bytes 1572872 | tf_op jit(solution)/shard_map/ppermute | solution.py:125
  42.1 0.8 copy-start.3
  43.8 0.8 copy-start.7
  55.6 1.0 copy-start.4
  56.7 1.0 copy-start.6
  57.7 1.0 copy-start.8
  58.8 1.0 copy-start.10
  59.8 0.9 copy-start.14
  60.8 0.9 copy-start.16
  61.7 0.9 copy-start.18
  62.7 11.6 %copy-start = (f32[384,768]{1,0:T(8,128)S(1)}, f32[384,768]{1,0:T(8,128)}, u32[]{:S(2)}) copy-start(f32[384,768]{1,0:T(8,128)} %refs_1_.1) | copy-start | bytes 3538948
  72.8 7.9 %copy-start.11 = (f32[512,128]{1,0:T(8,128)}, f32[512,128]{1,0:T(8,128)S(1)}, u32[]{:S(2)}) copy-start(f32[512,128]{1,0:T(8,128)S(1)} %get-tuple-element.23.refs_2_) | copy-start | bytes 786436
  72.8 13.8 %copy-start.23 = (f32[3,256,128]{2,1,0:T(8,128)}, f32[3,256,128]{2,1,0:T(8,128)S(1)}, u32[]{:S(2)}) copy-start(f32[3,256,128]{2,1,0:T(8,128)S(1)} %get-tuple-element.29) | copy-start | bytes 1179652
  72.9 33.8 %copy-start.2 = (f32[512,512]{1,0:T(8,128)S(1)}, f32[512,512]{1,0:T(8,128)}, u32[]{:S(2)}) copy-start(f32[512,512]{1,0:T(8,128)} %refs_9_.1) | copy-start | bytes 3145732
  72.9 7.8 %collective-permute-start.13 = (f32[256,128]{1,0:T(8,128)S(1)}, f32[256,128]{1,0:T(8,128)S(1)}, u32[]{:S(2)}, u32[]{:S(2)}) collective-permute-start(f32[256,128]{1,0:T(8,128)S(1)} %get-tuple-element.28), channel_id=1, source_target_pairs={{0,4},{4,8},{8,12},{1,5},{5,9},{9,13},{2,6},{6,10},{10,14},{3,7},{... | collective-permute-start | bytes 393224 | tf_op jit(solution)/shard_map/ppermute | solution.py:66
  75.1 7.5 %collective-permute-start.32 = (f32[96,512]{1,0:T(8,128)S(1)}, f32[96,512]{1,0:T(8,128)S(1)}, u32[]{:S(2)}, u32[]{:S(2)}) collective-permute-start(f32[96,512]{1,0:T(8,128)S(1)} %get-tuple-element.51), channel_id=1, source_target_pairs={{0,3},{4,7},{8,11},{12,15},{16,19},{20,23},{24,27},{28,31}} | collective-permute-start | bytes 589832 | tf_op jit(solution)/shard_map/ppermute | solution.py:500
  79.4 7.2 %collective-permute-start.31 = (f32[96,512]{1,0:T(8,128)S(1)}, f32[96,512]{1,0:T(8,128)S(1)}, u32[]{:S(2)}, u32[]{:S(2)}) collective-permute-start(f32[96,512]{1,0:T(8,128)S(1)} %get-tuple-element.52), channel_id=1, source_target_pairs={{0,2},{4,6},{8,10},{12,14},{16,18},{20,22},{24,26},{28,30}} | collective-permute-start | bytes 589832 | tf_op jit(solution)/shard_map/ppermute | solution.py:500
  82.0 7.5 %collective-permute-start.26 = (f32[384,128]{1,0:T(8,128)}, f32[384,128]{1,0:T(8,128)}, u32[]{:S(2)}, u32[]{:S(2)}) collective-permute-start(f32[384,128]{1,0:T(8,128)} %get-tuple-element.36), channel_id=1, source_target_pairs={{0,16},{16,0},{1,17},{17,1},{2,18},{18,2},{3,19},{19,3},{4,20},{20... | collective-permute-start | bytes 589832 | tf_op jit(solution)/shard_map/ppermute | solution.py:61
  82.0 16.7 %collective-permute-start.10 = (f32[512,128]{1,0:T(8,128)}, f32[512,128]{1,0:T(8,128)}, u32[]{:S(2)}, u32[]{:S(2)}) collective-permute-start(f32[512,128]{1,0:T(8,128)} %get-tuple-element.24), channel_id=1, source_target_pairs={{0,1},{1,0},{2,3},{3,2},{4,5},{5,4},{6,7},{7,6},{8,9},{9,8},{10,11... | collective-permute-start | bytes 786440 | tf_op jit(solution)/shard_map/ppermute | solution.py:61
  82.0 19.2 %collective-permute-start.11 = (f32[512,128]{1,0:T(8,128)}, f32[512,128]{1,0:T(8,128)}, u32[]{:S(2)}, u32[]{:S(2)}) collective-permute-start(f32[512,128]{1,0:T(8,128)} %get-tuple-element.25), channel_id=1, source_target_pairs={{0,2},{1,3},{2,0},{3,1},{4,6},{5,7},{6,4},{7,5},{8,10},{9,11},{10,... | collective-permute-start | bytes 786440 | tf_op jit(solution)/shard_map/ppermute | solution.py:61
  83.2 18.0 %collective-permute-start.12 = (f32[512,128]{1,0:T(8,128)}, f32[512,128]{1,0:T(8,128)}, u32[]{:S(2)}, u32[]{:S(2)}) collective-permute-start(f32[512,128]{1,0:T(8,128)} %get-tuple-element.26), channel_id=1, source_target_pairs={{0,3},{1,2},{2,1},{3,0},{4,7},{5,6},{6,5},{7,4},{8,11},{9,10},{10,... | collective-permute-start | bytes 786440 | tf_op jit(solution)/shard_map/ppermute | solution.py:61
  87.3 11.4 %collective-permute-start.30 = (f32[96,512]{1,0:T(8,128)}, f32[96,512]{1,0:T(8,128)}, u32[]{:S(2)}, u32[]{:S(2)}) collective-permute-start(f32[96,512]{1,0:T(8,128)} %get-tuple-element.53), channel_id=1, source_target_pairs={{0,1},{4,5},{8,9},{12,13},{16,17},{20,21},{24,25},{28,29}} | collective-permute-start | bytes 589832 | tf_op jit(solution)/shard_map/ppermute | solution.py:500
  89.4 21.2 %collective-permute-start.14 = (f32[3,256,128]{2,1,0:T(8,128)}, f32[3,256,128]{2,1,0:T(8,128)S(1)}, u32[]{:S(2)}, u32[]{:S(2)}) collective-permute-start(f32[3,256,128]{2,1,0:T(8,128)} %copy-done.23), channel_id=1, source_target_pairs={{0,4},{4,8},{8,12},{1,5},{5,9},{9,13},{2,6},{6,10},{10,14},{3,7},{... | collective-permute-start | bytes 1179656 | tf_op jit(solution)/shard_map/ppermute | solution.py:66
  98.7 5.5 %collective-permute-start.29 = (f32[2,96,128]{2,1,0:T(8,128)S(1)}, f32[2,96,128]{2,1,0:T(8,128)S(1)}, u32[]{:S(2)}, u32[]{:S(2)}) collective-permute-start(f32[2,96,128]{2,1,0:T(8,128)S(1)} %get-tuple-element.59), channel_id=1, source_target_pairs={{0,3},{1,2},{2,1},{3,0},{4,7},{5,6},{6,5},{7,4},{8,11},{9,10},{10,... | collective-permute-start | bytes 294920 | tf_op jit(solution)/shard_map/ppermute | solution.py:61
  98.7 7.5 %collective-permute-start.27 = (f32[2,96,128]{2,1,0:T(8,128)S(1)}, f32[2,96,128]{2,1,0:T(8,128)S(1)}, u32[]{:S(2)}, u32[]{:S(2)}) collective-permute-start(f32[2,96,128]{2,1,0:T(8,128)S(1)} %get-tuple-element.61), channel_id=1, source_target_pairs={{0,1},{1,0},{2,3},{3,2},{4,5},{5,4},{6,7},{7,6},{8,9},{9,8},{10,11... | collective-permute-start | bytes 294920 | tf_op jit(solution)/shard_map/ppermute | solution.py:61
  101.2 9.4 %collective-permute-start.18 = (f32[512,128]{1,0:T(8,128)}, f32[512,128]{1,0:T(8,128)S(1)}, u32[]{:S(2)}, u32[]{:S(2)}) collective-permute-start(f32[512,128]{1,0:T(8,128)} %copy-done.11), channel_id=1, source_target_pairs={{0,16},{16,0},{1,17},{17,1},{2,18},{18,2},{3,19},{19,3},{4,20},{20... | collective-permute-start | bytes 786440 | tf_op jit(solution)/shard_map/ppermute | solution.py:61
  101.2 5.2 %collective-permute-start.28 = (f32[2,96,128]{2,1,0:T(8,128)S(1)}, f32[2,96,128]{2,1,0:T(8,128)S(1)}, u32[]{:S(2)}, u32[]{:S(2)}) collective-permute-start(f32[2,96,128]{2,1,0:T(8,128)S(1)} %get-tuple-element.62), channel_id=1, source_target_pairs={{0,2},{1,3},{2,0},{3,1},{4,6},{5,7},{6,4},{7,5},{8,10},{9,11},{10,... | collective-permute-start | bytes 294920 | tf_op jit(solution)/shard_map/ppermute | solution.py:61
  104.2 7.9 %collective-permute-start.19 = (f32[512,128]{1,0:T(8,128)}, f32[512,128]{1,0:T(8,128)S(1)}, u32[]{:S(2)}, u32[]{:S(2)}) collective-permute-start(f32[512,128]{1,0:T(8,128)} %collective-permute-done.10.refs_3_), channel_id=1, source_target_pairs={{0,16},{16,0},{1,17},{17,1},{2,18},{18,2},{3,19},{19,3},{4,20},{20... | collective-permute-start | bytes 786440 | tf_op jit(solution)/shard_map/ppermute | solution.py:61
  106.2 7.1 %collective-permute-start.20 = (f32[512,128]{1,0:T(8,128)}, f32[512,128]{1,0:T(8,128)S(1)}, u32[]{:S(2)}, u32[]{:S(2)}) collective-permute-start(f32[512,128]{1,0:T(8,128)} %collective-permute-done.11.refs_4_), channel_id=1, source_target_pairs={{0,16},{16,0},{1,17},{17,1},{2,18},{18,2},{3,19},{19,3},{4,20},{20... | collective-permute-start | bytes 786440 | tf_op jit(solution)/shard_map/ppermute | solution.py:61
  106.4 9.6 %collective-permute-start.21 = (f32[512,128]{1,0:T(8,128)}, f32[512,128]{1,0:T(8,128)S(1)}, u32[]{:S(2)}, u32[]{:S(2)}) collective-permute-start(f32[512,128]{1,0:T(8,128)} %collective-permute-done.12.refs_5_), channel_id=1, source_target_pairs={{0,16},{16,0},{1,17},{17,1},{2,18},{18,2},{3,19},{19,3},{4,20},{20... | collective-permute-start | bytes 786440 | tf_op jit(solution)/shard_map/ppermute | solution.py:61
  106.7 0.9 copy-start.20
  107.6 0.9 copy-start.22
  110.6 61.4 %copy-start.12 = (f32[512,128]{1,0:T(8,128)S(1)}, f32[512,128]{1,0:T(8,128)}, u32[]{:S(2)}) copy-start(f32[512,128]{1,0:T(8,128)} %copy-done.11) | copy-start | bytes 786436
  110.6 7.7 %collective-permute-start.38 = (f32[96,512]{1,0:T(8,128)S(1)}, f32[96,512]{1,0:T(8,128)S(1)}, u32[]{:S(2)}, u32[]{:S(2)}) collective-permute-start(f32[96,512]{1,0:T(8,128)S(1)} %factor_slice.1.refs_1_.refs_18_), channel_id=1, source_target_pairs={{0,12},{4,0},{8,4},{12,8},{1,13},{5,1},{9,5},{13,9},{2,14},{6,2},{... | collective-permute-start | bytes 589832 | tf_op jit(solution)/shard_map/ppermute | solution.py:56
  110.7 19.1 %collective-permute-start.37 = (f32[96,512]{1,0:T(8,128)S(1)}, f32[96,512]{1,0:T(8,128)S(1)}, u32[]{:S(2)}, u32[]{:S(2)}) collective-permute-start(f32[96,512]{1,0:T(8,128)S(1)} %factor_slice.1.refs_1_.refs_18_), channel_id=1, source_target_pairs={{0,8},{4,12},{8,0},{12,4},{1,9},{5,13},{9,1},{13,5},{2,10},{6,14},... | collective-permute-start | bytes 589832 | tf_op jit(solution)/shard_map/ppermute | solution.py:56
  112.1 20.4 %collective-permute-start.36 = (f32[96,512]{1,0:T(8,128)S(1)}, f32[96,512]{1,0:T(8,128)S(1)}, u32[]{:S(2)}, u32[]{:S(2)}) collective-permute-start(f32[96,512]{1,0:T(8,128)S(1)} %factor_slice.1.refs_1_.refs_18_), channel_id=1, source_target_pairs={{0,4},{4,8},{8,12},{12,0},{1,5},{5,9},{9,13},{13,1},{2,6},{6,10},{... | collective-permute-start | bytes 589832 | tf_op jit(solution)/shard_map/ppermute | solution.py:56
  113.3 19.9 %collective-permute-start.35 = (f32[96,512]{1,0:T(8,128)S(1)}, f32[96,512]{1,0:T(8,128)S(1)}, u32[]{:S(2)}, u32[]{:S(2)}) collective-permute-start(f32[96,512]{1,0:T(8,128)S(1)} %factor_slice.1.refs_1_.refs_18_), channel_id=1, source_target_pairs={{0,3},{1,2},{2,1},{3,0},{4,7},{5,6},{6,5},{7,4},{8,11},{9,10},{10,... | collective-permute-start | bytes 589832 | tf_op jit(solution)/shard_map/ppermute | solution.py:61
  116.0 19.7 %collective-permute-start.34 = (f32[96,512]{1,0:T(8,128)S(1)}, f32[96,512]{1,0:T(8,128)S(1)}, u32[]{:S(2)}, u32[]{:S(2)}) collective-permute-start(f32[96,512]{1,0:T(8,128)S(1)} %factor_slice.1.refs_1_.refs_18_), channel_id=1, source_target_pairs={{0,2},{1,3},{2,0},{3,1},{4,6},{5,7},{6,4},{7,5},{8,10},{9,11},{10,... | collective-permute-start | bytes 589832 | tf_op jit(solution)/shard_map/ppermute | solution.py:61
  118.3 19.4 %collective-permute-start.33 = (f32[96,512]{1,0:T(8,128)S(1)}, f32[96,512]{1,0:T(8,128)S(1)}, u32[]{:S(2)}, u32[]{:S(2)}) collective-permute-start(f32[96,512]{1,0:T(8,128)S(1)} %factor_slice.1.refs_1_.refs_18_), channel_id=1, source_target_pairs={{0,1},{1,0},{2,3},{3,2},{4,5},{5,4},{6,7},{7,6},{8,9},{9,8},{10,11... | collective-permute-start | bytes 589832 | tf_op jit(solution)/shard_map/ppermute | solution.py:61
  129.8 36.7 %collective-permute-start.15 = (f32[1024,128]{1,0:T(8,128)S(1)}, f32[1024,128]{1,0:T(8,128)S(1)}, u32[]{:S(2)}, u32[]{:S(2)}) collective-permute-start(f32[1024,128]{1,0:T(8,128)S(1)} %get-tuple-element.31), channel_id=1, source_target_pairs={{0,1},{1,0},{2,3},{3,2},{4,5},{5,4},{6,7},{7,6},{8,9},{9,8},{10,11... | collective-permute-start | bytes 1572872 | tf_op jit(solution)/shard_map/ppermute | solution.py:61
  132.5 34.5 %collective-permute-start.16 = (f32[1024,128]{1,0:T(8,128)S(1)}, f32[1024,128]{1,0:T(8,128)S(1)}, u32[]{:S(2)}, u32[]{:S(2)}) collective-permute-start(f32[1024,128]{1,0:T(8,128)S(1)} %get-tuple-element.32), channel_id=1, source_target_pairs={{0,2},{1,3},{2,0},{3,1},{4,6},{5,7},{6,4},{7,5},{8,10},{9,11},{10,... | collective-permute-start | bytes 1572872 | tf_op jit(solution)/shard_map/ppermute | solution.py:61
  133.3 33.8 %collective-permute-start.17 = (f32[1024,128]{1,0:T(8,128)S(1)}, f32[1024,128]{1,0:T(8,128)S(1)}, u32[]{:S(2)}, u32[]{:S(2)}) collective-permute-start(f32[1024,128]{1,0:T(8,128)S(1)} %get-tuple-element.33), channel_id=1, source_target_pairs={{0,3},{1,2},{2,1},{3,0},{4,7},{5,6},{6,5},{7,4},{8,11},{9,10},{10,... | collective-permute-start | bytes 1572872 | tf_op jit(solution)/shard_map/ppermute | solution.py:61
  135.7 24.1 %collective-permute-start.39 = (f32[96,512]{1,0:T(8,128)S(1)}, f32[96,512]{1,0:T(8,128)S(1)}, u32[]{:S(2)}, u32[]{:S(2)}) collective-permute-start(f32[96,512]{1,0:T(8,128)S(1)} %get-tuple-element.38), channel_id=1, source_target_pairs={{0,1},{1,0},{2,3},{3,2},{4,5},{5,4},{6,7},{7,6},{8,9},{9,8},{10,11... | collective-permute-start | bytes 589832 | tf_op jit(solution)/shard_map/ppermute | solution.py:61
  137.8 23.9 %collective-permute-start.40 = (f32[96,512]{1,0:T(8,128)S(1)}, f32[96,512]{1,0:T(8,128)S(1)}, u32[]{:S(2)}, u32[]{:S(2)}) collective-permute-start(f32[96,512]{1,0:T(8,128)S(1)} %get-tuple-element.39), channel_id=1, source_target_pairs={{0,2},{1,3},{2,0},{3,1},{4,6},{5,7},{6,4},{7,5},{8,10},{9,11},{10,... | collective-permute-start | bytes 589832 | tf_op jit(solution)/shard_map/ppermute | solution.py:61
  159.7 6.8 %collective-permute-start.41 = (f32[96,512]{1,0:T(8,128)S(1)}, f32[96,512]{1,0:T(8,128)S(1)}, u32[]{:S(2)}, u32[]{:S(2)}) collective-permute-start(f32[96,512]{1,0:T(8,128)S(1)} %get-tuple-element.40), channel_id=1, source_target_pairs={{0,3},{1,2},{2,1},{3,0},{4,7},{5,6},{6,5},{7,4},{8,11},{9,10},{10,... | collective-permute-start | bytes 589832 | tf_op jit(solution)/shard_map/ppermute | solution.py:61
  161.7 6.4 %collective-permute-start.22 = (f32[1024,128]{1,0:T(8,128)S(1)}, f32[1024,128]{1,0:T(8,128)S(1)}, u32[]{:S(2)}, u32[]{:S(2)}) collective-permute-start(f32[1024,128]{1,0:T(8,128)S(1)} %get-tuple-element.30.refs_6_), channel_id=1, source_target_pairs={{0,16},{16,0},{1,17},{17,1},{2,18},{18,2},{3,19},{19,3},{4,20},{20... | collective-permute-start | bytes 1572872 | tf_op jit(solution)/shard_map/ppermute | solution.py:61
  166.5 1.4 collective-permute-start.42
  166.5 5.4 %collective-permute-start.23 = (f32[1024,128]{1,0:T(8,128)S(1)}, f32[1024,128]{1,0:T(8,128)S(1)}, u32[]{:S(2)}, u32[]{:S(2)}) collective-permute-start(f32[1024,128]{1,0:T(8,128)S(1)} %collective-permute-done.15.refs_7_), channel_id=1, source_target_pairs={{0,16},{16,0},{1,17},{17,1},{2,18},{18,2},{3,19},{19,3},{4,20},{20... | collective-permute-start | bytes 1572872 | tf_op jit(solution)/shard_map/ppermute | solution.py:61
  167.0 4.9 %collective-permute-start.24 = (f32[1024,128]{1,0:T(8,128)S(1)}, f32[1024,128]{1,0:T(8,128)S(1)}, u32[]{:S(2)}, u32[]{:S(2)}) collective-permute-start(f32[1024,128]{1,0:T(8,128)S(1)} %collective-permute-done.16.refs_8_), channel_id=1, source_target_pairs={{0,16},{16,0},{1,17},{17,1},{2,18},{18,2},{3,19},{19,3},{4,20},{20... | collective-permute-start | bytes 1572872 | tf_op jit(solution)/shard_map/ppermute | solution.py:61
  167.1 4.8 %collective-permute-start.25 = (f32[1024,128]{1,0:T(8,128)S(1)}, f32[1024,128]{1,0:T(8,128)S(1)}, u32[]{:S(2)}, u32[]{:S(2)}) collective-permute-start(f32[1024,128]{1,0:T(8,128)S(1)} %collective-permute-done.17.refs_9_), channel_id=1, source_target_pairs={{0,16},{16,0},{1,17},{17,1},{2,18},{18,2},{3,19},{19,3},{4,20},{20... | collective-permute-start | bytes 1572872 | tf_op jit(solution)/shard_map/ppermute | solution.py:61
  168.0 2.5 %collective-permute-start.43 = (f32[96,512]{1,0:T(8,128)S(1)}, f32[96,512]{1,0:T(8,128)S(1)}, u32[]{:S(2)}, u32[]{:S(2)}) collective-permute-start(f32[96,512]{1,0:T(8,128)S(1)} %collective-permute-done.39.refs_23_), channel_id=1, source_target_pairs={{0,16},{16,0},{1,17},{17,1},{2,18},{18,2},{3,19},{19,3},{4,20},{20... | collective-permute-start | bytes 589832 | tf_op jit(solution)/shard_map/ppermute | solution.py:61
  168.1 2.7 %collective-permute-start.44 = (f32[96,512]{1,0:T(8,128)S(1)}, f32[96,512]{1,0:T(8,128)S(1)}, u32[]{:S(2)}, u32[]{:S(2)}) collective-permute-start(f32[96,512]{1,0:T(8,128)S(1)} %collective-permute-done.40.refs_24_), channel_id=1, source_target_pairs={{0,16},{16,0},{1,17},{17,1},{2,18},{18,2},{3,19},{19,3},{4,20},{20... | collective-permute-start | bytes 589832 | tf_op jit(solution)/shard_map/ppermute | solution.py:61
  170.5 1.4 collective-permute-start.45
  (7 other events, 5.0 us)

commit v3 on v2

--- a/solution.py
+++ b/solution.py
@@ -138,96 +138,88 @@
         around_refs = refs[1 + count : 1 + count + many]
         front_refs = refs[1 + count + many : 1 + 2 * count + many]
         outs = refs[1 + 2 * count + many :][:count]
-        pivot, edge, up, previous, row_buf, col_buf, sems = refs[1 + 3 * count + many :]
+        edge, up, row_buf, col_buf, sems = refs[1 + 3 * count + many :]
+        places = [col_buf.at[m * sub : (m + 1) * sub] for m in range(count)]
+        rows_in = gather_copies(sc, row_refs, row_buf, sems, sub)
+        for copy in rows_in:
+            copy.start()
+        for m, place in enumerate(places):
+            start_chosen(slice_place(sc, m, count), around_refs, place, sems.at[count + m])
+        for copy in rows_in:
+            copy.wait()
+        left = halves(row_buf[...])
+        for m, place in enumerate(places):
+            pltpu.make_async_copy(around_refs[0], place, sems.at[count + m]).wait()
+        product = times_transpose(left, halves(col_buf[...]))
         for m in range(count):
             group = sc[COL] ^ m
-            start_chosen(
-                slice_place(sc, m, count),
-                around_refs,
-                col_buf.at[span(group, sub)],
-                sems.at[count + m],
-            )
-        run_copies(gather_copies(sc, row_refs, row_buf, sems, sub))
-        for m in range(count):
-            group = sc[COL] ^ m
-            pltpu.make_async_copy(
-                around_refs[0], col_buf.at[span(group, sub)], sems.at[count + m]
-            ).wait()
-        left = halves(row_buf[...])
-        for m in range(count):
-            group = sc[COL] ^ m
-            right = halves(col_buf[span(group, sub), :])
-            part = front_refs[m][...] - times_transpose(left, right)
+            part = front_refs[m][...] - product[:, m * sub : (m + 1) * sub]
             outs[m][...] = part
 
             @pl.when(group == 0)
             def _():
-                pivot[...] = part
                 edge[...] = part[-EDGE:]
 
             @pl.when(group > 0)
             def _():
                 up[group - 1] = part[-EDGE:]
 
-            @pl.when(group < count - 1)
-            def _():
-                previous[group] = part
-
     return pl.pallas_call(
         body,
         in_specs=[SMEM] + [ANY] * (count + many) + [VMEM] * count,
-        out_specs=[VMEM] * (count + 4),
-        out_shape=[f32(size, sub)] * (count + 1)
-        + [f32(EDGE, sub), f32(count - 1, EDGE, sub), f32(count - 1, size, sub)],
+        out_specs=[VMEM] * (count + 2),
+        out_shape=[f32(size, sub)] * count + [f32(EDGE, sub), f32(count - 1, EDGE, sub)],
         scratch_shapes=[
             pltpu.VMEM((size, depth), jnp.float32),
             pltpu.VMEM((size, depth), jnp.float32),
             pltpu.SemaphoreType.DMA((2 * count,)),
         ],
-        compiler_params=limit_for(sub, 24),
+        compiler_params=limit_for(sub, 20),
         name="slice_products",
     )(table, *rows, *around, *fronts)
 
 
-def pack_halo(table, previous, edge, up):
-    less, size, sub = previous.shape
-    count = less + 1
-
-    def body(sc, previous_ref, edge_ref, up_ref, *refs):
-        outs, ups, sems = refs[:count], refs[count], refs[count + 1]
-        run_copies(
-            [
-                pltpu.make_async_copy(edge_ref, ups.at[0], sems.at[0]),
-                pltpu.make_async_copy(up_ref, ups.at[pl.ds(1, less)], sems.at[1]),
-            ]
-        )
-        copies = []
+def pack_halo(table, homes, edge, up):
+    count = len(homes)
+    size, sub = homes[0].shape
+
+    def body(*refs):
+        sc = refs[0]
+        home_refs = refs[1 : 1 + count]
+        edge_ref, up_ref = refs[1 + count : 3 + count]
+        outs = refs[3 + count : 3 + 2 * count]
+        sems = refs[-1]
+        near, far = pl.ds(size, EDGE), pl.ds(size + EDGE, EDGE)
         for m, out in enumerate(outs):
             group = sc[COL] ^ m
             before = jnp.maximum(group - 1, 0)
-            parts = (
-                (previous_ref.at[before], pl.ds(0, size)),
-                (ups.at[group], pl.ds(size, EDGE)),
-                (ups.at[before], pl.ds(size + EDGE, EDGE)),
-            )
-            copies += [
-                pltpu.make_async_copy(part, out.at[place], sems.at[3 * m + i])
-                for i, (part, place) in enumerate(parts)
-            ]
-        run_copies(copies)
-
-    return pl.pallas_call(
-        body,
-        in_specs=[SMEM] + [ANY] * 3,
+            start_chosen(before ^ sc[COL], home_refs, out.at[pl.ds(0, size)], sems.at[3 * m])
+            for i, (wanted, place) in enumerate(((group, near), (before, far))):
+
+                @pl.when(wanted == 0)
+                def _():
+                    pltpu.make_async_copy(edge_ref, out.at[place], sems.at[3 * m + 1 + i]).start()
+
+                @pl.when(wanted > 0)
+                def _():
+                    pltpu.make_async_copy(
+                        up_ref.at[jnp.maximum(wanted - 1, 0)], out.at[place], sems.at[3 * m + 1 + i]
+                    ).start()
+
+        for m, out in enumerate(outs):
+            pltpu.make_async_copy(home_refs[0], out.at[pl.ds(0, size)], sems.at[3 * m]).wait()
+            for i, place in enumerate((near, far)):
+                pltpu.make_async_copy(edge_ref, out.at[place], sems.at[3 * m + 1 + i]).wait()
+
+    return pl.pallas_call(
+        body,
+        in_specs=[SMEM] + [ANY] * (count + 2),
         out_specs=[VMEM] * count,
         out_shape=[f32(size + 2 * EDGE, sub)] * count,
-        scratch_shapes=[
-            pltpu.VMEM((count, EDGE, sub), jnp.float32),
-            pltpu.SemaphoreType.DMA((3 * count,)),
-        ],
-        compiler_params=limit_for(sub, 16),
+        scratch_shapes=[pltpu.SemaphoreType.DMA((3 * count,))],
+        compiler_params=limit_for(sub, 8),
         name="pack_halo",
-    )(table, previous, edge, up)
+    )(table, *homes, edge, up)
 
 
 def pick_for_cols(table, pieces, masks):
@@ -254,13 +246,21 @@
     )(table, *pieces)
 
 
-def place_rows(table, part, edge):
-    size, width = part.shape
+def place_rows(table, homes, edge):
+    count = len(homes)
+    size, width = homes[0].shape
     rows = HALF * BLK
 
-    def body(sc, part_ref, edge_ref, keep, send, window):
-        window[:EDGE] = edge_ref[...]
-        window[EDGE:] = part_ref[...]
+    def body(*refs):
+        sc = refs[0]
+        home_refs = refs[1 : 1 + count]
+        edge_ref, keep, send, window, sems = refs[1 + count :]
+        main = window.at[pl.ds(EDGE, size)]
+        start_chosen(sc[COL], home_refs, main, sems.at[0])
+        copy = pltpu.make_async_copy(edge_ref, window.at[pl.ds(0, EDGE)], sems.at[1])
+        copy.start()
+        copy.wait()
+        pltpu.make_async_copy(home_refs[0], main, sems.at[0]).wait()
         for target, half in ((keep, sc[SIB]), (send, 1 - sc[SIB])):
             for slot in range(HALF):
                 place = sc[OWN_ROWS + half * HALF + slot]
@@ -269,13 +269,16 @@
 
     return pl.pallas_call(
         body,
-        in_specs=[SMEM, VMEM, VMEM],
+        in_specs=[SMEM] + [ANY] * (count + 1),
         out_specs=[VMEM, VMEM],
         out_shape=[f32(rows, width), f32(rows, width)],
-        scratch_shapes=[pltpu.VMEM((size + EDGE, width), jnp.float32)],
+        scratch_shapes=[
+            pltpu.VMEM((size + EDGE, width), jnp.float32),
+            pltpu.SemaphoreType.DMA((2,)),
+        ],
+        compiler_params=limit_for(width, 8),
         name="place_rows",
-        compiler_params=limit_for(width, 16),
-    )(table, part, edge)
+    )(table, *homes, edge)
 
 
 def factor_slice(table, small, dealt, pivot_inverse):
@@ -325,10 +328,9 @@
     )(table, *small, *dealt, pivot_inverse)
 
 
-def finish(table, parent, own, other, row_pieces, col_own, col_other):
-    count = len(row_pieces)
+def assemble(table, parent, own, other):
+    count = len(own) // 2
     rows, width = parent.shape
-    piece_rows = row_pieces[0].shape[0]
     size, sub = own[0].shape
     half = count // 2
     split = BLK // sub
@@ -336,20 +338,8 @@
     def body(*refs):
         sc, parent_ref = refs[:2]
         own_refs, other_refs = refs[2 : 2 + 2 * count], refs[2 + 2 * count : 2 + 4 * count]
-        at = 2 + 4 * count
-        row_refs = refs[at : at + count]
-        col_own_refs = refs[at + count : at + 2 * count]
-        col_other_refs = refs[at + 2 * count : at + 3 * count]
-        out = refs[at + 3 * count]
-        own_win, other_win, row_factor, col_factor, products, sems = refs[at + 3 * count + 1 :]
-        factors = gather_copies(sc, row_refs, row_factor, sems, piece_rows)
-        factors += gather_copies(
-            sc, col_own_refs, col_factor.at[sc[SIB]], sems, piece_rows, count
-        )
-        factors += gather_copies(
-            sc, col_other_refs, col_factor.at[1 - sc[SIB]], sems, piece_rows, 2 * count
-        )
-        at = 3 * count
+        out, own_win, other_win, sems = refs[2 + 4 * count :]
+        at = 0
         always, edges = [], []
         for refs_in, window in ((own_refs, own_win), (other_refs, other_win)):
             for m in range(count):
@@ -378,7 +368,7 @@
                     )
                 ]
                 at += 4
-        for copy in factors + always:
+        for copy in always:
             copy.start()
         for piece, first, second in edges:
 
@@ -387,12 +377,6 @@
                 first.start()
                 second.start()
 
-        for copy in factors:
-            copy.wait()
-        left = halves(row_factor[...])
-        for side in range(2):
-            right = halves(col_factor[side])
-            products[:, side * rows : (side + 1) * rows] = times_transpose(left, right)
         for copy in always:
             copy.wait()
         for piece, first, second in edges:
@@ -402,11 +386,8 @@
                 first.wait()
                 second.wait()
 
-        first_row = (sc[ROW] * 2 + sc[SIB]) * HALF
-        first_col = sc[COL] * PBD
         for q in range(PBD):
             cols = slice(q * BLK, (q + 1) * BLK)
-            col_inside = first_col + q >= PIV
             for p in range(HALF):
                 lines = slice(p * BLK, (p + 1) * BLK)
                 total = parent_ref[lines, cols]
@@ -422,28 +403,78 @@
                     ]
                     block = pieces[0] if split == 1 else jnp.concatenate(pieces, axis=1)
                     total += jnp.where((down >= 0) & (across >= 0), block, 0.0)
-                inside = col_inside & (first_row + p >= PIV)
-                total = jnp.where(inside, total - products[lines, cols], total)
-                if q < PIV:
-                    total = jnp.where(sc[COL] == 0, row_factor[lines, cols], total)
                 out[lines, cols] = total
 
     return pl.pallas_call(
         body,
-        in_specs=[SMEM, VMEM] + [ANY] * (7 * count),
+        in_specs=[SMEM, VMEM] + [ANY] * (4 * count),
         out_specs=VMEM,
         out_shape=f32(rows, width),
         scratch_shapes=[
             pltpu.VMEM((half + count, size + EDGE, sub), jnp.float32),
             pltpu.VMEM((half + count, size + EDGE, sub), jnp.float32),
+            pltpu.SemaphoreType.DMA((8 * count,)),
+        ],
+        compiler_params=limit_for(sub, 12),
+        name="assemble",
+    )(table, parent, *own, *other)
+
+
+def finish(table, assembled, row_pieces, col_own, col_other):
+    count = len(row_pieces)
+    rows, width = assembled.shape
+    piece_rows = row_pieces[0].shape[0]
+
+    def body(*refs):
+        sc = refs[0]
+        row_refs = refs[1 : 1 + count]
+        col_own_refs = refs[1 + count : 1 + 2 * count]
+        col_other_refs = refs[1 + 2 * count : 1 + 3 * count]
+        base_ref, out, row_factor, col_factor, sems = refs[1 + 3 * count :]
+        copies = [
+            gather_copies(sc, row_refs, row_factor, sems, piece_rows),
+            gather_copies(sc, col_own_refs, col_factor.at[sc[SIB]], sems, piece_rows, count),
+            gather_copies(
+                sc, col_other_refs, col_factor.at[1 - sc[SIB]], sems, piece_rows, 2 * count
+            ),
+        ]
+        for copy in sum(copies, []):
+            copy.start()
+        for copy in copies[0]:
+            copy.wait()
+        left = halves(row_factor[...])
+        for copy in copies[1] + copies[2]:
+            copy.wait()
+        first_row = (sc[ROW] * 2 + sc[SIB]) * HALF
+        first_col = sc[COL] * PBD
+        for side in range(2):
+            product = times_transpose(left, halves(col_factor[side]))
+            for i in range(HALF):
+                q = side * HALF + i
+                cols = slice(q * BLK, (q + 1) * BLK)
+                for p in range(HALF):
+                    lines = slice(p * BLK, (p + 1) * BLK)
+                    total = base_ref[lines, cols]
+                    inside = (first_col + q >= PIV) & (first_row + p >= PIV)
+                    reduced = total - product[lines, i * BLK : (i + 1) * BLK]
+                    total = jnp.where(inside, reduced, total)
+                    if q < PIV:
+                        total = jnp.where(sc[COL] == 0, row_factor[lines, cols], total)
+                    out[lines, cols] = total
+
+    return pl.pallas_call(
+        body,
+        in_specs=[SMEM] + [ANY] * (3 * count) + [VMEM],
+        out_specs=VMEM,
+        out_shape=f32(rows, width),
+        scratch_shapes=[
             pltpu.VMEM((rows, PANEL), jnp.float32),
             pltpu.VMEM((2, rows, PANEL), jnp.float32),
-            pltpu.VMEM((rows, 2 * rows), jnp.float32),
-            pltpu.SemaphoreType.DMA((11 * count,)),
+            pltpu.SemaphoreType.DMA((3 * count,)),
         ],
-        compiler_params=limit_for(sub, 24),
+        compiler_params=limit_for(BLK, 16),
         name="finish",
-    )(table, parent, *own, *other, *row_pieces, *col_own, *col_other)
+    )(table, *row_pieces, *col_own, *col_other, assembled)
 
 
 def shards(child_front, child_panel, block_map, parent_front, pivot_inverse):
@@ -499,19 +530,19 @@
         value = parent_front[j * deal : (j + 1) * deal, :PANEL]
         dealt.append(lax.ppermute(value, "col", [(0, j)]) if j else value)
 
-    *homes, pivot, edge, up, previous = slice_products(table, rows, around, fronts)
+    *homes, edge, up = slice_products(table, rows, around, fronts)
     edge = shifted(edge, "row")
+    up = shifted(up, "row")
     own = [homes[0]] + over_col(homes[1:])
-    up = shifted(up, "row")
-
-    keep, send = place_rows(table, pivot, edge)
+
+    keep, send = place_rows(table, homes, edge)
     both = jnp.stack([keep, to_sibling(send)])
     slices = [
         lax.dynamic_slice_in_dim(both, (col_index ^ k) * deal, deal, axis=1)
         for k in range(count)
     ]
     small = [slices[0]] + over_col(slices[1:])
-    packed = pack_halo(table, previous, edge, up)
+    packed = pack_halo(table, homes, edge, up)
     own = own + [packed[0]] + over_col(packed[1:])
     factor = factor_slice(table, small, dealt, pivot_inverse)
     factors = over_row(factor)
@@ -522,7 +553,8 @@
     col_other = [to_sibling(value) for value in col_own]
 
     other = [to_sibling(value) for value in own]
-    return finish(table, parent_front, own, other, row_pieces, col_own, col_other)
+    assembled = assemble(table, parent_front, own, other)
+    return finish(table, assembled, row_pieces, col_own, col_other)
 
 
 def solution(mesh):

time: 182 us -> 172 us (0.945)
  waiting for transfers between devices: 77.7 us -> 71.6 us
  Pallas kernels: 27.1 us -> 21.6 us
    ppermute x34, waiting for transfers between devices: 42 us -> 51.9 us  [swapped(): return lax.ppermute(value, axis, [(i, i ^ mask) for i in range(count)])]
    ppermute x4, waiting for transfers between devices: 21 us -> 12 us  [rotated(): lax.ppermute(value, axis, [(i, (i + steps) % count) for i in range(count)])]
    pallas_call x1, Pallas kernels: 10.1 us -> 4.33 us  [slice_products(): pl.pallas_call(body, in_specs=[SMEM] + [ANY] * (count + many) + [VMEM] *...]
    ppermute x3, waiting for transfers between devices: 6.95 us -> 1.39 us  [shards(): dealt.append(lax.ppermute(value, 'col', [(0, j)]) if j else value)]
    ppermute x3, starting transfers between devices: 7.77 us -> 10.8 us  [shards(): dealt.append(lax.ppermute(value, 'col', [(0, j)]) if j else value)]
    ppermute x4, starting transfers between devices: 7.9 us -> 5.02 us  [rotated(): lax.ppermute(value, axis, [(i, (i + steps) % count) for i in range(count)])]
    unnamed x50 -> x48, local copies, waits for them, and re-layouts: 15.5 us -> 14.1 us
    pallas_call x3 -> x4, Pallas kernels: 13.2 us -> 13.5 us  [the longest x1 6.28 us: finish(): pl.pallas_call(body, in_specs=[SMEM] + [ANY] * (3 * count) + [VMEM], out_...]
  transfers between devices with their start and end apart: 46 -> 46, of which waited for: 16 -> 14; matrix products, arithmetic and copies ran while one was open for 2% -> 2% of each run, Pallas kernels for 4% -> 6%
where the time goes in v3:
time: 172 us; the launch traced here: 171 us
  waiting for transfers between devices  71.6 us (42%)
  starting transfers between devices  59.2 us (34%)
  Pallas kernels  21.6 us (13%)
  local copies, waits for them, and re-layouts  17 us (10%)
    ppermute x34, waiting for transfers between devices, swapped(): return lax.ppermute(value, axis, [(i, i ^ mask) for i in range(count)])  51.9 us
    ppermute x34, starting transfers between devices, swapped(): return lax.ppermute(value, axis, [(i, i ^ mask) for i in range(count)])  33.1 us
    unnamed x48, local copies, waits for them, and re-layouts  14.1 us
    ppermute x4, waiting for transfers between devices, rotated(): lax.ppermute(value, axis, [(i, (i + steps) % count) for i in range(count)])  12 us
    ppermute x3, starting transfers between devices, shards(): dealt.append(lax.ppermute(value, 'col', [(0, j)]) if j else value)  10.8 us
    pallas_call x1, Pallas kernels, finish(): pl.pallas_call(body, in_specs=[SMEM] + [ANY] * (3 * count) + [VMEM], out_...  6.28 us
    ppermute x1, waiting for transfers between devices, around_row(): far.append(lax.ppermute(middle, 'row', pairs))  6.27 us
    ppermute x4, starting transfers between devices, rotated(): lax.ppermute(value, axis, [(i, (i + steps) % count) for i in range(count)])  5.02 us
  transfers between devices with their start and end apart: 46, of which 14 were waited for; matrix products, arithmetic and copies ran while one was open for 2% of the time, Pallas kernels for 6%

profile of v3, /device:TPU:0, one launch (start us, length us, event | category | flops | bytes accessed | tf_op | source)
XLA Modules:
  0.0 171.0 jit_solution(6270469599742825347)
XLA Ops:
  0.0 4.1 %collective-permute-start.4 = (f32[128,1024]{1,0:T(8,128)}, f32[128,1024]{1,0:T(8,128)S(1)}, u32[]{:S(2)}, u32[]{:S(2)}) collective-permute-start(f32[128,1024]{1,0:T(8,128)} %bitcast.20), channel_id=1, source_target_pairs={{0,8},{4,12},{8,0},{12,4},{1,9},{5,13},{9,1},{13,5},{2,10},{6,14},... | collective-permute-start | bytes 1572872 | tf_op jit(solution)/shard_map/ppermute | solution.py:56
  4.1 1.5 collective-permute-start
  5.6 2.0 %dynamic-slice_bitcast_fusion = (f32[512,128]{1,0:T(8,128)}, f32[512,128]{1,0:T(8,128)S(1)}, f32[512,128]{1,0:T(8,128)S(1)}, f32[512,128]{1,0:T(8,128)S(1)}) fusion(f32[1,512,512]{2,1,0:T(8,128)} %param.5, s32[]{:T(128)S(6)} %select_n.71, s32[]{:T(128)S(6)} %select_n.69, s32[]{:T(128)S(6)} %select_n.68, s32[]{:T(128)S(6)} %select_n.70), kind=kLoop, calls=%fused_computation.8 | loop fusion | bytes 2097168 | tf_op jit(solution)/shard_map/dynamic_slice | solution.py:524
  7.5 0.5 collective-permute-start.7
  8.1 1.5 collective-permute-start.8
  9.6 1.4 collective-permute-start.9
  11.4 13.3 %collective-permute-done.7.refs_11_ = f32[512,128]{1,0:T(8,128)S(1)} collective-permute-done((f32[512,128]{1,0:T(8,128)S(1)}, f32[512,128]{1,0:T(8,128)S(1)}, u32[]{:S(2)}, u32[]{:S(2)}) %collective-permute-start.7) | collective-permute-done | bytes 262176 | tf_op jit(solution)/shard_map/ppermute | solution.py:61
  24.7 1.5 collective-permute-start.1
  26.2 0.7 copy-done.15
  26.9 1.4 collective-permute-start.2
  28.4 3.1 %collective-permute-done.9.refs_13_ = f32[512,128]{1,0:T(8,128)} collective-permute-done((f32[512,128]{1,0:T(8,128)}, f32[512,128]{1,0:T(8,128)}, u32[]{:S(2)}, u32[]{:S(2)}) %collective-permute-start.9) | collective-permute-done | bytes 262176 | tf_op jit(solution)/shard_map/ppermute | solution.py:61
  31.5 4.3 %collective-permute-start.3 = (f32[128,1024]{1,0:T(8,128)S(1)}, f32[128,1024]{1,0:T(8,128)}, u32[]{:S(2)}, u32[]{:S(2)}) collective-permute-start(f32[128,1024]{1,0:T(8,128)S(1)} %bitcast.24), channel_id=1, source_target_pairs={{0,4},{4,8},{8,12},{1,5},{5,9},{9,13},{2,6},{6,10},{10,14},{3,7},{... | collective-permute-start | bytes 1572872 | tf_op jit(solution)/shard_map/ppermute | solution.py:121
  35.8 1.3 collective-permute-start.6
  37.1 0.8 copy-done.5
  37.9 1.3 collective-permute-start.5
  39.2 0.8 copy-done.3
  40.0 11.7 %collective-permute-done.1.refs_3_ = f32[128,1024]{1,0:T(8,128)S(1)} collective-permute-done((f32[128,1024]{1,0:T(8,128)S(1)}, f32[128,1024]{1,0:T(8,128)S(1)}, u32[]{:S(2)}, u32[]{:S(2)}) %collective-permute-start.1) | collective-permute-done | bytes 524320 | tf_op jit(solution)/shard_map/ppermute | solution.py:61
  51.8 0.8 copy-done.7
  52.6 0.8 copy-done.9
  53.4 6.3 %collective-permute-done.5.refs_8_ = f32[128,1024]{1,0:T(8,128)S(1)} collective-permute-done((f32[128,1024]{1,0:T(8,128)S(1)}, f32[128,1024]{1,0:T(8,128)S(1)}, u32[]{:S(2)}, u32[]{:S(2)}) %collective-permute-start.5) | collective-permute-done | bytes 524320 | tf_op jit(solution)/shard_map/ppermute | solution.py:125
  59.7 0.8 copy-done.11
  60.5 1.0 copy-done.4
  61.5 1.0 copy-done.6
  62.6 1.0 copy-done.8
  63.6 1.0 copy-done.10
  64.7 1.0 copy-done.12
  65.7 0.9 copy-done.16
  66.6 4.3 %slice_products.1 = (f32[512,128]{1,0:T(8,128)S(1)}, f32[512,128]{1,0:T(8,128)S(1)}, f32[512,128]{1,0:T(8,128)S(1)}, f32[512,128]{1,0:T(8,128)S(1)}, f32[256,128]{1,0:T(8,128)S(1)}, /*index=5*/f32[3,256,128]{2,1,0:T(8,128)S(1)}) custom-call(s32[35]{0:T(128)S(1)} %concatenate.15.refs_0_, f32[128,1024]{1,0:T(8,128)S(1)} %bitcast.26, ...), custom_call_target="tpu_custom_call" | custom-call | tf_op jit(solution)/shard_map/slice_products/pallas_call | solution.py:167
  71.0 1.6 collective-permute-start.10
  72.6 0.7 fusion.6
  73.3 3.6 %collective-permute-start.15 = (f32[96,512]{1,0:T(8,128)S(1)}, f32[96,512]{1,0:T(8,128)S(1)}, u32[]{:S(2)}, u32[]{:S(2)}) collective-permute-start(f32[96,512]{1,0:T(8,128)S(1)} %get-tuple-element.49), channel_id=1, source_target_pairs={{0,1},{4,5},{8,9},{12,13},{16,17},{20,21},{24,25},{28,29}} | collective-permute-start | bytes 589832 | tf_op jit(solution)/shard_map/ppermute | solution.py:531
  76.9 1.3 collective-permute-start.16
  78.3 1.5 place_rows.1
  80.1 0.7 copy-done.18
  80.8 5.9 %collective-permute-start.17 = (f32[96,512]{1,0:T(8,128)}, f32[96,512]{1,0:T(8,128)}, u32[]{:S(2)}, u32[]{:S(2)}) collective-permute-start(f32[96,512]{1,0:T(8,128)} %get-tuple-element.47), channel_id=1, source_target_pairs={{0,3},{4,7},{8,11},{12,15},{16,19},{20,23},{24,27},{28,31}} | collective-permute-start | bytes 589832 | tf_op jit(solution)/shard_map/ppermute | solution.py:531
  86.7 0.7 copy-done.20
  87.4 1.9 %collective-permute-start.34 = (f32[3,256,128]{2,1,0:T(8,128)}, f32[3,256,128]{2,1,0:T(8,128)S(1)}, u32[]{:S(2)}, u32[]{:S(2)}) collective-permute-start(f32[3,256,128]{2,1,0:T(8,128)} %copy-done.22), channel_id=1, source_target_pairs={{0,4},{4,8},{8,12},{1,5},{5,9},{9,13},{2,6},{6,10},{10,14},{3,7},{... | collective-permute-start | bytes 1179656 | tf_op jit(solution)/shard_map/ppermute | solution.py:66
  89.3 1.0 fusion
  90.3 1.3 collective-permute-done.17.refs_8_
  91.6 4.0 %collective-permute-start.13 = (f32[2,96,128]{2,1,0:T(8,128)S(1)}, f32[2,96,128]{2,1,0:T(8,128)S(1)}, u32[]{:S(2)}, u32[]{:S(2)}) collective-permute-start(f32[2,96,128]{2,1,0:T(8,128)S(1)} %get-tuple-element.58), channel_id=1, source_target_pairs={{0,2},{1,3},{2,0},{3,1},{4,6},{5,7},{6,4},{7,5},{8,10},{9,11},{10,... | collective-permute-start | bytes 294920 | tf_op jit(solution)/shard_map/ppermute | solution.py:61
  95.6 4.0 %collective-permute-start.14 = (f32[2,96,128]{2,1,0:T(8,128)S(1)}, f32[2,96,128]{2,1,0:T(8,128)S(1)}, u32[]{:S(2)}, u32[]{:S(2)}) collective-permute-start(f32[2,96,128]{2,1,0:T(8,128)S(1)} %get-tuple-element.55), channel_id=1, source_target_pairs={{0,3},{1,2},{2,1},{3,0},{4,7},{5,6},{6,5},{7,4},{8,11},{9,10},{10,... | collective-permute-start | bytes 294920 | tf_op jit(solution)/shard_map/ppermute | solution.py:61
  100.3 2.0 %collective-permute-done.14.refs_4_ = f32[2,96,128]{2,1,0:T(8,128)S(1)} collective-permute-done((f32[2,96,128]{2,1,0:T(8,128)S(1)}, f32[2,96,128]{2,1,0:T(8,128)S(1)}, u32[]{:S(2)}, u32[]{:S(2)}) %collective-permute-start.14) | collective-permute-done | bytes 98336 | tf_op jit(solution)/shard_map/ppermute | solution.py:61
  102.3 0.9 copy-done.19
  103.2 0.9 copy-done.21
  104.1 2.0 %factor_slice.1.refs_1_ = f32[96,512]{1,0:T(8,128)S(1)} custom-call(s32[35]{0:T(128)S(1)} %concatenate.15.refs_0_, f32[2,96,128]{2,1,0:T(8,128)S(1)} %get-tuple-element.56.refs_1_, f32[2,96,128]{2,1,0:T(8,128)S(1)} %collective-permute-done.12.refs_2_, f32[2,96,128]{2,1,0:T(8,128)S(1)} %collective-permute-done.13.refs_3_, ...), custom_call_target="tpu_custom_call" | custom-call | tf_op jit(solution)/shard_map/factor_slice/pallas_call | solution.py:315
  106.2 2.3 %pack_halo.1 = (f32[1024,128]{1,0:T(8,128)S(1)}, f32[1024,128]{1,0:T(8,128)S(1)}, f32[1024,128]{1,0:T(8,128)S(1)}, f32[1024,128]{1,0:T(8,128)S(1)}) custom-call(s32[35]{0:T(128)S(1)} %concatenate.15.refs_0_, f32[512,128]{1,0:T(8,128)S(1)} %get-tuple-element.21.refs_1_.refs_2_, f32[512,128]{1,0:T(8,128)S(1)} %get-tuple-element.22.refs_2_, ...), custom_call_target="tpu_custom_call" | custom-call | tf_op jit(solution)/shard_map/pack_halo/pallas_call | solution.py:214
  109.0 3.2 %collective-permute-start.36 = (f32[1024,128]{1,0:T(8,128)S(1)}, f32[1024,128]{1,0:T(8,128)S(1)}, u32[]{:S(2)}, u32[]{:S(2)}) collective-permute-start(f32[1024,128]{1,0:T(8,128)S(1)} %get-tuple-element.35), channel_id=1, source_target_pairs={{0,2},{1,3},{2,0},{3,1},{4,6},{5,7},{6,4},{7,5},{8,10},{9,11},{10,... | collective-permute-start | bytes 1572872 | tf_op jit(solution)/shard_map/ppermute | solution.py:61
  112.3 3.0 %collective-permute-done.21.refs_2_ = f32[96,512]{1,0:T(8,128)S(1)} collective-permute-done((f32[96,512]{1,0:T(8,128)S(1)}, f32[96,512]{1,0:T(8,128)S(1)}, u32[]{:S(2)}, u32[]{:S(2)}) %collective-permute-start.21) | collective-permute-done | bytes 196640 | tf_op jit(solution)/shard_map/ppermute | solution.py:56
  115.3 0.8 collective-permute-start.23
  116.1 9.0 %collective-permute-done.22.refs_3_ = f32[96,512]{1,0:T(8,128)S(1)} collective-permute-done((f32[96,512]{1,0:T(8,128)S(1)}, f32[96,512]{1,0:T(8,128)S(1)}, u32[]{:S(2)}, u32[]{:S(2)}) %collective-permute-start.22) | collective-permute-done | bytes 196640 | tf_op jit(solution)/shard_map/ppermute | solution.py:56
  125.1 1.5 collective-permute-start.18
  126.6 1.7 collective-permute-start.19
  128.3 1.7 pick_for_cols.1
  130.0 8.4 %collective-permute-done.18.refs_2_ = f32[96,512]{1,0:T(8,128)S(1)} collective-permute-done((f32[96,512]{1,0:T(8,128)S(1)}, f32[96,512]{1,0:T(8,128)S(1)}, u32[]{:S(2)}, u32[]{:S(2)}) %collective-permute-start.18) | collective-permute-done | bytes 196640 | tf_op jit(solution)/shard_map/ppermute | solution.py:61
  138.8 1.1 collective-permute-done.19.refs_3_
  140.0 0.5 collective-permute-start.43
  141.0 3.9 %collective-permute-done.24.refs_6_ = f32[96,512]{1,0:T(8,128)S(1)} collective-permute-done((f32[96,512]{1,0:T(8,128)S(1)}, f32[96,512]{1,0:T(8,128)S(1)}, u32[]{:S(2)}, u32[]{:S(2)}) %collective-permute-start.24) | collective-permute-done | bytes 196640 | tf_op jit(solution)/shard_map/ppermute | solution.py:61
  144.9 2.1 %collective-permute-start.25 = (f32[96,512]{1,0:T(8,128)S(1)}, f32[96,512]{1,0:T(8,128)S(1)}, u32[]{:S(2)}, u32[]{:S(2)}) collective-permute-start(f32[96,512]{1,0:T(8,128)S(1)} %get-tuple-element.30), channel_id=1, source_target_pairs={{0,2},{1,3},{2,0},{3,1},{4,6},{5,7},{6,4},{7,5},{8,10},{9,11},{10,... | collective-permute-start | bytes 589832 | tf_op jit(solution)/shard_map/ppermute | solution.py:61
  147.0 4.1 %collective-permute-done.25.refs_7_ = f32[96,512]{1,0:T(8,128)S(1)} collective-permute-done((f32[96,512]{1,0:T(8,128)S(1)}, f32[96,512]{1,0:T(8,128)S(1)}, u32[]{:S(2)}, u32[]{:S(2)}) %collective-permute-start.25) | collective-permute-done | bytes 196640 | tf_op jit(solution)/shard_map/ppermute | solution.py:61
  151.1 2.4 %collective-permute-start.26 = (f32[96,512]{1,0:T(8,128)S(1)}, f32[96,512]{1,0:T(8,128)S(1)}, u32[]{:S(2)}, u32[]{:S(2)}) collective-permute-start(f32[96,512]{1,0:T(8,128)S(1)} %get-tuple-element.31), channel_id=1, source_target_pairs={{0,3},{1,2},{2,1},{3,0},{4,7},{5,6},{6,5},{7,4},{8,11},{9,10},{10,... | collective-permute-start | bytes 589832 | tf_op jit(solution)/shard_map/ppermute | solution.py:61
  153.6 4.1 %collective-permute-done.26.refs_8_ = f32[96,512]{1,0:T(8,128)S(1)} collective-permute-done((f32[96,512]{1,0:T(8,128)S(1)}, f32[96,512]{1,0:T(8,128)S(1)}, u32[]{:S(2)}, u32[]{:S(2)}) %collective-permute-start.26) | collective-permute-done | bytes 196640 | tf_op jit(solution)/shard_map/ppermute | solution.py:61
  157.7 2.4 %collective-permute-start.20 = (f32[96,512]{1,0:T(8,128)S(1)}, f32[96,512]{1,0:T(8,128)S(1)}, u32[]{:S(2)}, u32[]{:S(2)}) collective-permute-start(f32[96,512]{1,0:T(8,128)S(1)} %factor_slice.1.refs_1_), channel_id=1, source_target_pairs={{0,3},{1,2},{2,1},{3,0},{4,7},{5,6},{6,5},{7,4},{8,11},{9,10},{10,... | collective-permute-start | bytes 589832 | tf_op jit(solution)/shard_map/ppermute | solution.py:61
  161.2 3.5 %assemble.1.refs_13_ = f32[384,768]{1,0:T(8,128)S(1)} custom-call(s32[35]{0:T(128)S(1)} %concatenate.15.refs_0_, f32[384,768]{1,0:T(8,128)S(1)} %copy-done, f32[512,128]{1,0:T(8,128)S(1)} %get-tuple-element.21.refs_1_.refs_2_, f32[512,128]{1,0:T(8,128)} %collective-permute-done.31.refs_3_, f32[512,128]{1,0:T(8,128)} %collective-permute-done.32.refs_4_, ...), custom_call_target="tpu_custom_call" | custom-call | tf_op jit(solution)/shard_map/assemble/pallas_call | solution.py:408
  164.8 6.3 %finish.1 = f32[384,768]{1,0:T(8,128)} custom-call(s32[35]{0:T(128)S(1)} %concatenate.15.refs_0_, f32[96,512]{1,0:T(8,128)S(1)} %factor_slice.1.refs_1_, f32[96,512]{1,0:T(8,128)S(1)} %collective-permute-done.18.refs_2_, f32[96,512]{1,0:T(8,128)S(1)} %collective-permute-done.19.refs_3_, f32[96,512]{1,0:T(8,128)S(1)} %collective-permute-done.20.refs_4_, ...), custom_call_target="tpu_custom_call" | custom-call | tf_op jit(solution)/shard_map/finish/pallas_call | solution.py:465
  (98 shorter events, 4.0 us)
Async XLA Ops:
  0.0 24.7 %copy-start.1 = (f32[1,128,1024]{2,1,0:T(8,128)S(1)}, f32[1,128,1024]{2,1,0:T(8,128)}, u32[]{:S(2)}) copy-start(f32[1,128,1024]{2,1,0:T(8,128)} %param.6) | copy-start | bytes 1572868
  0.0 11.0 %copy-start.23 = (s32[2,16]{1,0:T(2,128)S(1)}, s32[2,16]{1,0:T(2,128)}, u32[]{:S(2)}) copy-start(s32[2,16]{1,0:T(2,128)} %param.7) | copy-start | bytes 388
  0.0 35.8 %collective-permute-start.4 = (f32[128,1024]{1,0:T(8,128)}, f32[128,1024]{1,0:T(8,128)S(1)}, u32[]{:S(2)}, u32[]{:S(2)}) collective-permute-start(f32[128,1024]{1,0:T(8,128)} %bitcast.20), channel_id=1, source_target_pairs={{0,8},{4,12},{8,0},{12,4},{1,9},{5,13},{9,1},{13,5},{2,10},{6,14},... | collective-permute-start | bytes 1572872 | tf_op jit(solution)/shard_map/ppermute | solution.py:56
  4.1 33.0 %collective-permute-start = (f32[128,1024]{1,0:T(8,128)}, f32[128,1024]{1,0:T(8,128)S(1)}, u32[]{:S(2)}, u32[]{:S(2)}) collective-permute-start(f32[128,1024]{1,0:T(8,128)} %bitcast.21), channel_id=1, source_target_pairs={{0,1},{1,0},{2,3},{3,2},{4,5},{5,4},{6,7},{7,6},{8,9},{9,8},{10,11... | collective-permute-start | bytes 1572872 | tf_op jit(solution)/shard_map/ppermute | solution.py:61
  7.5 17.2 %collective-permute-start.7 = (f32[512,128]{1,0:T(8,128)S(1)}, f32[512,128]{1,0:T(8,128)S(1)}, u32[]{:S(2)}, u32[]{:S(2)}) collective-permute-start(f32[512,128]{1,0:T(8,128)S(1)} %get-tuple-element.52), channel_id=1, source_target_pairs={{0,1},{1,0},{2,3},{3,2},{4,5},{5,4},{6,7},{7,6},{8,9},{9,8},{10,11... | collective-permute-start | bytes 786440 | tf_op jit(solution)/shard_map/ppermute | solution.py:61
  8.1 18.2 %collective-permute-start.8 = (f32[512,128]{1,0:T(8,128)S(1)}, f32[512,128]{1,0:T(8,128)S(1)}, u32[]{:S(2)}, u32[]{:S(2)}) collective-permute-start(f32[512,128]{1,0:T(8,128)S(1)} %get-tuple-element.54), channel_id=1, source_target_pairs={{0,2},{1,3},{2,0},{3,1},{4,6},{5,7},{6,4},{7,5},{8,10},{9,11},{10,... | collective-permute-start | bytes 786440 | tf_op jit(solution)/shard_map/ppermute | solution.py:61
  9.6 21.9 %collective-permute-start.9 = (f32[512,128]{1,0:T(8,128)}, f32[512,128]{1,0:T(8,128)}, u32[]{:S(2)}, u32[]{:S(2)}) collective-permute-start(f32[512,128]{1,0:T(8,128)} %get-tuple-element.51), channel_id=1, source_target_pairs={{0,3},{1,2},{2,1},{3,0},{4,7},{5,6},{6,5},{7,4},{8,11},{9,10},{10,... | collective-permute-start | bytes 786440 | tf_op jit(solution)/shard_map/ppermute | solution.py:61
  24.7 27.1 %collective-permute-start.1 = (f32[128,1024]{1,0:T(8,128)S(1)}, f32[128,1024]{1,0:T(8,128)S(1)}, u32[]{:S(2)}, u32[]{:S(2)}) collective-permute-start(f32[128,1024]{1,0:T(8,128)S(1)} %bitcast.22), channel_id=1, source_target_pairs={{0,2},{1,3},{2,0},{3,1},{4,6},{5,7},{6,4},{7,5},{8,10},{9,11},{10,... | collective-permute-start | bytes 1572872 | tf_op jit(solution)/shard_map/ppermute | solution.py:61
  26.9 25.7 %collective-permute-start.2 = (f32[128,1024]{1,0:T(8,128)S(1)}, f32[128,1024]{1,0:T(8,128)S(1)}, u32[]{:S(2)}, u32[]{:S(2)}) collective-permute-start(f32[128,1024]{1,0:T(8,128)S(1)} %bitcast.23), channel_id=1, source_target_pairs={{0,3},{1,2},{2,1},{3,0},{4,7},{5,6},{6,5},{7,4},{8,11},{9,10},{10,... | collective-permute-start | bytes 1572872 | tf_op jit(solution)/shard_map/ppermute | solution.py:61
  31.5 21.9 %collective-permute-start.3 = (f32[128,1024]{1,0:T(8,128)S(1)}, f32[128,1024]{1,0:T(8,128)}, u32[]{:S(2)}, u32[]{:S(2)}) collective-permute-start(f32[128,1024]{1,0:T(8,128)S(1)} %bitcast.24), channel_id=1, source_target_pairs={{0,4},{4,8},{8,12},{1,5},{5,9},{9,13},{2,6},{6,10},{10,14},{3,7},{... | collective-permute-start | bytes 1572872 | tf_op jit(solution)/shard_map/ppermute | solution.py:121
  35.8 17.6 %collective-permute-start.6 = (f32[128,1024]{1,0:T(8,128)S(1)}, f32[128,1024]{1,0:T(8,128)}, u32[]{:S(2)}, u32[]{:S(2)}) collective-permute-start(f32[128,1024]{1,0:T(8,128)S(1)} %bitcast.25), channel_id=1, source_target_pairs={{4,0},{8,4},{12,8},{5,1},{9,5},{13,9},{6,2},{10,6},{14,10},{7,3},{... | collective-permute-start | bytes 1572872 | tf_op jit(solution)/shard_map/ppermute | solution.py:122
  37.9 21.8 %collective-permute-start.5 = (f32[128,1024]{1,0:T(8,128)S(1)}, f32[128,1024]{1,0:T(8,128)S(1)}, u32[]{:S(2)}, u32[]{:S(2)}) collective-permute-start(f32[128,1024]{1,0:T(8,128)S(1)} %collective-permute-done.4.refs_7_), channel_id=1, source_target_pairs={{8,12},{4,0},{9,13},{5,1},{10,14},{6,2},{11,15},{7,3},{24,28},{20,... | collective-permute-start | bytes 1572872 | tf_op jit(solution)/shard_map/ppermute | solution.py:125
  51.8 0.8 copy-start.7
  59.7 0.8 copy-start.11
  60.5 1.0 copy-start.4
  61.5 1.0 copy-start.6
  62.6 1.0 copy-start.8
  63.6 1.0 copy-start.10
  64.7 1.0 copy-start.12
  65.7 0.9 copy-start.16
  66.6 5.9 %copy-start = (f32[384,768]{1,0:T(8,128)S(1)}, f32[384,768]{1,0:T(8,128)}, u32[]{:S(2)}) copy-start(f32[384,768]{1,0:T(8,128)} %refs_1_.1) | copy-start | bytes 3538948
  71.0 15.7 %copy-start.22 = (f32[3,256,128]{2,1,0:T(8,128)}, f32[3,256,128]{2,1,0:T(8,128)S(1)}, u32[]{:S(2)}) copy-start(f32[3,256,128]{2,1,0:T(8,128)S(1)} %get-tuple-element.32) | copy-start | bytes 1179652
  71.0 7.2 %collective-permute-start.10 = (f32[256,128]{1,0:T(8,128)S(1)}, f32[256,128]{1,0:T(8,128)S(1)}, u32[]{:S(2)}, u32[]{:S(2)}) collective-permute-start(f32[256,128]{1,0:T(8,128)S(1)} %get-tuple-element.25), channel_id=1, source_target_pairs={{0,4},{4,8},{8,12},{1,5},{5,9},{9,13},{2,6},{6,10},{10,14},{3,7},{... | collective-permute-start | bytes 393224 | tf_op jit(solution)/shard_map/ppermute | solution.py:66
  73.3 28.9 %copy-start.2 = (f32[512,512]{1,0:T(8,128)S(1)}, f32[512,512]{1,0:T(8,128)}, u32[]{:S(2)}) copy-start(f32[512,512]{1,0:T(8,128)} %refs_9_.1) | copy-start | bytes 3145732
  73.3 6.8 %collective-permute-start.15 = (f32[96,512]{1,0:T(8,128)S(1)}, f32[96,512]{1,0:T(8,128)S(1)}, u32[]{:S(2)}, u32[]{:S(2)}) collective-permute-start(f32[96,512]{1,0:T(8,128)S(1)} %get-tuple-element.49), channel_id=1, source_target_pairs={{0,1},{4,5},{8,9},{12,13},{16,17},{20,21},{24,25},{28,29}} | collective-permute-start | bytes 589832 | tf_op jit(solution)/shard_map/ppermute | solution.py:531
  76.9 9.7 %collective-permute-start.16 = (f32[96,512]{1,0:T(8,128)S(1)}, f32[96,512]{1,0:T(8,128)S(1)}, u32[]{:S(2)}, u32[]{:S(2)}) collective-permute-start(f32[96,512]{1,0:T(8,128)S(1)} %get-tuple-element.48), channel_id=1, source_target_pairs={{0,2},{4,6},{8,10},{12,14},{16,18},{20,22},{24,26},{28,30}} | collective-permute-start | bytes 589832 | tf_op jit(solution)/shard_map/ppermute | solution.py:531
  78.2 8.4 %copy-start.13 = (f32[256,128]{1,0:T(8,128)}, f32[256,128]{1,0:T(8,128)S(1)}, u32[]{:S(2)}) copy-start(f32[256,128]{1,0:T(8,128)S(1)} %collective-permute-done.10.refs_5_) | copy-start | bytes 393220
  79.8 6.9 %copy-start.17 = (f32[384,128]{1,0:T(8,128)}, f32[384,128]{1,0:T(8,128)S(1)}, u32[]{:S(2)}) copy-start(f32[384,128]{1,0:T(8,128)S(1)} %get-tuple-element.26) | copy-start | bytes 589828
  79.8 7.6 %collective-permute-start.11 = (f32[384,128]{1,0:T(8,128)}, f32[384,128]{1,0:T(8,128)}, u32[]{:S(2)}, u32[]{:S(2)}) collective-permute-start(f32[384,128]{1,0:T(8,128)} %get-tuple-element.27), channel_id=1, source_target_pairs={{0,16},{16,0},{1,17},{17,1},{2,18},{18,2},{3,19},{19,3},{4,20},{20... | collective-permute-start | bytes 589832 | tf_op jit(solution)/shard_map/ppermute | solution.py:61
  79.9 11.8 %collective-permute-start.31 = (f32[512,128]{1,0:T(8,128)S(1)}, f32[512,128]{1,0:T(8,128)}, u32[]{:S(2)}, u32[]{:S(2)}) collective-permute-start(f32[512,128]{1,0:T(8,128)S(1)} %get-tuple-element.22.refs_2_), channel_id=1, source_target_pairs={{0,1},{1,0},{2,3},{3,2},{4,5},{5,4},{6,7},{7,6},{8,9},{9,8},{10,11... | collective-permute-start | bytes 786440 | tf_op jit(solution)/shard_map/ppermute | solution.py:61
  79.9 15.7 %collective-permute-start.32 = (f32[512,128]{1,0:T(8,128)S(1)}, f32[512,128]{1,0:T(8,128)}, u32[]{:S(2)}, u32[]{:S(2)}) collective-permute-start(f32[512,128]{1,0:T(8,128)S(1)} %get-tuple-element.23.refs_3_), channel_id=1, source_target_pairs={{0,2},{1,3},{2,0},{3,1},{4,6},{5,7},{6,4},{7,5},{8,10},{9,11},{10,... | collective-permute-start | bytes 786440 | tf_op jit(solution)/shard_map/ppermute | solution.py:61
  80.8 10.9 %collective-permute-start.17 = (f32[96,512]{1,0:T(8,128)}, f32[96,512]{1,0:T(8,128)}, u32[]{:S(2)}, u32[]{:S(2)}) collective-permute-start(f32[96,512]{1,0:T(8,128)} %get-tuple-element.47), channel_id=1, source_target_pairs={{0,3},{4,7},{8,11},{12,15},{16,19},{20,23},{24,27},{28,31}} | collective-permute-start | bytes 589832 | tf_op jit(solution)/shard_map/ppermute | solution.py:531
  87.4 12.3 %collective-permute-start.33 = (f32[512,128]{1,0:T(8,128)S(1)}, f32[512,128]{1,0:T(8,128)}, u32[]{:S(2)}, u32[]{:S(2)}) collective-permute-start(f32[512,128]{1,0:T(8,128)S(1)} %get-tuple-element.24.refs_4_), channel_id=1, source_target_pairs={{0,3},{1,2},{2,1},{3,0},{4,7},{5,6},{6,5},{7,4},{8,11},{9,10},{10,... | collective-permute-start | bytes 786440 | tf_op jit(solution)/shard_map/ppermute | solution.py:61
  87.4 18.8 %collective-permute-start.34 = (f32[3,256,128]{2,1,0:T(8,128)}, f32[3,256,128]{2,1,0:T(8,128)S(1)}, u32[]{:S(2)}, u32[]{:S(2)}) collective-permute-start(f32[3,256,128]{2,1,0:T(8,128)} %copy-done.22), channel_id=1, source_target_pairs={{0,4},{4,8},{8,12},{1,5},{5,9},{9,13},{2,6},{6,10},{10,14},{3,7},{... | collective-permute-start | bytes 1179656 | tf_op jit(solution)/shard_map/ppermute | solution.py:66
  91.6 8.0 %collective-permute-start.12 = (f32[2,96,128]{2,1,0:T(8,128)S(1)}, f32[2,96,128]{2,1,0:T(8,128)S(1)}, u32[]{:S(2)}, u32[]{:S(2)}) collective-permute-start(f32[2,96,128]{2,1,0:T(8,128)S(1)} %get-tuple-element.57), channel_id=1, source_target_pairs={{0,1},{1,0},{2,3},{3,2},{4,5},{5,4},{6,7},{7,6},{8,9},{9,8},{10,11... | collective-permute-start | bytes 294920 | tf_op jit(solution)/shard_map/ppermute | solution.py:61
  91.6 8.6 %collective-permute-start.13 = (f32[2,96,128]{2,1,0:T(8,128)S(1)}, f32[2,96,128]{2,1,0:T(8,128)S(1)}, u32[]{:S(2)}, u32[]{:S(2)}) collective-permute-start(f32[2,96,128]{2,1,0:T(8,128)S(1)} %get-tuple-element.58), channel_id=1, source_target_pairs={{0,2},{1,3},{2,0},{3,1},{4,6},{5,7},{6,4},{7,5},{8,10},{9,11},{10,... | collective-permute-start | bytes 294920 | tf_op jit(solution)/shard_map/ppermute | solution.py:61
  95.6 6.6 %collective-permute-start.14 = (f32[2,96,128]{2,1,0:T(8,128)S(1)}, f32[2,96,128]{2,1,0:T(8,128)S(1)}, u32[]{:S(2)}, u32[]{:S(2)}) collective-permute-start(f32[2,96,128]{2,1,0:T(8,128)S(1)} %get-tuple-element.55), channel_id=1, source_target_pairs={{0,3},{1,2},{2,1},{3,0},{4,7},{5,6},{6,5},{7,4},{8,11},{9,10},{10,... | collective-permute-start | bytes 294920 | tf_op jit(solution)/shard_map/ppermute | solution.py:61
  99.7 8.8 %collective-permute-start.38 = (f32[512,128]{1,0:T(8,128)S(1)}, f32[512,128]{1,0:T(8,128)S(1)}, u32[]{:S(2)}, u32[]{:S(2)}) collective-permute-start(f32[512,128]{1,0:T(8,128)S(1)} %get-tuple-element.21.refs_1_.refs_2_), channel_id=1, source_target_pairs={{0,16},{16,0},{1,17},{17,1},{2,18},{18,2},{3,19},{19,3},{4,20},{20... | collective-permute-start | bytes 786440 | tf_op jit(solution)/shard_map/ppermute | solution.py:61
  99.7 9.3 %collective-permute-start.39 = (f32[512,128]{1,0:T(8,128)}, f32[512,128]{1,0:T(8,128)S(1)}, u32[]{:S(2)}, u32[]{:S(2)}) collective-permute-start(f32[512,128]{1,0:T(8,128)} %collective-permute-done.31.refs_3_), channel_id=1, source_target_pairs={{0,16},{16,0},{1,17},{17,1},{2,18},{18,2},{3,19},{19,3},{4,20},{20... | collective-permute-start | bytes 786440 | tf_op jit(solution)/shard_map/ppermute | solution.py:61
  100.2 12.0 %collective-permute-start.40 = (f32[512,128]{1,0:T(8,128)}, f32[512,128]{1,0:T(8,128)S(1)}, u32[]{:S(2)}, u32[]{:S(2)}) collective-permute-start(f32[512,128]{1,0:T(8,128)} %collective-permute-done.32.refs_4_), channel_id=1, source_target_pairs={{0,16},{16,0},{1,17},{17,1},{2,18},{18,2},{3,19},{19,3},{4,20},{20... | collective-permute-start | bytes 786440 | tf_op jit(solution)/shard_map/ppermute | solution.py:61
  102.3 9.9 %collective-permute-start.41 = (f32[512,128]{1,0:T(8,128)}, f32[512,128]{1,0:T(8,128)S(1)}, u32[]{:S(2)}, u32[]{:S(2)}) collective-permute-start(f32[512,128]{1,0:T(8,128)} %collective-permute-done.33.refs_5_), channel_id=1, source_target_pairs={{0,16},{16,0},{1,17},{17,1},{2,18},{18,2},{3,19},{19,3},{4,20},{20... | collective-permute-start | bytes 786440 | tf_op jit(solution)/shard_map/ppermute | solution.py:61
  102.3 0.9 copy-start.19
  103.2 0.9 copy-start.21
  104.1 2.1 %copy-start.14 = (f32[256,128]{1,0:T(8,128)S(1)}, f32[256,128]{1,0:T(8,128)}, u32[]{:S(2)}) copy-start(f32[256,128]{1,0:T(8,128)} %copy-done.13) | copy-start | bytes 393220
  106.2 9.2 %collective-permute-start.21 = (f32[96,512]{1,0:T(8,128)S(1)}, f32[96,512]{1,0:T(8,128)S(1)}, u32[]{:S(2)}, u32[]{:S(2)}) collective-permute-start(f32[96,512]{1,0:T(8,128)S(1)} %factor_slice.1.refs_1_), channel_id=1, source_target_pairs={{0,4},{4,8},{8,12},{12,0},{1,5},{5,9},{9,13},{13,1},{2,6},{6,10},{... | collective-permute-start | bytes 589832 | tf_op jit(solution)/shard_map/ppermute | solution.py:56
  108.5 31.5 %collective-permute-start.35 = (f32[1024,128]{1,0:T(8,128)S(1)}, f32[1024,128]{1,0:T(8,128)S(1)}, u32[]{:S(2)}, u32[]{:S(2)}) collective-permute-start(f32[1024,128]{1,0:T(8,128)S(1)} %get-tuple-element.34), channel_id=1, source_target_pairs={{0,1},{1,0},{2,3},{3,2},{4,5},{5,4},{6,7},{7,6},{8,9},{9,8},{10,11... | collective-permute-start | bytes 1572872 | tf_op jit(solution)/shard_map/ppermute | solution.py:61
  109.0 31.5 %collective-permute-start.36 = (f32[1024,128]{1,0:T(8,128)S(1)}, f32[1024,128]{1,0:T(8,128)S(1)}, u32[]{:S(2)}, u32[]{:S(2)}) collective-permute-start(f32[1024,128]{1,0:T(8,128)S(1)} %get-tuple-element.35), channel_id=1, source_target_pairs={{0,2},{1,3},{2,0},{3,1},{4,6},{5,7},{6,4},{7,5},{8,10},{9,11},{10,... | collective-permute-start | bytes 1572872 | tf_op jit(solution)/shard_map/ppermute | solution.py:61
  112.2 28.3 %collective-permute-start.37 = (f32[1024,128]{1,0:T(8,128)S(1)}, f32[1024,128]{1,0:T(8,128)S(1)}, u32[]{:S(2)}, u32[]{:S(2)}) collective-permute-start(f32[1024,128]{1,0:T(8,128)S(1)} %get-tuple-element.36), channel_id=1, source_target_pairs={{0,3},{1,2},{2,1},{3,0},{4,7},{5,6},{6,5},{7,4},{8,11},{9,10},{10,... | collective-permute-start | bytes 1572872 | tf_op jit(solution)/shard_map/ppermute | solution.py:61
  112.2 12.9 %collective-permute-start.22 = (f32[96,512]{1,0:T(8,128)S(1)}, f32[96,512]{1,0:T(8,128)S(1)}, u32[]{:S(2)}, u32[]{:S(2)}) collective-permute-start(f32[96,512]{1,0:T(8,128)S(1)} %factor_slice.1.refs_1_), channel_id=1, source_target_pairs={{0,8},{4,12},{8,0},{12,4},{1,9},{5,13},{9,1},{13,5},{2,10},{6,14},... | collective-permute-start | bytes 589832 | tf_op jit(solution)/shard_map/ppermute | solution.py:56
  115.3 11.3 %collective-permute-start.23 = (f32[96,512]{1,0:T(8,128)S(1)}, f32[96,512]{1,0:T(8,128)S(1)}, u32[]{:S(2)}, u32[]{:S(2)}) collective-permute-start(f32[96,512]{1,0:T(8,128)S(1)} %factor_slice.1.refs_1_), channel_id=1, source_target_pairs={{0,12},{4,0},{8,4},{12,8},{1,13},{5,1},{9,5},{13,9},{2,14},{6,2},{... | collective-permute-start | bytes 589832 | tf_op jit(solution)/shard_map/ppermute | solution.py:56
  125.1 13.3 %collective-permute-start.18 = (f32[96,512]{1,0:T(8,128)S(1)}, f32[96,512]{1,0:T(8,128)S(1)}, u32[]{:S(2)}, u32[]{:S(2)}) collective-permute-start(f32[96,512]{1,0:T(8,128)S(1)} %factor_slice.1.refs_1_), channel_id=1, source_target_pairs={{0,1},{1,0},{2,3},{3,2},{4,5},{5,4},{6,7},{7,6},{8,9},{9,8},{10,11... | collective-permute-start | bytes 589832 | tf_op jit(solution)/shard_map/ppermute | solution.py:61
  126.6 13.3 %collective-permute-start.19 = (f32[96,512]{1,0:T(8,128)S(1)}, f32[96,512]{1,0:T(8,128)S(1)}, u32[]{:S(2)}, u32[]{:S(2)}) collective-permute-start(f32[96,512]{1,0:T(8,128)S(1)} %factor_slice.1.refs_1_), channel_id=1, source_target_pairs={{0,2},{1,3},{2,0},{3,1},{4,6},{5,7},{6,4},{7,5},{8,10},{9,11},{10,... | collective-permute-start | bytes 589832 | tf_op jit(solution)/shard_map/ppermute | solution.py:61
  138.4 6.5 %collective-permute-start.24 = (f32[96,512]{1,0:T(8,128)S(1)}, f32[96,512]{1,0:T(8,128)S(1)}, u32[]{:S(2)}, u32[]{:S(2)}) collective-permute-start(f32[96,512]{1,0:T(8,128)S(1)} %get-tuple-element.29), channel_id=1, source_target_pairs={{0,1},{1,0},{2,3},{3,2},{4,5},{5,4},{6,7},{7,6},{8,9},{9,8},{10,11... | collective-permute-start | bytes 589832 | tf_op jit(solution)/shard_map/ppermute | solution.py:61
  139.9 20.2 %collective-permute-start.42 = (f32[1024,128]{1,0:T(8,128)S(1)}, f32[1024,128]{1,0:T(8,128)S(1)}, u32[]{:S(2)}, u32[]{:S(2)}) collective-permute-start(f32[1024,128]{1,0:T(8,128)S(1)} %get-tuple-element.33.refs_6_), channel_id=1, source_target_pairs={{0,16},{16,0},{1,17},{17,1},{2,18},{18,2},{3,19},{19,3},{4,20},{20... | collective-permute-start | bytes 1572872 | tf_op jit(solution)/shard_map/ppermute | solution.py:61
  140.0 20.2 %collective-permute-start.43 = (f32[1024,128]{1,0:T(8,128)S(1)}, f32[1024,128]{1,0:T(8,128)S(1)}, u32[]{:S(2)}, u32[]{:S(2)}) collective-permute-start(f32[1024,128]{1,0:T(8,128)S(1)} %collective-permute-done.35.refs_7_), channel_id=1, source_target_pairs={{0,16},{16,0},{1,17},{17,1},{2,18},{18,2},{3,19},{19,3},{4,20},{20... | collective-permute-start | bytes 1572872 | tf_op jit(solution)/shard_map/ppermute | solution.py:61
  140.5 20.2 %collective-permute-start.44 = (f32[1024,128]{1,0:T(8,128)S(1)}, f32[1024,128]{1,0:T(8,128)S(1)}, u32[]{:S(2)}, u32[]{:S(2)}) collective-permute-start(f32[1024,128]{1,0:T(8,128)S(1)} %collective-permute-done.36.refs_8_), channel_id=1, source_target_pairs={{0,16},{16,0},{1,17},{17,1},{2,18},{18,2},{3,19},{19,3},{4,20},{20... | collective-permute-start | bytes 1572872 | tf_op jit(solution)/shard_map/ppermute | solution.py:61
  140.5 20.2 %collective-permute-start.45 = (f32[1024,128]{1,0:T(8,128)S(1)}, f32[1024,128]{1,0:T(8,128)S(1)}, u32[]{:S(2)}, u32[]{:S(2)}) collective-permute-start(f32[1024,128]{1,0:T(8,128)S(1)} %collective-permute-done.37.refs_9_), channel_id=1, source_target_pairs={{0,16},{16,0},{1,17},{17,1},{2,18},{18,2},{3,19},{19,3},{4,20},{20... | collective-permute-start | bytes 1572872 | tf_op jit(solution)/shard_map/ppermute | solution.py:61
  144.9 6.3 %collective-permute-start.25 = (f32[96,512]{1,0:T(8,128)S(1)}, f32[96,512]{1,0:T(8,128)S(1)}, u32[]{:S(2)}, u32[]{:S(2)}) collective-permute-start(f32[96,512]{1,0:T(8,128)S(1)} %get-tuple-element.30), channel_id=1, source_target_pairs={{0,2},{1,3},{2,0},{3,1},{4,6},{5,7},{6,4},{7,5},{8,10},{9,11},{10,... | collective-permute-start | bytes 589832 | tf_op jit(solution)/shard_map/ppermute | solution.py:61
  151.1 6.6 %collective-permute-start.26 = (f32[96,512]{1,0:T(8,128)S(1)}, f32[96,512]{1,0:T(8,128)S(1)}, u32[]{:S(2)}, u32[]{:S(2)}) collective-permute-start(f32[96,512]{1,0:T(8,128)S(1)} %get-tuple-element.31), channel_id=1, source_target_pairs={{0,3},{1,2},{2,1},{3,0},{4,7},{5,6},{6,5},{7,4},{8,11},{9,10},{10,... | collective-permute-start | bytes 589832 | tf_op jit(solution)/shard_map/ppermute | solution.py:61
  157.7 7.0 %collective-permute-start.20 = (f32[96,512]{1,0:T(8,128)S(1)}, f32[96,512]{1,0:T(8,128)S(1)}, u32[]{:S(2)}, u32[]{:S(2)}) collective-permute-start(f32[96,512]{1,0:T(8,128)S(1)} %factor_slice.1.refs_1_), channel_id=1, source_target_pairs={{0,3},{1,2},{2,1},{3,0},{4,7},{5,6},{6,5},{7,4},{8,11},{9,10},{10,... | collective-permute-start | bytes 589832 | tf_op jit(solution)/shard_map/ppermute | solution.py:61
  160.2 4.6 %collective-permute-start.27 = (f32[96,512]{1,0:T(8,128)S(1)}, f32[96,512]{1,0:T(8,128)S(1)}, u32[]{:S(2)}, u32[]{:S(2)}) collective-permute-start(f32[96,512]{1,0:T(8,128)S(1)} %get-tuple-element.28.refs_5_), channel_id=1, source_target_pairs={{0,16},{16,0},{1,17},{17,1},{2,18},{18,2},{3,19},{19,3},{4,20},{20... | collective-permute-start | bytes 589832 | tf_op jit(solution)/shard_map/ppermute | solution.py:61
  160.2 4.6 %collective-permute-start.28 = (f32[96,512]{1,0:T(8,128)S(1)}, f32[96,512]{1,0:T(8,128)S(1)}, u32[]{:S(2)}, u32[]{:S(2)}) collective-permute-start(f32[96,512]{1,0:T(8,128)S(1)} %collective-permute-done.24.refs_6_), channel_id=1, source_target_pairs={{0,16},{16,0},{1,17},{17,1},{2,18},{18,2},{3,19},{19,3},{4,20},{20... | collective-permute-start | bytes 589832 | tf_op jit(solution)/shard_map/ppermute | solution.py:61
  160.7 4.1 %collective-permute-start.29 = (f32[96,512]{1,0:T(8,128)S(1)}, f32[96,512]{1,0:T(8,128)S(1)}, u32[]{:S(2)}, u32[]{:S(2)}) collective-permute-start(f32[96,512]{1,0:T(8,128)S(1)} %collective-permute-done.25.refs_7_), channel_id=1, source_target_pairs={{0,16},{16,0},{1,17},{17,1},{2,18},{18,2},{3,19},{19,3},{4,20},{20... | collective-permute-start | bytes 589832 | tf_op jit(solution)/shard_map/ppermute | solution.py:61
  160.7 4.0 %collective-permute-start.30 = (f32[96,512]{1,0:T(8,128)S(1)}, f32[96,512]{1,0:T(8,128)S(1)}, u32[]{:S(2)}, u32[]{:S(2)}) collective-permute-start(f32[96,512]{1,0:T(8,128)S(1)} %collective-permute-done.26.refs_8_), channel_id=1, source_target_pairs={{0,16},{16,0},{1,17},{17,1},{2,18},{18,2},{3,19},{19,3},{4,20},{20... | collective-permute-start | bytes 589832 | tf_op jit(solution)/shard_map/ppermute | solution.py:61
  (6 other events, 4.4 us)

commit v4 on v3

--- a/solution.py
+++ b/solution.py
@@ -84,13 +84,76 @@
     ]
 
 
-def window_choice(block_row, group, parent_span):
-    padded = jnp.concatenate([jnp.full((HB,), -1, jnp.int32), block_row])
-    window = lax.dynamic_slice_in_dim(padded, group * CBD, CBD + HB)
-    target = group * parent_span + jnp.arange(parent_span, dtype=jnp.int32)
-    places = jnp.arange(1, CBD + HB + 1, dtype=jnp.int32)
-    hit = window[None, :] == target[:, None]
-    return jnp.sum(jnp.where(hit, places[None, :], 0), axis=1).astype(jnp.int32) - 1
+def lookup_table(block_map, parent_span):
+    def body(map_ref, out):
+        row, col, sib = (lax.axis_index(axis) for axis in ("row", "col", "sib"))
+        out[ROW], out[COL], out[SIB] = row, col, sib
+        for base, sibling, group, slots in (
+            (OWN_ROWS, sib, row, PBD),
+            (OTHER_ROWS, 1 - sib, row, PBD),
+            (OWN_COLS, sib, col, PBD),
+            (OTHER_COLS, 1 - sib, col, PBD),
+            (OWN_PIVOT, sib, 0, PIV),
+            (OTHER_PIVOT, 1 - sib, 0, PIV),
+        ):
+            window = []
+            for w in range(CBD + HB):
+                block = group * CBD + w - HB
+                landed = map_ref[sibling, jnp.maximum(block, 0)]
+                window.append(jnp.where(block >= 0, landed, -1))
+            for slot in range(slots):
+                place = jnp.int32(-1)
+                for w, landed in enumerate(window):
+                    place = jnp.where(landed == group * parent_span + slot, w, place)
+                out[base + slot] = place
+
+    return pl.pallas_call(
+        body,
+        in_specs=[SMEM],
+        out_specs=SMEM,
+        out_shape=jax.ShapeDtypeStruct((OTHER_PIVOT + PIV,), jnp.int32),
+        compiler_params=limit_for(BLK, 4),
+        name="lookup_table",
+    )(block_map)
+
+
+def cut_slices(table, front, parent, deal, sub):
+    size = front.shape[0]
+    count = parent.shape[0] // deal
+    aligned = sub % BLK == 0
+
+    def body(sc, front_ref, parent_ref, *refs):
+        fronts, deals, sems = refs[: count * aligned], refs[count * aligned : -1], refs[-1]
+        copies = [
+            pltpu.make_async_copy(
+                front_ref.at[:, span(sc[COL] ^ m, sub)], out, sems.at[m]
+            )
+            for m, out in enumerate(fronts)
+        ]
+        copies += [
+            pltpu.make_async_copy(
+                parent_ref.at[pl.ds(j * deal, deal), pl.ds(0, PANEL)], out, sems.at[count + j]
+            )
+            for j, out in enumerate(deals)
+        ]
+        run_copies(copies)
+
+    outs = pl.pallas_call(
+        body,
+        in_specs=[SMEM, ANY, ANY],
+        out_specs=[VMEM] * (count * aligned + count),
+        out_shape=[f32(size, sub)] * (count * aligned) + [f32(deal, PANEL)] * count,
+        scratch_shapes=[pltpu.SemaphoreType.DMA((2 * count,))],
+        compiler_params=limit_for(sub, 8),
+        name="cut_slices",
+    )(table, front, parent)
+    fronts, deals = outs[: count * aligned], outs[count * aligned :]
+    if not aligned:
+        col = lax.axis_index("col")
+        fronts = [
+            lax.dynamic_slice_in_dim(front, (col ^ k) * sub, sub, axis=1) for k in range(count)
+        ]
+    return fronts, deals
 
 
 def start_chosen(chosen, choices, target, sem):
@@ -246,7 +309,7 @@
     )(table, *pieces)
 
 
-def place_rows(table, homes, edge):
+def place_rows(table, homes, edge, deal):
     count = len(homes)
     size, width = homes[0].shape
     rows = HALF * BLK
@@ -254,26 +317,33 @@
     def body(*refs):
         sc = refs[0]
         home_refs = refs[1 : 1 + count]
-        edge_ref, keep, send, window, sems = refs[1 + count :]
+        edge_ref = refs[1 + count]
+        outs = refs[2 + count : 2 + 2 * count]
+        window, placed, sems = refs[2 + 2 * count :]
         main = window.at[pl.ds(EDGE, size)]
         start_chosen(sc[COL], home_refs, main, sems.at[0])
         copy = pltpu.make_async_copy(edge_ref, window.at[pl.ds(0, EDGE)], sems.at[1])
         copy.start()
         copy.wait()
         pltpu.make_async_copy(home_refs[0], main, sems.at[0]).wait()
-        for target, half in ((keep, sc[SIB]), (send, 1 - sc[SIB])):
+        for which, half in ((0, sc[SIB]), (1, 1 - sc[SIB])):
             for slot in range(HALF):
                 place = sc[OWN_ROWS + half * HALF + slot]
                 block = window[span(jnp.maximum(place, 0), BLK), :]
-                target[slot * BLK : (slot + 1) * BLK, :] = jnp.where(place >= 0, block, 0.0)
+                lines = slice(slot * BLK, (slot + 1) * BLK)
+                placed[which, lines, :] = jnp.where(place >= 0, block, 0.0)
+        for m, out in enumerate(outs):
+            for which in range(2):
+                out[which] = placed[which, span(sc[COL] ^ m, deal), :]
 
     return pl.pallas_call(
         body,
         in_specs=[SMEM] + [ANY] * (count + 1),
-        out_specs=[VMEM, VMEM],
-        out_shape=[f32(rows, width), f32(rows, width)],
+        out_specs=[VMEM] * count,
+        out_shape=[f32(2, deal, width)] * count,
         scratch_shapes=[
             pltpu.VMEM((size + EDGE, width), jnp.float32),
+            pltpu.VMEM((2, rows, width), jnp.float32),
             pltpu.SemaphoreType.DMA((2,)),
         ],
         compiler_params=limit_for(width, 8),
@@ -281,27 +351,30 @@
     )(table, *homes, edge)
 
 
-def factor_slice(table, small, dealt, pivot_inverse):
+def factor_slice(table, small, small_other, dealt, pivot_inverse):
     count = len(small)
     _, rows, sub = small[0].shape
 
     def body(*refs):
         sc = refs[0]
         pieces = refs[1 : 1 + count]
-        deal_refs = refs[1 + count : 1 + 2 * count]
-        inverse_ref, out, order, child, sums, sems = refs[1 + 2 * count :]
-        start_chosen(sc[COL], deal_refs, sums, sems.at[count])
-        run_copies(
-            [
-                pltpu.make_async_copy(piece, order.at[sc[COL] ^ k], sems.at[k])
-                for k, piece in enumerate(pieces)
+        other_refs = refs[1 + count : 1 + 2 * count]
+        deal_refs = refs[1 + 2 * count : 1 + 3 * count]
+        inverse_ref, out, order, child, sums, sems = refs[1 + 3 * count :]
+        start_chosen(sc[COL], deal_refs, sums, sems.at[2 * count])
+        copies = []
+        for k in range(count):
+            place = order.at[sc[COL] ^ k]
+            copies += [
+                pltpu.make_async_copy(pieces[k].at[0], place.at[0], sems.at[2 * k]),
+                pltpu.make_async_copy(other_refs[k].at[1], place.at[1], sems.at[2 * k + 1]),
             ]
-        )
+        run_copies(copies)
         for j in range(count):
             block, lane = divmod(j * sub, BLK)
             for sibling in range(2):
                 child[sibling, block, :, lane : lane + sub] = order[j, sibling]
-        pltpu.make_async_copy(deal_refs[0], sums, sems.at[count]).wait()
+        pltpu.make_async_copy(deal_refs[0], sums, sems.at[2 * count]).wait()
         for p in range(PIV):
             lanes = slice(p * BLK, (p + 1) * BLK)
             added = sums[:, lanes]
@@ -314,18 +387,18 @@
 
     return pl.pallas_call(
         body,
-        in_specs=[SMEM] + [ANY] * (2 * count) + [VMEM],
+        in_specs=[SMEM] + [ANY] * (3 * count) + [VMEM],
         out_specs=VMEM,
         out_shape=f32(rows, PANEL),
         scratch_shapes=[
             pltpu.VMEM((count, 2, rows, sub), jnp.float32),
             pltpu.VMEM((2, PIV, rows, BLK), jnp.float32),
             pltpu.VMEM((rows, PANEL), jnp.float32),
-            pltpu.SemaphoreType.DMA((count + 1,)),
+            pltpu.SemaphoreType.DMA((2 * count + 1,)),
         ],
         compiler_params=limit_for(sub, 16),
         name="factor_slice",
-    )(table, *small, *dealt, pivot_inverse)
+    )(table, *small, *small_other, *dealt, pivot_inverse)
 
 
 def assemble(table, parent, own, other):
@@ -478,9 +551,6 @@
 
 
 def shards(child_front, child_panel, block_map, parent_front, pivot_inverse):
-    front_index = lax.axis_index("sib")
-    row_index = lax.axis_index("row")
-    col_index = lax.axis_index("col")
     count = lax.axis_size("col")
     front = child_front[0]
     panel = child_panel[0]
@@ -489,19 +559,7 @@
     parent_span = parent_cols // BLK
     deal = parent_rows // count
 
-    own_map = lax.dynamic_index_in_dim(block_map, front_index, 0, keepdims=False)
-    other_map = lax.dynamic_index_in_dim(block_map, 1 - front_index, 0, keepdims=False)
-    table = jnp.concatenate(
-        [
-            jnp.stack([row_index, col_index, front_index]).astype(jnp.int32),
-            window_choice(own_map, row_index, parent_span),
-            window_choice(other_map, row_index, parent_span),
-            window_choice(own_map, col_index, parent_span),
-            window_choice(other_map, col_index, parent_span),
-            window_choice(own_map, 0, parent_span)[:PIV],
-            window_choice(other_map, 0, parent_span)[:PIV],
-        ]
-    )
+    table = lookup_table(block_map, parent_span)
 
     def over_col(values):
         got = []
@@ -520,14 +578,12 @@
 
     around = around_row(panel)
     rows = [panel] + over_col([panel] * (count - 1))
-    slices = [
-        lax.dynamic_slice_in_dim(front, (col_index ^ k) * sub, sub, axis=1) for k in range(count)
-    ]
+    slices, deals = cut_slices(table, front, parent_front, deal, sub)
     fronts = [slices[0]] + over_col(slices[1:])
 
     dealt = []
     for j in range(count):
-        value = parent_front[j * deal : (j + 1) * deal, :PANEL]
+        value = deals[j]
         dealt.append(lax.ppermute(value, "col", [(0, j)]) if j else value)
 
     *homes, edge, up = slice_products(table, rows, around, fronts)
@@ -535,16 +591,12 @@
     up = shifted(up, "row")
     own = [homes[0]] + over_col(homes[1:])
 
-    keep, send = place_rows(table, homes, edge)
-    both = jnp.stack([keep, to_sibling(send)])
-    slices = [
-        lax.dynamic_slice_in_dim(both, (col_index ^ k) * deal, deal, axis=1)
-        for k in range(count)
-    ]
-    small = [slices[0]] + over_col(slices[1:])
+    small = place_rows(table, homes, edge, deal)
+    small = [small[0]] + over_col(small[1:])
+    small_other = [to_sibling(value) for value in small]
     packed = pack_halo(table, homes, edge, up)
     own = own + [packed[0]] + over_col(packed[1:])
-    factor = factor_slice(table, small, dealt, pivot_inverse)
+    factor = factor_slice(table, small, small_other, dealt, pivot_inverse)
     factors = over_row(factor)
     row_pieces = [factor] + over_col([factor] * (count - 1))
 

time: 172 us -> 159 us (0.924)
  local copies, waits for them, and re-layouts: 17 us -> 3.18 us
  waiting for transfers between devices: 71.6 us -> 75.3 us
  starting transfers between devices: 59.2 us -> 57.1 us
    unnamed x48 -> x12, local copies, waits for them, and re-layouts: 14.1 us -> 3.18 us
    ppermute x34 -> x37, waiting for transfers between devices: 51.9 us -> 60.5 us  [swapped(): return lax.ppermute(value, axis, [(i, i ^ mask) for i in range(count)])]
    ppermute x4, waiting for transfers between devices: 12 us -> 8.58 us  [rotated(): lax.ppermute(value, axis, [(i, (i + steps) % count) for i in range(count)])]
    ppermute x4, starting transfers between devices: 5.02 us -> 8.39 us  [rotated(): lax.ppermute(value, axis, [(i, (i + steps) % count) for i in range(count)])]
    ppermute x3, starting transfers between devices: 10.8 us -> 7.43 us  [shards(): dealt.append(lax.ppermute(value, 'col', [(0, j)]) if j else value)]
    ppermute x34 -> x37, starting transfers between devices: 33.1 us -> 30.2 us  [swapped(): return lax.ppermute(value, axis, [(i, i ^ mask) for i in range(count)])]
    ppermute x1, waiting for transfers between devices: 6.27 us -> 3.57 us  [around_row(): far.append(lax.ppermute(middle, 'row', pairs))]
    pallas_call x1 -> x3, Pallas kernels: 2.01 us -> 4.28 us  [the longest x1 2.09 us: factor_slice(): pl.pallas_call(body, in_specs=[SMEM] + [ANY] * (3 * count) + [VMEM], out_...]
  transfers between devices with their start and end apart: 46 -> 49, of which waited for: 14 -> 14; matrix products, arithmetic and copies ran while one was open for 2% -> 0% of each run, Pallas kernels for 6% -> 10%
where the time goes in v4:
time: 159 us; the launch traced here: 158 us
  waiting for transfers between devices  75.3 us (47%)
  starting transfers between devices  57.1 us (36%)
  Pallas kernels  22.3 us (14%)
  local copies, waits for them, and re-layouts  3.18 us (2%)
    ppermute x37, waiting for transfers between devices, swapped(): return lax.ppermute(value, axis, [(i, i ^ mask) for i in range(count)])  60.5 us
    ppermute x37, starting transfers between devices, swapped(): return lax.ppermute(value, axis, [(i, i ^ mask) for i in range(count)])  30.2 us
    ppermute x4, waiting for transfers between devices, rotated(): lax.ppermute(value, axis, [(i, (i + steps) % count) for i in range(count)])  8.58 us
    ppermute x4, starting transfers between devices, rotated(): lax.ppermute(value, axis, [(i, (i + steps) % count) for i in range(count)])  8.39 us
    ppermute x3, starting transfers between devices, shards(): dealt.append(lax.ppermute(value, 'col', [(0, j)]) if j else value)  7.43 us
    pallas_call x1, Pallas kernels, finish(): pl.pallas_call(body, in_specs=[SMEM] + [ANY] * (3 * count) + [VMEM], out_...  6.28 us
    ppermute x2, starting transfers between devices, shifted(): return lax.ppermute(value, axis, [(i, i + 1) for i in range(count - 1)])  5.04 us
    ppermute x1, waiting for transfers between devices, around_row(): far.append(lax.ppermute(middle, 'row', pairs))  3.57 us
  transfers between devices with their start and end apart: 49, of which 14 were waited for; matrix products, arithmetic and copies ran while one was open for 0% of the time, Pallas kernels for 10%

profile of v4, /device:TPU:0, one launch (start us, length us, event | category | flops | bytes accessed | tf_op | source)
XLA Modules:
  0.0 158.2 jit_solution(1140036354084223656)
XLA Ops:
  0.0 4.1 %collective-permute-start.4 = (f32[128,1024]{1,0:T(8,128)}, f32[128,1024]{1,0:T(8,128)S(1)}, u32[]{:S(2)}, u32[]{:S(2)}) collective-permute-start(f32[128,1024]{1,0:T(8,128)} %bitcast.2), channel_id=1, source_target_pairs={{0,8},{4,12},{8,0},{12,4},{1,9},{5,13},{9,1},{13,5},{2,10},{6,14},... | collective-permute-start | bytes 1572872 | tf_op jit(solution)/shard_map/ppermute | solution.py:56
  4.1 1.5 collective-permute-start
  5.6 0.7 copy-done.5
  6.2 1.3 lookup_table.1.sc.refs_0_
  7.6 1.3 copy-done
  8.9 1.2 copy-done.4
  10.1 0.9 cut_slices.1
  10.9 0.6 collective-permute-start.7
  11.5 1.5 collective-permute-start.8
  13.1 1.4 collective-permute-start.9
  14.5 10.2 %collective-permute-done.7.refs_11_ = f32[512,128]{1,0:T(8,128)S(1)} collective-permute-done((f32[512,128]{1,0:T(8,128)S(1)}, f32[512,128]{1,0:T(8,128)S(1)}, u32[]{:S(2)}, u32[]{:S(2)}) %collective-permute-start.7) | collective-permute-done | bytes 262176 | tf_op jit(solution)/shard_map/ppermute | solution.py:61
  24.7 1.5 collective-permute-start.1
  26.2 1.4 collective-permute-start.2
  27.6 3.7 %collective-permute-done.9.refs_13_ = f32[512,128]{1,0:T(8,128)S(1)} collective-permute-done((f32[512,128]{1,0:T(8,128)S(1)}, f32[512,128]{1,0:T(8,128)S(1)}, u32[]{:S(2)}, u32[]{:S(2)}) %collective-permute-start.9) | collective-permute-done | bytes 262176 | tf_op jit(solution)/shard_map/ppermute | solution.py:61
  31.4 3.5 %collective-permute-start.3 = (f32[128,1024]{1,0:T(8,128)S(1)}, f32[128,1024]{1,0:T(8,128)S(1)}, u32[]{:S(2)}, u32[]{:S(2)}) collective-permute-start(f32[128,1024]{1,0:T(8,128)S(1)} %bitcast.6), channel_id=1, source_target_pairs={{0,4},{4,8},{8,12},{1,5},{5,9},{9,13},{2,6},{6,10},{10,14},{3,7},{... | collective-permute-start | bytes 1572872 | tf_op jit(solution)/shard_map/ppermute | solution.py:184
  34.9 1.3 collective-permute-start.6
  36.2 1.3 collective-permute-start.5
  37.5 14.3 %collective-permute-done.1.refs_3_ = f32[128,1024]{1,0:T(8,128)S(1)} collective-permute-done((f32[128,1024]{1,0:T(8,128)S(1)}, f32[128,1024]{1,0:T(8,128)S(1)}, u32[]{:S(2)}, u32[]{:S(2)}) %collective-permute-start.1) | collective-permute-done | bytes 524320 | tf_op jit(solution)/shard_map/ppermute | solution.py:61
  51.8 3.4 %collective-permute-start.18 = (f32[96,512]{1,0:T(8,128)S(1)}, f32[96,512]{1,0:T(8,128)S(1)}, u32[]{:S(2)}, u32[]{:S(2)}) collective-permute-start(f32[96,512]{1,0:T(8,128)S(1)} %get-tuple-element.45), channel_id=1, source_target_pairs={{0,1},{4,5},{8,9},{12,13},{16,17},{20,21},{24,25},{28,29}} | collective-permute-start | bytes 589832 | tf_op jit(solution)/shard_map/ppermute | solution.py:587
  55.2 3.6 %collective-permute-done.5.refs_8_ = f32[128,1024]{1,0:T(8,128)S(1)} collective-permute-done((f32[128,1024]{1,0:T(8,128)S(1)}, f32[128,1024]{1,0:T(8,128)S(1)}, u32[]{:S(2)}, u32[]{:S(2)}) %collective-permute-start.5) | collective-permute-done | bytes 524320 | tf_op jit(solution)/shard_map/ppermute | solution.py:188
  58.8 3.4 %slice_products.1 = (f32[512,128]{1,0:T(8,128)S(1)}, f32[512,128]{1,0:T(8,128)S(1)}, f32[512,128]{1,0:T(8,128)S(1)}, f32[512,128]{1,0:T(8,128)S(1)}, f32[256,128]{1,0:T(8,128)S(1)}, /*index=5*/f32[3,256,128]{2,1,0:T(8,128)S(1)}) custom-call(s32[35]{0:T(128)S(1)} %lookup_table.1.sc.refs_0_, f32[128,1024]{1,0:T(8,128)S(1)} %bitcast.8, ...), custom_call_target="tpu_custom_call" | custom-call | tf_op jit(solution)/shard_map/slice_products/pallas_call | solution.py:230
  62.2 1.6 %collective-permute-start.10 = (f32[256,128]{1,0:T(8,128)S(1)}, f32[256,128]{1,0:T(8,128)S(1)}, u32[]{:S(2)}, u32[]{:S(2)}) collective-permute-start(f32[256,128]{1,0:T(8,128)S(1)} %get-tuple-element.39), channel_id=1, source_target_pairs={{0,4},{4,8},{8,12},{1,5},{5,9},{9,13},{2,6},{6,10},{10,14},{3,7},{... | collective-permute-start | bytes 393224 | tf_op jit(solution)/shard_map/ppermute | solution.py:66
  63.8 2.4 %collective-permute-start.19 = (f32[96,512]{1,0:T(8,128)S(1)}, f32[96,512]{1,0:T(8,128)S(1)}, u32[]{:S(2)}, u32[]{:S(2)}) collective-permute-start(f32[96,512]{1,0:T(8,128)S(1)} %get-tuple-element.46), channel_id=1, source_target_pairs={{0,2},{4,6},{8,10},{12,14},{16,18},{20,22},{24,26},{28,30}} | collective-permute-start | bytes 589832 | tf_op jit(solution)/shard_map/ppermute | solution.py:587
  66.3 1.6 %collective-permute-start.20 = (f32[96,512]{1,0:T(8,128)S(1)}, f32[96,512]{1,0:T(8,128)S(1)}, u32[]{:S(2)}, u32[]{:S(2)}) collective-permute-start(f32[96,512]{1,0:T(8,128)S(1)} %get-tuple-element.47), channel_id=1, source_target_pairs={{0,3},{4,7},{8,11},{12,15},{16,19},{20,23},{24,27},{28,31}} | collective-permute-start | bytes 589832 | tf_op jit(solution)/shard_map/ppermute | solution.py:587
  67.9 0.8 place_rows.1
  68.8 2.0 %collective-permute-start.34 = (f32[512,128]{1,0:T(8,128)S(1)}, f32[512,128]{1,0:T(8,128)S(1)}, u32[]{:S(2)}, u32[]{:S(2)}) collective-permute-start(f32[512,128]{1,0:T(8,128)S(1)} %get-tuple-element.36.refs_2_), channel_id=1, source_target_pairs={{0,1},{1,0},{2,3},{3,2},{4,5},{5,4},{6,7},{7,6},{8,9},{9,8},{10,11... | collective-permute-start | bytes 786440 | tf_op jit(solution)/shard_map/ppermute | solution.py:61
  70.8 2.6 %collective-permute-done.19.refs_11_ = f32[96,512]{1,0:T(8,128)S(1)} collective-permute-done((f32[96,512]{1,0:T(8,128)S(1)}, f32[96,512]{1,0:T(8,128)S(1)}, u32[]{:S(2)}, u32[]{:S(2)}) %collective-permute-start.19) | collective-permute-done | bytes 196640 | tf_op jit(solution)/shard_map/ppermute | solution.py:587
  73.4 3.0 %collective-permute-start.12 = (f32[2,96,128]{2,1,0:T(8,128)S(1)}, f32[2,96,128]{2,1,0:T(8,128)S(1)}, u32[]{:S(2)}, u32[]{:S(2)}) collective-permute-start(f32[2,96,128]{2,1,0:T(8,128)S(1)} %get-tuple-element.42), channel_id=1, source_target_pairs={{0,2},{1,3},{2,0},{3,1},{4,6},{5,7},{6,4},{7,5},{8,10},{9,11},{10,... | collective-permute-start | bytes 294920 | tf_op jit(solution)/shard_map/ppermute | solution.py:61
  76.4 0.2 collective-permute-start.13
  76.6 2.7 %collective-permute-start.36 = (f32[512,128]{1,0:T(8,128)S(1)}, f32[512,128]{1,0:T(8,128)S(1)}, u32[]{:S(2)}, u32[]{:S(2)}) collective-permute-start(f32[512,128]{1,0:T(8,128)S(1)} %get-tuple-element.38.refs_4_), channel_id=1, source_target_pairs={{0,3},{1,2},{2,1},{3,0},{4,7},{5,6},{6,5},{7,4},{8,11},{9,10},{10,... | collective-permute-start | bytes 786440 | tf_op jit(solution)/shard_map/ppermute | solution.py:61
  79.3 4.9 %collective-permute-done.12.refs_3_ = f32[2,96,128]{2,1,0:T(8,128)S(1)} collective-permute-done((f32[2,96,128]{2,1,0:T(8,128)S(1)}, f32[2,96,128]{2,1,0:T(8,128)S(1)}, u32[]{:S(2)}, u32[]{:S(2)}) %collective-permute-start.12) | collective-permute-done | bytes 98336 | tf_op jit(solution)/shard_map/ppermute | solution.py:61
  84.2 3.4 %collective-permute-start.37 = (f32[3,256,128]{2,1,0:T(8,128)S(1)}, f32[3,256,128]{2,1,0:T(8,128)S(1)}, u32[]{:S(2)}, u32[]{:S(2)}) collective-permute-start(f32[3,256,128]{2,1,0:T(8,128)S(1)} %get-tuple-element.52), channel_id=1, source_target_pairs={{0,4},{4,8},{8,12},{1,5},{5,9},{9,13},{2,6},{6,10},{10,14},{3,7},{... | collective-permute-start | bytes 1179656 | tf_op jit(solution)/shard_map/ppermute | solution.py:66
  87.7 1.3 collective-permute-done.14.refs_5_
  89.2 0.4 collective-permute-start.16
  89.7 0.4 collective-permute-start.41
  90.0 0.3 collective-permute-done.15.refs_6_
  90.5 0.4 collective-permute-start.43
  91.0 2.1 %factor_slice.1.refs_1_ = f32[96,512]{1,0:T(8,128)S(1)} custom-call(s32[35]{0:T(128)S(1)} %lookup_table.1.sc.refs_0_, f32[2,96,128]{2,1,0:T(8,128)S(1)} %get-tuple-element.40.refs_1_, f32[2,96,128]{2,1,0:T(8,128)S(1)} %collective-permute-done.11.refs_2_, f32[2,96,128]{2,1,0:T(8,128)S(1)} %collective-permute-done.12.refs_3_, ...), custom_call_target="tpu_custom_call" | custom-call | tf_op jit(solution)/shard_map/factor_slice/pallas_call | solution.py:388
  93.1 2.3 %collective-permute-start.24 = (f32[96,512]{1,0:T(8,128)S(1)}, f32[96,512]{1,0:T(8,128)S(1)}, u32[]{:S(2)}, u32[]{:S(2)}) collective-permute-start(f32[96,512]{1,0:T(8,128)S(1)} %factor_slice.1.refs_1_), channel_id=1, source_target_pairs={{0,4},{4,8},{8,12},{12,0},{1,5},{5,9},{9,13},{13,1},{2,6},{6,10},{... | collective-permute-start | bytes 589832 | tf_op jit(solution)/shard_map/ppermute | solution.py:56
  95.4 2.2 %pack_halo.1 = (f32[1024,128]{1,0:T(8,128)S(1)}, f32[1024,128]{1,0:T(8,128)S(1)}, f32[1024,128]{1,0:T(8,128)S(1)}, f32[1024,128]{1,0:T(8,128)S(1)}) custom-call(s32[35]{0:T(128)S(1)} %lookup_table.1.sc.refs_0_, f32[512,128]{1,0:T(8,128)S(1)} %get-tuple-element.35.refs_1_.refs_2_, f32[512,128]{1,0:T(8,128)S(1)} %get-tuple-element.36.refs_2_, ...), custom_call_target="tpu_custom_call" | custom-call | tf_op jit(solution)/shard_map/pack_halo/pallas_call | solution.py:277
  97.6 0.4 collective-permute-start.38
  98.1 1.4 collective-permute-start.39
  99.4 1.8 %collective-permute-start.40 = (f32[1024,128]{1,0:T(8,128)S(1)}, f32[1024,128]{1,0:T(8,128)S(1)}, u32[]{:S(2)}, u32[]{:S(2)}) collective-permute-start(f32[1024,128]{1,0:T(8,128)S(1)} %get-tuple-element.56), channel_id=1, source_target_pairs={{0,3},{1,2},{2,1},{3,0},{4,7},{5,6},{6,5},{7,4},{8,11},{9,10},{10,... | collective-permute-start | bytes 1572872 | tf_op jit(solution)/shard_map/ppermute | solution.py:61
  101.2 0.3 collective-permute-start.25
  101.5 0.6 collective-permute-done.24.refs_2_
  102.1 1.7 %collective-permute-start.26 = (f32[96,512]{1,0:T(8,128)S(1)}, f32[96,512]{1,0:T(8,128)S(1)}, u32[]{:S(2)}, u32[]{:S(2)}) collective-permute-start(f32[96,512]{1,0:T(8,128)S(1)} %factor_slice.1.refs_1_), channel_id=1, source_target_pairs={{0,12},{4,0},{8,4},{12,8},{1,13},{5,1},{9,5},{13,9},{2,14},{6,2},{... | collective-permute-start | bytes 589832 | tf_op jit(solution)/shard_map/ppermute | solution.py:56
  103.9 8.0 %collective-permute-done.25.refs_3_ = f32[96,512]{1,0:T(8,128)S(1)} collective-permute-done((f32[96,512]{1,0:T(8,128)S(1)}, f32[96,512]{1,0:T(8,128)S(1)}, u32[]{:S(2)}, u32[]{:S(2)}) %collective-permute-start.25) | collective-permute-done | bytes 196640 | tf_op jit(solution)/shard_map/ppermute | solution.py:56
  111.8 0.4 collective-permute-start.21
  112.2 1.2 collective-permute-start.22
  113.4 1.7 %pick_for_cols.1 = (f32[96,512]{1,0:T(8,128)S(1)}, f32[96,512]{1,0:T(8,128)S(1)}, f32[96,512]{1,0:T(8,128)S(1)}, f32[96,512]{1,0:T(8,128)S(1)}) custom-call(s32[35]{0:T(128)S(1)} %lookup_table.1.sc.refs_0_, f32[96,512]{1,0:T(8,128)S(1)} %factor_slice.1.refs_1_, f32[96,512]{1,0:T(8,128)S(1)} %collective-permute-done.24.refs_2_, ...), custom_call_target="tpu_custom_call" | custom-call | tf_op jit(solution)/shard_map/pick_for_cols/pallas_call | solution.py:301
  115.1 10.1 %collective-permute-done.21.refs_2_ = f32[96,512]{1,0:T(8,128)S(1)} collective-permute-done((f32[96,512]{1,0:T(8,128)S(1)}, f32[96,512]{1,0:T(8,128)S(1)}, u32[]{:S(2)}, u32[]{:S(2)}) %collective-permute-start.21) | collective-permute-done | bytes 196640 | tf_op jit(solution)/shard_map/ppermute | solution.py:61
  125.3 0.4 collective-permute-start.27
  125.7 0.5 collective-permute-start.46
  126.2 0.4 collective-permute-start.48
  126.7 4.3 %collective-permute-done.27.refs_6_ = f32[96,512]{1,0:T(8,128)S(1)} collective-permute-done((f32[96,512]{1,0:T(8,128)S(1)}, f32[96,512]{1,0:T(8,128)S(1)}, u32[]{:S(2)}, u32[]{:S(2)}) %collective-permute-start.27) | collective-permute-done | bytes 196640 | tf_op jit(solution)/shard_map/ppermute | solution.py:61
  131.0 1.6 %collective-permute-start.28 = (f32[96,512]{1,0:T(8,128)S(1)}, f32[96,512]{1,0:T(8,128)S(1)}, u32[]{:S(2)}, u32[]{:S(2)}) collective-permute-start(f32[96,512]{1,0:T(8,128)S(1)} %get-tuple-element.50), channel_id=1, source_target_pairs={{0,2},{1,3},{2,0},{3,1},{4,6},{5,7},{6,4},{7,5},{8,10},{9,11},{10,... | collective-permute-start | bytes 589832 | tf_op jit(solution)/shard_map/ppermute | solution.py:61
  132.6 6.1 %collective-permute-done.28.refs_7_ = f32[96,512]{1,0:T(8,128)S(1)} collective-permute-done((f32[96,512]{1,0:T(8,128)S(1)}, f32[96,512]{1,0:T(8,128)S(1)}, u32[]{:S(2)}, u32[]{:S(2)}) %collective-permute-start.28) | collective-permute-done | bytes 196640 | tf_op jit(solution)/shard_map/ppermute | solution.py:61
  138.7 1.3 collective-permute-start.29
  140.0 5.3 %collective-permute-done.29.refs_8_ = f32[96,512]{1,0:T(8,128)S(1)} collective-permute-done((f32[96,512]{1,0:T(8,128)S(1)}, f32[96,512]{1,0:T(8,128)S(1)}, u32[]{:S(2)}, u32[]{:S(2)}) %collective-permute-start.29) | collective-permute-done | bytes 196640 | tf_op jit(solution)/shard_map/ppermute | solution.py:61
  145.3 2.0 %collective-permute-start.23 = (f32[96,512]{1,0:T(8,128)S(1)}, f32[96,512]{1,0:T(8,128)S(1)}, u32[]{:S(2)}, u32[]{:S(2)}) collective-permute-start(f32[96,512]{1,0:T(8,128)S(1)} %factor_slice.1.refs_1_), channel_id=1, source_target_pairs={{0,3},{1,2},{2,1},{3,0},{4,7},{5,6},{6,5},{7,4},{8,11},{9,10},{10,... | collective-permute-start | bytes 589832 | tf_op jit(solution)/shard_map/ppermute | solution.py:61
  147.3 0.5 collective-permute-start.31
  147.9 0.4 collective-permute-start.33
  148.3 3.6 %assemble.1.refs_13_ = f32[384,768]{1,0:T(8,128)S(1)} custom-call(s32[35]{0:T(128)S(1)} %lookup_table.1.sc.refs_0_, f32[384,768]{1,0:T(8,128)S(1)} %copy-done.1, f32[512,128]{1,0:T(8,128)S(1)} %get-tuple-element.35.refs_1_.refs_2_, f32[512,128]{1,0:T(8,128)S(1)} %collective-permute-done.34.refs_3_, f32[512,128]{1,0:T(8,128)S(1)} %collective-permute-done.35.refs_4_, ...), custom_call_target="tpu_custom_call" | custom-call | tf_op jit(solution)/shard_map/assemble/pallas_call | solution.py:481
  151.9 6.3 %finish.1 = f32[384,768]{1,0:T(8,128)} custom-call(s32[35]{0:T(128)S(1)} %lookup_table.1.sc.refs_0_, f32[96,512]{1,0:T(8,128)S(1)} %factor_slice.1.refs_1_, f32[96,512]{1,0:T(8,128)S(1)} %collective-permute-done.21.refs_2_, f32[96,512]{1,0:T(8,128)S(1)} %collective-permute-done.22.refs_3_, f32[96,512]{1,0:T(8,128)S(1)} %collective-permute-done.23.refs_4_, ...), custom_call_target="tpu_custom_call" | custom-call | tf_op jit(solution)/shard_map/finish/pallas_call | solution.py:538
  (55 shorter events, 1.0 us)
Async XLA Ops:
  0.0 34.9 %collective-permute-start.4 = (f32[128,1024]{1,0:T(8,128)}, f32[128,1024]{1,0:T(8,128)S(1)}, u32[]{:S(2)}, u32[]{:S(2)}) collective-permute-start(f32[128,1024]{1,0:T(8,128)} %bitcast.2), channel_id=1, source_target_pairs={{0,8},{4,12},{8,0},{12,4},{1,9},{5,13},{9,1},{13,5},{2,10},{6,14},... | collective-permute-start | bytes 1572872 | tf_op jit(solution)/shard_map/ppermute | solution.py:56
  4.1 32.1 %collective-permute-start = (f32[128,1024]{1,0:T(8,128)}, f32[128,1024]{1,0:T(8,128)S(1)}, u32[]{:S(2)}, u32[]{:S(2)}) collective-permute-start(f32[128,1024]{1,0:T(8,128)} %bitcast.3), channel_id=1, source_target_pairs={{0,1},{1,0},{2,3},{3,2},{4,5},{5,4},{6,7},{7,6},{8,9},{9,8},{10,11... | collective-permute-start | bytes 1572872 | tf_op jit(solution)/shard_map/ppermute | solution.py:61
  5.6 0.7 copy-start.5
  7.6 1.3 copy-start
  8.9 1.2 copy-start.4
  10.1 14.6 %copy-start.2 = (f32[1,128,1024]{2,1,0:T(8,128)S(1)}, f32[1,128,1024]{2,1,0:T(8,128)}, u32[]{:S(2)}) copy-start(f32[1,128,1024]{2,1,0:T(8,128)} %param.6) | copy-start | bytes 1572868
  10.9 13.7 %collective-permute-start.7 = (f32[512,128]{1,0:T(8,128)S(1)}, f32[512,128]{1,0:T(8,128)S(1)}, u32[]{:S(2)}, u32[]{:S(2)}) collective-permute-start(f32[512,128]{1,0:T(8,128)S(1)} %get-tuple-element.32), channel_id=1, source_target_pairs={{0,1},{1,0},{2,3},{3,2},{4,5},{5,4},{6,7},{7,6},{8,9},{9,8},{10,11... | collective-permute-start | bytes 786440 | tf_op jit(solution)/shard_map/ppermute | solution.py:61
  11.5 14.7 %collective-permute-start.8 = (f32[512,128]{1,0:T(8,128)S(1)}, f32[512,128]{1,0:T(8,128)S(1)}, u32[]{:S(2)}, u32[]{:S(2)}) collective-permute-start(f32[512,128]{1,0:T(8,128)S(1)} %get-tuple-element.33), channel_id=1, source_target_pairs={{0,2},{1,3},{2,0},{3,1},{4,6},{5,7},{6,4},{7,5},{8,10},{9,11},{10,... | collective-permute-start | bytes 786440 | tf_op jit(solution)/shard_map/ppermute | solution.py:61
  13.1 18.3 %collective-permute-start.9 = (f32[512,128]{1,0:T(8,128)S(1)}, f32[512,128]{1,0:T(8,128)S(1)}, u32[]{:S(2)}, u32[]{:S(2)}) collective-permute-start(f32[512,128]{1,0:T(8,128)S(1)} %get-tuple-element.34), channel_id=1, source_target_pairs={{0,3},{1,2},{2,1},{3,0},{4,7},{5,6},{6,5},{7,4},{8,11},{9,10},{10,... | collective-permute-start | bytes 786440 | tf_op jit(solution)/shard_map/ppermute | solution.py:61
  24.7 27.1 %collective-permute-start.1 = (f32[128,1024]{1,0:T(8,128)S(1)}, f32[128,1024]{1,0:T(8,128)S(1)}, u32[]{:S(2)}, u32[]{:S(2)}) collective-permute-start(f32[128,1024]{1,0:T(8,128)S(1)} %bitcast.4), channel_id=1, source_target_pairs={{0,2},{1,3},{2,0},{3,1},{4,6},{5,7},{6,4},{7,5},{8,10},{9,11},{10,... | collective-permute-start | bytes 1572872 | tf_op jit(solution)/shard_map/ppermute | solution.py:61
  26.2 29.0 %collective-permute-start.2 = (f32[128,1024]{1,0:T(8,128)S(1)}, f32[128,1024]{1,0:T(8,128)S(1)}, u32[]{:S(2)}, u32[]{:S(2)}) collective-permute-start(f32[128,1024]{1,0:T(8,128)S(1)} %bitcast.5), channel_id=1, source_target_pairs={{0,3},{1,2},{2,1},{3,0},{4,7},{5,6},{6,5},{7,4},{8,11},{9,10},{10,... | collective-permute-start | bytes 1572872 | tf_op jit(solution)/shard_map/ppermute | solution.py:61
  31.4 23.8 %collective-permute-start.3 = (f32[128,1024]{1,0:T(8,128)S(1)}, f32[128,1024]{1,0:T(8,128)S(1)}, u32[]{:S(2)}, u32[]{:S(2)}) collective-permute-start(f32[128,1024]{1,0:T(8,128)S(1)} %bitcast.6), channel_id=1, source_target_pairs={{0,4},{4,8},{8,12},{1,5},{5,9},{9,13},{2,6},{6,10},{10,14},{3,7},{... | collective-permute-start | bytes 1572872 | tf_op jit(solution)/shard_map/ppermute | solution.py:184
  34.9 20.3 %collective-permute-start.6 = (f32[128,1024]{1,0:T(8,128)S(1)}, f32[128,1024]{1,0:T(8,128)S(1)}, u32[]{:S(2)}, u32[]{:S(2)}) collective-permute-start(f32[128,1024]{1,0:T(8,128)S(1)} %bitcast.7), channel_id=1, source_target_pairs={{4,0},{8,4},{12,8},{5,1},{9,5},{13,9},{6,2},{10,6},{14,10},{7,3},{... | collective-permute-start | bytes 1572872 | tf_op jit(solution)/shard_map/ppermute | solution.py:185
  36.2 22.6 %collective-permute-start.5 = (f32[128,1024]{1,0:T(8,128)S(1)}, f32[128,1024]{1,0:T(8,128)S(1)}, u32[]{:S(2)}, u32[]{:S(2)}) collective-permute-start(f32[128,1024]{1,0:T(8,128)S(1)} %collective-permute-done.4.refs_7_), channel_id=1, source_target_pairs={{8,12},{4,0},{9,13},{5,1},{10,14},{6,2},{11,15},{7,3},{24,28},{20,... | collective-permute-start | bytes 1572872 | tf_op jit(solution)/shard_map/ppermute | solution.py:188
  51.8 19.0 %collective-permute-start.18 = (f32[96,512]{1,0:T(8,128)S(1)}, f32[96,512]{1,0:T(8,128)S(1)}, u32[]{:S(2)}, u32[]{:S(2)}) collective-permute-start(f32[96,512]{1,0:T(8,128)S(1)} %get-tuple-element.45), channel_id=1, source_target_pairs={{0,1},{4,5},{8,9},{12,13},{16,17},{20,21},{24,25},{28,29}} | collective-permute-start | bytes 589832 | tf_op jit(solution)/shard_map/ppermute | solution.py:587
  62.2 28.8 %copy-start.3 = (f32[512,512]{1,0:T(8,128)S(1)}, f32[512,512]{1,0:T(8,128)}, u32[]{:S(2)}) copy-start(f32[512,512]{1,0:T(8,128)} %refs_13_.1) | copy-start | bytes 3145732
  62.2 5.6 %collective-permute-start.10 = (f32[256,128]{1,0:T(8,128)S(1)}, f32[256,128]{1,0:T(8,128)S(1)}, u32[]{:S(2)}, u32[]{:S(2)}) collective-permute-start(f32[256,128]{1,0:T(8,128)S(1)} %get-tuple-element.39), channel_id=1, source_target_pairs={{0,4},{4,8},{8,12},{1,5},{5,9},{9,13},{2,6},{6,10},{10,14},{3,7},{... | collective-permute-start | bytes 393224 | tf_op jit(solution)/shard_map/ppermute | solution.py:66
  63.8 9.6 %collective-permute-start.19 = (f32[96,512]{1,0:T(8,128)S(1)}, f32[96,512]{1,0:T(8,128)S(1)}, u32[]{:S(2)}, u32[]{:S(2)}) collective-permute-start(f32[96,512]{1,0:T(8,128)S(1)} %get-tuple-element.46), channel_id=1, source_target_pairs={{0,2},{4,6},{8,10},{12,14},{16,18},{20,22},{24,26},{28,30}} | collective-permute-start | bytes 589832 | tf_op jit(solution)/shard_map/ppermute | solution.py:587
  66.3 10.1 %collective-permute-start.20 = (f32[96,512]{1,0:T(8,128)S(1)}, f32[96,512]{1,0:T(8,128)S(1)}, u32[]{:S(2)}, u32[]{:S(2)}) collective-permute-start(f32[96,512]{1,0:T(8,128)S(1)} %get-tuple-element.47), channel_id=1, source_target_pairs={{0,3},{4,7},{8,11},{12,15},{16,19},{20,23},{24,27},{28,31}} | collective-permute-start | bytes 589832 | tf_op jit(solution)/shard_map/ppermute | solution.py:587
  68.7 7.9 %collective-permute-start.11 = (f32[2,96,128]{2,1,0:T(8,128)S(1)}, f32[2,96,128]{2,1,0:T(8,128)S(1)}, u32[]{:S(2)}, u32[]{:S(2)}) collective-permute-start(f32[2,96,128]{2,1,0:T(8,128)S(1)} %get-tuple-element.41), channel_id=1, source_target_pairs={{0,1},{1,0},{2,3},{3,2},{4,5},{5,4},{6,7},{7,6},{8,9},{9,8},{10,11... | collective-permute-start | bytes 294920 | tf_op jit(solution)/shard_map/ppermute | solution.py:61
  68.8 20.4 %collective-permute-start.34 = (f32[512,128]{1,0:T(8,128)S(1)}, f32[512,128]{1,0:T(8,128)S(1)}, u32[]{:S(2)}, u32[]{:S(2)}) collective-permute-start(f32[512,128]{1,0:T(8,128)S(1)} %get-tuple-element.36.refs_2_), channel_id=1, source_target_pairs={{0,1},{1,0},{2,3},{3,2},{4,5},{5,4},{6,7},{7,6},{8,9},{9,8},{10,11... | collective-permute-start | bytes 786440 | tf_op jit(solution)/shard_map/ppermute | solution.py:61
  70.8 18.7 %collective-permute-start.35 = (f32[512,128]{1,0:T(8,128)S(1)}, f32[512,128]{1,0:T(8,128)S(1)}, u32[]{:S(2)}, u32[]{:S(2)}) collective-permute-start(f32[512,128]{1,0:T(8,128)S(1)} %get-tuple-element.37.refs_3_), channel_id=1, source_target_pairs={{0,2},{1,3},{2,0},{3,1},{4,6},{5,7},{6,4},{7,5},{8,10},{9,11},{10,... | collective-permute-start | bytes 786440 | tf_op jit(solution)/shard_map/ppermute | solution.py:61
  73.4 10.8 %collective-permute-start.12 = (f32[2,96,128]{2,1,0:T(8,128)S(1)}, f32[2,96,128]{2,1,0:T(8,128)S(1)}, u32[]{:S(2)}, u32[]{:S(2)}) collective-permute-start(f32[2,96,128]{2,1,0:T(8,128)S(1)} %get-tuple-element.42), channel_id=1, source_target_pairs={{0,2},{1,3},{2,0},{3,1},{4,6},{5,7},{6,4},{7,5},{8,10},{9,11},{10,... | collective-permute-start | bytes 294920 | tf_op jit(solution)/shard_map/ppermute | solution.py:61
  76.4 11.3 %collective-permute-start.13 = (f32[2,96,128]{2,1,0:T(8,128)S(1)}, f32[2,96,128]{2,1,0:T(8,128)S(1)}, u32[]{:S(2)}, u32[]{:S(2)}) collective-permute-start(f32[2,96,128]{2,1,0:T(8,128)S(1)} %get-tuple-element.43), channel_id=1, source_target_pairs={{0,3},{1,2},{2,1},{3,0},{4,7},{5,6},{6,5},{7,4},{8,11},{9,10},{10,... | collective-permute-start | bytes 294920 | tf_op jit(solution)/shard_map/ppermute | solution.py:61
  76.6 13.1 %collective-permute-start.36 = (f32[512,128]{1,0:T(8,128)S(1)}, f32[512,128]{1,0:T(8,128)S(1)}, u32[]{:S(2)}, u32[]{:S(2)}) collective-permute-start(f32[512,128]{1,0:T(8,128)S(1)} %get-tuple-element.38.refs_4_), channel_id=1, source_target_pairs={{0,3},{1,2},{2,1},{3,0},{4,7},{5,6},{6,5},{7,4},{8,11},{9,10},{10,... | collective-permute-start | bytes 786440 | tf_op jit(solution)/shard_map/ppermute | solution.py:61
  84.2 8.9 %collective-permute-start.37 = (f32[3,256,128]{2,1,0:T(8,128)S(1)}, f32[3,256,128]{2,1,0:T(8,128)S(1)}, u32[]{:S(2)}, u32[]{:S(2)}) collective-permute-start(f32[3,256,128]{2,1,0:T(8,128)S(1)} %get-tuple-element.52), channel_id=1, source_target_pairs={{0,4},{4,8},{8,12},{1,5},{5,9},{9,13},{2,6},{6,10},{10,14},{3,7},{... | collective-permute-start | bytes 1179656 | tf_op jit(solution)/shard_map/ppermute | solution.py:66
  87.6 1.4 collective-permute-start.14
  89.0 1.3 collective-permute-start.15
  89.2 1.3 collective-permute-start.16
  89.5 1.3 collective-permute-start.17
  89.7 7.9 %collective-permute-start.41 = (f32[512,128]{1,0:T(8,128)S(1)}, f32[512,128]{1,0:T(8,128)S(1)}, u32[]{:S(2)}, u32[]{:S(2)}) collective-permute-start(f32[512,128]{1,0:T(8,128)S(1)} %get-tuple-element.35.refs_1_.refs_2_), channel_id=1, source_target_pairs={{0,16},{16,0},{1,17},{17,1},{2,18},{18,2},{3,19},{19,3},{4,20},{20... | collective-permute-start | bytes 786440 | tf_op jit(solution)/shard_map/ppermute | solution.py:61
  90.3 7.8 %collective-permute-start.42 = (f32[512,128]{1,0:T(8,128)S(1)}, f32[512,128]{1,0:T(8,128)S(1)}, u32[]{:S(2)}, u32[]{:S(2)}) collective-permute-start(f32[512,128]{1,0:T(8,128)S(1)} %collective-permute-done.34.refs_3_), channel_id=1, source_target_pairs={{0,16},{16,0},{1,17},{17,1},{2,18},{18,2},{3,19},{19,3},{4,20},{20... | collective-permute-start | bytes 786440 | tf_op jit(solution)/shard_map/ppermute | solution.py:61
  90.5 9.0 %collective-permute-start.43 = (f32[512,128]{1,0:T(8,128)S(1)}, f32[512,128]{1,0:T(8,128)S(1)}, u32[]{:S(2)}, u32[]{:S(2)}) collective-permute-start(f32[512,128]{1,0:T(8,128)S(1)} %collective-permute-done.35.refs_4_), channel_id=1, source_target_pairs={{0,16},{16,0},{1,17},{17,1},{2,18},{18,2},{3,19},{19,3},{4,20},{20... | collective-permute-start | bytes 786440 | tf_op jit(solution)/shard_map/ppermute | solution.py:61
  90.8 10.4 %collective-permute-start.44 = (f32[512,128]{1,0:T(8,128)S(1)}, f32[512,128]{1,0:T(8,128)S(1)}, u32[]{:S(2)}, u32[]{:S(2)}) collective-permute-start(f32[512,128]{1,0:T(8,128)S(1)} %collective-permute-done.36.refs_5_), channel_id=1, source_target_pairs={{0,16},{16,0},{1,17},{17,1},{2,18},{18,2},{3,19},{19,3},{4,20},{20... | collective-permute-start | bytes 786440 | tf_op jit(solution)/shard_map/ppermute | solution.py:61
  93.1 55.2 %copy-start.1 = (f32[384,768]{1,0:T(8,128)S(1)}, f32[384,768]{1,0:T(8,128)}, u32[]{:S(2)}) copy-start(f32[384,768]{1,0:T(8,128)} %refs_1_.1) | copy-start | bytes 3538948
  93.1 9.0 %collective-permute-start.24 = (f32[96,512]{1,0:T(8,128)S(1)}, f32[96,512]{1,0:T(8,128)S(1)}, u32[]{:S(2)}, u32[]{:S(2)}) collective-permute-start(f32[96,512]{1,0:T(8,128)S(1)} %factor_slice.1.refs_1_), channel_id=1, source_target_pairs={{0,4},{4,8},{8,12},{12,0},{1,5},{5,9},{9,13},{13,1},{2,6},{6,10},{... | collective-permute-start | bytes 589832 | tf_op jit(solution)/shard_map/ppermute | solution.py:56
  97.6 28.0 %collective-permute-start.38 = (f32[1024,128]{1,0:T(8,128)S(1)}, f32[1024,128]{1,0:T(8,128)S(1)}, u32[]{:S(2)}, u32[]{:S(2)}) collective-permute-start(f32[1024,128]{1,0:T(8,128)S(1)} %get-tuple-element.54), channel_id=1, source_target_pairs={{0,1},{1,0},{2,3},{3,2},{4,5},{5,4},{6,7},{7,6},{8,9},{9,8},{10,11... | collective-permute-start | bytes 1572872 | tf_op jit(solution)/shard_map/ppermute | solution.py:61
  98.1 28.1 %collective-permute-start.39 = (f32[1024,128]{1,0:T(8,128)S(1)}, f32[1024,128]{1,0:T(8,128)S(1)}, u32[]{:S(2)}, u32[]{:S(2)}) collective-permute-start(f32[1024,128]{1,0:T(8,128)S(1)} %get-tuple-element.55), channel_id=1, source_target_pairs={{0,2},{1,3},{2,0},{3,1},{4,6},{5,7},{6,4},{7,5},{8,10},{9,11},{10,... | collective-permute-start | bytes 1572872 | tf_op jit(solution)/shard_map/ppermute | solution.py:61
  99.4 26.8 %collective-permute-start.40 = (f32[1024,128]{1,0:T(8,128)S(1)}, f32[1024,128]{1,0:T(8,128)S(1)}, u32[]{:S(2)}, u32[]{:S(2)}) collective-permute-start(f32[1024,128]{1,0:T(8,128)S(1)} %get-tuple-element.56), channel_id=1, source_target_pairs={{0,3},{1,2},{2,1},{3,0},{4,7},{5,6},{6,5},{7,4},{8,11},{9,10},{10,... | collective-permute-start | bytes 1572872 | tf_op jit(solution)/shard_map/ppermute | solution.py:61
  101.2 10.6 %collective-permute-start.25 = (f32[96,512]{1,0:T(8,128)S(1)}, f32[96,512]{1,0:T(8,128)S(1)}, u32[]{:S(2)}, u32[]{:S(2)}) collective-permute-start(f32[96,512]{1,0:T(8,128)S(1)} %factor_slice.1.refs_1_), channel_id=1, source_target_pairs={{0,8},{4,12},{8,0},{12,4},{1,9},{5,13},{9,1},{13,5},{2,10},{6,14},... | collective-permute-start | bytes 589832 | tf_op jit(solution)/shard_map/ppermute | solution.py:56
  102.1 10.1 %collective-permute-start.26 = (f32[96,512]{1,0:T(8,128)S(1)}, f32[96,512]{1,0:T(8,128)S(1)}, u32[]{:S(2)}, u32[]{:S(2)}) collective-permute-start(f32[96,512]{1,0:T(8,128)S(1)} %factor_slice.1.refs_1_), channel_id=1, source_target_pairs={{0,12},{4,0},{8,4},{12,8},{1,13},{5,1},{9,5},{13,9},{2,14},{6,2},{... | collective-permute-start | bytes 589832 | tf_op jit(solution)/shard_map/ppermute | solution.py:56
  111.8 13.4 %collective-permute-start.21 = (f32[96,512]{1,0:T(8,128)S(1)}, f32[96,512]{1,0:T(8,128)S(1)}, u32[]{:S(2)}, u32[]{:S(2)}) collective-permute-start(f32[96,512]{1,0:T(8,128)S(1)} %factor_slice.1.refs_1_), channel_id=1, source_target_pairs={{0,1},{1,0},{2,3},{3,2},{4,5},{5,4},{6,7},{7,6},{8,9},{9,8},{10,11... | collective-permute-start | bytes 589832 | tf_op jit(solution)/shard_map/ppermute | solution.py:61
  112.2 13.4 %collective-permute-start.22 = (f32[96,512]{1,0:T(8,128)S(1)}, f32[96,512]{1,0:T(8,128)S(1)}, u32[]{:S(2)}, u32[]{:S(2)}) collective-permute-start(f32[96,512]{1,0:T(8,128)S(1)} %factor_slice.1.refs_1_), channel_id=1, source_target_pairs={{0,2},{1,3},{2,0},{3,1},{4,6},{5,7},{6,4},{7,5},{8,10},{9,11},{10,... | collective-permute-start | bytes 589832 | tf_op jit(solution)/shard_map/ppermute | solution.py:61
  125.3 5.7 %collective-permute-start.27 = (f32[96,512]{1,0:T(8,128)S(1)}, f32[96,512]{1,0:T(8,128)S(1)}, u32[]{:S(2)}, u32[]{:S(2)}) collective-permute-start(f32[96,512]{1,0:T(8,128)S(1)} %get-tuple-element.49), channel_id=1, source_target_pairs={{0,1},{1,0},{2,3},{3,2},{4,5},{5,4},{6,7},{7,6},{8,9},{9,8},{10,11... | collective-permute-start | bytes 589832 | tf_op jit(solution)/shard_map/ppermute | solution.py:61
  125.7 21.6 %collective-permute-start.45 = (f32[1024,128]{1,0:T(8,128)S(1)}, f32[1024,128]{1,0:T(8,128)S(1)}, u32[]{:S(2)}, u32[]{:S(2)}) collective-permute-start(f32[1024,128]{1,0:T(8,128)S(1)} %get-tuple-element.53.refs_6_), channel_id=1, source_target_pairs={{0,16},{16,0},{1,17},{17,1},{2,18},{18,2},{3,19},{19,3},{4,20},{20... | collective-permute-start | bytes 1572872 | tf_op jit(solution)/shard_map/ppermute | solution.py:61
  125.7 21.6 %collective-permute-start.46 = (f32[1024,128]{1,0:T(8,128)S(1)}, f32[1024,128]{1,0:T(8,128)S(1)}, u32[]{:S(2)}, u32[]{:S(2)}) collective-permute-start(f32[1024,128]{1,0:T(8,128)S(1)} %collective-permute-done.38.refs_7_), channel_id=1, source_target_pairs={{0,16},{16,0},{1,17},{17,1},{2,18},{18,2},{3,19},{19,3},{4,20},{20... | collective-permute-start | bytes 1572872 | tf_op jit(solution)/shard_map/ppermute | solution.py:61
  126.2 21.6 %collective-permute-start.47 = (f32[1024,128]{1,0:T(8,128)S(1)}, f32[1024,128]{1,0:T(8,128)S(1)}, u32[]{:S(2)}, u32[]{:S(2)}) collective-permute-start(f32[1024,128]{1,0:T(8,128)S(1)} %collective-permute-done.39.refs_8_), channel_id=1, source_target_pairs={{0,16},{16,0},{1,17},{17,1},{2,18},{18,2},{3,19},{19,3},{4,20},{20... | collective-permute-start | bytes 1572872 | tf_op jit(solution)/shard_map/ppermute | solution.py:61
  126.2 21.6 %collective-permute-start.48 = (f32[1024,128]{1,0:T(8,128)S(1)}, f32[1024,128]{1,0:T(8,128)S(1)}, u32[]{:S(2)}, u32[]{:S(2)}) collective-permute-start(f32[1024,128]{1,0:T(8,128)S(1)} %collective-permute-done.40.refs_9_), channel_id=1, source_target_pairs={{0,16},{16,0},{1,17},{17,1},{2,18},{18,2},{3,19},{19,3},{4,20},{20... | collective-permute-start | bytes 1572872 | tf_op jit(solution)/shard_map/ppermute | solution.py:61
  131.0 7.8 %collective-permute-start.28 = (f32[96,512]{1,0:T(8,128)S(1)}, f32[96,512]{1,0:T(8,128)S(1)}, u32[]{:S(2)}, u32[]{:S(2)}) collective-permute-start(f32[96,512]{1,0:T(8,128)S(1)} %get-tuple-element.50), channel_id=1, source_target_pairs={{0,2},{1,3},{2,0},{3,1},{4,6},{5,7},{6,4},{7,5},{8,10},{9,11},{10,... | collective-permute-start | bytes 589832 | tf_op jit(solution)/shard_map/ppermute | solution.py:61
  138.7 6.6 %collective-permute-start.29 = (f32[96,512]{1,0:T(8,128)S(1)}, f32[96,512]{1,0:T(8,128)S(1)}, u32[]{:S(2)}, u32[]{:S(2)}) collective-permute-start(f32[96,512]{1,0:T(8,128)S(1)} %get-tuple-element.51), channel_id=1, source_target_pairs={{0,3},{1,2},{2,1},{3,0},{4,7},{5,6},{6,5},{7,4},{8,11},{9,10},{10,... | collective-permute-start | bytes 589832 | tf_op jit(solution)/shard_map/ppermute | solution.py:61
  145.3 6.6 %collective-permute-start.23 = (f32[96,512]{1,0:T(8,128)S(1)}, f32[96,512]{1,0:T(8,128)S(1)}, u32[]{:S(2)}, u32[]{:S(2)}) collective-permute-start(f32[96,512]{1,0:T(8,128)S(1)} %factor_slice.1.refs_1_), channel_id=1, source_target_pairs={{0,3},{1,2},{2,1},{3,0},{4,7},{5,6},{6,5},{7,4},{8,11},{9,10},{10,... | collective-permute-start | bytes 589832 | tf_op jit(solution)/shard_map/ppermute | solution.py:61
  147.3 4.6 %collective-permute-start.30 = (f32[96,512]{1,0:T(8,128)S(1)}, f32[96,512]{1,0:T(8,128)S(1)}, u32[]{:S(2)}, u32[]{:S(2)}) collective-permute-start(f32[96,512]{1,0:T(8,128)S(1)} %get-tuple-element.48.refs_5_), channel_id=1, source_target_pairs={{0,16},{16,0},{1,17},{17,1},{2,18},{18,2},{3,19},{19,3},{4,20},{20... | collective-permute-start | bytes 589832 | tf_op jit(solution)/shard_map/ppermute | solution.py:61
  147.3 4.6 %collective-permute-start.31 = (f32[96,512]{1,0:T(8,128)S(1)}, f32[96,512]{1,0:T(8,128)S(1)}, u32[]{:S(2)}, u32[]{:S(2)}) collective-permute-start(f32[96,512]{1,0:T(8,128)S(1)} %collective-permute-done.27.refs_6_), channel_id=1, source_target_pairs={{0,16},{16,0},{1,17},{17,1},{2,18},{18,2},{3,19},{19,3},{4,20},{20... | collective-permute-start | bytes 589832 | tf_op jit(solution)/shard_map/ppermute | solution.py:61
  147.8 4.1 %collective-permute-start.32 = (f32[96,512]{1,0:T(8,128)S(1)}, f32[96,512]{1,0:T(8,128)S(1)}, u32[]{:S(2)}, u32[]{:S(2)}) collective-permute-start(f32[96,512]{1,0:T(8,128)S(1)} %collective-permute-done.28.refs_7_), channel_id=1, source_target_pairs={{0,16},{16,0},{1,17},{17,1},{2,18},{18,2},{3,19},{19,3},{4,20},{20... | collective-permute-start | bytes 589832 | tf_op jit(solution)/shard_map/ppermute | solution.py:61
  147.9 4.1 %collective-permute-start.33 = (f32[96,512]{1,0:T(8,128)S(1)}, f32[96,512]{1,0:T(8,128)S(1)}, u32[]{:S(2)}, u32[]{:S(2)}) collective-permute-start(f32[96,512]{1,0:T(8,128)S(1)} %collective-permute-done.29.refs_8_), channel_id=1, source_target_pairs={{0,16},{16,0},{1,17},{17,1},{2,18},{18,2},{3,19},{19,3},{4,20},{20... | collective-permute-start | bytes 589832 | tf_op jit(solution)/shard_map/ppermute | solution.py:61

commit v5 on v4

--- a/solution.py
+++ b/solution.py
@@ -250,39 +250,63 @@
         sc = refs[0]
         home_refs = refs[1 : 1 + count]
         edge_ref, up_ref = refs[1 + count : 3 + count]
-        outs = refs[3 + count : 3 + 2 * count]
+        above_outs = refs[3 + count : 3 + 2 * count]
+        side_outs = refs[3 + 2 * count : 3 + 3 * count]
         sems = refs[-1]
-        near, far = pl.ds(size, EDGE), pl.ds(size + EDGE, EDGE)
-        for m, out in enumerate(outs):
+        for m in range(count):
             group = sc[COL] ^ m
             before = jnp.maximum(group - 1, 0)
-            start_chosen(before ^ sc[COL], home_refs, out.at[pl.ds(0, size)], sems.at[3 * m])
-            for i, (wanted, place) in enumerate(((group, near), (before, far))):
+            main, tail = side_outs[m].at[pl.ds(0, size)], side_outs[m].at[pl.ds(size, EDGE)]
+            start_chosen(before ^ sc[COL], home_refs, main, sems.at[3 * m])
+            for i, (wanted, place) in enumerate(((group, above_outs[m]), (before, tail))):
 
                 @pl.when(wanted == 0)
                 def _():
-                    pltpu.make_async_copy(edge_ref, out.at[place], sems.at[3 * m + 1 + i]).start()
+                    pltpu.make_async_copy(edge_ref, place, sems.at[3 * m + 1 + i]).start()
 
                 @pl.when(wanted > 0)
                 def _():
                     pltpu.make_async_copy(
-                        up_ref.at[jnp.maximum(wanted - 1, 0)], out.at[place], sems.at[3 * m + 1 + i]
+                        up_ref.at[jnp.maximum(wanted - 1, 0)], place, sems.at[3 * m + 1 + i]
                     ).start()
 
-        for m, out in enumerate(outs):
-            pltpu.make_async_copy(home_refs[0], out.at[pl.ds(0, size)], sems.at[3 * m]).wait()
-            for i, place in enumerate((near, far)):
-                pltpu.make_async_copy(edge_ref, out.at[place], sems.at[3 * m + 1 + i]).wait()
-
-    return pl.pallas_call(
+        for m in range(count):
+            main, tail = side_outs[m].at[pl.ds(0, size)], side_outs[m].at[pl.ds(size, EDGE)]
+            pltpu.make_async_copy(home_refs[0], main, sems.at[3 * m]).wait()
+            pltpu.make_async_copy(edge_ref, above_outs[m], sems.at[3 * m + 1]).wait()
+            pltpu.make_async_copy(edge_ref, tail, sems.at[3 * m + 2]).wait()
+
+    outs = pl.pallas_call(
         body,
         in_specs=[SMEM] + [ANY] * (count + 2),
-        out_specs=[VMEM] * count,
-        out_shape=[f32(size + 2 * EDGE, sub)] * count,
+        out_specs=[VMEM] * (2 * count),
+        out_shape=[f32(EDGE, sub)] * count + [f32(size + EDGE, sub)] * count,
         scratch_shapes=[pltpu.SemaphoreType.DMA((3 * count,))],
         compiler_params=limit_for(sub, 8),
         name="pack_halo",
     )(table, *homes, edge, up)
+    return outs[:count], outs[count:]
+
+
+def to_next_group(packed):
+    count = len(packed)
+    half = count // 2
+
+    def send(mask):
+        pairs = [(i, i ^ mask) for i in range(half, count)]
+        if mask > half:
+            pairs = [(i, j) for i, j in pairs if j > 0 and (i, j) != (half, 1)]
+        if not pairs:
+            return None
+        return lax.ppermute(packed[mask], "col", pairs)
+
+    got = [packed[0]] + [send(mask) for mask in range(1, count)]
+    forwarded = lax.ppermute(got[half], "col", [(0, 1)])
+    direct = got[half + 1]
+    if direct is not None:
+        forwarded = jnp.where(lax.axis_index("col") == 1, forwarded, direct)
+    got[half + 1] = forwarded
+    return got
 
 
 def pick_for_cols(table, pieces, masks):
@@ -401,42 +425,41 @@
     )(table, *small, *small_other, *dealt, pivot_inverse)
 
 
-def assemble(table, parent, own, other):
-    count = len(own) // 2
+def assemble(table, parent, own, other, row_pieces):
+    count = len(row_pieces)
     rows, width = parent.shape
+    piece_rows = row_pieces[0].shape[0]
     size, sub = own[0].shape
     half = count // 2
     split = BLK // sub
 
     def body(*refs):
         sc, parent_ref = refs[:2]
-        own_refs, other_refs = refs[2 : 2 + 2 * count], refs[2 + 2 * count : 2 + 4 * count]
-        out, own_win, other_win, sems = refs[2 + 4 * count :]
-        at = 0
-        always, edges = [], []
+        own_refs, other_refs = refs[2 : 2 + 3 * count], refs[2 + 3 * count : 2 + 6 * count]
+        row_refs = refs[2 + 6 * count : 2 + 7 * count]
+        out, high_out, low_out, own_win, other_win, row_factor, sems = refs[2 + 7 * count :]
+        low, high = pl.ds(0, EDGE), pl.ds(EDGE, size)
+        always = gather_copies(sc, row_refs, row_factor, sems, piece_rows)
+        at = count
+        edges = []
         for refs_in, window in ((own_refs, own_win), (other_refs, other_win)):
             for m in range(count):
-                home, halo = refs_in[m], refs_in[count + m]
+                home, above, packed = (refs_in[i * count + m] for i in range(3))
                 piece = sc[COL] ^ m
                 main = half + piece
                 side = jnp.maximum(piece - half, 0)
-                low, high = pl.ds(0, EDGE), pl.ds(EDGE, size)
                 always += [
                     pltpu.make_async_copy(home, window.at[main, high], sems.at[at]),
-                    pltpu.make_async_copy(
-                        halo.at[pl.ds(size, EDGE)], window.at[main, low], sems.at[at + 1]
-                    ),
+                    pltpu.make_async_copy(above, window.at[main, low], sems.at[at + 1]),
                 ]
                 edges += [
                     (
                         piece,
                         pltpu.make_async_copy(
-                            halo.at[pl.ds(0, size)], window.at[side, high], sems.at[at + 2]
+                            packed.at[pl.ds(0, size)], window.at[side, high], sems.at[at + 2]
                         ),
                         pltpu.make_async_copy(
-                            halo.at[pl.ds(size + EDGE, EDGE)],
-                            window.at[side, low],
-                            sems.at[at + 3],
+                            packed.at[pl.ds(size, EDGE)], window.at[side, low], sems.at[at + 3]
                         ),
                     )
                 ]
@@ -450,7 +473,10 @@
                 first.start()
                 second.start()
 
-        for copy in always:
+        for copy in always[:count]:
+            copy.wait()
+        high_out[...], low_out[...] = halves(row_factor[...])
+        for copy in always[count:]:
             copy.wait()
         for piece, first, second in edges:
 
@@ -476,48 +502,43 @@
                     ]
                     block = pieces[0] if split == 1 else jnp.concatenate(pieces, axis=1)
                     total += jnp.where((down >= 0) & (across >= 0), block, 0.0)
+                if q < PIV:
+                    total = jnp.where(sc[COL] == 0, row_factor[lines, cols], total)
                 out[lines, cols] = total
 
+    part = jax.ShapeDtypeStruct((rows, PANEL), jnp.bfloat16)
     return pl.pallas_call(
         body,
-        in_specs=[SMEM, VMEM] + [ANY] * (4 * count),
-        out_specs=VMEM,
-        out_shape=f32(rows, width),
+        in_specs=[SMEM, VMEM] + [ANY] * (7 * count),
+        out_specs=[VMEM] * 3,
+        out_shape=[f32(rows, width), part, part],
         scratch_shapes=[
             pltpu.VMEM((half + count, size + EDGE, sub), jnp.float32),
             pltpu.VMEM((half + count, size + EDGE, sub), jnp.float32),
-            pltpu.SemaphoreType.DMA((8 * count,)),
+            pltpu.VMEM((rows, PANEL), jnp.float32),
+            pltpu.SemaphoreType.DMA((9 * count,)),
         ],
-        compiler_params=limit_for(sub, 12),
+        compiler_params=limit_for(sub, 14),
         name="assemble",
-    )(table, parent, *own, *other)
-
-
-def finish(table, assembled, row_pieces, col_own, col_other):
-    count = len(row_pieces)
+    )(table, parent, *own, *other, *row_pieces)
+
+
+def finish(table, assembled, row_high, row_low, col_own, col_other):
+    count = len(col_own)
     rows, width = assembled.shape
-    piece_rows = row_pieces[0].shape[0]
+    piece_rows = col_own[0].shape[0]
 
     def body(*refs):
         sc = refs[0]
-        row_refs = refs[1 : 1 + count]
-        col_own_refs = refs[1 + count : 1 + 2 * count]
-        col_other_refs = refs[1 + 2 * count : 1 + 3 * count]
-        base_ref, out, row_factor, col_factor, sems = refs[1 + 3 * count :]
-        copies = [
-            gather_copies(sc, row_refs, row_factor, sems, piece_rows),
-            gather_copies(sc, col_own_refs, col_factor.at[sc[SIB]], sems, piece_rows, count),
-            gather_copies(
-                sc, col_other_refs, col_factor.at[1 - sc[SIB]], sems, piece_rows, 2 * count
-            ),
-        ]
-        for copy in sum(copies, []):
-            copy.start()
-        for copy in copies[0]:
-            copy.wait()
-        left = halves(row_factor[...])
-        for copy in copies[1] + copies[2]:
-            copy.wait()
+        own_refs = refs[1 : 1 + count]
+        other_refs = refs[1 + count : 1 + 2 * count]
+        base_ref, high_ref, low_ref, out, col_factor, sems = refs[1 + 2 * count :]
+        own = gather_copies(sc, own_refs, col_factor.at[sc[SIB]], sems, piece_rows)
+        other = gather_copies(
+            sc, other_refs, col_factor.at[1 - sc[SIB]], sems, piece_rows, count
+        )
+        run_copies(own + other)
+        left = high_ref[...], low_ref[...]
         first_row = (sc[ROW] * 2 + sc[SIB]) * HALF
         first_col = sc[COL] * PBD
         for side in range(2):
@@ -530,24 +551,20 @@
                     total = base_ref[lines, cols]
                     inside = (first_col + q >= PIV) & (first_row + p >= PIV)
                     reduced = total - product[lines, i * BLK : (i + 1) * BLK]
-                    total = jnp.where(inside, reduced, total)
-                    if q < PIV:
-                        total = jnp.where(sc[COL] == 0, row_factor[lines, cols], total)
-                    out[lines, cols] = total
+                    out[lines, cols] = jnp.where(inside, reduced, total)
 
     return pl.pallas_call(
         body,
-        in_specs=[SMEM] + [ANY] * (3 * count) + [VMEM],
+        in_specs=[SMEM] + [ANY] * (2 * count) + [VMEM] * 3,
         out_specs=VMEM,
         out_shape=f32(rows, width),
         scratch_shapes=[
-            pltpu.VMEM((rows, PANEL), jnp.float32),
             pltpu.VMEM((2, rows, PANEL), jnp.float32),
-            pltpu.SemaphoreType.DMA((3 * count,)),
+            pltpu.SemaphoreType.DMA((2 * count,)),
         ],
         compiler_params=limit_for(BLK, 16),
         name="finish",
-    )(table, *row_pieces, *col_own, *col_other, assembled)
+    )(table, *col_own, *col_other, assembled, row_high, row_low)
 
 
 def shards(child_front, child_panel, block_map, parent_front, pivot_inverse):
@@ -594,8 +611,8 @@
     small = place_rows(table, homes, edge, deal)
     small = [small[0]] + over_col(small[1:])
     small_other = [to_sibling(value) for value in small]
-    packed = pack_halo(table, homes, edge, up)
-    own = own + [packed[0]] + over_col(packed[1:])
+    above, packed = pack_halo(table, homes, edge, up)
+    own = own + [above[0]] + over_col(above[1:]) + to_next_group(packed)
     factor = factor_slice(table, small, small_other, dealt, pivot_inverse)
     factors = over_row(factor)
     row_pieces = [factor] + over_col([factor] * (count - 1))
@@ -605,8 +622,8 @@
     col_other = [to_sibling(value) for value in col_own]
 
     other = [to_sibling(value) for value in own]
-    assembled = assemble(table, parent_front, own, other)
-    return finish(table, assembled, row_pieces, col_own, col_other)
+    assembled, high, low = assemble(table, parent_front, own, other, row_pieces)
+    return finish(table, assembled, high, low, col_own, col_other)
 
 
 def solution(mesh):

time: 159 us -> 155 us (0.975)
  waiting for transfers between devices: 75.3 us -> 68.5 us
  starting transfers between devices: 57.1 us -> 59 us
    ppermute x0 -> x3, starting transfers between devices: none -> 6.9 us  [the longest x1 4.94 us: to_next_group(): forwarded = lax.ppermute(got[half], 'col', [(0, 1)])]
    ppermute x37 -> x41, waiting for transfers between devices: 60.5 us -> 55 us  [swapped(): return lax.ppermute(value, axis, [(i, i ^ mask) for i in range(count)])]
    ppermute x4, starting transfers between devices: 8.39 us -> 6.03 us  [rotated(): lax.ppermute(value, axis, [(i, (i + steps) % count) for i in range(count)])]
    ppermute x3, waiting for transfers between devices: 2.59 us -> 0.3 us  [shards(): dealt.append(lax.ppermute(value, 'col', [(0, j)]) if j else value)]
    ppermute x2, starting transfers between devices: 5.04 us -> 3.39 us  [shifted(): return lax.ppermute(value, axis, [(i, i + 1) for i in range(count - 1)])]
    ppermute x37 -> x41, starting transfers between devices: 30.2 us -> 29.2 us  [swapped(): return lax.ppermute(value, axis, [(i, i ^ mask) for i in range(count)])]
  transfers between devices with their start and end apart: 49 -> 56, of which waited for: 14 -> 17; matrix products, arithmetic and copies ran while one was open for 0% -> 0% of each run, Pallas kernels for 10% -> 12%
where the time goes in v5:
time: 155 us; the launch traced here: 154 us
  waiting for transfers between devices  68.5 us (44%)
  starting transfers between devices  59 us (38%)
  Pallas kernels  23.2 us (15%)
  local copies, waits for them, and re-layouts  3.18 us (2%)
    ppermute x41, waiting for transfers between devices, swapped(): return lax.ppermute(value, axis, [(i, i ^ mask) for i in range(count)])  55 us
    ppermute x41, starting transfers between devices, swapped(): return lax.ppermute(value, axis, [(i, i ^ mask) for i in range(count)])  29.2 us
    ppermute x4, waiting for transfers between devices, rotated(): lax.ppermute(value, axis, [(i, (i + steps) % count) for i in range(count)])  9.63 us
    ppermute x3, starting transfers between devices, shards(): dealt.append(lax.ppermute(value, 'col', [(0, j)]) if j else value)  7.43 us
    ppermute x4, starting transfers between devices, rotated(): lax.ppermute(value, axis, [(i, (i + steps) % count) for i in range(count)])  6.03 us
    pallas_call x1, Pallas kernels, finish(): pl.pallas_call(body, in_specs=[SMEM] + [ANY] * (2 * count) + [VMEM] * 3,...  5.12 us
    ppermute x1, starting transfers between devices, to_next_group(): forwarded = lax.ppermute(got[half], 'col', [(0, 1)])  4.94 us
    pallas_call x1, Pallas kernels, assemble(): pl.pallas_call(body, in_specs=[SMEM, VMEM] + [ANY] * (7 * count), out_spe...  4.91 us
  transfers between devices with their start and end apart: 56, of which 17 were waited for; matrix products, arithmetic and copies ran while one was open for 0% of the time, Pallas kernels for 12%

profile of v5, /device:TPU:0, one launch (start us, length us, event | category | flops | bytes accessed | tf_op | source)
XLA Modules:
  0.0 154.4 jit_solution(7873666995629931146)
XLA Ops:
  0.0 4.1 %collective-permute-start.4 = (f32[128,1024]{1,0:T(8,128)}, f32[128,1024]{1,0:T(8,128)S(1)}, u32[]{:S(2)}, u32[]{:S(2)}) collective-permute-start(f32[128,1024]{1,0:T(8,128)} %bitcast.2), channel_id=1, source_target_pairs={{0,8},{4,12},{8,0},{12,4},{1,9},{5,13},{9,1},{13,5},{2,10},{6,14},... | collective-permute-start | bytes 1572872 | tf_op jit(solution)/shard_map/ppermute | solution.py:56
  4.1 1.5 collective-permute-start
  5.6 0.7 copy-done.5
  6.2 1.3 lookup_table.1.sc.refs_0_
  7.6 1.3 copy-done
  8.9 1.2 copy-done.4
  10.1 0.9 cut_slices.1
  10.9 0.6 collective-permute-start.7
  11.5 1.5 collective-permute-start.8
  13.1 1.4 collective-permute-start.9
  14.5 10.2 %collective-permute-done.7.refs_11_ = f32[512,128]{1,0:T(8,128)S(1)} collective-permute-done((f32[512,128]{1,0:T(8,128)S(1)}, f32[512,128]{1,0:T(8,128)S(1)}, u32[]{:S(2)}, u32[]{:S(2)}) %collective-permute-start.7) | collective-permute-done | bytes 262176 | tf_op jit(solution)/shard_map/ppermute | solution.py:61
  24.7 1.5 collective-permute-start.1
  26.2 1.4 collective-permute-start.2
  27.6 3.7 %collective-permute-done.9.refs_13_ = f32[512,128]{1,0:T(8,128)S(1)} collective-permute-done((f32[512,128]{1,0:T(8,128)S(1)}, f32[512,128]{1,0:T(8,128)S(1)}, u32[]{:S(2)}, u32[]{:S(2)}) %collective-permute-start.9) | collective-permute-done | bytes 262176 | tf_op jit(solution)/shard_map/ppermute | solution.py:61
  31.4 3.5 %collective-permute-start.3 = (f32[128,1024]{1,0:T(8,128)S(1)}, f32[128,1024]{1,0:T(8,128)S(1)}, u32[]{:S(2)}, u32[]{:S(2)}) collective-permute-start(f32[128,1024]{1,0:T(8,128)S(1)} %bitcast.6), channel_id=1, source_target_pairs={{0,4},{4,8},{8,12},{1,5},{5,9},{9,13},{2,6},{6,10},{10,14},{3,7},{... | collective-permute-start | bytes 1572872 | tf_op jit(solution)/shard_map/ppermute | solution.py:184
  34.9 1.3 collective-permute-start.6
  36.2 1.3 collective-permute-start.5
  37.5 14.3 %collective-permute-done.1.refs_3_ = f32[128,1024]{1,0:T(8,128)S(1)} collective-permute-done((f32[128,1024]{1,0:T(8,128)S(1)}, f32[128,1024]{1,0:T(8,128)S(1)}, u32[]{:S(2)}, u32[]{:S(2)}) %collective-permute-start.1) | collective-permute-done | bytes 524320 | tf_op jit(solution)/shard_map/ppermute | solution.py:61
  51.8 3.4 %collective-permute-start.18 = (f32[96,512]{1,0:T(8,128)S(1)}, f32[96,512]{1,0:T(8,128)S(1)}, u32[]{:S(2)}, u32[]{:S(2)}) collective-permute-start(f32[96,512]{1,0:T(8,128)S(1)} %get-tuple-element.51), channel_id=1, source_target_pairs={{0,1},{4,5},{8,9},{12,13},{16,17},{20,21},{24,25},{28,29}} | collective-permute-start | bytes 589832 | tf_op jit(solution)/shard_map/ppermute | solution.py:604
  55.2 3.6 %collective-permute-done.5.refs_8_ = f32[128,1024]{1,0:T(8,128)S(1)} collective-permute-done((f32[128,1024]{1,0:T(8,128)S(1)}, f32[128,1024]{1,0:T(8,128)S(1)}, u32[]{:S(2)}, u32[]{:S(2)}) %collective-permute-start.5) | collective-permute-done | bytes 524320 | tf_op jit(solution)/shard_map/ppermute | solution.py:188
  58.8 3.4 %slice_products.1 = (f32[512,128]{1,0:T(8,128)S(1)}, f32[512,128]{1,0:T(8,128)S(1)}, f32[512,128]{1,0:T(8,128)S(1)}, f32[512,128]{1,0:T(8,128)S(1)}, f32[256,128]{1,0:T(8,128)S(1)}, /*index=5*/f32[3,256,128]{2,1,0:T(8,128)S(1)}) custom-call(s32[35]{0:T(128)S(1)} %lookup_table.1.sc.refs_0_, f32[128,1024]{1,0:T(8,128)S(1)} %bitcast.8, ...), custom_call_target="tpu_custom_call" | custom-call | tf_op jit(solution)/shard_map/slice_products/pallas_call | solution.py:230
  62.2 1.5 collective-permute-start.10
  63.7 2.4 %collective-permute-start.19 = (f32[96,512]{1,0:T(8,128)S(1)}, f32[96,512]{1,0:T(8,128)S(1)}, u32[]{:S(2)}, u32[]{:S(2)}) collective-permute-start(f32[96,512]{1,0:T(8,128)S(1)} %get-tuple-element.52), channel_id=1, source_target_pairs={{0,2},{4,6},{8,10},{12,14},{16,18},{20,22},{24,26},{28,30}} | collective-permute-start | bytes 589832 | tf_op jit(solution)/shard_map/ppermute | solution.py:604
  66.1 1.6 %collective-permute-start.20 = (f32[96,512]{1,0:T(8,128)S(1)}, f32[96,512]{1,0:T(8,128)S(1)}, u32[]{:S(2)}, u32[]{:S(2)}) collective-permute-start(f32[96,512]{1,0:T(8,128)S(1)} %get-tuple-element.53), channel_id=1, source_target_pairs={{0,3},{4,7},{8,11},{12,15},{16,19},{20,23},{24,27},{28,31}} | collective-permute-start | bytes 589832 | tf_op jit(solution)/shard_map/ppermute | solution.py:604
  67.7 1.9 %collective-permute-start.34 = (f32[3,256,128]{2,1,0:T(8,128)S(1)}, f32[3,256,128]{2,1,0:T(8,128)S(1)}, u32[]{:S(2)}, u32[]{:S(2)}) collective-permute-start(f32[3,256,128]{2,1,0:T(8,128)S(1)} %get-tuple-element.58), channel_id=1, source_target_pairs={{0,4},{4,8},{8,12},{1,5},{5,9},{9,13},{2,6},{6,10},{10,14},{3,7},{... | collective-permute-start | bytes 1179656 | tf_op jit(solution)/shard_map/ppermute | solution.py:66
  69.8 0.8 place_rows.1
  70.6 2.1 %collective-permute-start.11 = (f32[2,96,128]{2,1,0:T(8,128)S(1)}, f32[2,96,128]{2,1,0:T(8,128)S(1)}, u32[]{:S(2)}, u32[]{:S(2)}) collective-permute-start(f32[2,96,128]{2,1,0:T(8,128)S(1)} %get-tuple-element.47), channel_id=1, source_target_pairs={{0,1},{1,0},{2,3},{3,2},{4,5},{5,4},{6,7},{7,6},{8,9},{9,8},{10,11... | collective-permute-start | bytes 294920 | tf_op jit(solution)/shard_map/ppermute | solution.py:61
  73.0 3.4 %collective-permute-start.13 = (f32[2,96,128]{2,1,0:T(8,128)S(1)}, f32[2,96,128]{2,1,0:T(8,128)S(1)}, u32[]{:S(2)}, u32[]{:S(2)}) collective-permute-start(f32[2,96,128]{2,1,0:T(8,128)S(1)} %get-tuple-element.49), channel_id=1, source_target_pairs={{0,3},{1,2},{2,1},{3,0},{4,7},{5,6},{6,5},{7,4},{8,11},{9,10},{10,... | collective-permute-start | bytes 294920 | tf_op jit(solution)/shard_map/ppermute | solution.py:61
  76.4 0.7 collective-permute-done.11.refs_2_
  77.3 0.4 collective-permute-start.15
  77.7 1.3 collective-permute-done.13.refs_4_
  79.0 1.2 collective-permute-start.32
  80.2 1.7 %collective-permute-start.33 = (f32[512,128]{1,0:T(8,128)S(1)}, f32[512,128]{1,0:T(8,128)S(1)}, u32[]{:S(2)}, u32[]{:S(2)}) collective-permute-start(f32[512,128]{1,0:T(8,128)S(1)} %get-tuple-element.44.refs_4_), channel_id=1, source_target_pairs={{0,3},{1,2},{2,1},{3,0},{4,7},{5,6},{6,5},{7,4},{8,11},{9,10},{10,... | collective-permute-start | bytes 786440 | tf_op jit(solution)/shard_map/ppermute | solution.py:61
  82.0 0.5 collective-permute-start.16
  82.5 3.0 %pack_halo.1 = (f32[256,128]{1,0:T(8,128)S(1)}, f32[256,128]{1,0:T(8,128)S(1)}, f32[256,128]{1,0:T(8,128)S(1)}, f32[256,128]{1,0:T(8,128)S(1)}, f32[768,128]{1,0...) custom-call(s32[35]{0:T(128)S(1)} %lookup_table.1.sc.refs_0_, ...), custom_call_target="tpu_custom_call" | custom-call | tf_op jit(solution)/shard_map/pack_halo/pallas_call | solution.py:279
  85.6 0.7 collective-permute-start.35
  86.3 1.5 collective-permute-start.36
  87.7 2.1 %factor_slice.1.refs_1_.refs_26_ = f32[96,512]{1,0:T(8,128)S(1)} custom-call(s32[35]{0:T(128)S(1)} %lookup_table.1.sc.refs_0_, f32[2,96,128]{2,1,0:T(8,128)S(1)} %get-tuple-element.46.refs_1_, f32[2,96,128]{2,1,0:T(8,128)S(1)} %collective-permute-done.11.refs_2_, f32[2,96,128]{2,1,0:T(8,128)S(1)} %collective-permute-done.12.refs_3_, ...), custom_call_target="tpu_custom_call" | custom-call | tf_op jit(solution)/shard_map/factor_slice/pallas_call | solution.py:412
  89.8 3.2 %collective-permute-done.32.refs_4_ = f32[512,128]{1,0:T(8,128)S(1)} collective-permute-done((f32[512,128]{1,0:T(8,128)S(1)}, f32[512,128]{1,0:T(8,128)S(1)}, u32[]{:S(2)}, u32[]{:S(2)}) %collective-permute-start.32) | collective-permute-done | bytes 262176 | tf_op jit(solution)/shard_map/ppermute | solution.py:61
  93.1 2.0 %collective-permute-start.37 = (f32[256,128]{1,0:T(8,128)S(1)}, f32[256,128]{1,0:T(8,128)S(1)}, u32[]{:S(2)}, u32[]{:S(2)}) collective-permute-start(f32[256,128]{1,0:T(8,128)S(1)} %get-tuple-element.62), channel_id=1, source_target_pairs={{0,3},{1,2},{2,1},{3,0},{4,7},{5,6},{6,5},{7,4},{8,11},{9,10},{10,... | collective-permute-start | bytes 393224 | tf_op jit(solution)/shard_map/ppermute | solution.py:61
  95.3 1.5 collective-permute-start.54
  96.8 0.5 collective-permute-start.42
  97.3 2.2 %collective-permute-done.37.refs_9_ = f32[256,128]{1,0:T(8,128)S(1)} collective-permute-done((f32[256,128]{1,0:T(8,128)S(1)}, f32[256,128]{1,0:T(8,128)S(1)}, u32[]{:S(2)}, u32[]{:S(2)}) %collective-permute-start.37) | collective-permute-done | bytes 131104 | tf_op jit(solution)/shard_map/ppermute | solution.py:61
  99.5 1.5 collective-permute-start.55
  101.0 0.5 collective-permute-start.21
  101.6 1.3 collective-permute-start.39
  102.9 1.1 collective-permute-start.22
  104.0 2.2 %collective-permute-done.55.refs_29_ = f32[96,512]{1,0:T(8,128)S(1)} collective-permute-done((f32[96,512]{1,0:T(8,128)S(1)}, f32[96,512]{1,0:T(8,128)S(1)}, u32[]{:S(2)}, u32[]{:S(2)}) %collective-permute-start.55) | collective-permute-done | bytes 196640 | tf_op jit(solution)/shard_map/ppermute | solution.py:61
  106.2 0.4 collective-permute-start.23
  106.5 4.1 %collective-permute-done.21.refs_2_ = f32[96,512]{1,0:T(8,128)S(1)} collective-permute-done((f32[96,512]{1,0:T(8,128)S(1)}, f32[96,512]{1,0:T(8,128)S(1)}, u32[]{:S(2)}, u32[]{:S(2)}) %collective-permute-start.21) | collective-permute-done | bytes 196640 | tf_op jit(solution)/shard_map/ppermute | solution.py:56
  110.7 5.4 %collective-permute-done.22.refs_3_ = f32[96,512]{1,0:T(8,128)S(1)} collective-permute-done((f32[96,512]{1,0:T(8,128)S(1)}, f32[96,512]{1,0:T(8,128)S(1)}, u32[]{:S(2)}, u32[]{:S(2)}) %collective-permute-start.22) | collective-permute-done | bytes 196640 | tf_op jit(solution)/shard_map/ppermute | solution.py:56
  116.1 0.7 collective-permute-start.38
  116.9 4.9 %collective-permute-start.40 = (f32[768,128]{1,0:T(8,128)S(1)}, f32[768,128]{1,0:T(8,128)S(1)}, u32[]{:S(2)}, u32[]{:S(2)}) collective-permute-start(f32[768,128]{1,0:T(8,128)S(1)} %collective-permute-done.39.refs_12_), channel_id=1, source_target_pairs={{0,1},{4,5},{8,9},{12,13},{16,17},{20,21},{24,25},{28,29}} | collective-permute-start | bytes 1179656 | tf_op jit(solution)/shard_map/ppermute | solution.py:304
  121.8 1.7 %pick_for_cols.1 = (f32[96,512]{1,0:T(8,128)S(1)}, f32[96,512]{1,0:T(8,128)S(1)}, f32[96,512]{1,0:T(8,128)S(1)}, f32[96,512]{1,0:T(8,128)S(1)}) custom-call(s32[35]{0:T(128)S(1)} %lookup_table.1.sc.refs_0_, f32[96,512]{1,0:T(8,128)S(1)} %factor_slice.1.refs_1_.refs_26_, f32[96,512]{1,0:T(8,128)S(1)} %collective-permute-done.21.refs_2_, ...), custom_call_target="tpu_custom_call" | custom-call | tf_op jit(solution)/shard_map/pick_for_cols/pallas_call | solution.py:325
  124.2 0.8 collective-permute-done.47.refs_20_
  125.1 1.0 collective-permute-start.25
  126.0 0.5 collective-permute-start.50
  126.5 8.5 %collective-permute-done.24.refs_2_ = f32[96,512]{1,0:T(8,128)S(1)} collective-permute-done((f32[96,512]{1,0:T(8,128)S(1)}, f32[96,512]{1,0:T(8,128)S(1)}, u32[]{:S(2)}, u32[]{:S(2)}) %collective-permute-start.24) | collective-permute-done | bytes 196640 | tf_op jit(solution)/shard_map/ppermute | solution.py:61
  135.0 0.6 collective-permute-start.52
  135.6 7.6 %collective-permute-done.26.refs_4_ = f32[96,512]{1,0:T(8,128)S(1)} collective-permute-done((f32[96,512]{1,0:T(8,128)S(1)}, f32[96,512]{1,0:T(8,128)S(1)}, u32[]{:S(2)}, u32[]{:S(2)}) %collective-permute-start.26) | collective-permute-done | bytes 196640 | tf_op jit(solution)/shard_map/ppermute | solution.py:61
  143.3 0.5 collective-permute-start.28
  143.8 0.4 collective-permute-start.30
  144.3 4.9 %assemble.1 = (f32[384,768]{1,0:T(8,128)S(1)}, bf16[384,512]{1,0:T(8,128)(2,1)S(1)}, bf16[384,512]{1,0:T(8,128)(2,1)S(1)}) custom-call(s32[35]{0:T(128)S(1)} %lookup_table.1.sc.refs_0_, f32[384,768]{1,0:T(8,128)S(1)} %copy-done.1, f32[512,128]{1,0:T(8,128)S(1)} %get-tuple-element.41.refs_1_.refs_2_, f32[512,128]{1,0:T(8,128)S(1)} %collective-permute-done.31.refs_3_, ...), custom_call_target="tpu_custom_call" | custom-call | tf_op jit(solution)/shard_map/assemble/pallas_call | solution.py:510
  149.2 5.1 %finish.1 = f32[384,768]{1,0:T(8,128)} custom-call(s32[35]{0:T(128)S(1)} %lookup_table.1.sc.refs_0_, f32[96,512]{1,0:T(8,128)S(1)} %get-tuple-element.54.refs_1_, f32[96,512]{1,0:T(8,128)S(1)} %collective-permute-done.24.refs_2_, f32[96,512]{1,0:T(8,128)S(1)} %collective-permute-done.25.refs_3_, f32[96,512]{1,0:T(8,128)S(1)} %collective-permute-done.26.refs_4_, ...), custom_call_target="tpu_custom_call" | custom-call | tf_op jit(solution)/shard_map/finish/pallas_call | solution.py:556
  (69 shorter events, 1.7 us)
Async XLA Ops:
  0.0 34.9 %collective-permute-start.4 = (f32[128,1024]{1,0:T(8,128)}, f32[128,1024]{1,0:T(8,128)S(1)}, u32[]{:S(2)}, u32[]{:S(2)}) collective-permute-start(f32[128,1024]{1,0:T(8,128)} %bitcast.2), channel_id=1, source_target_pairs={{0,8},{4,12},{8,0},{12,4},{1,9},{5,13},{9,1},{13,5},{2,10},{6,14},... | collective-permute-start | bytes 1572872 | tf_op jit(solution)/shard_map/ppermute | solution.py:56
  4.1 32.1 %collective-permute-start = (f32[128,1024]{1,0:T(8,128)}, f32[128,1024]{1,0:T(8,128)S(1)}, u32[]{:S(2)}, u32[]{:S(2)}) collective-permute-start(f32[128,1024]{1,0:T(8,128)} %bitcast.3), channel_id=1, source_target_pairs={{0,1},{1,0},{2,3},{3,2},{4,5},{5,4},{6,7},{7,6},{8,9},{9,8},{10,11... | collective-permute-start | bytes 1572872 | tf_op jit(solution)/shard_map/ppermute | solution.py:61
  5.6 0.7 copy-start.5
  7.6 1.3 copy-start
  8.9 1.2 copy-start.4
  10.1 14.6 %copy-start.2 = (f32[1,128,1024]{2,1,0:T(8,128)S(1)}, f32[1,128,1024]{2,1,0:T(8,128)}, u32[]{:S(2)}) copy-start(f32[1,128,1024]{2,1,0:T(8,128)} %param.6) | copy-start | bytes 1572868
  10.9 13.7 %collective-permute-start.7 = (f32[512,128]{1,0:T(8,128)S(1)}, f32[512,128]{1,0:T(8,128)S(1)}, u32[]{:S(2)}, u32[]{:S(2)}) collective-permute-start(f32[512,128]{1,0:T(8,128)S(1)} %get-tuple-element.38), channel_id=1, source_target_pairs={{0,1},{1,0},{2,3},{3,2},{4,5},{5,4},{6,7},{7,6},{8,9},{9,8},{10,11... | collective-permute-start | bytes 786440 | tf_op jit(solution)/shard_map/ppermute | solution.py:61
  11.5 14.7 %collective-permute-start.8 = (f32[512,128]{1,0:T(8,128)S(1)}, f32[512,128]{1,0:T(8,128)S(1)}, u32[]{:S(2)}, u32[]{:S(2)}) collective-permute-start(f32[512,128]{1,0:T(8,128)S(1)} %get-tuple-element.39), channel_id=1, source_target_pairs={{0,2},{1,3},{2,0},{3,1},{4,6},{5,7},{6,4},{7,5},{8,10},{9,11},{10,... | collective-permute-start | bytes 786440 | tf_op jit(solution)/shard_map/ppermute | solution.py:61
  13.1 18.3 %collective-permute-start.9 = (f32[512,128]{1,0:T(8,128)S(1)}, f32[512,128]{1,0:T(8,128)S(1)}, u32[]{:S(2)}, u32[]{:S(2)}) collective-permute-start(f32[512,128]{1,0:T(8,128)S(1)} %get-tuple-element.40), channel_id=1, source_target_pairs={{0,3},{1,2},{2,1},{3,0},{4,7},{5,6},{6,5},{7,4},{8,11},{9,10},{10,... | collective-permute-start | bytes 786440 | tf_op jit(solution)/shard_map/ppermute | solution.py:61
  24.7 27.1 %collective-permute-start.1 = (f32[128,1024]{1,0:T(8,128)S(1)}, f32[128,1024]{1,0:T(8,128)S(1)}, u32[]{:S(2)}, u32[]{:S(2)}) collective-permute-start(f32[128,1024]{1,0:T(8,128)S(1)} %bitcast.4), channel_id=1, source_target_pairs={{0,2},{1,3},{2,0},{3,1},{4,6},{5,7},{6,4},{7,5},{8,10},{9,11},{10,... | collective-permute-start | bytes 1572872 | tf_op jit(solution)/shard_map/ppermute | solution.py:61
  26.2 29.0 %collective-permute-start.2 = (f32[128,1024]{1,0:T(8,128)S(1)}, f32[128,1024]{1,0:T(8,128)S(1)}, u32[]{:S(2)}, u32[]{:S(2)}) collective-permute-start(f32[128,1024]{1,0:T(8,128)S(1)} %bitcast.5), channel_id=1, source_target_pairs={{0,3},{1,2},{2,1},{3,0},{4,7},{5,6},{6,5},{7,4},{8,11},{9,10},{10,... | collective-permute-start | bytes 1572872 | tf_op jit(solution)/shard_map/ppermute | solution.py:61
  31.4 23.8 %collective-permute-start.3 = (f32[128,1024]{1,0:T(8,128)S(1)}, f32[128,1024]{1,0:T(8,128)S(1)}, u32[]{:S(2)}, u32[]{:S(2)}) collective-permute-start(f32[128,1024]{1,0:T(8,128)S(1)} %bitcast.6), channel_id=1, source_target_pairs={{0,4},{4,8},{8,12},{1,5},{5,9},{9,13},{2,6},{6,10},{10,14},{3,7},{... | collective-permute-start | bytes 1572872 | tf_op jit(solution)/shard_map/ppermute | solution.py:184
  34.9 20.3 %collective-permute-start.6 = (f32[128,1024]{1,0:T(8,128)S(1)}, f32[128,1024]{1,0:T(8,128)S(1)}, u32[]{:S(2)}, u32[]{:S(2)}) collective-permute-start(f32[128,1024]{1,0:T(8,128)S(1)} %bitcast.7), channel_id=1, source_target_pairs={{4,0},{8,4},{12,8},{5,1},{9,5},{13,9},{6,2},{10,6},{14,10},{7,3},{... | collective-permute-start | bytes 1572872 | tf_op jit(solution)/shard_map/ppermute | solution.py:185
  36.2 22.6 %collective-permute-start.5 = (f32[128,1024]{1,0:T(8,128)S(1)}, f32[128,1024]{1,0:T(8,128)S(1)}, u32[]{:S(2)}, u32[]{:S(2)}) collective-permute-start(f32[128,1024]{1,0:T(8,128)S(1)} %collective-permute-done.4.refs_7_), channel_id=1, source_target_pairs={{8,12},{4,0},{9,13},{5,1},{10,14},{6,2},{11,15},{7,3},{24,28},{20,... | collective-permute-start | bytes 1572872 | tf_op jit(solution)/shard_map/ppermute | solution.py:188
  51.8 18.8 %collective-permute-start.18 = (f32[96,512]{1,0:T(8,128)S(1)}, f32[96,512]{1,0:T(8,128)S(1)}, u32[]{:S(2)}, u32[]{:S(2)}) collective-permute-start(f32[96,512]{1,0:T(8,128)S(1)} %get-tuple-element.51), channel_id=1, source_target_pairs={{0,1},{4,5},{8,9},{12,13},{16,17},{20,21},{24,25},{28,29}} | collective-permute-start | bytes 589832 | tf_op jit(solution)/shard_map/ppermute | solution.py:604
  62.2 7.5 %collective-permute-start.10 = (f32[256,128]{1,0:T(8,128)S(1)}, f32[256,128]{1,0:T(8,128)S(1)}, u32[]{:S(2)}, u32[]{:S(2)}) collective-permute-start(f32[256,128]{1,0:T(8,128)S(1)} %get-tuple-element.45), channel_id=1, source_target_pairs={{0,4},{4,8},{8,12},{1,5},{5,9},{9,13},{2,6},{6,10},{10,14},{3,7},{... | collective-permute-start | bytes 393224 | tf_op jit(solution)/shard_map/ppermute | solution.py:66
  63.7 9.0 %collective-permute-start.19 = (f32[96,512]{1,0:T(8,128)S(1)}, f32[96,512]{1,0:T(8,128)S(1)}, u32[]{:S(2)}, u32[]{:S(2)}) collective-permute-start(f32[96,512]{1,0:T(8,128)S(1)} %get-tuple-element.52), channel_id=1, source_target_pairs={{0,2},{4,6},{8,10},{12,14},{16,18},{20,22},{24,26},{28,30}} | collective-permute-start | bytes 589832 | tf_op jit(solution)/shard_map/ppermute | solution.py:604
  66.1 6.9 %collective-permute-start.20 = (f32[96,512]{1,0:T(8,128)S(1)}, f32[96,512]{1,0:T(8,128)S(1)}, u32[]{:S(2)}, u32[]{:S(2)}) collective-permute-start(f32[96,512]{1,0:T(8,128)S(1)} %get-tuple-element.53), channel_id=1, source_target_pairs={{0,3},{4,7},{8,11},{12,15},{16,19},{20,23},{24,27},{28,31}} | collective-permute-start | bytes 589832 | tf_op jit(solution)/shard_map/ppermute | solution.py:604
  67.7 14.7 %collective-permute-start.34 = (f32[3,256,128]{2,1,0:T(8,128)S(1)}, f32[3,256,128]{2,1,0:T(8,128)S(1)}, u32[]{:S(2)}, u32[]{:S(2)}) collective-permute-start(f32[3,256,128]{2,1,0:T(8,128)S(1)} %get-tuple-element.58), channel_id=1, source_target_pairs={{0,4},{4,8},{8,12},{1,5},{5,9},{9,13},{2,6},{6,10},{10,14},{3,7},{... | collective-permute-start | bytes 1179656 | tf_op jit(solution)/shard_map/ppermute | solution.py:66
  69.7 12.3 %collective-permute-start.31 = (f32[512,128]{1,0:T(8,128)S(1)}, f32[512,128]{1,0:T(8,128)S(1)}, u32[]{:S(2)}, u32[]{:S(2)}) collective-permute-start(f32[512,128]{1,0:T(8,128)S(1)} %get-tuple-element.42.refs_2_), channel_id=1, source_target_pairs={{0,1},{1,0},{2,3},{3,2},{4,5},{5,4},{6,7},{7,6},{8,9},{9,8},{10,11... | collective-permute-start | bytes 786440 | tf_op jit(solution)/shard_map/ppermute | solution.py:61
  69.8 18.0 %copy-start.3 = (f32[512,512]{1,0:T(8,128)S(1)}, f32[512,512]{1,0:T(8,128)}, u32[]{:S(2)}) copy-start(f32[512,512]{1,0:T(8,128)} %refs_13_.1) | copy-start | bytes 3145732
  70.6 6.5 %collective-permute-start.11 = (f32[2,96,128]{2,1,0:T(8,128)S(1)}, f32[2,96,128]{2,1,0:T(8,128)S(1)}, u32[]{:S(2)}, u32[]{:S(2)}) collective-permute-start(f32[2,96,128]{2,1,0:T(8,128)S(1)} %get-tuple-element.47), channel_id=1, source_target_pairs={{0,1},{1,0},{2,3},{3,2},{4,5},{5,4},{6,7},{7,6},{8,9},{9,8},{10,11... | collective-permute-start | bytes 294920 | tf_op jit(solution)/shard_map/ppermute | solution.py:61
  72.7 4.6 %collective-permute-start.12 = (f32[2,96,128]{2,1,0:T(8,128)S(1)}, f32[2,96,128]{2,1,0:T(8,128)S(1)}, u32[]{:S(2)}, u32[]{:S(2)}) collective-permute-start(f32[2,96,128]{2,1,0:T(8,128)S(1)} %get-tuple-element.48), channel_id=1, source_target_pairs={{0,2},{1,3},{2,0},{3,1},{4,6},{5,7},{6,4},{7,5},{8,10},{9,11},{10,... | collective-permute-start | bytes 294920 | tf_op jit(solution)/shard_map/ppermute | solution.py:61
  73.0 6.0 %collective-permute-start.13 = (f32[2,96,128]{2,1,0:T(8,128)S(1)}, f32[2,96,128]{2,1,0:T(8,128)S(1)}, u32[]{:S(2)}, u32[]{:S(2)}) collective-permute-start(f32[2,96,128]{2,1,0:T(8,128)S(1)} %get-tuple-element.49), channel_id=1, source_target_pairs={{0,3},{1,2},{2,1},{3,0},{4,7},{5,6},{6,5},{7,4},{8,11},{9,10},{10,... | collective-permute-start | bytes 294920 | tf_op jit(solution)/shard_map/ppermute | solution.py:61
  77.2 3.1 %collective-permute-start.14 = (f32[2,96,128]{2,1,0:T(8,128)S(1)}, f32[2,96,128]{2,1,0:T(8,128)S(1)}, u32[]{:S(2)}, u32[]{:S(2)}) collective-permute-start(f32[2,96,128]{2,1,0:T(8,128)S(1)} %get-tuple-element.46.refs_1_), channel_id=1, source_target_pairs={{0,16},{16,0},{1,17},{17,1},{2,18},{18,2},{3,19},{19,3},{4,20},{20... | collective-permute-start | bytes 294920 | tf_op jit(solution)/shard_map/ppermute | solution.py:61
  77.3 4.7 %collective-permute-start.15 = (f32[2,96,128]{2,1,0:T(8,128)S(1)}, f32[2,96,128]{2,1,0:T(8,128)S(1)}, u32[]{:S(2)}, u32[]{:S(2)}) collective-permute-start(f32[2,96,128]{2,1,0:T(8,128)S(1)} %collective-permute-done.11.refs_2_), channel_id=1, source_target_pairs={{0,16},{16,0},{1,17},{17,1},{2,18},{18,2},{3,19},{19,3},{4,20},{20... | collective-permute-start | bytes 294920 | tf_op jit(solution)/shard_map/ppermute | solution.py:61
  79.0 14.0 %collective-permute-start.32 = (f32[512,128]{1,0:T(8,128)S(1)}, f32[512,128]{1,0:T(8,128)S(1)}, u32[]{:S(2)}, u32[]{:S(2)}) collective-permute-start(f32[512,128]{1,0:T(8,128)S(1)} %get-tuple-element.43.refs_3_), channel_id=1, source_target_pairs={{0,2},{1,3},{2,0},{3,1},{4,6},{5,7},{6,4},{7,5},{8,10},{9,11},{10,... | collective-permute-start | bytes 786440 | tf_op jit(solution)/shard_map/ppermute | solution.py:61
  80.2 14.8 %collective-permute-start.33 = (f32[512,128]{1,0:T(8,128)S(1)}, f32[512,128]{1,0:T(8,128)S(1)}, u32[]{:S(2)}, u32[]{:S(2)}) collective-permute-start(f32[512,128]{1,0:T(8,128)S(1)} %get-tuple-element.44.refs_4_), channel_id=1, source_target_pairs={{0,3},{1,2},{2,1},{3,0},{4,7},{5,6},{6,5},{7,4},{8,11},{9,10},{10,... | collective-permute-start | bytes 786440 | tf_op jit(solution)/shard_map/ppermute | solution.py:61
  82.0 13.3 %collective-permute-start.41 = (f32[512,128]{1,0:T(8,128)S(1)}, f32[512,128]{1,0:T(8,128)S(1)}, u32[]{:S(2)}, u32[]{:S(2)}) collective-permute-start(f32[512,128]{1,0:T(8,128)S(1)} %get-tuple-element.41.refs_1_.refs_2_), channel_id=1, source_target_pairs={{0,16},{16,0},{1,17},{17,1},{2,18},{18,2},{3,19},{19,3},{4,20},{20... | collective-permute-start | bytes 786440 | tf_op jit(solution)/shard_map/ppermute | solution.py:61
  82.0 3.6 %collective-permute-start.16 = (f32[2,96,128]{2,1,0:T(8,128)S(1)}, f32[2,96,128]{2,1,0:T(8,128)S(1)}, u32[]{:S(2)}, u32[]{:S(2)}) collective-permute-start(f32[2,96,128]{2,1,0:T(8,128)S(1)} %collective-permute-done.12.refs_3_), channel_id=1, source_target_pairs={{0,16},{16,0},{1,17},{17,1},{2,18},{18,2},{3,19},{19,3},{4,20},{20... | collective-permute-start | bytes 294920 | tf_op jit(solution)/shard_map/ppermute | solution.py:61
  82.5 3.8 %collective-permute-start.17 = (f32[2,96,128]{2,1,0:T(8,128)S(1)}, f32[2,96,128]{2,1,0:T(8,128)S(1)}, u32[]{:S(2)}, u32[]{:S(2)}) collective-permute-start(f32[2,96,128]{2,1,0:T(8,128)S(1)} %collective-permute-done.13.refs_4_), channel_id=1, source_target_pairs={{0,16},{16,0},{1,17},{17,1},{2,18},{18,2},{3,19},{19,3},{4,20},{20... | collective-permute-start | bytes 294920 | tf_op jit(solution)/shard_map/ppermute | solution.py:61
  85.6 11.3 %collective-permute-start.35 = (f32[256,128]{1,0:T(8,128)S(1)}, f32[256,128]{1,0:T(8,128)S(1)}, u32[]{:S(2)}, u32[]{:S(2)}) collective-permute-start(f32[256,128]{1,0:T(8,128)S(1)} %get-tuple-element.60), channel_id=1, source_target_pairs={{0,1},{1,0},{2,3},{3,2},{4,5},{5,4},{6,7},{7,6},{8,9},{9,8},{10,11... | collective-permute-start | bytes 393224 | tf_op jit(solution)/shard_map/ppermute | solution.py:61
  86.3 10.6 %collective-permute-start.36 = (f32[256,128]{1,0:T(8,128)S(1)}, f32[256,128]{1,0:T(8,128)S(1)}, u32[]{:S(2)}, u32[]{:S(2)}) collective-permute-start(f32[256,128]{1,0:T(8,128)S(1)} %get-tuple-element.61), channel_id=1, source_target_pairs={{0,2},{1,3},{2,0},{3,1},{4,6},{5,7},{6,4},{7,5},{8,10},{9,11},{10,... | collective-permute-start | bytes 393224 | tf_op jit(solution)/shard_map/ppermute | solution.py:61
  87.7 56.6 %copy-start.1 = (f32[384,768]{1,0:T(8,128)S(1)}, f32[384,768]{1,0:T(8,128)}, u32[]{:S(2)}) copy-start(f32[384,768]{1,0:T(8,128)} %refs_1_.1) | copy-start | bytes 3538948
  93.1 6.5 %collective-permute-start.37 = (f32[256,128]{1,0:T(8,128)S(1)}, f32[256,128]{1,0:T(8,128)S(1)}, u32[]{:S(2)}, u32[]{:S(2)}) collective-permute-start(f32[256,128]{1,0:T(8,128)S(1)} %get-tuple-element.62), channel_id=1, source_target_pairs={{0,3},{1,2},{2,1},{3,0},{4,7},{5,6},{6,5},{7,4},{8,11},{9,10},{10,... | collective-permute-start | bytes 393224 | tf_op jit(solution)/shard_map/ppermute | solution.py:61
  95.1 6.5 %collective-permute-start.53 = (f32[96,512]{1,0:T(8,128)S(1)}, f32[96,512]{1,0:T(8,128)S(1)}, u32[]{:S(2)}, u32[]{:S(2)}) collective-permute-start(f32[96,512]{1,0:T(8,128)S(1)} %factor_slice.1.refs_1_.refs_26_), channel_id=1, source_target_pairs={{0,1},{1,0},{2,3},{3,2},{4,5},{5,4},{6,7},{7,6},{8,9},{9,8},{10,11... | collective-permute-start | bytes 589832 | tf_op jit(solution)/shard_map/ppermute | solution.py:61
  95.3 7.6 %collective-permute-start.54 = (f32[96,512]{1,0:T(8,128)S(1)}, f32[96,512]{1,0:T(8,128)S(1)}, u32[]{:S(2)}, u32[]{:S(2)}) collective-permute-start(f32[96,512]{1,0:T(8,128)S(1)} %factor_slice.1.refs_1_.refs_26_), channel_id=1, source_target_pairs={{0,2},{1,3},{2,0},{3,1},{4,6},{5,7},{6,4},{7,5},{8,10},{9,11},{10,... | collective-permute-start | bytes 589832 | tf_op jit(solution)/shard_map/ppermute | solution.py:61
  96.8 4.2 %collective-permute-start.45 = (f32[256,128]{1,0:T(8,128)S(1)}, f32[256,128]{1,0:T(8,128)S(1)}, u32[]{:S(2)}, u32[]{:S(2)}) collective-permute-start(f32[256,128]{1,0:T(8,128)S(1)} %get-tuple-element.59.refs_6_), channel_id=1, source_target_pairs={{0,16},{16,0},{1,17},{17,1},{2,18},{18,2},{3,19},{19,3},{4,20},{20... | collective-permute-start | bytes 393224 | tf_op jit(solution)/shard_map/ppermute | solution.py:61
  96.8 9.7 %collective-permute-start.42 = (f32[512,128]{1,0:T(8,128)S(1)}, f32[512,128]{1,0:T(8,128)S(1)}, u32[]{:S(2)}, u32[]{:S(2)}) collective-permute-start(f32[512,128]{1,0:T(8,128)S(1)} %collective-permute-done.31.refs_3_), channel_id=1, source_target_pairs={{0,16},{16,0},{1,17},{17,1},{2,18},{18,2},{3,19},{19,3},{4,20},{20... | collective-permute-start | bytes 786440 | tf_op jit(solution)/shard_map/ppermute | solution.py:61
  99.5 6.7 %collective-permute-start.55 = (f32[96,512]{1,0:T(8,128)S(1)}, f32[96,512]{1,0:T(8,128)S(1)}, u32[]{:S(2)}, u32[]{:S(2)}) collective-permute-start(f32[96,512]{1,0:T(8,128)S(1)} %factor_slice.1.refs_1_.refs_26_), channel_id=1, source_target_pairs={{0,3},{1,2},{2,1},{3,0},{4,7},{5,6},{6,5},{7,4},{8,11},{9,10},{10,... | collective-permute-start | bytes 589832 | tf_op jit(solution)/shard_map/ppermute | solution.py:61
  101.0 9.6 %collective-permute-start.21 = (f32[96,512]{1,0:T(8,128)S(1)}, f32[96,512]{1,0:T(8,128)S(1)}, u32[]{:S(2)}, u32[]{:S(2)}) collective-permute-start(f32[96,512]{1,0:T(8,128)S(1)} %factor_slice.1.refs_1_.refs_26_), channel_id=1, source_target_pairs={{0,4},{4,8},{8,12},{12,0},{1,5},{5,9},{9,13},{13,1},{2,6},{6,10},{... | collective-permute-start | bytes 589832 | tf_op jit(solution)/shard_map/ppermute | solution.py:56
  101.6 15.3 %collective-permute-start.39 = (f32[768,128]{1,0:T(8,128)S(1)}, f32[768,128]{1,0:T(8,128)S(1)}, u32[]{:S(2)}, u32[]{:S(2)}) collective-permute-start(f32[768,128]{1,0:T(8,128)S(1)} %get-tuple-element.65), channel_id=1, source_target_pairs={{2,0},{3,1},{6,4},{7,5},{10,8},{11,9},{14,12},{15,13},{18,16},{19,... | collective-permute-start | bytes 1179656 | tf_op jit(solution)/shard_map/ppermute | solution.py:301
  102.9 13.2 %collective-permute-start.22 = (f32[96,512]{1,0:T(8,128)S(1)}, f32[96,512]{1,0:T(8,128)S(1)}, u32[]{:S(2)}, u32[]{:S(2)}) collective-permute-start(f32[96,512]{1,0:T(8,128)S(1)} %factor_slice.1.refs_1_.refs_26_), channel_id=1, source_target_pairs={{0,8},{4,12},{8,0},{12,4},{1,9},{5,13},{9,1},{13,5},{2,10},{6,14},... | collective-permute-start | bytes 589832 | tf_op jit(solution)/shard_map/ppermute | solution.py:56
  106.2 10.7 %collective-permute-start.23 = (f32[96,512]{1,0:T(8,128)S(1)}, f32[96,512]{1,0:T(8,128)S(1)}, u32[]{:S(2)}, u32[]{:S(2)}) collective-permute-start(f32[96,512]{1,0:T(8,128)S(1)} %factor_slice.1.refs_1_.refs_26_), channel_id=1, source_target_pairs={{0,12},{4,0},{8,4},{12,8},{1,13},{5,1},{9,5},{13,9},{2,14},{6,2},{... | collective-permute-start | bytes 589832 | tf_op jit(solution)/shard_map/ppermute | solution.py:56
  106.5 17.0 %collective-permute-start.43 = (f32[512,128]{1,0:T(8,128)S(1)}, f32[512,128]{1,0:T(8,128)S(1)}, u32[]{:S(2)}, u32[]{:S(2)}) collective-permute-start(f32[512,128]{1,0:T(8,128)S(1)} %collective-permute-done.32.refs_4_), channel_id=1, source_target_pairs={{0,16},{16,0},{1,17},{17,1},{2,18},{18,2},{3,19},{19,3},{4,20},{20... | collective-permute-start | bytes 786440 | tf_op jit(solution)/shard_map/ppermute | solution.py:61
  110.7 13.0 %collective-permute-start.44 = (f32[512,128]{1,0:T(8,128)S(1)}, f32[512,128]{1,0:T(8,128)S(1)}, u32[]{:S(2)}, u32[]{:S(2)}) collective-permute-start(f32[512,128]{1,0:T(8,128)S(1)} %collective-permute-done.33.refs_5_), channel_id=1, source_target_pairs={{0,16},{16,0},{1,17},{17,1},{2,18},{18,2},{3,19},{19,3},{4,20},{20... | collective-permute-start | bytes 786440 | tf_op jit(solution)/shard_map/ppermute | solution.py:61
  116.1 9.9 %collective-permute-start.38 = (f32[768,128]{1,0:T(8,128)S(1)}, f32[768,128]{1,0:T(8,128)S(1)}, u32[]{:S(2)}, u32[]{:S(2)}) collective-permute-start(f32[768,128]{1,0:T(8,128)S(1)} %get-tuple-element.64), channel_id=1, source_target_pairs={{2,3},{3,2},{6,7},{7,6},{10,11},{11,10},{14,15},{15,14},{18,19},{1... | collective-permute-start | bytes 1179656 | tf_op jit(solution)/shard_map/ppermute | solution.py:301
  116.8 7.1 %collective-permute-start.46 = (f32[256,128]{1,0:T(8,128)S(1)}, f32[256,128]{1,0:T(8,128)S(1)}, u32[]{:S(2)}, u32[]{:S(2)}) collective-permute-start(f32[256,128]{1,0:T(8,128)S(1)} %collective-permute-done.35.refs_7_), channel_id=1, source_target_pairs={{0,16},{16,0},{1,17},{17,1},{2,18},{18,2},{3,19},{19,3},{4,20},{20... | collective-permute-start | bytes 393224 | tf_op jit(solution)/shard_map/ppermute | solution.py:61
  116.9 18.2 %collective-permute-start.40 = (f32[768,128]{1,0:T(8,128)S(1)}, f32[768,128]{1,0:T(8,128)S(1)}, u32[]{:S(2)}, u32[]{:S(2)}) collective-permute-start(f32[768,128]{1,0:T(8,128)S(1)} %collective-permute-done.39.refs_12_), channel_id=1, source_target_pairs={{0,1},{4,5},{8,9},{12,13},{16,17},{20,21},{24,25},{28,29}} | collective-permute-start | bytes 1179656 | tf_op jit(solution)/shard_map/ppermute | solution.py:304
  123.5 11.5 %collective-permute-start.24 = (f32[96,512]{1,0:T(8,128)S(1)}, f32[96,512]{1,0:T(8,128)S(1)}, u32[]{:S(2)}, u32[]{:S(2)}) collective-permute-start(f32[96,512]{1,0:T(8,128)S(1)} %get-tuple-element.55), channel_id=1, source_target_pairs={{0,1},{1,0},{2,3},{3,2},{4,5},{5,4},{6,7},{7,6},{8,9},{9,8},{10,11... | collective-permute-start | bytes 589832 | tf_op jit(solution)/shard_map/ppermute | solution.py:61
  123.6 1.4 collective-permute-start.47
  123.9 2.1 %collective-permute-start.48 = (f32[256,128]{1,0:T(8,128)S(1)}, f32[256,128]{1,0:T(8,128)S(1)}, u32[]{:S(2)}, u32[]{:S(2)}) collective-permute-start(f32[256,128]{1,0:T(8,128)S(1)} %collective-permute-done.37.refs_9_), channel_id=1, source_target_pairs={{0,16},{16,0},{1,17},{17,1},{2,18},{18,2},{3,19},{19,3},{4,20},{20... | collective-permute-start | bytes 393224 | tf_op jit(solution)/shard_map/ppermute | solution.py:61
  125.1 10.0 %collective-permute-start.25 = (f32[96,512]{1,0:T(8,128)S(1)}, f32[96,512]{1,0:T(8,128)S(1)}, u32[]{:S(2)}, u32[]{:S(2)}) collective-permute-start(f32[96,512]{1,0:T(8,128)S(1)} %get-tuple-element.56), channel_id=1, source_target_pairs={{0,2},{1,3},{2,0},{3,1},{4,6},{5,7},{6,4},{7,5},{8,10},{9,11},{10,... | collective-permute-start | bytes 589832 | tf_op jit(solution)/shard_map/ppermute | solution.py:61
  126.0 17.2 %collective-permute-start.49 = (f32[768,128]{1,0:T(8,128)S(1)}, f32[768,128]{1,0:T(8,128)S(1)}, u32[]{:S(2)}, u32[]{:S(2)}) collective-permute-start(f32[768,128]{1,0:T(8,128)S(1)} %get-tuple-element.63.refs_10_), channel_id=1, source_target_pairs={{0,16},{16,0},{1,17},{17,1},{2,18},{18,2},{3,19},{19,3},{4,20},{20... | collective-permute-start | bytes 1179656 | tf_op jit(solution)/shard_map/ppermute | solution.py:61
  126.0 17.7 %collective-permute-start.50 = (f32[768,128]{1,0:T(8,128)S(1)}, f32[768,128]{1,0:T(8,128)S(1)}, u32[]{:S(2)}, u32[]{:S(2)}) collective-permute-start(f32[768,128]{1,0:T(8,128)S(1)} %collective-permute-done.38.refs_11_), channel_id=1, source_target_pairs={{0,16},{16,0},{1,17},{17,1},{2,18},{18,2},{3,19},{19,3},{4,20},{20... | collective-permute-start | bytes 1179656 | tf_op jit(solution)/shard_map/ppermute | solution.py:61
  135.0 8.8 %collective-permute-start.51 = (f32[768,128]{1,0:T(8,128)S(1)}, f32[768,128]{1,0:T(8,128)S(1)}, u32[]{:S(2)}, u32[]{:S(2)}) collective-permute-start(f32[768,128]{1,0:T(8,128)S(1)} %collective-permute-done.39.refs_12_), channel_id=1, source_target_pairs={{0,16},{16,0},{1,17},{17,1},{2,18},{18,2},{3,19},{19,3},{4,20},{20... | collective-permute-start | bytes 1179656 | tf_op jit(solution)/shard_map/ppermute | solution.py:61
  135.0 8.2 %collective-permute-start.26 = (f32[96,512]{1,0:T(8,128)S(1)}, f32[96,512]{1,0:T(8,128)S(1)}, u32[]{:S(2)}, u32[]{:S(2)}) collective-permute-start(f32[96,512]{1,0:T(8,128)S(1)} %get-tuple-element.57), channel_id=1, source_target_pairs={{0,3},{1,2},{2,1},{3,0},{4,7},{5,6},{6,5},{7,4},{8,11},{9,10},{10,... | collective-permute-start | bytes 589832 | tf_op jit(solution)/shard_map/ppermute | solution.py:61
  135.0 9.2 %collective-permute-start.52 = (f32[768,128]{1,0:T(8,128)S(1)}, f32[768,128]{1,0:T(8,128)S(1)}, u32[]{:S(2)}, u32[]{:S(2)}) collective-permute-start(f32[768,128]{1,0:T(8,128)S(1)} %collective-permute-done.40.refs_13_), channel_id=1, source_target_pairs={{0,16},{16,0},{1,17},{17,1},{2,18},{18,2},{3,19},{19,3},{4,20},{20... | collective-permute-start | bytes 1179656 | tf_op jit(solution)/shard_map/ppermute | solution.py:61
  143.2 6.0 %collective-permute-start.27 = (f32[96,512]{1,0:T(8,128)S(1)}, f32[96,512]{1,0:T(8,128)S(1)}, u32[]{:S(2)}, u32[]{:S(2)}) collective-permute-start(f32[96,512]{1,0:T(8,128)S(1)} %get-tuple-element.54.refs_1_), channel_id=1, source_target_pairs={{0,16},{16,0},{1,17},{17,1},{2,18},{18,2},{3,19},{19,3},{4,20},{20... | collective-permute-start | bytes 589832 | tf_op jit(solution)/shard_map/ppermute | solution.py:61
  143.3 6.0 %collective-permute-start.28 = (f32[96,512]{1,0:T(8,128)S(1)}, f32[96,512]{1,0:T(8,128)S(1)}, u32[]{:S(2)}, u32[]{:S(2)}) collective-permute-start(f32[96,512]{1,0:T(8,128)S(1)} %collective-permute-done.24.refs_2_), channel_id=1, source_target_pairs={{0,16},{16,0},{1,17},{17,1},{2,18},{18,2},{3,19},{19,3},{4,20},{20... | collective-permute-start | bytes 589832 | tf_op jit(solution)/shard_map/ppermute | solution.py:61
  143.8 5.5 %collective-permute-start.29 = (f32[96,512]{1,0:T(8,128)S(1)}, f32[96,512]{1,0:T(8,128)S(1)}, u32[]{:S(2)}, u32[]{:S(2)}) collective-permute-start(f32[96,512]{1,0:T(8,128)S(1)} %collective-permute-done.25.refs_3_), channel_id=1, source_target_pairs={{0,16},{16,0},{1,17},{17,1},{2,18},{18,2},{3,19},{19,3},{4,20},{20... | collective-permute-start | bytes 589832 | tf_op jit(solution)/shard_map/ppermute | solution.py:61
  143.8 5.4 %collective-permute-start.30 = (f32[96,512]{1,0:T(8,128)S(1)}, f32[96,512]{1,0:T(8,128)S(1)}, u32[]{:S(2)}, u32[]{:S(2)}) collective-permute-start(f32[96,512]{1,0:T(8,128)S(1)} %collective-permute-done.26.refs_4_), channel_id=1, source_target_pairs={{0,16},{16,0},{1,17},{17,1},{2,18},{18,2},{3,19},{19,3},{4,20},{20... | collective-permute-start | bytes 589832 | tf_op jit(solution)/shard_map/ppermute | solution.py:61

commit v6 on v5

--- a/solution.py
+++ b/solution.py
@@ -201,7 +201,8 @@
         around_refs = refs[1 + count : 1 + count + many]
         front_refs = refs[1 + count + many : 1 + 2 * count + many]
         outs = refs[1 + 2 * count + many :][:count]
-        edge, up, row_buf, col_buf, sems = refs[1 + 3 * count + many :]
+        sides = refs[1 + 3 * count + many :][:count]
+        edge, up, row_buf, col_buf, sems = refs[1 + 4 * count + many :]
         places = [col_buf.at[m * sub : (m + 1) * sub] for m in range(count)]
         rows_in = gather_copies(sc, row_refs, row_buf, sems, sub)
         for copy in rows_in:
@@ -227,11 +228,17 @@
             def _():
                 up[group - 1] = part[-EDGE:]
 
+            for mask, side in enumerate(sides):
+
+                @pl.when(group == jnp.maximum((sc[COL] ^ mask) - 1, 0))
+                def _():
+                    side[...] = part
+
     return pl.pallas_call(
         body,
         in_specs=[SMEM] + [ANY] * (count + many) + [VMEM] * count,
-        out_specs=[VMEM] * (count + 2),
-        out_shape=[f32(size, sub)] * count + [f32(EDGE, sub), f32(count - 1, EDGE, sub)],
+        out_specs=[VMEM] * (2 * count + 2),
+        out_shape=[f32(size, sub)] * (2 * count) + [f32(EDGE, sub), f32(count - 1, EDGE, sub)],
         scratch_shapes=[
             pltpu.VMEM((size, depth), jnp.float32),
             pltpu.VMEM((size, depth), jnp.float32),
@@ -242,50 +249,40 @@
     )(table, *rows, *around, *fronts)
 
 
-def pack_halo(table, homes, edge, up):
-    count = len(homes)
-    size, sub = homes[0].shape
-
-    def body(*refs):
-        sc = refs[0]
-        home_refs = refs[1 : 1 + count]
-        edge_ref, up_ref = refs[1 + count : 3 + count]
-        above_outs = refs[3 + count : 3 + 2 * count]
-        side_outs = refs[3 + 2 * count : 3 + 3 * count]
-        sems = refs[-1]
+def pack_halo(table, edge, up):
+    count = up.shape[0] + 1
+    sub = edge.shape[1]
+
+    def body(sc, edge_ref, up_ref, *refs):
+        outs, sems = refs[:count], refs[count]
+        places = [[out.at[pl.ds(i * EDGE, EDGE)] for i in range(2)] for out in outs]
         for m in range(count):
             group = sc[COL] ^ m
-            before = jnp.maximum(group - 1, 0)
-            main, tail = side_outs[m].at[pl.ds(0, size)], side_outs[m].at[pl.ds(size, EDGE)]
-            start_chosen(before ^ sc[COL], home_refs, main, sems.at[3 * m])
-            for i, (wanted, place) in enumerate(((group, above_outs[m]), (before, tail))):
+            for i, wanted in enumerate((group, jnp.maximum(group - 1, 0))):
 
                 @pl.when(wanted == 0)
                 def _():
-                    pltpu.make_async_copy(edge_ref, place, sems.at[3 * m + 1 + i]).start()
+                    pltpu.make_async_copy(edge_ref, places[m][i], sems.at[2 * m + i]).start()
 
                 @pl.when(wanted > 0)
                 def _():
                     pltpu.make_async_copy(
-                        up_ref.at[jnp.maximum(wanted - 1, 0)], place, sems.at[3 * m + 1 + i]
+                        up_ref.at[jnp.maximum(wanted - 1, 0)], places[m][i], sems.at[2 * m + i]
                     ).start()
 
         for m in range(count):
-            main, tail = side_outs[m].at[pl.ds(0, size)], side_outs[m].at[pl.ds(size, EDGE)]
-            pltpu.make_async_copy(home_refs[0], main, sems.at[3 * m]).wait()
-            pltpu.make_async_copy(edge_ref, above_outs[m], sems.at[3 * m + 1]).wait()
-            pltpu.make_async_copy(edge_ref, tail, sems.at[3 * m + 2]).wait()
-
-    outs = pl.pallas_call(
-        body,
-        in_specs=[SMEM] + [ANY] * (count + 2),
-        out_specs=[VMEM] * (2 * count),
-        out_shape=[f32(EDGE, sub)] * count + [f32(size + EDGE, sub)] * count,
-        scratch_shapes=[pltpu.SemaphoreType.DMA((3 * count,))],
+            for i in range(2):
+                pltpu.make_async_copy(edge_ref, places[m][i], sems.at[2 * m + i]).wait()
+
+    return pl.pallas_call(
+        body,
+        in_specs=[SMEM] + [ANY] * 2,
+        out_specs=[VMEM] * count,
+        out_shape=[f32(2 * EDGE, sub)] * count,
+        scratch_shapes=[pltpu.SemaphoreType.DMA((2 * count,))],
         compiler_params=limit_for(sub, 8),
         name="pack_halo",
-    )(table, *homes, edge, up)
-    return outs[:count], outs[count:]
+    )(table, edge, up)
 
 
 def to_next_group(packed):
@@ -425,10 +422,33 @@
     )(table, *small, *small_other, *dealt, pivot_inverse)
 
 
-def assemble(table, parent, own, other, row_pieces):
-    count = len(row_pieces)
+def lay_rows(table, pieces):
+    count = len(pieces)
+    piece_rows, width = pieces[0].shape
+    rows = count * piece_rows
+
+    def body(*refs):
+        sc = refs[0]
+        ins = refs[1 : 1 + count]
+        out, high, low, sems = refs[1 + count :]
+        run_copies(gather_copies(sc, ins, out, sems, piece_rows))
+        high[...], low[...] = halves(out[...])
+
+    part = jax.ShapeDtypeStruct((rows, width), jnp.bfloat16)
+    return pl.pallas_call(
+        body,
+        in_specs=[SMEM] + [ANY] * count,
+        out_specs=[VMEM] * 3,
+        out_shape=[f32(rows, width), part, part],
+        scratch_shapes=[pltpu.SemaphoreType.DMA((count,))],
+        compiler_params=limit_for(BLK, 8),
+        name="lay_rows",
+    )(table, *pieces)
+
+
+def assemble(table, parent, own, other, row_factor):
+    count = len(own) // 3
     rows, width = parent.shape
-    piece_rows = row_pieces[0].shape[0]
     size, sub = own[0].shape
     half = count // 2
     split = BLK // sub
@@ -436,30 +456,28 @@
     def body(*refs):
         sc, parent_ref = refs[:2]
         own_refs, other_refs = refs[2 : 2 + 3 * count], refs[2 + 3 * count : 2 + 6 * count]
-        row_refs = refs[2 + 6 * count : 2 + 7 * count]
-        out, high_out, low_out, own_win, other_win, row_factor, sems = refs[2 + 7 * count :]
+        factor_ref, out, own_win, other_win, sems = refs[2 + 6 * count :]
         low, high = pl.ds(0, EDGE), pl.ds(EDGE, size)
-        always = gather_copies(sc, row_refs, row_factor, sems, piece_rows)
-        at = count
-        edges = []
+        always, edges = [], []
+        at = 0
         for refs_in, window in ((own_refs, own_win), (other_refs, other_win)):
             for m in range(count):
-                home, above, packed = (refs_in[i * count + m] for i in range(3))
+                home, above, before = (refs_in[i * count + m] for i in range(3))
                 piece = sc[COL] ^ m
                 main = half + piece
                 side = jnp.maximum(piece - half, 0)
                 always += [
                     pltpu.make_async_copy(home, window.at[main, high], sems.at[at]),
-                    pltpu.make_async_copy(above, window.at[main, low], sems.at[at + 1]),
+                    pltpu.make_async_copy(
+                        above.at[low], window.at[main, low], sems.at[at + 1]
+                    ),
                 ]
                 edges += [
                     (
                         piece,
+                        pltpu.make_async_copy(before, window.at[side, high], sems.at[at + 2]),
                         pltpu.make_async_copy(
-                            packed.at[pl.ds(0, size)], window.at[side, high], sems.at[at + 2]
-                        ),
-                        pltpu.make_async_copy(
-                            packed.at[pl.ds(size, EDGE)], window.at[side, low], sems.at[at + 3]
+                            above.at[pl.ds(EDGE, EDGE)], window.at[side, low], sems.at[at + 3]
                         ),
                     )
                 ]
@@ -473,10 +491,7 @@
                 first.start()
                 second.start()
 
-        for copy in always[:count]:
-            copy.wait()
-        high_out[...], low_out[...] = halves(row_factor[...])
-        for copy in always[count:]:
+        for copy in always:
             copy.wait()
         for piece, first, second in edges:
 
@@ -503,24 +518,22 @@
                     block = pieces[0] if split == 1 else jnp.concatenate(pieces, axis=1)
                     total += jnp.where((down >= 0) & (across >= 0), block, 0.0)
                 if q < PIV:
-                    total = jnp.where(sc[COL] == 0, row_factor[lines, cols], total)
+                    total = jnp.where(sc[COL] == 0, factor_ref[lines, cols], total)
                 out[lines, cols] = total
 
-    part = jax.ShapeDtypeStruct((rows, PANEL), jnp.bfloat16)
-    return pl.pallas_call(
-        body,
-        in_specs=[SMEM, VMEM] + [ANY] * (7 * count),
-        out_specs=[VMEM] * 3,
-        out_shape=[f32(rows, width), part, part],
+    return pl.pallas_call(
+        body,
+        in_specs=[SMEM, VMEM] + [ANY] * (6 * count) + [VMEM],
+        out_specs=VMEM,
+        out_shape=f32(rows, width),
         scratch_shapes=[
             pltpu.VMEM((half + count, size + EDGE, sub), jnp.float32),
             pltpu.VMEM((half + count, size + EDGE, sub), jnp.float32),
-            pltpu.VMEM((rows, PANEL), jnp.float32),
-            pltpu.SemaphoreType.DMA((9 * count,)),
+            pltpu.SemaphoreType.DMA((8 * count,)),
         ],
         compiler_params=limit_for(sub, 14),
         name="assemble",
-    )(table, parent, *own, *other, *row_pieces)
+    )(table, parent, *own, *other, row_factor)
 
 
 def finish(table, assembled, row_high, row_low, col_own, col_other):
@@ -603,7 +616,8 @@
         value = deals[j]
         dealt.append(lax.ppermute(value, "col", [(0, j)]) if j else value)
 
-    *homes, edge, up = slice_products(table, rows, around, fronts)
+    *slices, edge, up = slice_products(table, rows, around, fronts)
+    homes, sides = slices[:count], slices[count:]
     edge = shifted(edge, "row")
     up = shifted(up, "row")
     own = [homes[0]] + over_col(homes[1:])
@@ -611,18 +625,20 @@
     small = place_rows(table, homes, edge, deal)
     small = [small[0]] + over_col(small[1:])
     small_other = [to_sibling(value) for value in small]
-    above, packed = pack_halo(table, homes, edge, up)
-    own = own + [above[0]] + over_col(above[1:]) + to_next_group(packed)
+    above = pack_halo(table, edge, up)
+    own = own + [above[0]] + over_col(above[1:]) + to_next_group(sides)
     factor = factor_slice(table, small, small_other, dealt, pivot_inverse)
     factors = over_row(factor)
     row_pieces = [factor] + over_col([factor] * (count - 1))
 
+    row_factor, high, low = lay_rows(table, row_pieces)
+
     picked = pick_for_cols(table, factors, range(count))
     col_own = [picked[0]] + over_col(picked[1:])
     col_other = [to_sibling(value) for value in col_own]
 
     other = [to_sibling(value) for value in own]
-    assembled, high, low = assemble(table, parent_front, own, other, row_pieces)
+    assembled = assemble(table, parent_front, own, other, row_factor)
     return finish(table, assembled, high, low, col_own, col_other)
 
 

time: 155 us -> 161 us (1.039)
  starting transfers between devices: 59 us -> 70.6 us
  waiting for transfers between devices: 68.5 us -> 61.8 us
    ppermute x41, starting transfers between devices: 29.2 us -> 38.2 us  [swapped(): return lax.ppermute(value, axis, [(i, i ^ mask) for i in range(count)])]
    ppermute x41, waiting for transfers between devices: 55 us -> 49.2 us  [swapped(): return lax.ppermute(value, axis, [(i, i ^ mask) for i in range(count)])]
    ppermute x2, starting transfers between devices: 3.39 us -> 6.77 us  [shifted(): return lax.ppermute(value, axis, [(i, i + 1) for i in range(count - 1)])]
    ppermute x1, waiting for transfers between devices: 3.57 us -> 0.95 us  [around_row(): far.append(lax.ppermute(middle, 'row', pairs))]
    ppermute x2, waiting for transfers between devices: 0.01 us -> 2.5 us  [shifted(): return lax.ppermute(value, axis, [(i, i + 1) for i in range(count - 1)])]
    ppermute x4, starting transfers between devices: 6.03 us -> 7.95 us  [rotated(): lax.ppermute(value, axis, [(i, (i + steps) % count) for i in range(count)])]
    ppermute x4, waiting for transfers between devices: 9.63 us -> 7.74 us  [rotated(): lax.ppermute(value, axis, [(i, (i + steps) % count) for i in range(count)])]
    pallas_call x2 -> x3, Pallas kernels: 7.91 us -> 7.48 us  [the longest x1 3.69 us: assemble(): pl.pallas_call(body, in_specs=[SMEM, VMEM] + [ANY] * (6 * count) + [VMEM]...]
  transfers between devices with their start and end apart: 56 -> 56, of which waited for: 17 -> 15; matrix products, arithmetic and copies ran while one was open for 0% -> 0% of each run, Pallas kernels for 12% -> 12%
where the time goes in v6:
time: 161 us; the launch traced here: 160 us
  starting transfers between devices  70.6 us (44%)
  waiting for transfers between devices  61.8 us (38%)
  Pallas kernels  23.7 us (15%)
  local copies, waits for them, and re-layouts  3.18 us (2%)
    ppermute x41, waiting for transfers between devices, swapped(): return lax.ppermute(value, axis, [(i, i ^ mask) for i in range(count)])  49.2 us
    ppermute x41, starting transfers between devices, swapped(): return lax.ppermute(value, axis, [(i, i ^ mask) for i in range(count)])  38.2 us
    ppermute x4, starting transfers between devices, rotated(): lax.ppermute(value, axis, [(i, (i + steps) % count) for i in range(count)])  7.95 us
    ppermute x4, waiting for transfers between devices, rotated(): lax.ppermute(value, axis, [(i, (i + steps) % count) for i in range(count)])  7.74 us
    ppermute x2, starting transfers between devices, shifted(): return lax.ppermute(value, axis, [(i, i + 1) for i in range(count - 1)])  6.77 us
    ppermute x3, starting transfers between devices, shards(): dealt.append(lax.ppermute(value, 'col', [(0, j)]) if j else value)  6 us
    pallas_call x1, Pallas kernels, finish(): pl.pallas_call(body, in_specs=[SMEM] + [ANY] * (2 * count) + [VMEM] * 3,...  5.12 us
    pallas_call x1, Pallas kernels, slice_products(): pl.pallas_call(body, in_specs=[SMEM] + [ANY] * (count + many) + [VMEM] *...  4.33 us
  transfers between devices with their start and end apart: 56, of which 15 were waited for; matrix products, arithmetic and copies ran while one was open for 0% of the time, Pallas kernels for 12%

profile of v6, /device:TPU:0, one launch (start us, length us, event | category | flops | bytes accessed | tf_op | source)
XLA Modules:
  0.0 159.7 jit_solution(4551091584283218744)
XLA Ops:
  0.0 4.1 %collective-permute-start.4 = (f32[128,1024]{1,0:T(8,128)}, f32[128,1024]{1,0:T(8,128)S(1)}, u32[]{:S(2)}, u32[]{:S(2)}) collective-permute-start(f32[128,1024]{1,0:T(8,128)} %bitcast.2), channel_id=1, source_target_pairs={{0,8},{4,12},{8,0},{12,4},{1,9},{5,13},{9,1},{13,5},{2,10},{6,14},... | collective-permute-start | bytes 1572872 | tf_op jit(solution)/shard_map/ppermute | solution.py:56
  4.1 1.5 collective-permute-start
  5.6 0.7 copy-done.5
  6.2 1.3 lookup_table.1.sc.refs_0_
  7.6 1.3 copy-done
  8.9 1.2 copy-done.4
  10.1 0.9 cut_slices.1
  10.9 0.6 collective-permute-start.7
  11.5 1.5 collective-permute-start.8
  13.1 1.4 collective-permute-start.9
  14.5 10.2 %collective-permute-done.7.refs_11_ = f32[512,128]{1,0:T(8,128)S(1)} collective-permute-done((f32[512,128]{1,0:T(8,128)S(1)}, f32[512,128]{1,0:T(8,128)S(1)}, u32[]{:S(2)}, u32[]{:S(2)}) %collective-permute-start.7) | collective-permute-done | bytes 262176 | tf_op jit(solution)/shard_map/ppermute | solution.py:61
  24.7 1.5 collective-permute-start.1
  26.2 1.4 collective-permute-start.2
  27.6 3.7 %collective-permute-done.9.refs_13_ = f32[512,128]{1,0:T(8,128)S(1)} collective-permute-done((f32[512,128]{1,0:T(8,128)S(1)}, f32[512,128]{1,0:T(8,128)S(1)}, u32[]{:S(2)}, u32[]{:S(2)}) %collective-permute-start.9) | collective-permute-done | bytes 262176 | tf_op jit(solution)/shard_map/ppermute | solution.py:61
  31.4 3.5 %collective-permute-start.3 = (f32[128,1024]{1,0:T(8,128)S(1)}, f32[128,1024]{1,0:T(8,128)S(1)}, u32[]{:S(2)}, u32[]{:S(2)}) collective-permute-start(f32[128,1024]{1,0:T(8,128)S(1)} %bitcast.6), channel_id=1, source_target_pairs={{0,4},{4,8},{8,12},{1,5},{5,9},{9,13},{2,6},{6,10},{10,14},{3,7},{... | collective-permute-start | bytes 1572872 | tf_op jit(solution)/shard_map/ppermute | solution.py:184
  34.9 1.3 collective-permute-start.6
  36.2 1.3 collective-permute-start.5
  37.5 14.3 %collective-permute-done.1.refs_3_ = f32[128,1024]{1,0:T(8,128)S(1)} collective-permute-done((f32[128,1024]{1,0:T(8,128)S(1)}, f32[128,1024]{1,0:T(8,128)S(1)}, u32[]{:S(2)}, u32[]{:S(2)}) %collective-permute-start.1) | collective-permute-done | bytes 524320 | tf_op jit(solution)/shard_map/ppermute | solution.py:61
  51.8 3.4 %collective-permute-start.18 = (f32[96,512]{1,0:T(8,128)S(1)}, f32[96,512]{1,0:T(8,128)S(1)}, u32[]{:S(2)}, u32[]{:S(2)}) collective-permute-start(f32[96,512]{1,0:T(8,128)S(1)} %get-tuple-element.51), channel_id=1, source_target_pairs={{0,1},{4,5},{8,9},{12,13},{16,17},{20,21},{24,25},{28,29}} | collective-permute-start | bytes 589832 | tf_op jit(solution)/shard_map/ppermute | solution.py:617
  55.2 1.3 collective-permute-start.19
  56.5 1.3 collective-permute-start.20
  57.8 1.0 collective-permute-done.5.refs_8_
  58.8 4.3 %slice_products.1 = (f32[512,128]{1,0:T(8,128)S(1)}, f32[512,128]{1,0:T(8,128)S(1)}, f32[512,128]{1,0:T(8,128)S(1)}, f32[512,128]{1,0:T(8,128)S(1)}, f32[512,128...) custom-call(s32[35]{0:T(128)S(1)} %lookup_table.1.sc.refs_0_, ...), custom_call_target="tpu_custom_call" | custom-call | tf_op jit(solution)/shard_map/slice_products/pallas_call | solution.py:237
  63.1 2.7 %collective-permute-start.10 = (f32[256,128]{1,0:T(8,128)S(1)}, f32[256,128]{1,0:T(8,128)S(1)}, u32[]{:S(2)}, u32[]{:S(2)}) collective-permute-start(f32[256,128]{1,0:T(8,128)S(1)} %get-tuple-element.45), channel_id=1, source_target_pairs={{0,4},{4,8},{8,12},{1,5},{5,9},{9,13},{2,6},{6,10},{10,14},{3,7},{... | collective-permute-start | bytes 393224 | tf_op jit(solution)/shard_map/ppermute | solution.py:66
  65.8 2.5 %collective-permute-done.10.refs_5_.edge_ref = f32[256,128]{1,0:T(8,128)S(1)} collective-permute-done((f32[256,128]{1,0:T(8,128)S(1)}, f32[256,128]{1,0:T(8,128)S(1)}, u32[]{:S(2)}, u32[]{:S(2)}) %collective-permute-start.10) | collective-permute-done | bytes 131104 | tf_op jit(solution)/shard_map/ppermute | solution.py:66
  68.3 0.8 place_rows.1
  69.2 0.5 collective-permute-start.11
  69.6 1.3 collective-permute-start.39
  70.9 1.7 %collective-permute-start.31 = (f32[512,128]{1,0:T(8,128)S(1)}, f32[512,128]{1,0:T(8,128)S(1)}, u32[]{:S(2)}, u32[]{:S(2)}) collective-permute-start(f32[512,128]{1,0:T(8,128)S(1)} %get-tuple-element.42.refs_2_), channel_id=1, source_target_pairs={{0,1},{1,0},{2,3},{3,2},{4,5},{5,4},{6,7},{7,6},{8,9},{9,8},{10,11... | collective-permute-start | bytes 786440 | tf_op jit(solution)/shard_map/ppermute | solution.py:61
  72.6 2.7 %collective-permute-start.12 = (f32[2,96,128]{2,1,0:T(8,128)S(1)}, f32[2,96,128]{2,1,0:T(8,128)S(1)}, u32[]{:S(2)}, u32[]{:S(2)}) collective-permute-start(f32[2,96,128]{2,1,0:T(8,128)S(1)} %get-tuple-element.48), channel_id=1, source_target_pairs={{0,2},{1,3},{2,0},{3,1},{4,6},{5,7},{6,4},{7,5},{8,10},{9,11},{10,... | collective-permute-start | bytes 294920 | tf_op jit(solution)/shard_map/ppermute | solution.py:61
  75.4 1.8 %collective-permute-start.13 = (f32[2,96,128]{2,1,0:T(8,128)S(1)}, f32[2,96,128]{2,1,0:T(8,128)S(1)}, u32[]{:S(2)}, u32[]{:S(2)}) collective-permute-start(f32[2,96,128]{2,1,0:T(8,128)S(1)} %get-tuple-element.49), channel_id=1, source_target_pairs={{0,3},{1,2},{2,1},{3,0},{4,7},{5,6},{6,5},{7,4},{8,11},{9,10},{10,... | collective-permute-start | bytes 294920 | tf_op jit(solution)/shard_map/ppermute | solution.py:61
  77.2 7.6 %collective-permute-done.12.refs_3_ = f32[2,96,128]{2,1,0:T(8,128)S(1)} collective-permute-done((f32[2,96,128]{2,1,0:T(8,128)S(1)}, f32[2,96,128]{2,1,0:T(8,128)S(1)}, u32[]{:S(2)}, u32[]{:S(2)}) %collective-permute-start.12) | collective-permute-done | bytes 98336 | tf_op jit(solution)/shard_map/ppermute | solution.py:61
  84.7 0.5 collective-permute-start.15
  85.2 0.8 collective-permute-done.14.refs_5_
  86.0 0.7 collective-permute-start.33
  86.7 4.1 %collective-permute-start.34 = (f32[3,256,128]{2,1,0:T(8,128)S(1)}, f32[3,256,128]{2,1,0:T(8,128)S(1)}, u32[]{:S(2)}, u32[]{:S(2)}) collective-permute-start(f32[3,256,128]{2,1,0:T(8,128)S(1)} %get-tuple-element.58), channel_id=1, source_target_pairs={{0,4},{4,8},{8,12},{1,5},{5,9},{9,13},{2,6},{6,10},{10,14},{3,7},{... | collective-permute-start | bytes 1179656 | tf_op jit(solution)/shard_map/ppermute | solution.py:66
  91.4 0.8 collective-permute-done.16.refs_7_
  92.2 0.7 collective-permute-start.38
  93.2 2.1 %factor_slice.1.refs_1_ = f32[96,512]{1,0:T(8,128)S(1)} custom-call(s32[35]{0:T(128)S(1)} %lookup_table.1.sc.refs_0_, f32[2,96,128]{2,1,0:T(8,128)S(1)} %get-tuple-element.46.refs_1_, f32[2,96,128]{2,1,0:T(8,128)S(1)} %collective-permute-done.11.refs_2_, f32[2,96,128]{2,1,0:T(8,128)S(1)} %collective-permute-done.12.refs_3_, ...), custom_call_target="tpu_custom_call" | custom-call | tf_op jit(solution)/shard_map/factor_slice/pallas_call | solution.py:409
  95.3 1.7 %collective-permute-start.53 = (f32[96,512]{1,0:T(8,128)S(1)}, f32[96,512]{1,0:T(8,128)S(1)}, u32[]{:S(2)}, u32[]{:S(2)}) collective-permute-start(f32[96,512]{1,0:T(8,128)S(1)} %factor_slice.1.refs_1_), channel_id=1, source_target_pairs={{0,1},{1,0},{2,3},{3,2},{4,5},{5,4},{6,7},{7,6},{8,9},{9,8},{10,11... | collective-permute-start | bytes 589832 | tf_op jit(solution)/shard_map/ppermute | solution.py:61
  97.0 3.9 %collective-permute-start.54 = (f32[96,512]{1,0:T(8,128)S(1)}, f32[96,512]{1,0:T(8,128)S(1)}, u32[]{:S(2)}, u32[]{:S(2)}) collective-permute-start(f32[96,512]{1,0:T(8,128)S(1)} %factor_slice.1.refs_1_), channel_id=1, source_target_pairs={{0,2},{1,3},{2,0},{3,1},{4,6},{5,7},{6,4},{7,5},{8,10},{9,11},{10,... | collective-permute-start | bytes 589832 | tf_op jit(solution)/shard_map/ppermute | solution.py:61
  100.9 4.6 %collective-permute-start.55 = (f32[96,512]{1,0:T(8,128)S(1)}, f32[96,512]{1,0:T(8,128)S(1)}, u32[]{:S(2)}, u32[]{:S(2)}) collective-permute-start(f32[96,512]{1,0:T(8,128)S(1)} %factor_slice.1.refs_1_), channel_id=1, source_target_pairs={{0,3},{1,2},{2,1},{3,0},{4,7},{5,6},{6,5},{7,4},{8,11},{9,10},{10,... | collective-permute-start | bytes 589832 | tf_op jit(solution)/shard_map/ppermute | solution.py:61
  105.5 3.6 %collective-permute-start.40 = (f32[512,128]{1,0:T(8,128)S(1)}, f32[512,128]{1,0:T(8,128)S(1)}, u32[]{:S(2)}, u32[]{:S(2)}) collective-permute-start(f32[512,128]{1,0:T(8,128)S(1)} %collective-permute-done.39.refs_12_), channel_id=1, source_target_pairs={{0,1},{4,5},{8,9},{12,13},{16,17},{20,21},{24,25},{28,29}} | collective-permute-start | bytes 786440 | tf_op jit(solution)/shard_map/ppermute | solution.py:301
  109.2 0.5 collective-permute-start.43
  109.8 3.0 %collective-permute-done.55.refs_4_ = f32[96,512]{1,0:T(8,128)S(1)} collective-permute-done((f32[96,512]{1,0:T(8,128)S(1)}, f32[96,512]{1,0:T(8,128)S(1)}, u32[]{:S(2)}, u32[]{:S(2)}) %collective-permute-start.55) | collective-permute-done | bytes 196640 | tf_op jit(solution)/shard_map/ppermute | solution.py:61
  112.9 1.4 collective-permute-done.40.refs_13_
  114.8 3.4 %collective-permute-start.23 = (f32[96,512]{1,0:T(8,128)S(1)}, f32[96,512]{1,0:T(8,128)S(1)}, u32[]{:S(2)}, u32[]{:S(2)}) collective-permute-start(f32[96,512]{1,0:T(8,128)S(1)} %factor_slice.1.refs_1_), channel_id=1, source_target_pairs={{0,12},{4,0},{8,4},{12,8},{1,13},{5,1},{9,5},{13,9},{2,14},{6,2},{... | collective-permute-start | bytes 589832 | tf_op jit(solution)/shard_map/ppermute | solution.py:56
  118.2 2.0 %pack_halo.1 = (f32[512,128]{1,0:T(8,128)S(1)}, f32[512,128]{1,0:T(8,128)S(1)}, f32[512,128]{1,0:T(8,128)S(1)}, f32[512,128]{1,0:T(8,128)S(1)}) custom-call(s32[35]{0:T(128)S(1)} %lookup_table.1.sc.refs_0_, f32[256,128]{1,0:T(8,128)S(1)} %collective-permute-done.10.refs_5_.edge_ref, f32[3,256,128]{2,1,0:T(8,128)S(1)} %collective-permute-done.34.up_ref), custom_call_target="tpu_custom_call" | custom-call | tf_op jit(solution)/shard_map/pack_halo/pallas_call | solution.py:277
  120.3 2.5 %collective-permute-start.35 = (f32[512,128]{1,0:T(8,128)S(1)}, f32[512,128]{1,0:T(8,128)S(1)}, u32[]{:S(2)}, u32[]{:S(2)}) collective-permute-start(f32[512,128]{1,0:T(8,128)S(1)} %get-tuple-element.60), channel_id=1, source_target_pairs={{0,1},{1,0},{2,3},{3,2},{4,5},{5,4},{6,7},{7,6},{8,9},{9,8},{10,11... | collective-permute-start | bytes 786440 | tf_op jit(solution)/shard_map/ppermute | solution.py:61
  122.8 1.2 collective-permute-done.21.refs_2_
  124.0 6.6 %collective-permute-done.22.refs_3_ = f32[96,512]{1,0:T(8,128)S(1)} collective-permute-done((f32[96,512]{1,0:T(8,128)S(1)}, f32[96,512]{1,0:T(8,128)S(1)}, u32[]{:S(2)}, u32[]{:S(2)}) %collective-permute-start.22) | collective-permute-done | bytes 196640 | tf_op jit(solution)/shard_map/ppermute | solution.py:56
  130.6 1.7 %pick_for_cols.1 = (f32[96,512]{1,0:T(8,128)S(1)}, f32[96,512]{1,0:T(8,128)S(1)}, f32[96,512]{1,0:T(8,128)S(1)}, f32[96,512]{1,0:T(8,128)S(1)}) custom-call(s32[35]{0:T(128)S(1)} %lookup_table.1.sc.refs_0_, f32[96,512]{1,0:T(8,128)S(1)} %factor_slice.1.refs_1_, f32[96,512]{1,0:T(8,128)S(1)} %collective-permute-done.21.refs_2_, ...), custom_call_target="tpu_custom_call" | custom-call | tf_op jit(solution)/shard_map/pick_for_cols/pallas_call | solution.py:322
  132.3 2.0 %collective-permute-start.24 = (f32[96,512]{1,0:T(8,128)S(1)}, f32[96,512]{1,0:T(8,128)S(1)}, u32[]{:S(2)}, u32[]{:S(2)}) collective-permute-start(f32[96,512]{1,0:T(8,128)S(1)} %get-tuple-element.55), channel_id=1, source_target_pairs={{0,1},{1,0},{2,3},{3,2},{4,5},{5,4},{6,7},{7,6},{8,9},{9,8},{10,11... | collective-permute-start | bytes 589832 | tf_op jit(solution)/shard_map/ppermute | solution.py:61
  134.4 1.5 collective-permute-start.25
  136.1 1.9 %collective-permute-done.37.refs_9_ = f32[512,128]{1,0:T(8,128)S(1)} collective-permute-done((f32[512,128]{1,0:T(8,128)S(1)}, f32[512,128]{1,0:T(8,128)S(1)}, u32[]{:S(2)}, u32[]{:S(2)}) %collective-permute-start.37) | collective-permute-done | bytes 262176 | tf_op jit(solution)/shard_map/ppermute | solution.py:61
  138.0 0.5 collective-permute-start.47
  138.5 2.9 %collective-permute-done.24.refs_2_ = f32[96,512]{1,0:T(8,128)S(1)} collective-permute-done((f32[96,512]{1,0:T(8,128)S(1)}, f32[96,512]{1,0:T(8,128)S(1)}, u32[]{:S(2)}, u32[]{:S(2)}) %collective-permute-start.24) | collective-permute-done | bytes 196640 | tf_op jit(solution)/shard_map/ppermute | solution.py:61
  141.4 2.7 %collective-permute-start.26 = (f32[96,512]{1,0:T(8,128)S(1)}, f32[96,512]{1,0:T(8,128)S(1)}, u32[]{:S(2)}, u32[]{:S(2)}) collective-permute-start(f32[96,512]{1,0:T(8,128)S(1)} %get-tuple-element.57), channel_id=1, source_target_pairs={{0,3},{1,2},{2,1},{3,0},{4,7},{5,6},{6,5},{7,4},{8,11},{9,10},{10,... | collective-permute-start | bytes 589832 | tf_op jit(solution)/shard_map/ppermute | solution.py:61
  144.1 4.0 %collective-permute-done.26.refs_4_ = f32[96,512]{1,0:T(8,128)S(1)} collective-permute-done((f32[96,512]{1,0:T(8,128)S(1)}, f32[96,512]{1,0:T(8,128)S(1)}, u32[]{:S(2)}, u32[]{:S(2)}) %collective-permute-start.26) | collective-permute-done | bytes 196640 | tf_op jit(solution)/shard_map/ppermute | solution.py:61
  148.0 0.5 collective-permute-start.28
  148.6 0.4 collective-permute-start.30
  149.1 1.7 %lay_rows.1 = (f32[384,512]{1,0:T(8,128)S(1)}, bf16[384,512]{1,0:T(8,128)(2,1)S(1)}, bf16[384,512]{1,0:T(8,128)(2,1)S(1)}) custom-call(s32[35]{0:T(128)S(1)} %lookup_table.1.sc.refs_0_, f32[96,512]{1,0:T(8,128)S(1)} %factor_slice.1.refs_1_, f32[96,512]{1,0:T(8,128)S(1)} %collective-permute-done.53.refs_2_, f32[96,512]{1,0:T(8,128)S(1)} %collective-permute-done.54.refs_3_, ...), custom_call_target="tpu_custom_call" | custom-call | tf_op jit(solution)/shard_map/lay_rows/pallas_call | solution.py:438
  150.8 3.7 %assemble.1.refs_9_ = f32[384,768]{1,0:T(8,128)S(1)} custom-call(s32[35]{0:T(128)S(1)} %lookup_table.1.sc.refs_0_, f32[384,768]{1,0:T(8,128)S(1)} %copy-done.1, f32[512,128]{1,0:T(8,128)S(1)} %get-tuple-element.41.refs_1_.refs_2_, f32[512,128]{1,0:T(8,128)S(1)} %collective-permute-done.31.refs_3_, f32[512,128]{1,0:T(8,128)S(1)} %collective-permute-done.32.refs_4_, ...), custom_call_target="tpu_custom_call" | custom-call | tf_op jit(solution)/shard_map/assemble/pallas_call | solution.py:524
  154.6 5.1 %finish.1 = f32[384,768]{1,0:T(8,128)} custom-call(s32[35]{0:T(128)S(1)} %lookup_table.1.sc.refs_0_, f32[96,512]{1,0:T(8,128)S(1)} %get-tuple-element.54.refs_1_, f32[96,512]{1,0:T(8,128)S(1)} %collective-permute-done.24.refs_2_, f32[96,512]{1,0:T(8,128)S(1)} %collective-permute-done.25.refs_3_, f32[96,512]{1,0:T(8,128)S(1)} %collective-permute-done.26.refs_4_, ...), custom_call_target="tpu_custom_call" | custom-call | tf_op jit(solution)/shard_map/finish/pallas_call | solution.py:569
  (70 shorter events, 2.1 us)
Async XLA Ops:
  0.0 34.9 %collective-permute-start.4 = (f32[128,1024]{1,0:T(8,128)}, f32[128,1024]{1,0:T(8,128)S(1)}, u32[]{:S(2)}, u32[]{:S(2)}) collective-permute-start(f32[128,1024]{1,0:T(8,128)} %bitcast.2), channel_id=1, source_target_pairs={{0,8},{4,12},{8,0},{12,4},{1,9},{5,13},{9,1},{13,5},{2,10},{6,14},... | collective-permute-start | bytes 1572872 | tf_op jit(solution)/shard_map/ppermute | solution.py:56
  4.1 32.1 %collective-permute-start = (f32[128,1024]{1,0:T(8,128)}, f32[128,1024]{1,0:T(8,128)S(1)}, u32[]{:S(2)}, u32[]{:S(2)}) collective-permute-start(f32[128,1024]{1,0:T(8,128)} %bitcast.3), channel_id=1, source_target_pairs={{0,1},{1,0},{2,3},{3,2},{4,5},{5,4},{6,7},{7,6},{8,9},{9,8},{10,11... | collective-permute-start | bytes 1572872 | tf_op jit(solution)/shard_map/ppermute | solution.py:61
  5.6 0.7 copy-start.5
  7.6 1.3 copy-start
  8.9 1.2 copy-start.4
  10.1 14.6 %copy-start.2 = (f32[1,128,1024]{2,1,0:T(8,128)S(1)}, f32[1,128,1024]{2,1,0:T(8,128)}, u32[]{:S(2)}) copy-start(f32[1,128,1024]{2,1,0:T(8,128)} %param.6) | copy-start | bytes 1572868
  10.9 13.7 %collective-permute-start.7 = (f32[512,128]{1,0:T(8,128)S(1)}, f32[512,128]{1,0:T(8,128)S(1)}, u32[]{:S(2)}, u32[]{:S(2)}) collective-permute-start(f32[512,128]{1,0:T(8,128)S(1)} %get-tuple-element.38), channel_id=1, source_target_pairs={{0,1},{1,0},{2,3},{3,2},{4,5},{5,4},{6,7},{7,6},{8,9},{9,8},{10,11... | collective-permute-start | bytes 786440 | tf_op jit(solution)/shard_map/ppermute | solution.py:61
  11.5 14.7 %collective-permute-start.8 = (f32[512,128]{1,0:T(8,128)S(1)}, f32[512,128]{1,0:T(8,128)S(1)}, u32[]{:S(2)}, u32[]{:S(2)}) collective-permute-start(f32[512,128]{1,0:T(8,128)S(1)} %get-tuple-element.39), channel_id=1, source_target_pairs={{0,2},{1,3},{2,0},{3,1},{4,6},{5,7},{6,4},{7,5},{8,10},{9,11},{10,... | collective-permute-start | bytes 786440 | tf_op jit(solution)/shard_map/ppermute | solution.py:61
  13.1 18.3 %collective-permute-start.9 = (f32[512,128]{1,0:T(8,128)S(1)}, f32[512,128]{1,0:T(8,128)S(1)}, u32[]{:S(2)}, u32[]{:S(2)}) collective-permute-start(f32[512,128]{1,0:T(8,128)S(1)} %get-tuple-element.40), channel_id=1, source_target_pairs={{0,3},{1,2},{2,1},{3,0},{4,7},{5,6},{6,5},{7,4},{8,11},{9,10},{10,... | collective-permute-start | bytes 786440 | tf_op jit(solution)/shard_map/ppermute | solution.py:61
  24.7 27.1 %collective-permute-start.1 = (f32[128,1024]{1,0:T(8,128)S(1)}, f32[128,1024]{1,0:T(8,128)S(1)}, u32[]{:S(2)}, u32[]{:S(2)}) collective-permute-start(f32[128,1024]{1,0:T(8,128)S(1)} %bitcast.4), channel_id=1, source_target_pairs={{0,2},{1,3},{2,0},{3,1},{4,6},{5,7},{6,4},{7,5},{8,10},{9,11},{10,... | collective-permute-start | bytes 1572872 | tf_op jit(solution)/shard_map/ppermute | solution.py:61
  26.2 29.0 %collective-permute-start.2 = (f32[128,1024]{1,0:T(8,128)S(1)}, f32[128,1024]{1,0:T(8,128)S(1)}, u32[]{:S(2)}, u32[]{:S(2)}) collective-permute-start(f32[128,1024]{1,0:T(8,128)S(1)} %bitcast.5), channel_id=1, source_target_pairs={{0,3},{1,2},{2,1},{3,0},{4,7},{5,6},{6,5},{7,4},{8,11},{9,10},{10,... | collective-permute-start | bytes 1572872 | tf_op jit(solution)/shard_map/ppermute | solution.py:61
  31.4 25.2 %collective-permute-start.3 = (f32[128,1024]{1,0:T(8,128)S(1)}, f32[128,1024]{1,0:T(8,128)S(1)}, u32[]{:S(2)}, u32[]{:S(2)}) collective-permute-start(f32[128,1024]{1,0:T(8,128)S(1)} %bitcast.6), channel_id=1, source_target_pairs={{0,4},{4,8},{8,12},{1,5},{5,9},{9,13},{2,6},{6,10},{10,14},{3,7},{... | collective-permute-start | bytes 1572872 | tf_op jit(solution)/shard_map/ppermute | solution.py:184
  34.9 23.0 %collective-permute-start.6 = (f32[128,1024]{1,0:T(8,128)S(1)}, f32[128,1024]{1,0:T(8,128)S(1)}, u32[]{:S(2)}, u32[]{:S(2)}) collective-permute-start(f32[128,1024]{1,0:T(8,128)S(1)} %bitcast.7), channel_id=1, source_target_pairs={{4,0},{8,4},{12,8},{5,1},{9,5},{13,9},{6,2},{10,6},{14,10},{7,3},{... | collective-permute-start | bytes 1572872 | tf_op jit(solution)/shard_map/ppermute | solution.py:185
  36.2 22.6 %collective-permute-start.5 = (f32[128,1024]{1,0:T(8,128)S(1)}, f32[128,1024]{1,0:T(8,128)S(1)}, u32[]{:S(2)}, u32[]{:S(2)}) collective-permute-start(f32[128,1024]{1,0:T(8,128)S(1)} %collective-permute-done.4.refs_7_), channel_id=1, source_target_pairs={{8,12},{4,0},{9,13},{5,1},{10,14},{6,2},{11,15},{7,3},{24,28},{20,... | collective-permute-start | bytes 1572872 | tf_op jit(solution)/shard_map/ppermute | solution.py:188
  51.8 19.1 %collective-permute-start.18 = (f32[96,512]{1,0:T(8,128)S(1)}, f32[96,512]{1,0:T(8,128)S(1)}, u32[]{:S(2)}, u32[]{:S(2)}) collective-permute-start(f32[96,512]{1,0:T(8,128)S(1)} %get-tuple-element.51), channel_id=1, source_target_pairs={{0,1},{4,5},{8,9},{12,13},{16,17},{20,21},{24,25},{28,29}} | collective-permute-start | bytes 589832 | tf_op jit(solution)/shard_map/ppermute | solution.py:617
  55.2 17.4 %collective-permute-start.19 = (f32[96,512]{1,0:T(8,128)S(1)}, f32[96,512]{1,0:T(8,128)S(1)}, u32[]{:S(2)}, u32[]{:S(2)}) collective-permute-start(f32[96,512]{1,0:T(8,128)S(1)} %get-tuple-element.52), channel_id=1, source_target_pairs={{0,2},{4,6},{8,10},{12,14},{16,18},{20,22},{24,26},{28,30}} | collective-permute-start | bytes 589832 | tf_op jit(solution)/shard_map/ppermute | solution.py:617
  56.5 18.8 %collective-permute-start.20 = (f32[96,512]{1,0:T(8,128)S(1)}, f32[96,512]{1,0:T(8,128)S(1)}, u32[]{:S(2)}, u32[]{:S(2)}) collective-permute-start(f32[96,512]{1,0:T(8,128)S(1)} %get-tuple-element.53), channel_id=1, source_target_pairs={{0,3},{4,7},{8,11},{12,15},{16,19},{20,23},{24,27},{28,31}} | collective-permute-start | bytes 589832 | tf_op jit(solution)/shard_map/ppermute | solution.py:617
  63.1 30.0 %copy-start.3 = (f32[512,512]{1,0:T(8,128)S(1)}, f32[512,512]{1,0:T(8,128)}, u32[]{:S(2)}) copy-start(f32[512,512]{1,0:T(8,128)} %refs_13_.1) | copy-start | bytes 3145732
  63.1 5.2 %collective-permute-start.10 = (f32[256,128]{1,0:T(8,128)S(1)}, f32[256,128]{1,0:T(8,128)S(1)}, u32[]{:S(2)}, u32[]{:S(2)}) collective-permute-start(f32[256,128]{1,0:T(8,128)S(1)} %get-tuple-element.45), channel_id=1, source_target_pairs={{0,4},{4,8},{8,12},{1,5},{5,9},{9,13},{2,6},{6,10},{10,14},{3,7},{... | collective-permute-start | bytes 393224 | tf_op jit(solution)/shard_map/ppermute | solution.py:66
  69.2 6.2 %collective-permute-start.11 = (f32[2,96,128]{2,1,0:T(8,128)S(1)}, f32[2,96,128]{2,1,0:T(8,128)S(1)}, u32[]{:S(2)}, u32[]{:S(2)}) collective-permute-start(f32[2,96,128]{2,1,0:T(8,128)S(1)} %get-tuple-element.47), channel_id=1, source_target_pairs={{0,1},{1,0},{2,3},{3,2},{4,5},{5,4},{6,7},{7,6},{8,9},{9,8},{10,11... | collective-permute-start | bytes 294920 | tf_op jit(solution)/shard_map/ppermute | solution.py:61
  69.6 17.1 %collective-permute-start.39 = (f32[512,128]{1,0:T(8,128)S(1)}, f32[512,128]{1,0:T(8,128)S(1)}, u32[]{:S(2)}, u32[]{:S(2)}) collective-permute-start(f32[512,128]{1,0:T(8,128)S(1)} %get-tuple-element.65), channel_id=1, source_target_pairs={{2,0},{3,1},{6,4},{7,5},{10,8},{11,9},{14,12},{15,13},{18,16},{19,... | collective-permute-start | bytes 786440 | tf_op jit(solution)/shard_map/ppermute | solution.py:298
  70.9 15.8 %collective-permute-start.31 = (f32[512,128]{1,0:T(8,128)S(1)}, f32[512,128]{1,0:T(8,128)S(1)}, u32[]{:S(2)}, u32[]{:S(2)}) collective-permute-start(f32[512,128]{1,0:T(8,128)S(1)} %get-tuple-element.42.refs_2_), channel_id=1, source_target_pairs={{0,1},{1,0},{2,3},{3,2},{4,5},{5,4},{6,7},{7,6},{8,9},{9,8},{10,11... | collective-permute-start | bytes 786440 | tf_op jit(solution)/shard_map/ppermute | solution.py:61
  72.6 12.1 %collective-permute-start.12 = (f32[2,96,128]{2,1,0:T(8,128)S(1)}, f32[2,96,128]{2,1,0:T(8,128)S(1)}, u32[]{:S(2)}, u32[]{:S(2)}) collective-permute-start(f32[2,96,128]{2,1,0:T(8,128)S(1)} %get-tuple-element.48), channel_id=1, source_target_pairs={{0,2},{1,3},{2,0},{3,1},{4,6},{5,7},{6,4},{7,5},{8,10},{9,11},{10,... | collective-permute-start | bytes 294920 | tf_op jit(solution)/shard_map/ppermute | solution.py:61
  75.3 15.5 %collective-permute-start.32 = (f32[512,128]{1,0:T(8,128)S(1)}, f32[512,128]{1,0:T(8,128)S(1)}, u32[]{:S(2)}, u32[]{:S(2)}) collective-permute-start(f32[512,128]{1,0:T(8,128)S(1)} %get-tuple-element.43.refs_3_), channel_id=1, source_target_pairs={{0,2},{1,3},{2,0},{3,1},{4,6},{5,7},{6,4},{7,5},{8,10},{9,11},{10,... | collective-permute-start | bytes 786440 | tf_op jit(solution)/shard_map/ppermute | solution.py:61
  75.4 9.4 %collective-permute-start.13 = (f32[2,96,128]{2,1,0:T(8,128)S(1)}, f32[2,96,128]{2,1,0:T(8,128)S(1)}, u32[]{:S(2)}, u32[]{:S(2)}) collective-permute-start(f32[2,96,128]{2,1,0:T(8,128)S(1)} %get-tuple-element.49), channel_id=1, source_target_pairs={{0,3},{1,2},{2,1},{3,0},{4,7},{5,6},{6,5},{7,4},{8,11},{9,10},{10,... | collective-permute-start | bytes 294920 | tf_op jit(solution)/shard_map/ppermute | solution.py:61
  84.7 1.3 collective-permute-start.14
  84.7 6.4 %collective-permute-start.15 = (f32[2,96,128]{2,1,0:T(8,128)S(1)}, f32[2,96,128]{2,1,0:T(8,128)S(1)}, u32[]{:S(2)}, u32[]{:S(2)}) collective-permute-start(f32[2,96,128]{2,1,0:T(8,128)S(1)} %collective-permute-done.11.refs_2_), channel_id=1, source_target_pairs={{0,16},{16,0},{1,17},{17,1},{2,18},{18,2},{3,19},{19,3},{4,20},{20... | collective-permute-start | bytes 294920 | tf_op jit(solution)/shard_map/ppermute | solution.py:61
  86.0 9.3 %collective-permute-start.33 = (f32[512,128]{1,0:T(8,128)S(1)}, f32[512,128]{1,0:T(8,128)S(1)}, u32[]{:S(2)}, u32[]{:S(2)}) collective-permute-start(f32[512,128]{1,0:T(8,128)S(1)} %get-tuple-element.44.refs_4_), channel_id=1, source_target_pairs={{0,3},{1,2},{2,1},{3,0},{4,7},{5,6},{6,5},{7,4},{8,11},{9,10},{10,... | collective-permute-start | bytes 786440 | tf_op jit(solution)/shard_map/ppermute | solution.py:61
  86.7 10.3 %collective-permute-start.41 = (f32[512,128]{1,0:T(8,128)S(1)}, f32[512,128]{1,0:T(8,128)S(1)}, u32[]{:S(2)}, u32[]{:S(2)}) collective-permute-start(f32[512,128]{1,0:T(8,128)S(1)} %get-tuple-element.41.refs_1_.refs_2_), channel_id=1, source_target_pairs={{0,16},{16,0},{1,17},{17,1},{2,18},{18,2},{3,19},{19,3},{4,20},{20... | collective-permute-start | bytes 786440 | tf_op jit(solution)/shard_map/ppermute | solution.py:61
  86.7 22.4 %collective-permute-start.34 = (f32[3,256,128]{2,1,0:T(8,128)S(1)}, f32[3,256,128]{2,1,0:T(8,128)S(1)}, u32[]{:S(2)}, u32[]{:S(2)}) collective-permute-start(f32[3,256,128]{2,1,0:T(8,128)S(1)} %get-tuple-element.58), channel_id=1, source_target_pairs={{0,4},{4,8},{8,12},{1,5},{5,9},{9,13},{2,6},{6,10},{10,14},{3,7},{... | collective-permute-start | bytes 1179656 | tf_op jit(solution)/shard_map/ppermute | solution.py:66
  90.8 1.4 collective-permute-start.16
  91.1 1.8 %collective-permute-start.17 = (f32[2,96,128]{2,1,0:T(8,128)S(1)}, f32[2,96,128]{2,1,0:T(8,128)S(1)}, u32[]{:S(2)}, u32[]{:S(2)}) collective-permute-start(f32[2,96,128]{2,1,0:T(8,128)S(1)} %collective-permute-done.13.refs_4_), channel_id=1, source_target_pairs={{0,16},{16,0},{1,17},{17,1},{2,18},{18,2},{3,19},{19,3},{4,20},{20... | collective-permute-start | bytes 294920 | tf_op jit(solution)/shard_map/ppermute | solution.py:61
  92.2 8.7 %collective-permute-start.38 = (f32[512,128]{1,0:T(8,128)S(1)}, f32[512,128]{1,0:T(8,128)S(1)}, u32[]{:S(2)}, u32[]{:S(2)}) collective-permute-start(f32[512,128]{1,0:T(8,128)S(1)} %get-tuple-element.64), channel_id=1, source_target_pairs={{2,3},{3,2},{6,7},{7,6},{10,11},{11,10},{14,15},{15,14},{18,19},{1... | collective-permute-start | bytes 786440 | tf_op jit(solution)/shard_map/ppermute | solution.py:298
  92.9 12.6 %collective-permute-start.49 = (f32[512,128]{1,0:T(8,128)S(1)}, f32[512,128]{1,0:T(8,128)S(1)}, u32[]{:S(2)}, u32[]{:S(2)}) collective-permute-start(f32[512,128]{1,0:T(8,128)S(1)} %get-tuple-element.63.refs_10_), channel_id=1, source_target_pairs={{0,16},{16,0},{1,17},{17,1},{2,18},{18,2},{3,19},{19,3},{4,20},{20... | collective-permute-start | bytes 786440 | tf_op jit(solution)/shard_map/ppermute | solution.py:61
  95.3 55.5 %copy-start.1 = (f32[384,768]{1,0:T(8,128)S(1)}, f32[384,768]{1,0:T(8,128)}, u32[]{:S(2)}) copy-start(f32[384,768]{1,0:T(8,128)} %refs_1_.1) | copy-start | bytes 3538948
  95.3 13.9 %collective-permute-start.53 = (f32[96,512]{1,0:T(8,128)S(1)}, f32[96,512]{1,0:T(8,128)S(1)}, u32[]{:S(2)}, u32[]{:S(2)}) collective-permute-start(f32[96,512]{1,0:T(8,128)S(1)} %factor_slice.1.refs_1_), channel_id=1, source_target_pairs={{0,1},{1,0},{2,3},{3,2},{4,5},{5,4},{6,7},{7,6},{8,9},{9,8},{10,11... | collective-permute-start | bytes 589832 | tf_op jit(solution)/shard_map/ppermute | solution.py:61
  97.0 12.7 %collective-permute-start.54 = (f32[96,512]{1,0:T(8,128)S(1)}, f32[96,512]{1,0:T(8,128)S(1)}, u32[]{:S(2)}, u32[]{:S(2)}) collective-permute-start(f32[96,512]{1,0:T(8,128)S(1)} %factor_slice.1.refs_1_), channel_id=1, source_target_pairs={{0,2},{1,3},{2,0},{3,1},{4,6},{5,7},{6,4},{7,5},{8,10},{9,11},{10,... | collective-permute-start | bytes 589832 | tf_op jit(solution)/shard_map/ppermute | solution.py:61
  100.9 11.9 %collective-permute-start.55 = (f32[96,512]{1,0:T(8,128)S(1)}, f32[96,512]{1,0:T(8,128)S(1)}, u32[]{:S(2)}, u32[]{:S(2)}) collective-permute-start(f32[96,512]{1,0:T(8,128)S(1)} %factor_slice.1.refs_1_), channel_id=1, source_target_pairs={{0,3},{1,2},{2,1},{3,0},{4,7},{5,6},{6,5},{7,4},{8,11},{9,10},{10,... | collective-permute-start | bytes 589832 | tf_op jit(solution)/shard_map/ppermute | solution.py:61
  105.5 8.8 %collective-permute-start.40 = (f32[512,128]{1,0:T(8,128)S(1)}, f32[512,128]{1,0:T(8,128)S(1)}, u32[]{:S(2)}, u32[]{:S(2)}) collective-permute-start(f32[512,128]{1,0:T(8,128)S(1)} %collective-permute-done.39.refs_12_), channel_id=1, source_target_pairs={{0,1},{4,5},{8,9},{12,13},{16,17},{20,21},{24,25},{28,29}} | collective-permute-start | bytes 786440 | tf_op jit(solution)/shard_map/ppermute | solution.py:301
  109.1 5.4 %collective-permute-start.42 = (f32[512,128]{1,0:T(8,128)S(1)}, f32[512,128]{1,0:T(8,128)S(1)}, u32[]{:S(2)}, u32[]{:S(2)}) collective-permute-start(f32[512,128]{1,0:T(8,128)S(1)} %collective-permute-done.31.refs_3_), channel_id=1, source_target_pairs={{0,16},{16,0},{1,17},{17,1},{2,18},{18,2},{3,19},{19,3},{4,20},{20... | collective-permute-start | bytes 786440 | tf_op jit(solution)/shard_map/ppermute | solution.py:61
  109.2 5.5 %collective-permute-start.43 = (f32[512,128]{1,0:T(8,128)S(1)}, f32[512,128]{1,0:T(8,128)S(1)}, u32[]{:S(2)}, u32[]{:S(2)}) collective-permute-start(f32[512,128]{1,0:T(8,128)S(1)} %collective-permute-done.32.refs_4_), channel_id=1, source_target_pairs={{0,16},{16,0},{1,17},{17,1},{2,18},{18,2},{3,19},{19,3},{4,20},{20... | collective-permute-start | bytes 786440 | tf_op jit(solution)/shard_map/ppermute | solution.py:61
  109.7 8.5 %collective-permute-start.44 = (f32[512,128]{1,0:T(8,128)S(1)}, f32[512,128]{1,0:T(8,128)S(1)}, u32[]{:S(2)}, u32[]{:S(2)}) collective-permute-start(f32[512,128]{1,0:T(8,128)S(1)} %collective-permute-done.33.refs_5_), channel_id=1, source_target_pairs={{0,16},{16,0},{1,17},{17,1},{2,18},{18,2},{3,19},{19,3},{4,20},{20... | collective-permute-start | bytes 786440 | tf_op jit(solution)/shard_map/ppermute | solution.py:61
  112.9 7.4 %collective-permute-start.51 = (f32[512,128]{1,0:T(8,128)S(1)}, f32[512,128]{1,0:T(8,128)S(1)}, u32[]{:S(2)}, u32[]{:S(2)}) collective-permute-start(f32[512,128]{1,0:T(8,128)S(1)} %collective-permute-done.39.refs_12_), channel_id=1, source_target_pairs={{0,16},{16,0},{1,17},{17,1},{2,18},{18,2},{3,19},{19,3},{4,20},{20... | collective-permute-start | bytes 786440 | tf_op jit(solution)/shard_map/ppermute | solution.py:61
  114.3 9.7 %collective-permute-start.21 = (f32[96,512]{1,0:T(8,128)S(1)}, f32[96,512]{1,0:T(8,128)S(1)}, u32[]{:S(2)}, u32[]{:S(2)}) collective-permute-start(f32[96,512]{1,0:T(8,128)S(1)} %factor_slice.1.refs_1_), channel_id=1, source_target_pairs={{0,4},{4,8},{8,12},{12,0},{1,5},{5,9},{9,13},{13,1},{2,6},{6,10},{... | collective-permute-start | bytes 589832 | tf_op jit(solution)/shard_map/ppermute | solution.py:56
  114.6 16.0 %collective-permute-start.22 = (f32[96,512]{1,0:T(8,128)S(1)}, f32[96,512]{1,0:T(8,128)S(1)}, u32[]{:S(2)}, u32[]{:S(2)}) collective-permute-start(f32[96,512]{1,0:T(8,128)S(1)} %factor_slice.1.refs_1_), channel_id=1, source_target_pairs={{0,8},{4,12},{8,0},{12,4},{1,9},{5,13},{9,1},{13,5},{2,10},{6,14},... | collective-permute-start | bytes 589832 | tf_op jit(solution)/shard_map/ppermute | solution.py:56
  114.8 15.9 %collective-permute-start.23 = (f32[96,512]{1,0:T(8,128)S(1)}, f32[96,512]{1,0:T(8,128)S(1)}, u32[]{:S(2)}, u32[]{:S(2)}) collective-permute-start(f32[96,512]{1,0:T(8,128)S(1)} %factor_slice.1.refs_1_), channel_id=1, source_target_pairs={{0,12},{4,0},{8,4},{12,8},{1,13},{5,1},{9,5},{13,9},{2,14},{6,2},{... | collective-permute-start | bytes 589832 | tf_op jit(solution)/shard_map/ppermute | solution.py:56
  118.2 14.1 %collective-permute-start.50 = (f32[512,128]{1,0:T(8,128)S(1)}, f32[512,128]{1,0:T(8,128)S(1)}, u32[]{:S(2)}, u32[]{:S(2)}) collective-permute-start(f32[512,128]{1,0:T(8,128)S(1)} %collective-permute-done.38.refs_11_), channel_id=1, source_target_pairs={{0,16},{16,0},{1,17},{17,1},{2,18},{18,2},{3,19},{19,3},{4,20},{20... | collective-permute-start | bytes 786440 | tf_op jit(solution)/shard_map/ppermute | solution.py:61
  120.3 14.1 %collective-permute-start.35 = (f32[512,128]{1,0:T(8,128)S(1)}, f32[512,128]{1,0:T(8,128)S(1)}, u32[]{:S(2)}, u32[]{:S(2)}) collective-permute-start(f32[512,128]{1,0:T(8,128)S(1)} %get-tuple-element.60), channel_id=1, source_target_pairs={{0,1},{1,0},{2,3},{3,2},{4,5},{5,4},{6,7},{7,6},{8,9},{9,8},{10,11... | collective-permute-start | bytes 786440 | tf_op jit(solution)/shard_map/ppermute | solution.py:61
  124.0 11.9 %collective-permute-start.36 = (f32[512,128]{1,0:T(8,128)S(1)}, f32[512,128]{1,0:T(8,128)S(1)}, u32[]{:S(2)}, u32[]{:S(2)}) collective-permute-start(f32[512,128]{1,0:T(8,128)S(1)} %get-tuple-element.61), channel_id=1, source_target_pairs={{0,2},{1,3},{2,0},{3,1},{4,6},{5,7},{6,4},{7,5},{8,10},{9,11},{10,... | collective-permute-start | bytes 786440 | tf_op jit(solution)/shard_map/ppermute | solution.py:61
  130.5 7.4 %collective-permute-start.37 = (f32[512,128]{1,0:T(8,128)S(1)}, f32[512,128]{1,0:T(8,128)S(1)}, u32[]{:S(2)}, u32[]{:S(2)}) collective-permute-start(f32[512,128]{1,0:T(8,128)S(1)} %get-tuple-element.62), channel_id=1, source_target_pairs={{0,3},{1,2},{2,1},{3,0},{4,7},{5,6},{6,5},{7,4},{8,11},{9,10},{10,... | collective-permute-start | bytes 786440 | tf_op jit(solution)/shard_map/ppermute | solution.py:61
  130.6 7.4 %collective-permute-start.45 = (f32[512,128]{1,0:T(8,128)S(1)}, f32[512,128]{1,0:T(8,128)S(1)}, u32[]{:S(2)}, u32[]{:S(2)}) collective-permute-start(f32[512,128]{1,0:T(8,128)S(1)} %get-tuple-element.59.refs_6_), channel_id=1, source_target_pairs={{0,16},{16,0},{1,17},{17,1},{2,18},{18,2},{3,19},{19,3},{4,20},{20... | collective-permute-start | bytes 786440 | tf_op jit(solution)/shard_map/ppermute | solution.py:61
  132.3 9.0 %collective-permute-start.24 = (f32[96,512]{1,0:T(8,128)S(1)}, f32[96,512]{1,0:T(8,128)S(1)}, u32[]{:S(2)}, u32[]{:S(2)}) collective-permute-start(f32[96,512]{1,0:T(8,128)S(1)} %get-tuple-element.55), channel_id=1, source_target_pairs={{0,1},{1,0},{2,3},{3,2},{4,5},{5,4},{6,7},{7,6},{8,9},{9,8},{10,11... | collective-permute-start | bytes 589832 | tf_op jit(solution)/shard_map/ppermute | solution.py:61
  134.4 9.7 %collective-permute-start.25 = (f32[96,512]{1,0:T(8,128)S(1)}, f32[96,512]{1,0:T(8,128)S(1)}, u32[]{:S(2)}, u32[]{:S(2)}) collective-permute-start(f32[96,512]{1,0:T(8,128)S(1)} %get-tuple-element.56), channel_id=1, source_target_pairs={{0,2},{1,3},{2,0},{3,1},{4,6},{5,7},{6,4},{7,5},{8,10},{9,11},{10,... | collective-permute-start | bytes 589832 | tf_op jit(solution)/shard_map/ppermute | solution.py:61
  135.9 12.1 %collective-permute-start.52 = (f32[512,128]{1,0:T(8,128)S(1)}, f32[512,128]{1,0:T(8,128)S(1)}, u32[]{:S(2)}, u32[]{:S(2)}) collective-permute-start(f32[512,128]{1,0:T(8,128)S(1)} %collective-permute-done.40.refs_13_), channel_id=1, source_target_pairs={{0,16},{16,0},{1,17},{17,1},{2,18},{18,2},{3,19},{19,3},{4,20},{20... | collective-permute-start | bytes 786440 | tf_op jit(solution)/shard_map/ppermute | solution.py:61
  138.0 10.5 %collective-permute-start.46 = (f32[512,128]{1,0:T(8,128)S(1)}, f32[512,128]{1,0:T(8,128)S(1)}, u32[]{:S(2)}, u32[]{:S(2)}) collective-permute-start(f32[512,128]{1,0:T(8,128)S(1)} %collective-permute-done.35.refs_7_), channel_id=1, source_target_pairs={{0,16},{16,0},{1,17},{17,1},{2,18},{18,2},{3,19},{19,3},{4,20},{20... | collective-permute-start | bytes 786440 | tf_op jit(solution)/shard_map/ppermute | solution.py:61
  138.0 10.6 %collective-permute-start.47 = (f32[512,128]{1,0:T(8,128)S(1)}, f32[512,128]{1,0:T(8,128)S(1)}, u32[]{:S(2)}, u32[]{:S(2)}) collective-permute-start(f32[512,128]{1,0:T(8,128)S(1)} %collective-permute-done.36.refs_8_), channel_id=1, source_target_pairs={{0,16},{16,0},{1,17},{17,1},{2,18},{18,2},{3,19},{19,3},{4,20},{20... | collective-permute-start | bytes 786440 | tf_op jit(solution)/shard_map/ppermute | solution.py:61
  141.4 6.6 %collective-permute-start.26 = (f32[96,512]{1,0:T(8,128)S(1)}, f32[96,512]{1,0:T(8,128)S(1)}, u32[]{:S(2)}, u32[]{:S(2)}) collective-permute-start(f32[96,512]{1,0:T(8,128)S(1)} %get-tuple-element.57), channel_id=1, source_target_pairs={{0,3},{1,2},{2,1},{3,0},{4,7},{5,6},{6,5},{7,4},{8,11},{9,10},{10,... | collective-permute-start | bytes 589832 | tf_op jit(solution)/shard_map/ppermute | solution.py:61
  144.1 6.8 %collective-permute-start.48 = (f32[512,128]{1,0:T(8,128)S(1)}, f32[512,128]{1,0:T(8,128)S(1)}, u32[]{:S(2)}, u32[]{:S(2)}) collective-permute-start(f32[512,128]{1,0:T(8,128)S(1)} %collective-permute-done.37.refs_9_), channel_id=1, source_target_pairs={{0,16},{16,0},{1,17},{17,1},{2,18},{18,2},{3,19},{19,3},{4,20},{20... | collective-permute-start | bytes 786440 | tf_op jit(solution)/shard_map/ppermute | solution.py:61
  148.0 6.5 %collective-permute-start.27 = (f32[96,512]{1,0:T(8,128)S(1)}, f32[96,512]{1,0:T(8,128)S(1)}, u32[]{:S(2)}, u32[]{:S(2)}) collective-permute-start(f32[96,512]{1,0:T(8,128)S(1)} %get-tuple-element.54.refs_1_), channel_id=1, source_target_pairs={{0,16},{16,0},{1,17},{17,1},{2,18},{18,2},{3,19},{19,3},{4,20},{20... | collective-permute-start | bytes 589832 | tf_op jit(solution)/shard_map/ppermute | solution.py:61
  148.0 6.5 %collective-permute-start.28 = (f32[96,512]{1,0:T(8,128)S(1)}, f32[96,512]{1,0:T(8,128)S(1)}, u32[]{:S(2)}, u32[]{:S(2)}) collective-permute-start(f32[96,512]{1,0:T(8,128)S(1)} %collective-permute-done.24.refs_2_), channel_id=1, source_target_pairs={{0,16},{16,0},{1,17},{17,1},{2,18},{18,2},{3,19},{19,3},{4,20},{20... | collective-permute-start | bytes 589832 | tf_op jit(solution)/shard_map/ppermute | solution.py:61
  148.5 6.0 %collective-permute-start.29 = (f32[96,512]{1,0:T(8,128)S(1)}, f32[96,512]{1,0:T(8,128)S(1)}, u32[]{:S(2)}, u32[]{:S(2)}) collective-permute-start(f32[96,512]{1,0:T(8,128)S(1)} %collective-permute-done.25.refs_3_), channel_id=1, source_target_pairs={{0,16},{16,0},{1,17},{17,1},{2,18},{18,2},{3,19},{19,3},{4,20},{20... | collective-permute-start | bytes 589832 | tf_op jit(solution)/shard_map/ppermute | solution.py:61
  148.6 5.9 %collective-permute-start.30 = (f32[96,512]{1,0:T(8,128)S(1)}, f32[96,512]{1,0:T(8,128)S(1)}, u32[]{:S(2)}, u32[]{:S(2)}) collective-permute-start(f32[96,512]{1,0:T(8,128)S(1)} %collective-permute-done.26.refs_4_), channel_id=1, source_target_pairs={{0,16},{16,0},{1,17},{17,1},{2,18},{18,2},{3,19},{19,3},{4,20},{20... | collective-permute-start | bytes 589832 | tf_op jit(solution)/shard_map/ppermute | solution.py:61

commit v7 on v4

--- a/solution.py
+++ b/solution.py
@@ -178,22 +178,28 @@
 def around_row(value):
     count = lax.axis_size("row")
     half = count // 2
-    middle = rotated(value, "row", half)
-    below, above, far = [], [], []
+    rows = value.shape[0] // 2
+    middle, far = [], [[] for _ in range(1, half)]
+    for part in range(2):
+        middle.append(rotated(value[part * rows : (part + 1) * rows], "row", half))
+    below, above = [], []
     for d in range(1, half):
         below.append(lax.ppermute(value, "row", [(i, i + d) for i in range(count - d)]))
         above.append(lax.ppermute(value, "row", [(i + d, i) for i in range(count - d)]))
         pairs = [(i, i + d) for i in range(half, count - d)]
         pairs += [(i, i - d) for i in range(d, half)]
-        far.append(lax.ppermute(middle, "row", pairs))
-    return [value] + below + [middle] + far + above
+        for part in range(2):
+            far[d - 1].append(lax.ppermute(middle[part], "row", pairs))
+    return [[value]] + [[v] for v in below] + [middle] + far + [[v] for v in above]
 
 
 def slice_products(table, rows, around, fronts):
     count = len(rows)
-    many = len(around)
+    flat = sum(around, [])
+    many = len(flat)
     sub, depth = rows[0].shape
     size = count * sub
+    part_rows = sub // 2
 
     def body(*refs):
         sc = refs[0]
@@ -206,13 +212,27 @@
         rows_in = gather_copies(sc, row_refs, row_buf, sems, sub)
         for copy in rows_in:
             copy.start()
-        for m, place in enumerate(places):
-            start_chosen(slice_place(sc, m, count), around_refs, place, sems.at[count + m])
+        choices, taken = ([], []), 0
+        for group_parts in around:
+            found = around_refs[taken : taken + len(group_parts)]
+            taken += len(group_parts)
+            for part in range(2):
+                lines = pl.ds(part * part_rows, part_rows)
+                choices[part].append(found[part] if len(found) == 2 else found[0].at[lines])
+        targets = [
+            (m, part, place.at[part * part_rows : (part + 1) * part_rows])
+            for m, place in enumerate(places)
+            for part in range(2)
+        ]
+        for m, part, target in targets:
+            start_chosen(
+                slice_place(sc, m, count), choices[part], target, sems.at[count + 2 * m + part]
+            )
         for copy in rows_in:
             copy.wait()
         left = halves(row_buf[...])
-        for m, place in enumerate(places):
-            pltpu.make_async_copy(around_refs[0], place, sems.at[count + m]).wait()
+        for m, part, target in targets:
+            pltpu.make_async_copy(choices[part][0], target, sems.at[count + 2 * m + part]).wait()
         product = times_transpose(left, halves(col_buf[...]))
         for m in range(count):
             group = sc[COL] ^ m
@@ -235,11 +255,11 @@
         scratch_shapes=[
             pltpu.VMEM((size, depth), jnp.float32),
             pltpu.VMEM((size, depth), jnp.float32),
-            pltpu.SemaphoreType.DMA((2 * count,)),
+            pltpu.SemaphoreType.DMA((3 * count,)),
         ],
         compiler_params=limit_for(sub, 20),
         name="slice_products",
-    )(table, *rows, *around, *fronts)
+    )(table, *rows, *flat, *fronts)
 
 
 def pack_halo(table, homes, edge, up):
@@ -401,7 +421,31 @@
     )(table, *small, *small_other, *dealt, pivot_inverse)
 
 
-def assemble(table, parent, own, other):
+def lay_rows(table, pieces):
+    count = len(pieces)
+    piece_rows, width = pieces[0].shape
+    rows = count * piece_rows
+
+    def body(*refs):
+        sc = refs[0]
+        ins = refs[1 : 1 + count]
+        out, high, low, sems = refs[1 + count :]
+        run_copies(gather_copies(sc, ins, out, sems, piece_rows))
+        high[...], low[...] = halves(out[...])
+
+    part = jax.ShapeDtypeStruct((rows, width), jnp.bfloat16)
+    return pl.pallas_call(
+        body,
+        in_specs=[SMEM] + [ANY] * count,
+        out_specs=[VMEM] * 3,
+        out_shape=[f32(rows, width), part, part],
+        scratch_shapes=[pltpu.SemaphoreType.DMA((count,))],
+        compiler_params=limit_for(BLK, 8),
+        name="lay_rows",
+    )(table, *pieces)
+
+
+def assemble(table, parent, own, other, row_factor):
     count = len(own) // 2
     rows, width = parent.shape
     size, sub = own[0].shape
@@ -411,7 +455,7 @@
     def body(*refs):
         sc, parent_ref = refs[:2]
         own_refs, other_refs = refs[2 : 2 + 2 * count], refs[2 + 2 * count : 2 + 4 * count]
-        out, own_win, other_win, sems = refs[2 + 4 * count :]
+        factor_ref, out, own_win, other_win, sems = refs[2 + 4 * count :]
         at = 0
         always, edges = [], []
         for refs_in, window in ((own_refs, own_win), (other_refs, other_win)):
@@ -476,11 +520,13 @@
                     ]
                     block = pieces[0] if split == 1 else jnp.concatenate(pieces, axis=1)
                     total += jnp.where((down >= 0) & (across >= 0), block, 0.0)
+                if q < PIV:
+                    total = jnp.where(sc[COL] == 0, factor_ref[lines, cols], total)
                 out[lines, cols] = total
 
     return pl.pallas_call(
         body,
-        in_specs=[SMEM, VMEM] + [ANY] * (4 * count),
+        in_specs=[SMEM, VMEM] + [ANY] * (4 * count) + [VMEM],
         out_specs=VMEM,
         out_shape=f32(rows, width),
         scratch_shapes=[
@@ -488,36 +534,27 @@
             pltpu.VMEM((half + count, size + EDGE, sub), jnp.float32),
             pltpu.SemaphoreType.DMA((8 * count,)),
         ],
-        compiler_params=limit_for(sub, 12),
+        compiler_params=limit_for(sub, 14),
         name="assemble",
-    )(table, parent, *own, *other)
-
-
-def finish(table, assembled, row_pieces, col_own, col_other):
-    count = len(row_pieces)
+    )(table, parent, *own, *other, row_factor)
+
+
+def finish(table, assembled, row_high, row_low, col_own, col_other):
+    count = len(col_own)
     rows, width = assembled.shape
-    piece_rows = row_pieces[0].shape[0]
+    piece_rows = col_own[0].shape[0]
 
     def body(*refs):
         sc = refs[0]
-        row_refs = refs[1 : 1 + count]
-        col_own_refs = refs[1 + count : 1 + 2 * count]
-        col_other_refs = refs[1 + 2 * count : 1 + 3 * count]
-        base_ref, out, row_factor, col_factor, sems = refs[1 + 3 * count :]
-        copies = [
-            gather_copies(sc, row_refs, row_factor, sems, piece_rows),
-            gather_copies(sc, col_own_refs, col_factor.at[sc[SIB]], sems, piece_rows, count),
-            gather_copies(
-                sc, col_other_refs, col_factor.at[1 - sc[SIB]], sems, piece_rows, 2 * count
-            ),
-        ]
-        for copy in sum(copies, []):
-            copy.start()
-        for copy in copies[0]:
-            copy.wait()
-        left = halves(row_factor[...])
-        for copy in copies[1] + copies[2]:
-            copy.wait()
+        own_refs = refs[1 : 1 + count]
+        other_refs = refs[1 + count : 1 + 2 * count]
+        base_ref, high_ref, low_ref, out, col_factor, sems = refs[1 + 2 * count :]
+        own = gather_copies(sc, own_refs, col_factor.at[sc[SIB]], sems, piece_rows)
+        other = gather_copies(
+            sc, other_refs, col_factor.at[1 - sc[SIB]], sems, piece_rows, count
+        )
+        run_copies(own + other)
+        left = high_ref[...], low_ref[...]
         first_row = (sc[ROW] * 2 + sc[SIB]) * HALF
         first_col = sc[COL] * PBD
         for side in range(2):
@@ -530,24 +567,20 @@
                     total = base_ref[lines, cols]
                     inside = (first_col + q >= PIV) & (first_row + p >= PIV)
                     reduced = total - product[lines, i * BLK : (i + 1) * BLK]
-                    total = jnp.where(inside, reduced, total)
-                    if q < PIV:
-                        total = jnp.where(sc[COL] == 0, row_factor[lines, cols], total)
-                    out[lines, cols] = total
-
-    return pl.pallas_call(
-        body,
-        in_specs=[SMEM] + [ANY] * (3 * count) + [VMEM],
+                    out[lines, cols] = jnp.where(inside, reduced, total)
+
+    return pl.pallas_call(
+        body,
+        in_specs=[SMEM] + [ANY] * (2 * count) + [VMEM] * 3,
         out_specs=VMEM,
         out_shape=f32(rows, width),
         scratch_shapes=[
-            pltpu.VMEM((rows, PANEL), jnp.float32),
             pltpu.VMEM((2, rows, PANEL), jnp.float32),
-            pltpu.SemaphoreType.DMA((3 * count,)),
+            pltpu.SemaphoreType.DMA((2 * count,)),
         ],
         compiler_params=limit_for(BLK, 16),
         name="finish",
-    )(table, *row_pieces, *col_own, *col_other, assembled)
+    )(table, *col_own, *col_other, assembled, row_high, row_low)
 
 
 def shards(child_front, child_panel, block_map, parent_front, pivot_inverse):
@@ -600,13 +633,15 @@
     factors = over_row(factor)
     row_pieces = [factor] + over_col([factor] * (count - 1))
 
+    row_factor, high, low = lay_rows(table, row_pieces)
+
     picked = pick_for_cols(table, factors, range(count))
     col_own = [picked[0]] + over_col(picked[1:])
     col_other = [to_sibling(value) for value in col_own]
 
     other = [to_sibling(value) for value in own]
-    assembled = assemble(table, parent_front, own, other)
-    return finish(table, assembled, row_pieces, col_own, col_other)
+    assembled = assemble(table, parent_front, own, other, row_factor)
+    return finish(table, assembled, high, low, col_own, col_other)
 
 
 def solution(mesh):

time: 159 us -> 160 us (level)
  starting transfers between devices: 57.1 us -> 62.4 us
  waiting for transfers between devices: 75.3 us -> 70.7 us
    ppermute x37, waiting for transfers between devices: 60.5 us -> 45.5 us  [swapped(): return lax.ppermute(value, axis, [(i, i ^ mask) for i in range(count)])]
    ppermute x1 -> x2, waiting for transfers between devices: 3.57 us -> 9.27 us  [around_row(): far[d - 1].append(lax.ppermute(middle[part], 'row', pairs))]
    ppermute x4 -> x5, waiting for transfers between devices: 8.58 us -> 14.2 us  [rotated(): lax.ppermute(value, axis, [(i, (i + steps) % count) for i in range(count)])]
    ppermute x37, starting transfers between devices: 30.2 us -> 33.7 us  [swapped(): return lax.ppermute(value, axis, [(i, i ^ mask) for i in range(count)])]
    ppermute x3, waiting for transfers between devices: 2.59 us -> 0.01 us  [shards(): dealt.append(lax.ppermute(value, 'col', [(0, j)]) if j else value)]
    ppermute x1, starting transfers between devices: 3.5 us -> 1.58 us  [around_row(): lax.ppermute(value, 'row', [(i, i + d) for i in range(count - d)])]
    ppermute x4 -> x5, starting transfers between devices: 8.39 us -> 10.1 us  [rotated(): lax.ppermute(value, axis, [(i, (i + steps) % count) for i in range(count)])]
    ppermute x1, waiting for transfers between devices: 0.01 us -> 1.71 us  [around_row(): lax.ppermute(value, 'row', [(i + d, i) for i in range(count - d)])]
  transfers between devices with their start and end apart: 49 -> 51, of which waited for: 14 -> 19; matrix products, arithmetic and copies ran while one was open for 0% -> 0% of each run, Pallas kernels for 10% -> 10%
where the time goes in v7:
time: 160 us
  waiting for transfers between devices  70.7 us (44%)
  starting transfers between devices  62.4 us (39%)
  Pallas kernels  23.1 us (14%)
  local copies, waits for them, and re-layouts  3.22 us (2%)
    ppermute x37, waiting for transfers between devices, swapped(): return lax.ppermute(value, axis, [(i, i ^ mask) for i in range(count)])  45.5 us
    ppermute x37, starting transfers between devices, swapped(): return lax.ppermute(value, axis, [(i, i ^ mask) for i in range(count)])  33.7 us
    ppermute x5, waiting for transfers between devices, rotated(): lax.ppermute(value, axis, [(i, (i + steps) % count) for i in range(count)])  14.2 us
    ppermute x5, starting transfers between devices, rotated(): lax.ppermute(value, axis, [(i, (i + steps) % count) for i in range(count)])  10.1 us
    ppermute x2, waiting for transfers between devices, around_row(): far[d - 1].append(lax.ppermute(middle[part], 'row', pairs))  9.27 us
    ppermute x3, starting transfers between devices, shards(): dealt.append(lax.ppermute(value, 'col', [(0, j)]) if j else value)  8.15 us
    pallas_call x1, Pallas kernels, finish(): pl.pallas_call(body, in_specs=[SMEM] + [ANY] * (2 * count) + [VMEM] * 3,...  5.12 us
    ppermute x2, starting transfers between devices, shifted(): return lax.ppermute(value, axis, [(i, i + 1) for i in range(count - 1)])  5.01 us
  transfers between devices with their start and end apart: 51, of which 19 were waited for; matrix products, arithmetic and copies ran while one was open for 0% of the time, Pallas kernels for 10%

profile of v7, /device:TPU:0, one launch (start us, length us, event | category | flops | bytes accessed | tf_op | source)
XLA Modules:
  0.0 159.8 jit_solution(6070598445090110935)
XLA Ops:
  0.0 0.7 copy-done.5
  0.7 1.3 lookup_table.1.sc.refs_0_
  2.0 1.3 copy-done
  3.3 1.2 copy-done.4
  4.5 0.9 cut_slices.1
  5.4 3.1 %collective-permute-start.10 = (f32[512,128]{1,0:T(8,128)S(1)}, f32[512,128]{1,0:T(8,128)S(1)}, u32[]{:S(2)}, u32[]{:S(2)}) collective-permute-start(f32[512,128]{1,0:T(8,128)S(1)} %get-tuple-element.36), channel_id=1, source_target_pairs={{0,2},{1,3},{2,0},{3,1},{4,6},{5,7},{6,4},{7,5},{8,10},{9,11},{10,... | collective-permute-start | bytes 786440 | tf_op jit(solution)/shard_map/ppermute | solution.py:61
  8.5 1.4 collective-permute-start.11
  10.0 1.9 %collective-permute-start = (f32[128,1024]{1,0:T(8,128)S(1)}, f32[128,1024]{1,0:T(8,128)S(1)}, u32[]{:S(2)}, u32[]{:S(2)}) collective-permute-start(f32[128,1024]{1,0:T(8,128)S(1)} %bitcast.6), channel_id=1, source_target_pairs={{0,1},{1,0},{2,3},{3,2},{4,5},{5,4},{6,7},{7,6},{8,9},{9,8},{10,11... | collective-permute-start | bytes 1572872 | tf_op jit(solution)/shard_map/ppermute | solution.py:61
  12.0 2.7 %collective-permute-start.4 = (f32[64,1024]{1,0:T(8,128)S(1)}, f32[64,1024]{1,0:T(8,128)S(1)}, u32[]{:S(2)}, u32[]{:S(2)}) collective-permute-start(f32[64,1024]{1,0:T(8,128)S(1)} %get-tuple-element.64), channel_id=1, source_target_pairs={{0,8},{4,12},{8,0},{12,4},{1,9},{5,13},{9,1},{13,5},{2,10},{6,14},... | collective-permute-start | bytes 786440 | tf_op jit(solution)/shard_map/ppermute | solution.py:56
  14.6 5.8 %collective-permute-done.10.refs_14_ = f32[512,128]{1,0:T(8,128)S(1)} collective-permute-done((f32[512,128]{1,0:T(8,128)S(1)}, f32[512,128]{1,0:T(8,128)S(1)}, u32[]{:S(2)}, u32[]{:S(2)}) %collective-permute-start.10) | collective-permute-done | bytes 262176 | tf_op jit(solution)/shard_map/ppermute | solution.py:61
  20.4 2.8 %collective-permute-start.5 = (f32[64,1024]{1,0:T(8,128)S(1)}, f32[64,1024]{1,0:T(8,128)S(1)}, u32[]{:S(2)}, u32[]{:S(2)}) collective-permute-start(f32[64,1024]{1,0:T(8,128)S(1)} %get-tuple-element.63), channel_id=1, source_target_pairs={{0,8},{4,12},{8,0},{12,4},{1,9},{5,13},{9,1},{13,5},{2,10},{6,14},... | collective-permute-start | bytes 786440 | tf_op jit(solution)/shard_map/ppermute | solution.py:56
  23.2 1.5 collective-permute-start.1
  24.7 1.4 collective-permute-start.2
  26.1 6.0 %collective-permute-done.4.refs_7_ = f32[64,1024]{1,0:T(8,128)S(1)} collective-permute-done((f32[64,1024]{1,0:T(8,128)S(1)}, f32[64,1024]{1,0:T(8,128)S(1)}, u32[]{:S(2)}, u32[]{:S(2)}) %collective-permute-start.4) | collective-permute-done | bytes 262176 | tf_op jit(solution)/shard_map/ppermute | solution.py:56
  32.2 1.6 collective-permute-start.3
  33.8 2.9 %collective-permute-done.5.refs_8_ = f32[64,1024]{1,0:T(8,128)S(1)} collective-permute-done((f32[64,1024]{1,0:T(8,128)S(1)}, f32[64,1024]{1,0:T(8,128)S(1)}, u32[]{:S(2)}, u32[]{:S(2)}) %collective-permute-start.5) | collective-permute-done | bytes 262176 | tf_op jit(solution)/shard_map/ppermute | solution.py:56
  36.7 1.3 collective-permute-start.8
  38.0 1.3 collective-permute-start.6
  39.3 7.6 %collective-permute-done.1.refs_3_ = f32[128,1024]{1,0:T(8,128)S(1)} collective-permute-done((f32[128,1024]{1,0:T(8,128)S(1)}, f32[128,1024]{1,0:T(8,128)S(1)}, u32[]{:S(2)}, u32[]{:S(2)}) %collective-permute-start.1) | collective-permute-done | bytes 524320 | tf_op jit(solution)/shard_map/ppermute | solution.py:61
  47.0 1.3 collective-permute-start.7
  48.3 3.4 %collective-permute-start.20 = (f32[96,512]{1,0:T(8,128)S(1)}, f32[96,512]{1,0:T(8,128)S(1)}, u32[]{:S(2)}, u32[]{:S(2)}) collective-permute-start(f32[96,512]{1,0:T(8,128)S(1)} %get-tuple-element.48), channel_id=1, source_target_pairs={{0,1},{4,5},{8,9},{12,13},{16,17},{20,21},{24,25},{28,29}} | collective-permute-start | bytes 589832 | tf_op jit(solution)/shard_map/ppermute | solution.py:620
  51.7 1.7 %collective-permute-done.8.refs_11_ = f32[128,1024]{1,0:T(8,128)S(1)} collective-permute-done((f32[128,1024]{1,0:T(8,128)S(1)}, f32[128,1024]{1,0:T(8,128)S(1)}, u32[]{:S(2)}, u32[]{:S(2)}) %collective-permute-start.8) | collective-permute-done | bytes 524320 | tf_op jit(solution)/shard_map/ppermute | solution.py:188
  53.4 5.6 %collective-permute-done.6.refs_9_ = f32[64,1024]{1,0:T(8,128)S(1)} collective-permute-done((f32[64,1024]{1,0:T(8,128)S(1)}, f32[64,1024]{1,0:T(8,128)S(1)}, u32[]{:S(2)}, u32[]{:S(2)}) %collective-permute-start.6) | collective-permute-done | bytes 262176 | tf_op jit(solution)/shard_map/ppermute | solution.py:192
  59.0 3.7 %collective-permute-done.7.refs_10_ = f32[64,1024]{1,0:T(8,128)S(1)} collective-permute-done((f32[64,1024]{1,0:T(8,128)S(1)}, f32[64,1024]{1,0:T(8,128)S(1)}, u32[]{:S(2)}, u32[]{:S(2)}) %collective-permute-start.7) | collective-permute-done | bytes 262176 | tf_op jit(solution)/shard_map/ppermute | solution.py:192
  62.7 3.6 %slice_products.1 = (f32[512,128]{1,0:T(8,128)S(1)}, f32[512,128]{1,0:T(8,128)S(1)}, f32[512,128]{1,0:T(8,128)S(1)}, f32[512,128]{1,0:T(8,128)S(1)}, f32[256,128]{1,0:T(8,128)S(1)}, /*index=5*/f32[3,256,128]{2,1,0:T(8,128)S(1)}) custom-call(s32[35]{0:T(128)S(1)} %lookup_table.1.sc.refs_0_, f32[128,1024]{1,0:T(8,128)S(1)} %bitcast.11, ...), custom_call_target="tpu_custom_call" | custom-call | tf_op jit(solution)/shard_map/slice_products/pallas_call | solution.py:250
  66.3 1.6 collective-permute-start.12
  67.8 3.4 %collective-permute-start.21 = (f32[96,512]{1,0:T(8,128)S(1)}, f32[96,512]{1,0:T(8,128)S(1)}, u32[]{:S(2)}, u32[]{:S(2)}) collective-permute-start(f32[96,512]{1,0:T(8,128)S(1)} %get-tuple-element.49), channel_id=1, source_target_pairs={{0,2},{4,6},{8,10},{12,14},{16,18},{20,22},{24,26},{28,30}} | collective-permute-start | bytes 589832 | tf_op jit(solution)/shard_map/ppermute | solution.py:620
  71.3 1.3 collective-permute-start.22
  72.6 0.8 place_rows.1
  73.6 3.4 %collective-permute-start.15 = (f32[2,96,128]{2,1,0:T(8,128)S(1)}, f32[2,96,128]{2,1,0:T(8,128)S(1)}, u32[]{:S(2)}, u32[]{:S(2)}) collective-permute-start(f32[2,96,128]{2,1,0:T(8,128)S(1)} %get-tuple-element.46), channel_id=1, source_target_pairs={{0,3},{1,2},{2,1},{3,0},{4,7},{5,6},{6,5},{7,4},{8,11},{9,10},{10,... | collective-permute-start | bytes 294920 | tf_op jit(solution)/shard_map/ppermute | solution.py:61
  77.0 1.1 collective-permute-done.13.refs_2_
  78.2 0.4 collective-permute-start.18
  78.7 1.0 collective-permute-done.15.refs_4_
  79.6 2.1 %collective-permute-start.33 = (f32[512,128]{1,0:T(8,128)S(1)}, f32[512,128]{1,0:T(8,128)S(1)}, u32[]{:S(2)}, u32[]{:S(2)}) collective-permute-start(f32[512,128]{1,0:T(8,128)S(1)} %get-tuple-element.39.refs_2_), channel_id=1, source_target_pairs={{0,1},{1,0},{2,3},{3,2},{4,5},{5,4},{6,7},{7,6},{8,9},{9,8},{10,11... | collective-permute-start | bytes 786440 | tf_op jit(solution)/shard_map/ppermute | solution.py:61
  81.7 1.4 collective-permute-start.34
  83.3 3.4 %collective-permute-start.36 = (f32[3,256,128]{2,1,0:T(8,128)S(1)}, f32[3,256,128]{2,1,0:T(8,128)S(1)}, u32[]{:S(2)}, u32[]{:S(2)}) collective-permute-start(f32[3,256,128]{2,1,0:T(8,128)S(1)} %get-tuple-element.55), channel_id=1, source_target_pairs={{0,4},{4,8},{8,12},{1,5},{5,9},{9,13},{2,6},{6,10},{10,14},{3,7},{... | collective-permute-start | bytes 1179656 | tf_op jit(solution)/shard_map/ppermute | solution.py:66
  86.7 2.1 %factor_slice.1.refs_1_ = f32[96,512]{1,0:T(8,128)S(1)} custom-call(s32[35]{0:T(128)S(1)} %lookup_table.1.sc.refs_0_, f32[2,96,128]{2,1,0:T(8,128)S(1)} %get-tuple-element.43.refs_1_, f32[2,96,128]{2,1,0:T(8,128)S(1)} %collective-permute-done.13.refs_2_, f32[2,96,128]{2,1,0:T(8,128)S(1)} %collective-permute-done.14.refs_3_, ...), custom_call_target="tpu_custom_call" | custom-call | tf_op jit(solution)/shard_map/factor_slice/pallas_call | solution.py:408
  88.9 2.0 %collective-permute-start.48 = (f32[96,512]{1,0:T(8,128)S(1)}, f32[96,512]{1,0:T(8,128)S(1)}, u32[]{:S(2)}, u32[]{:S(2)}) collective-permute-start(f32[96,512]{1,0:T(8,128)S(1)} %factor_slice.1.refs_1_), channel_id=1, source_target_pairs={{0,1},{1,0},{2,3},{3,2},{4,5},{5,4},{6,7},{7,6},{8,9},{9,8},{10,11... | collective-permute-start | bytes 589832 | tf_op jit(solution)/shard_map/ppermute | solution.py:61
  90.9 4.5 %collective-permute-done.34.refs_4_ = f32[512,128]{1,0:T(8,128)S(1)} collective-permute-done((f32[512,128]{1,0:T(8,128)S(1)}, f32[512,128]{1,0:T(8,128)S(1)}, u32[]{:S(2)}, u32[]{:S(2)}) %collective-permute-start.34) | collective-permute-done | bytes 262176 | tf_op jit(solution)/shard_map/ppermute | solution.py:61
  95.4 1.7 %collective-permute-start.49 = (f32[96,512]{1,0:T(8,128)S(1)}, f32[96,512]{1,0:T(8,128)S(1)}, u32[]{:S(2)}, u32[]{:S(2)}) collective-permute-start(f32[96,512]{1,0:T(8,128)S(1)} %factor_slice.1.refs_1_), channel_id=1, source_target_pairs={{0,2},{1,3},{2,0},{3,1},{4,6},{5,7},{6,4},{7,5},{8,10},{9,11},{10,... | collective-permute-start | bytes 589832 | tf_op jit(solution)/shard_map/ppermute | solution.py:61
  97.2 1.6 %collective-permute-start.50 = (f32[96,512]{1,0:T(8,128)S(1)}, f32[96,512]{1,0:T(8,128)S(1)}, u32[]{:S(2)}, u32[]{:S(2)}) collective-permute-start(f32[96,512]{1,0:T(8,128)S(1)} %factor_slice.1.refs_1_), channel_id=1, source_target_pairs={{0,3},{1,2},{2,1},{3,0},{4,7},{5,6},{6,5},{7,4},{8,11},{9,10},{10,... | collective-permute-start | bytes 589832 | tf_op jit(solution)/shard_map/ppermute | solution.py:61
  98.8 0.8 collective-permute-start.23
  99.6 2.0 %collective-permute-start.24 = (f32[96,512]{1,0:T(8,128)S(1)}, f32[96,512]{1,0:T(8,128)S(1)}, u32[]{:S(2)}, u32[]{:S(2)}) collective-permute-start(f32[96,512]{1,0:T(8,128)S(1)} %factor_slice.1.refs_1_), channel_id=1, source_target_pairs={{0,8},{4,12},{8,0},{12,4},{1,9},{5,13},{9,1},{13,5},{2,10},{6,14},... | collective-permute-start | bytes 589832 | tf_op jit(solution)/shard_map/ppermute | solution.py:56
  101.6 2.2 %pack_halo.1 = (f32[1024,128]{1,0:T(8,128)S(1)}, f32[1024,128]{1,0:T(8,128)S(1)}, f32[1024,128]{1,0:T(8,128)S(1)}, f32[1024,128]{1,0:T(8,128)S(1)}) custom-call(s32[35]{0:T(128)S(1)} %lookup_table.1.sc.refs_0_, f32[512,128]{1,0:T(8,128)S(1)} %get-tuple-element.38.refs_1_.refs_2_, f32[512,128]{1,0:T(8,128)S(1)} %get-tuple-element.39.refs_2_, ...), custom_call_target="tpu_custom_call" | custom-call | tf_op jit(solution)/shard_map/pack_halo/pallas_call | solution.py:297
  103.9 3.1 %collective-permute-done.49.refs_3_ = f32[96,512]{1,0:T(8,128)S(1)} collective-permute-done((f32[96,512]{1,0:T(8,128)S(1)}, f32[96,512]{1,0:T(8,128)S(1)}, u32[]{:S(2)}, u32[]{:S(2)}) %collective-permute-start.49) | collective-permute-done | bytes 196640 | tf_op jit(solution)/shard_map/ppermute | solution.py:61
  107.0 0.6 collective-permute-start.37
  107.6 1.2 collective-permute-start.38
  108.7 1.8 %collective-permute-start.25 = (f32[96,512]{1,0:T(8,128)S(1)}, f32[96,512]{1,0:T(8,128)S(1)}, u32[]{:S(2)}, u32[]{:S(2)}) collective-permute-start(f32[96,512]{1,0:T(8,128)S(1)} %factor_slice.1.refs_1_), channel_id=1, source_target_pairs={{0,12},{4,0},{8,4},{12,8},{1,13},{5,1},{9,5},{13,9},{2,14},{6,2},{... | collective-permute-start | bytes 589832 | tf_op jit(solution)/shard_map/ppermute | solution.py:56
  110.5 4.1 %collective-permute-done.24.refs_3_ = f32[96,512]{1,0:T(8,128)S(1)} collective-permute-done((f32[96,512]{1,0:T(8,128)S(1)}, f32[96,512]{1,0:T(8,128)S(1)}, u32[]{:S(2)}, u32[]{:S(2)}) %collective-permute-start.24) | collective-permute-done | bytes 196640 | tf_op jit(solution)/shard_map/ppermute | solution.py:56
  114.6 2.6 %collective-permute-start.39 = (f32[1024,128]{1,0:T(8,128)S(1)}, f32[1024,128]{1,0:T(8,128)S(1)}, u32[]{:S(2)}, u32[]{:S(2)}) collective-permute-start(f32[1024,128]{1,0:T(8,128)S(1)} %get-tuple-element.59), channel_id=1, source_target_pairs={{0,3},{1,2},{2,1},{3,0},{4,7},{5,6},{6,5},{7,4},{8,11},{9,10},{10,... | collective-permute-start | bytes 1572872 | tf_op jit(solution)/shard_map/ppermute | solution.py:61
  117.2 1.1 collective-permute-done.25.refs_4_
  118.4 1.7 %pick_for_cols.1 = (f32[96,512]{1,0:T(8,128)S(1)}, f32[96,512]{1,0:T(8,128)S(1)}, f32[96,512]{1,0:T(8,128)S(1)}, f32[96,512]{1,0:T(8,128)S(1)}) custom-call(s32[35]{0:T(128)S(1)} %lookup_table.1.sc.refs_0_, f32[96,512]{1,0:T(8,128)S(1)} %factor_slice.1.refs_1_, f32[96,512]{1,0:T(8,128)S(1)} %collective-permute-done.23.refs_2_, ...), custom_call_target="tpu_custom_call" | custom-call | tf_op jit(solution)/shard_map/pick_for_cols/pallas_call | solution.py:321
  120.1 1.9 %collective-permute-start.26 = (f32[96,512]{1,0:T(8,128)S(1)}, f32[96,512]{1,0:T(8,128)S(1)}, u32[]{:S(2)}, u32[]{:S(2)}) collective-permute-start(f32[96,512]{1,0:T(8,128)S(1)} %get-tuple-element.52), channel_id=1, source_target_pairs={{0,1},{1,0},{2,3},{3,2},{4,5},{5,4},{6,7},{7,6},{8,9},{9,8},{10,11... | collective-permute-start | bytes 589832 | tf_op jit(solution)/shard_map/ppermute | solution.py:61
  122.5 7.2 %collective-permute-done.38.refs_8_ = f32[1024,128]{1,0:T(8,128)S(1)} collective-permute-done((f32[1024,128]{1,0:T(8,128)S(1)}, f32[1024,128]{1,0:T(8,128)S(1)}, u32[]{:S(2)}, u32[]{:S(2)}) %collective-permute-start.38) | collective-permute-done | bytes 524320 | tf_op jit(solution)/shard_map/ppermute | solution.py:61
  129.7 6.2 %collective-permute-done.26.refs_2_ = f32[96,512]{1,0:T(8,128)S(1)} collective-permute-done((f32[96,512]{1,0:T(8,128)S(1)}, f32[96,512]{1,0:T(8,128)S(1)}, u32[]{:S(2)}, u32[]{:S(2)}) %collective-permute-start.26) | collective-permute-done | bytes 196640 | tf_op jit(solution)/shard_map/ppermute | solution.py:61
  135.9 1.7 %collective-permute-start.27 = (f32[96,512]{1,0:T(8,128)S(1)}, f32[96,512]{1,0:T(8,128)S(1)}, u32[]{:S(2)}, u32[]{:S(2)}) collective-permute-start(f32[96,512]{1,0:T(8,128)S(1)} %get-tuple-element.53), channel_id=1, source_target_pairs={{0,2},{1,3},{2,0},{3,1},{4,6},{5,7},{6,4},{7,5},{8,10},{9,11},{10,... | collective-permute-start | bytes 589832 | tf_op jit(solution)/shard_map/ppermute | solution.py:61
  137.6 4.0 %collective-permute-done.27.refs_3_ = f32[96,512]{1,0:T(8,128)S(1)} collective-permute-done((f32[96,512]{1,0:T(8,128)S(1)}, f32[96,512]{1,0:T(8,128)S(1)}, u32[]{:S(2)}, u32[]{:S(2)}) %collective-permute-start.27) | collective-permute-done | bytes 196640 | tf_op jit(solution)/shard_map/ppermute | solution.py:61
  141.6 1.7 %collective-permute-start.28 = (f32[96,512]{1,0:T(8,128)S(1)}, f32[96,512]{1,0:T(8,128)S(1)}, u32[]{:S(2)}, u32[]{:S(2)}) collective-permute-start(f32[96,512]{1,0:T(8,128)S(1)} %get-tuple-element.54), channel_id=1, source_target_pairs={{0,3},{1,2},{2,1},{3,0},{4,7},{5,6},{6,5},{7,4},{8,11},{9,10},{10,... | collective-permute-start | bytes 589832 | tf_op jit(solution)/shard_map/ppermute | solution.py:61
  143.3 4.9 %collective-permute-done.28.refs_4_ = f32[96,512]{1,0:T(8,128)S(1)} collective-permute-done((f32[96,512]{1,0:T(8,128)S(1)}, f32[96,512]{1,0:T(8,128)S(1)}, u32[]{:S(2)}, u32[]{:S(2)}) %collective-permute-start.28) | collective-permute-done | bytes 196640 | tf_op jit(solution)/shard_map/ppermute | solution.py:61
  148.2 0.5 collective-permute-start.30
  148.8 0.4 collective-permute-start.32
  149.2 1.7 %lay_rows.1 = (f32[384,512]{1,0:T(8,128)S(1)}, bf16[384,512]{1,0:T(8,128)(2,1)S(1)}, bf16[384,512]{1,0:T(8,128)(2,1)S(1)}) custom-call(s32[35]{0:T(128)S(1)} %lookup_table.1.sc.refs_0_, f32[96,512]{1,0:T(8,128)S(1)} %factor_slice.1.refs_1_, f32[96,512]{1,0:T(8,128)S(1)} %collective-permute-done.48.refs_2_, f32[96,512]{1,0:T(8,128)S(1)} %collective-permute-done.49.refs_3_, ...), custom_call_target="tpu_custom_call" | custom-call | tf_op jit(solution)/shard_map/lay_rows/pallas_call | solution.py:437
  151.0 3.6 %assemble.1.refs_9_ = f32[384,768]{1,0:T(8,128)S(1)} custom-call(s32[35]{0:T(128)S(1)} %lookup_table.1.sc.refs_0_, f32[384,768]{1,0:T(8,128)S(1)} %copy-done.1, f32[512,128]{1,0:T(8,128)S(1)} %get-tuple-element.38.refs_1_.refs_2_, f32[512,128]{1,0:T(8,128)S(1)} %collective-permute-done.33.refs_3_, f32[512,128]{1,0:T(8,128)S(1)} %collective-permute-done.34.refs_4_, ...), custom_call_target="tpu_custom_call" | custom-call | tf_op jit(solution)/shard_map/assemble/pallas_call | solution.py:527
  154.6 5.1 %finish.1 = f32[384,768]{1,0:T(8,128)} custom-call(s32[35]{0:T(128)S(1)} %lookup_table.1.sc.refs_0_, f32[96,512]{1,0:T(8,128)S(1)} %get-tuple-element.51.refs_1_, f32[96,512]{1,0:T(8,128)S(1)} %collective-permute-done.26.refs_2_, f32[96,512]{1,0:T(8,128)S(1)} %collective-permute-done.27.refs_3_, f32[96,512]{1,0:T(8,128)S(1)} %collective-permute-done.28.refs_4_, ...), custom_call_target="tpu_custom_call" | custom-call | tf_op jit(solution)/shard_map/finish/pallas_call | solution.py:572
  (61 shorter events, 1.3 us)
Async XLA Ops:
  0.0 0.7 copy-start.5
  2.0 1.3 copy-start
  3.3 1.2 copy-start.4
  4.5 5.5 %copy-start.2 = (f32[1,128,1024]{2,1,0:T(8,128)S(1)}, f32[1,128,1024]{2,1,0:T(8,128)}, u32[]{:S(2)}) copy-start(f32[1,128,1024]{2,1,0:T(8,128)} %param.6) | copy-start | bytes 1572868
  5.4 15.0 %collective-permute-start.10 = (f32[512,128]{1,0:T(8,128)S(1)}, f32[512,128]{1,0:T(8,128)S(1)}, u32[]{:S(2)}, u32[]{:S(2)}) collective-permute-start(f32[512,128]{1,0:T(8,128)S(1)} %get-tuple-element.36), channel_id=1, source_target_pairs={{0,2},{1,3},{2,0},{3,1},{4,6},{5,7},{6,4},{7,5},{8,10},{9,11},{10,... | collective-permute-start | bytes 786440 | tf_op jit(solution)/shard_map/ppermute | solution.py:61
  8.5 14.7 %collective-permute-start.11 = (f32[512,128]{1,0:T(8,128)S(1)}, f32[512,128]{1,0:T(8,128)S(1)}, u32[]{:S(2)}, u32[]{:S(2)}) collective-permute-start(f32[512,128]{1,0:T(8,128)S(1)} %get-tuple-element.37), channel_id=1, source_target_pairs={{0,3},{1,2},{2,1},{3,0},{4,7},{5,6},{6,5},{7,4},{8,11},{9,10},{10,... | collective-permute-start | bytes 786440 | tf_op jit(solution)/shard_map/ppermute | solution.py:61
  9.9 14.8 %collective-permute-start.9 = (f32[512,128]{1,0:T(8,128)S(1)}, f32[512,128]{1,0:T(8,128)S(1)}, u32[]{:S(2)}, u32[]{:S(2)}) collective-permute-start(f32[512,128]{1,0:T(8,128)S(1)} %get-tuple-element.35), channel_id=1, source_target_pairs={{0,1},{1,0},{2,3},{3,2},{4,5},{5,4},{6,7},{7,6},{8,9},{9,8},{10,11... | collective-permute-start | bytes 786440 | tf_op jit(solution)/shard_map/ppermute | solution.py:61
  10.0 28.0 %collective-permute-start = (f32[128,1024]{1,0:T(8,128)S(1)}, f32[128,1024]{1,0:T(8,128)S(1)}, u32[]{:S(2)}, u32[]{:S(2)}) collective-permute-start(f32[128,1024]{1,0:T(8,128)S(1)} %bitcast.6), channel_id=1, source_target_pairs={{0,1},{1,0},{2,3},{3,2},{4,5},{5,4},{6,7},{7,6},{8,9},{9,8},{10,11... | collective-permute-start | bytes 1572872 | tf_op jit(solution)/shard_map/ppermute | solution.py:61
  12.0 20.2 %collective-permute-start.4 = (f32[64,1024]{1,0:T(8,128)S(1)}, f32[64,1024]{1,0:T(8,128)S(1)}, u32[]{:S(2)}, u32[]{:S(2)}) collective-permute-start(f32[64,1024]{1,0:T(8,128)S(1)} %get-tuple-element.64), channel_id=1, source_target_pairs={{0,8},{4,12},{8,0},{12,4},{1,9},{5,13},{9,1},{13,5},{2,10},{6,14},... | collective-permute-start | bytes 786440 | tf_op jit(solution)/shard_map/ppermute | solution.py:56
  20.4 16.3 %collective-permute-start.5 = (f32[64,1024]{1,0:T(8,128)S(1)}, f32[64,1024]{1,0:T(8,128)S(1)}, u32[]{:S(2)}, u32[]{:S(2)}) collective-permute-start(f32[64,1024]{1,0:T(8,128)S(1)} %get-tuple-element.63), channel_id=1, source_target_pairs={{0,8},{4,12},{8,0},{12,4},{1,9},{5,13},{9,1},{13,5},{2,10},{6,14},... | collective-permute-start | bytes 786440 | tf_op jit(solution)/shard_map/ppermute | solution.py:56
  23.2 23.8 %collective-permute-start.1 = (f32[128,1024]{1,0:T(8,128)S(1)}, f32[128,1024]{1,0:T(8,128)S(1)}, u32[]{:S(2)}, u32[]{:S(2)}) collective-permute-start(f32[128,1024]{1,0:T(8,128)S(1)} %bitcast.7), channel_id=1, source_target_pairs={{0,2},{1,3},{2,0},{3,1},{4,6},{5,7},{6,4},{7,5},{8,10},{9,11},{10,... | collective-permute-start | bytes 1572872 | tf_op jit(solution)/shard_map/ppermute | solution.py:61
  24.7 23.5 %collective-permute-start.2 = (f32[128,1024]{1,0:T(8,128)S(1)}, f32[128,1024]{1,0:T(8,128)S(1)}, u32[]{:S(2)}, u32[]{:S(2)}) collective-permute-start(f32[128,1024]{1,0:T(8,128)S(1)} %bitcast.8), channel_id=1, source_target_pairs={{0,3},{1,2},{2,1},{3,0},{4,7},{5,6},{6,5},{7,4},{8,11},{9,10},{10,... | collective-permute-start | bytes 1572872 | tf_op jit(solution)/shard_map/ppermute | solution.py:61
  32.2 19.5 %collective-permute-start.3 = (f32[128,1024]{1,0:T(8,128)S(1)}, f32[128,1024]{1,0:T(8,128)S(1)}, u32[]{:S(2)}, u32[]{:S(2)}) collective-permute-start(f32[128,1024]{1,0:T(8,128)S(1)} %bitcast.9), channel_id=1, source_target_pairs={{0,4},{4,8},{8,12},{1,5},{5,9},{9,13},{2,6},{6,10},{10,14},{3,7},{... | collective-permute-start | bytes 1572872 | tf_op jit(solution)/shard_map/ppermute | solution.py:187
  36.7 16.7 %collective-permute-start.8 = (f32[128,1024]{1,0:T(8,128)S(1)}, f32[128,1024]{1,0:T(8,128)S(1)}, u32[]{:S(2)}, u32[]{:S(2)}) collective-permute-start(f32[128,1024]{1,0:T(8,128)S(1)} %bitcast.10), channel_id=1, source_target_pairs={{4,0},{8,4},{12,8},{5,1},{9,5},{13,9},{6,2},{10,6},{14,10},{7,3},{... | collective-permute-start | bytes 1572872 | tf_op jit(solution)/shard_map/ppermute | solution.py:188
  38.0 21.0 %collective-permute-start.6 = (f32[64,1024]{1,0:T(8,128)S(1)}, f32[64,1024]{1,0:T(8,128)S(1)}, u32[]{:S(2)}, u32[]{:S(2)}) collective-permute-start(f32[64,1024]{1,0:T(8,128)S(1)} %collective-permute-done.4.refs_7_), channel_id=1, source_target_pairs={{8,12},{4,0},{9,13},{5,1},{10,14},{6,2},{11,15},{7,3},{24,28},{20,... | collective-permute-start | bytes 786440 | tf_op jit(solution)/shard_map/ppermute | solution.py:192
  47.0 15.7 %collective-permute-start.7 = (f32[64,1024]{1,0:T(8,128)S(1)}, f32[64,1024]{1,0:T(8,128)S(1)}, u32[]{:S(2)}, u32[]{:S(2)}) collective-permute-start(f32[64,1024]{1,0:T(8,128)S(1)} %collective-permute-done.5.refs_8_), channel_id=1, source_target_pairs={{8,12},{4,0},{9,13},{5,1},{10,14},{6,2},{11,15},{7,3},{24,28},{20,... | collective-permute-start | bytes 786440 | tf_op jit(solution)/shard_map/ppermute | solution.py:192
  48.3 25.4 %collective-permute-start.20 = (f32[96,512]{1,0:T(8,128)S(1)}, f32[96,512]{1,0:T(8,128)S(1)}, u32[]{:S(2)}, u32[]{:S(2)}) collective-permute-start(f32[96,512]{1,0:T(8,128)S(1)} %get-tuple-element.48), channel_id=1, source_target_pairs={{0,1},{4,5},{8,9},{12,13},{16,17},{20,21},{24,25},{28,29}} | collective-permute-start | bytes 589832 | tf_op jit(solution)/shard_map/ppermute | solution.py:620
  66.2 20.5 %copy-start.3 = (f32[512,512]{1,0:T(8,128)S(1)}, f32[512,512]{1,0:T(8,128)}, u32[]{:S(2)}) copy-start(f32[512,512]{1,0:T(8,128)} %refs_13_.1) | copy-start | bytes 3145732
  66.3 6.4 %collective-permute-start.12 = (f32[256,128]{1,0:T(8,128)S(1)}, f32[256,128]{1,0:T(8,128)S(1)}, u32[]{:S(2)}, u32[]{:S(2)}) collective-permute-start(f32[256,128]{1,0:T(8,128)S(1)} %get-tuple-element.42), channel_id=1, source_target_pairs={{0,4},{4,8},{8,12},{1,5},{5,9},{9,13},{2,6},{6,10},{10,14},{3,7},{... | collective-permute-start | bytes 393224 | tf_op jit(solution)/shard_map/ppermute | solution.py:66
  67.8 9.2 %collective-permute-start.21 = (f32[96,512]{1,0:T(8,128)S(1)}, f32[96,512]{1,0:T(8,128)S(1)}, u32[]{:S(2)}, u32[]{:S(2)}) collective-permute-start(f32[96,512]{1,0:T(8,128)S(1)} %get-tuple-element.49), channel_id=1, source_target_pairs={{0,2},{4,6},{8,10},{12,14},{16,18},{20,22},{24,26},{28,30}} | collective-permute-start | bytes 589832 | tf_op jit(solution)/shard_map/ppermute | solution.py:620
  71.3 8.3 %collective-permute-start.22 = (f32[96,512]{1,0:T(8,128)S(1)}, f32[96,512]{1,0:T(8,128)S(1)}, u32[]{:S(2)}, u32[]{:S(2)}) collective-permute-start(f32[96,512]{1,0:T(8,128)S(1)} %get-tuple-element.50), channel_id=1, source_target_pairs={{0,3},{4,7},{8,11},{12,15},{16,19},{20,23},{24,27},{28,31}} | collective-permute-start | bytes 589832 | tf_op jit(solution)/shard_map/ppermute | solution.py:620
  73.5 4.7 %collective-permute-start.13 = (f32[2,96,128]{2,1,0:T(8,128)S(1)}, f32[2,96,128]{2,1,0:T(8,128)S(1)}, u32[]{:S(2)}, u32[]{:S(2)}) collective-permute-start(f32[2,96,128]{2,1,0:T(8,128)S(1)} %get-tuple-element.44), channel_id=1, source_target_pairs={{0,1},{1,0},{2,3},{3,2},{4,5},{5,4},{6,7},{7,6},{8,9},{9,8},{10,11... | collective-permute-start | bytes 294920 | tf_op jit(solution)/shard_map/ppermute | solution.py:61
  73.5 4.7 %collective-permute-start.14 = (f32[2,96,128]{2,1,0:T(8,128)S(1)}, f32[2,96,128]{2,1,0:T(8,128)S(1)}, u32[]{:S(2)}, u32[]{:S(2)}) collective-permute-start(f32[2,96,128]{2,1,0:T(8,128)S(1)} %get-tuple-element.45), channel_id=1, source_target_pairs={{0,2},{1,3},{2,0},{3,1},{4,6},{5,7},{6,4},{7,5},{8,10},{9,11},{10,... | collective-permute-start | bytes 294920 | tf_op jit(solution)/shard_map/ppermute | solution.py:61
  73.6 6.0 %collective-permute-start.15 = (f32[2,96,128]{2,1,0:T(8,128)S(1)}, f32[2,96,128]{2,1,0:T(8,128)S(1)}, u32[]{:S(2)}, u32[]{:S(2)}) collective-permute-start(f32[2,96,128]{2,1,0:T(8,128)S(1)} %get-tuple-element.46), channel_id=1, source_target_pairs={{0,3},{1,2},{2,1},{3,0},{4,7},{5,6},{6,5},{7,4},{8,11},{9,10},{10,... | collective-permute-start | bytes 294920 | tf_op jit(solution)/shard_map/ppermute | solution.py:61
  77.0 4.7 %collective-permute-start.16 = (f32[2,96,128]{2,1,0:T(8,128)S(1)}, f32[2,96,128]{2,1,0:T(8,128)S(1)}, u32[]{:S(2)}, u32[]{:S(2)}) collective-permute-start(f32[2,96,128]{2,1,0:T(8,128)S(1)} %get-tuple-element.43.refs_1_), channel_id=1, source_target_pairs={{0,16},{16,0},{1,17},{17,1},{2,18},{18,2},{3,19},{19,3},{4,20},{20... | collective-permute-start | bytes 294920 | tf_op jit(solution)/shard_map/ppermute | solution.py:61
  78.1 5.0 %collective-permute-start.17 = (f32[2,96,128]{2,1,0:T(8,128)S(1)}, f32[2,96,128]{2,1,0:T(8,128)S(1)}, u32[]{:S(2)}, u32[]{:S(2)}) collective-permute-start(f32[2,96,128]{2,1,0:T(8,128)S(1)} %collective-permute-done.13.refs_2_), channel_id=1, source_target_pairs={{0,16},{16,0},{1,17},{17,1},{2,18},{18,2},{3,19},{19,3},{4,20},{20... | collective-permute-start | bytes 294920 | tf_op jit(solution)/shard_map/ppermute | solution.py:61
  78.2 5.1 %collective-permute-start.18 = (f32[2,96,128]{2,1,0:T(8,128)S(1)}, f32[2,96,128]{2,1,0:T(8,128)S(1)}, u32[]{:S(2)}, u32[]{:S(2)}) collective-permute-start(f32[2,96,128]{2,1,0:T(8,128)S(1)} %collective-permute-done.14.refs_3_), channel_id=1, source_target_pairs={{0,16},{16,0},{1,17},{17,1},{2,18},{18,2},{3,19},{19,3},{4,20},{20... | collective-permute-start | bytes 294920 | tf_op jit(solution)/shard_map/ppermute | solution.py:61
  79.6 3.7 %collective-permute-start.19 = (f32[2,96,128]{2,1,0:T(8,128)S(1)}, f32[2,96,128]{2,1,0:T(8,128)S(1)}, u32[]{:S(2)}, u32[]{:S(2)}) collective-permute-start(f32[2,96,128]{2,1,0:T(8,128)S(1)} %collective-permute-done.15.refs_4_), channel_id=1, source_target_pairs={{0,16},{16,0},{1,17},{17,1},{2,18},{18,2},{3,19},{19,3},{4,20},{20... | collective-permute-start | bytes 294920 | tf_op jit(solution)/shard_map/ppermute | solution.py:61
  79.6 9.3 %collective-permute-start.33 = (f32[512,128]{1,0:T(8,128)S(1)}, f32[512,128]{1,0:T(8,128)S(1)}, u32[]{:S(2)}, u32[]{:S(2)}) collective-permute-start(f32[512,128]{1,0:T(8,128)S(1)} %get-tuple-element.39.refs_2_), channel_id=1, source_target_pairs={{0,1},{1,0},{2,3},{3,2},{4,5},{5,4},{6,7},{7,6},{8,9},{9,8},{10,11... | collective-permute-start | bytes 786440 | tf_op jit(solution)/shard_map/ppermute | solution.py:61
  81.7 13.7 %collective-permute-start.34 = (f32[512,128]{1,0:T(8,128)S(1)}, f32[512,128]{1,0:T(8,128)S(1)}, u32[]{:S(2)}, u32[]{:S(2)}) collective-permute-start(f32[512,128]{1,0:T(8,128)S(1)} %get-tuple-element.40.refs_3_), channel_id=1, source_target_pairs={{0,2},{1,3},{2,0},{3,1},{4,6},{5,7},{6,4},{7,5},{8,10},{9,11},{10,... | collective-permute-start | bytes 786440 | tf_op jit(solution)/shard_map/ppermute | solution.py:61
  83.1 12.3 %collective-permute-start.35 = (f32[512,128]{1,0:T(8,128)S(1)}, f32[512,128]{1,0:T(8,128)S(1)}, u32[]{:S(2)}, u32[]{:S(2)}) collective-permute-start(f32[512,128]{1,0:T(8,128)S(1)} %get-tuple-element.41.refs_4_), channel_id=1, source_target_pairs={{0,3},{1,2},{2,1},{3,0},{4,7},{5,6},{6,5},{7,4},{8,11},{9,10},{10,... | collective-permute-start | bytes 786440 | tf_op jit(solution)/shard_map/ppermute | solution.py:61
  83.3 13.9 %collective-permute-start.40 = (f32[512,128]{1,0:T(8,128)S(1)}, f32[512,128]{1,0:T(8,128)S(1)}, u32[]{:S(2)}, u32[]{:S(2)}) collective-permute-start(f32[512,128]{1,0:T(8,128)S(1)} %get-tuple-element.38.refs_1_.refs_2_), channel_id=1, source_target_pairs={{0,16},{16,0},{1,17},{17,1},{2,18},{18,2},{3,19},{19,3},{4,20},{20... | collective-permute-start | bytes 786440 | tf_op jit(solution)/shard_map/ppermute | solution.py:61
  83.3 15.5 %collective-permute-start.36 = (f32[3,256,128]{2,1,0:T(8,128)S(1)}, f32[3,256,128]{2,1,0:T(8,128)S(1)}, u32[]{:S(2)}, u32[]{:S(2)}) collective-permute-start(f32[3,256,128]{2,1,0:T(8,128)S(1)} %get-tuple-element.55), channel_id=1, source_target_pairs={{0,4},{4,8},{8,12},{1,5},{5,9},{9,13},{2,6},{6,10},{10,14},{3,7},{... | collective-permute-start | bytes 1179656 | tf_op jit(solution)/shard_map/ppermute | solution.py:66
  88.9 10.7 %collective-permute-start.48 = (f32[96,512]{1,0:T(8,128)S(1)}, f32[96,512]{1,0:T(8,128)S(1)}, u32[]{:S(2)}, u32[]{:S(2)}) collective-permute-start(f32[96,512]{1,0:T(8,128)S(1)} %factor_slice.1.refs_1_), channel_id=1, source_target_pairs={{0,1},{1,0},{2,3},{3,2},{4,5},{5,4},{6,7},{7,6},{8,9},{9,8},{10,11... | collective-permute-start | bytes 589832 | tf_op jit(solution)/shard_map/ppermute | solution.py:61
  95.4 13.3 %collective-permute-start.41 = (f32[512,128]{1,0:T(8,128)S(1)}, f32[512,128]{1,0:T(8,128)S(1)}, u32[]{:S(2)}, u32[]{:S(2)}) collective-permute-start(f32[512,128]{1,0:T(8,128)S(1)} %collective-permute-done.33.refs_3_), channel_id=1, source_target_pairs={{0,16},{16,0},{1,17},{17,1},{2,18},{18,2},{3,19},{19,3},{4,20},{20... | collective-permute-start | bytes 786440 | tf_op jit(solution)/shard_map/ppermute | solution.py:61
  95.4 11.5 %collective-permute-start.49 = (f32[96,512]{1,0:T(8,128)S(1)}, f32[96,512]{1,0:T(8,128)S(1)}, u32[]{:S(2)}, u32[]{:S(2)}) collective-permute-start(f32[96,512]{1,0:T(8,128)S(1)} %factor_slice.1.refs_1_), channel_id=1, source_target_pairs={{0,2},{1,3},{2,0},{3,1},{4,6},{5,7},{6,4},{7,5},{8,10},{9,11},{10,... | collective-permute-start | bytes 589832 | tf_op jit(solution)/shard_map/ppermute | solution.py:61
  97.2 10.4 %collective-permute-start.50 = (f32[96,512]{1,0:T(8,128)S(1)}, f32[96,512]{1,0:T(8,128)S(1)}, u32[]{:S(2)}, u32[]{:S(2)}) collective-permute-start(f32[96,512]{1,0:T(8,128)S(1)} %factor_slice.1.refs_1_), channel_id=1, source_target_pairs={{0,3},{1,2},{2,1},{3,0},{4,7},{5,6},{6,5},{7,4},{8,11},{9,10},{10,... | collective-permute-start | bytes 589832 | tf_op jit(solution)/shard_map/ppermute | solution.py:61
  98.8 11.7 %collective-permute-start.23 = (f32[96,512]{1,0:T(8,128)S(1)}, f32[96,512]{1,0:T(8,128)S(1)}, u32[]{:S(2)}, u32[]{:S(2)}) collective-permute-start(f32[96,512]{1,0:T(8,128)S(1)} %factor_slice.1.refs_1_), channel_id=1, source_target_pairs={{0,4},{4,8},{8,12},{12,0},{1,5},{5,9},{9,13},{13,1},{2,6},{6,10},{... | collective-permute-start | bytes 589832 | tf_op jit(solution)/shard_map/ppermute | solution.py:56
  99.6 15.0 %collective-permute-start.24 = (f32[96,512]{1,0:T(8,128)S(1)}, f32[96,512]{1,0:T(8,128)S(1)}, u32[]{:S(2)}, u32[]{:S(2)}) collective-permute-start(f32[96,512]{1,0:T(8,128)S(1)} %factor_slice.1.refs_1_), channel_id=1, source_target_pairs={{0,8},{4,12},{8,0},{12,4},{1,9},{5,13},{9,1},{13,5},{2,10},{6,14},... | collective-permute-start | bytes 589832 | tf_op jit(solution)/shard_map/ppermute | solution.py:56
  103.9 47.1 %copy-start.1 = (f32[384,768]{1,0:T(8,128)S(1)}, f32[384,768]{1,0:T(8,128)}, u32[]{:S(2)}) copy-start(f32[384,768]{1,0:T(8,128)} %refs_1_.1) | copy-start | bytes 3538948
  107.0 15.2 %collective-permute-start.37 = (f32[1024,128]{1,0:T(8,128)S(1)}, f32[1024,128]{1,0:T(8,128)S(1)}, u32[]{:S(2)}, u32[]{:S(2)}) collective-permute-start(f32[1024,128]{1,0:T(8,128)S(1)} %get-tuple-element.57), channel_id=1, source_target_pairs={{0,1},{1,0},{2,3},{3,2},{4,5},{5,4},{6,7},{7,6},{8,9},{9,8},{10,11... | collective-permute-start | bytes 1572872 | tf_op jit(solution)/shard_map/ppermute | solution.py:61
  107.6 22.2 %collective-permute-start.38 = (f32[1024,128]{1,0:T(8,128)S(1)}, f32[1024,128]{1,0:T(8,128)S(1)}, u32[]{:S(2)}, u32[]{:S(2)}) collective-permute-start(f32[1024,128]{1,0:T(8,128)S(1)} %get-tuple-element.58), channel_id=1, source_target_pairs={{0,2},{1,3},{2,0},{3,1},{4,6},{5,7},{6,4},{7,5},{8,10},{9,11},{10,... | collective-permute-start | bytes 1572872 | tf_op jit(solution)/shard_map/ppermute | solution.py:61
  108.7 9.6 %collective-permute-start.25 = (f32[96,512]{1,0:T(8,128)S(1)}, f32[96,512]{1,0:T(8,128)S(1)}, u32[]{:S(2)}, u32[]{:S(2)}) collective-permute-start(f32[96,512]{1,0:T(8,128)S(1)} %factor_slice.1.refs_1_), channel_id=1, source_target_pairs={{0,12},{4,0},{8,4},{12,8},{1,13},{5,1},{9,5},{13,9},{2,14},{6,2},{... | collective-permute-start | bytes 589832 | tf_op jit(solution)/shard_map/ppermute | solution.py:56
  110.5 9.5 %collective-permute-start.42 = (f32[512,128]{1,0:T(8,128)S(1)}, f32[512,128]{1,0:T(8,128)S(1)}, u32[]{:S(2)}, u32[]{:S(2)}) collective-permute-start(f32[512,128]{1,0:T(8,128)S(1)} %collective-permute-done.34.refs_4_), channel_id=1, source_target_pairs={{0,16},{16,0},{1,17},{17,1},{2,18},{18,2},{3,19},{19,3},{4,20},{20... | collective-permute-start | bytes 786440 | tf_op jit(solution)/shard_map/ppermute | solution.py:61
  114.6 23.0 %collective-permute-start.39 = (f32[1024,128]{1,0:T(8,128)S(1)}, f32[1024,128]{1,0:T(8,128)S(1)}, u32[]{:S(2)}, u32[]{:S(2)}) collective-permute-start(f32[1024,128]{1,0:T(8,128)S(1)} %get-tuple-element.59), channel_id=1, source_target_pairs={{0,3},{1,2},{2,1},{3,0},{4,7},{5,6},{6,5},{7,4},{8,11},{9,10},{10,... | collective-permute-start | bytes 1572872 | tf_op jit(solution)/shard_map/ppermute | solution.py:61
  118.3 3.6 %collective-permute-start.43 = (f32[512,128]{1,0:T(8,128)S(1)}, f32[512,128]{1,0:T(8,128)S(1)}, u32[]{:S(2)}, u32[]{:S(2)}) collective-permute-start(f32[512,128]{1,0:T(8,128)S(1)} %collective-permute-done.35.refs_5_), channel_id=1, source_target_pairs={{0,16},{16,0},{1,17},{17,1},{2,18},{18,2},{3,19},{19,3},{4,20},{20... | collective-permute-start | bytes 786440 | tf_op jit(solution)/shard_map/ppermute | solution.py:61
  120.1 15.9 %collective-permute-start.26 = (f32[96,512]{1,0:T(8,128)S(1)}, f32[96,512]{1,0:T(8,128)S(1)}, u32[]{:S(2)}, u32[]{:S(2)}) collective-permute-start(f32[96,512]{1,0:T(8,128)S(1)} %get-tuple-element.52), channel_id=1, source_target_pairs={{0,1},{1,0},{2,3},{3,2},{4,5},{5,4},{6,7},{7,6},{8,9},{9,8},{10,11... | collective-permute-start | bytes 589832 | tf_op jit(solution)/shard_map/ppermute | solution.py:61
  122.0 26.2 %collective-permute-start.44 = (f32[1024,128]{1,0:T(8,128)S(1)}, f32[1024,128]{1,0:T(8,128)S(1)}, u32[]{:S(2)}, u32[]{:S(2)}) collective-permute-start(f32[1024,128]{1,0:T(8,128)S(1)} %get-tuple-element.56.refs_6_), channel_id=1, source_target_pairs={{0,16},{16,0},{1,17},{17,1},{2,18},{18,2},{3,19},{19,3},{4,20},{20... | collective-permute-start | bytes 1572872 | tf_op jit(solution)/shard_map/ppermute | solution.py:61
  122.2 26.5 %collective-permute-start.45 = (f32[1024,128]{1,0:T(8,128)S(1)}, f32[1024,128]{1,0:T(8,128)S(1)}, u32[]{:S(2)}, u32[]{:S(2)}) collective-permute-start(f32[1024,128]{1,0:T(8,128)S(1)} %collective-permute-done.37.refs_7_), channel_id=1, source_target_pairs={{0,16},{16,0},{1,17},{17,1},{2,18},{18,2},{3,19},{19,3},{4,20},{20... | collective-permute-start | bytes 1572872 | tf_op jit(solution)/shard_map/ppermute | solution.py:61
  129.7 19.0 %collective-permute-start.46 = (f32[1024,128]{1,0:T(8,128)S(1)}, f32[1024,128]{1,0:T(8,128)S(1)}, u32[]{:S(2)}, u32[]{:S(2)}) collective-permute-start(f32[1024,128]{1,0:T(8,128)S(1)} %collective-permute-done.38.refs_8_), channel_id=1, source_target_pairs={{0,16},{16,0},{1,17},{17,1},{2,18},{18,2},{3,19},{19,3},{4,20},{20... | collective-permute-start | bytes 1572872 | tf_op jit(solution)/shard_map/ppermute | solution.py:61
  135.9 5.7 %collective-permute-start.27 = (f32[96,512]{1,0:T(8,128)S(1)}, f32[96,512]{1,0:T(8,128)S(1)}, u32[]{:S(2)}, u32[]{:S(2)}) collective-permute-start(f32[96,512]{1,0:T(8,128)S(1)} %get-tuple-element.53), channel_id=1, source_target_pairs={{0,2},{1,3},{2,0},{3,1},{4,6},{5,7},{6,4},{7,5},{8,10},{9,11},{10,... | collective-permute-start | bytes 589832 | tf_op jit(solution)/shard_map/ppermute | solution.py:61
  137.6 13.3 %collective-permute-start.47 = (f32[1024,128]{1,0:T(8,128)S(1)}, f32[1024,128]{1,0:T(8,128)S(1)}, u32[]{:S(2)}, u32[]{:S(2)}) collective-permute-start(f32[1024,128]{1,0:T(8,128)S(1)} %collective-permute-done.39.refs_9_), channel_id=1, source_target_pairs={{0,16},{16,0},{1,17},{17,1},{2,18},{18,2},{3,19},{19,3},{4,20},{20... | collective-permute-start | bytes 1572872 | tf_op jit(solution)/shard_map/ppermute | solution.py:61
  141.6 6.6 %collective-permute-start.28 = (f32[96,512]{1,0:T(8,128)S(1)}, f32[96,512]{1,0:T(8,128)S(1)}, u32[]{:S(2)}, u32[]{:S(2)}) collective-permute-start(f32[96,512]{1,0:T(8,128)S(1)} %get-tuple-element.54), channel_id=1, source_target_pairs={{0,3},{1,2},{2,1},{3,0},{4,7},{5,6},{6,5},{7,4},{8,11},{9,10},{10,... | collective-permute-start | bytes 589832 | tf_op jit(solution)/shard_map/ppermute | solution.py:61
  148.2 6.4 %collective-permute-start.29 = (f32[96,512]{1,0:T(8,128)S(1)}, f32[96,512]{1,0:T(8,128)S(1)}, u32[]{:S(2)}, u32[]{:S(2)}) collective-permute-start(f32[96,512]{1,0:T(8,128)S(1)} %get-tuple-element.51.refs_1_), channel_id=1, source_target_pairs={{0,16},{16,0},{1,17},{17,1},{2,18},{18,2},{3,19},{19,3},{4,20},{20... | collective-permute-start | bytes 589832 | tf_op jit(solution)/shard_map/ppermute | solution.py:61
  148.2 6.4 %collective-permute-start.30 = (f32[96,512]{1,0:T(8,128)S(1)}, f32[96,512]{1,0:T(8,128)S(1)}, u32[]{:S(2)}, u32[]{:S(2)}) collective-permute-start(f32[96,512]{1,0:T(8,128)S(1)} %collective-permute-done.26.refs_2_), channel_id=1, source_target_pairs={{0,16},{16,0},{1,17},{17,1},{2,18},{18,2},{3,19},{19,3},{4,20},{20... | collective-permute-start | bytes 589832 | tf_op jit(solution)/shard_map/ppermute | solution.py:61
  148.7 5.9 %collective-permute-start.31 = (f32[96,512]{1,0:T(8,128)S(1)}, f32[96,512]{1,0:T(8,128)S(1)}, u32[]{:S(2)}, u32[]{:S(2)}) collective-permute-start(f32[96,512]{1,0:T(8,128)S(1)} %collective-permute-done.27.refs_3_), channel_id=1, source_target_pairs={{0,16},{16,0},{1,17},{17,1},{2,18},{18,2},{3,19},{19,3},{4,20},{20... | collective-permute-start | bytes 589832 | tf_op jit(solution)/shard_map/ppermute | solution.py:61
  148.8 5.9 %collective-permute-start.32 = (f32[96,512]{1,0:T(8,128)S(1)}, f32[96,512]{1,0:T(8,128)S(1)}, u32[]{:S(2)}, u32[]{:S(2)}) collective-permute-start(f32[96,512]{1,0:T(8,128)S(1)} %collective-permute-done.28.refs_4_), channel_id=1, source_target_pairs={{0,16},{16,0},{1,17},{17,1},{2,18},{18,2},{3,19},{19,3},{4,20},{20... | collective-permute-start | bytes 589832 | tf_op jit(solution)/shard_map/ppermute | solution.py:61

commit v8 on v7

--- a/solution.py
+++ b/solution.py
@@ -178,28 +178,22 @@
 def around_row(value):
     count = lax.axis_size("row")
     half = count // 2
-    rows = value.shape[0] // 2
-    middle, far = [], [[] for _ in range(1, half)]
-    for part in range(2):
-        middle.append(rotated(value[part * rows : (part + 1) * rows], "row", half))
-    below, above = [], []
+    middle = rotated(value, "row", half)
+    below, above, far = [], [], []
     for d in range(1, half):
         below.append(lax.ppermute(value, "row", [(i, i + d) for i in range(count - d)]))
         above.append(lax.ppermute(value, "row", [(i + d, i) for i in range(count - d)]))
         pairs = [(i, i + d) for i in range(half, count - d)]
         pairs += [(i, i - d) for i in range(d, half)]
-        for part in range(2):
-            far[d - 1].append(lax.ppermute(middle[part], "row", pairs))
-    return [[value]] + [[v] for v in below] + [middle] + far + [[v] for v in above]
+        far.append(lax.ppermute(middle, "row", pairs))
+    return [value] + below + [middle] + far + above
 
 
 def slice_products(table, rows, around, fronts):
     count = len(rows)
-    flat = sum(around, [])
-    many = len(flat)
+    many = len(around)
     sub, depth = rows[0].shape
     size = count * sub
-    part_rows = sub // 2
 
     def body(*refs):
         sc = refs[0]
@@ -212,27 +206,13 @@
         rows_in = gather_copies(sc, row_refs, row_buf, sems, sub)
         for copy in rows_in:
             copy.start()
-        choices, taken = ([], []), 0
-        for group_parts in around:
-            found = around_refs[taken : taken + len(group_parts)]
-            taken += len(group_parts)
-            for part in range(2):
-                lines = pl.ds(part * part_rows, part_rows)
-                choices[part].append(found[part] if len(found) == 2 else found[0].at[lines])
-        targets = [
-            (m, part, place.at[part * part_rows : (part + 1) * part_rows])
-            for m, place in enumerate(places)
-            for part in range(2)
-        ]
-        for m, part, target in targets:
-            start_chosen(
-                slice_place(sc, m, count), choices[part], target, sems.at[count + 2 * m + part]
-            )
+        for m, place in enumerate(places):
+            start_chosen(slice_place(sc, m, count), around_refs, place, sems.at[count + m])
         for copy in rows_in:
             copy.wait()
         left = halves(row_buf[...])
-        for m, part, target in targets:
-            pltpu.make_async_copy(choices[part][0], target, sems.at[count + 2 * m + part]).wait()
+        for m, place in enumerate(places):
+            pltpu.make_async_copy(around_refs[0], place, sems.at[count + m]).wait()
         product = times_transpose(left, halves(col_buf[...]))
         for m in range(count):
             group = sc[COL] ^ m
@@ -255,11 +235,11 @@
         scratch_shapes=[
             pltpu.VMEM((size, depth), jnp.float32),
             pltpu.VMEM((size, depth), jnp.float32),
-            pltpu.SemaphoreType.DMA((3 * count,)),
+            pltpu.SemaphoreType.DMA((2 * count,)),
         ],
         compiler_params=limit_for(sub, 20),
         name="slice_products",
-    )(table, *rows, *flat, *fronts)
+    )(table, *rows, *around, *fronts)
 
 
 def pack_halo(table, homes, edge, up):
@@ -548,35 +528,47 @@
         sc = refs[0]
         own_refs = refs[1 : 1 + count]
         other_refs = refs[1 + count : 1 + 2 * count]
-        base_ref, high_ref, low_ref, out, col_factor, sems = refs[1 + 2 * count :]
-        own = gather_copies(sc, own_refs, col_factor.at[sc[SIB]], sems, piece_rows)
-        other = gather_copies(
-            sc, other_refs, col_factor.at[1 - sc[SIB]], sems, piece_rows, count
-        )
-        run_copies(own + other)
+        base_ref, high_ref, low_ref, out, col_factor, result, sems = refs[1 + 2 * count :]
+        own = gather_copies(sc, own_refs, col_factor.at[0], sems, piece_rows)
+        other = gather_copies(sc, other_refs, col_factor.at[1], sems, piece_rows, count)
+        for copy in own + other:
+            copy.start()
         left = high_ref[...], low_ref[...]
         first_row = (sc[ROW] * 2 + sc[SIB]) * HALF
         first_col = sc[COL] * PBD
-        for side in range(2):
-            product = times_transpose(left, halves(col_factor[side]))
-            for i in range(HALF):
-                q = side * HALF + i
-                cols = slice(q * BLK, (q + 1) * BLK)
-                for p in range(HALF):
-                    lines = slice(p * BLK, (p + 1) * BLK)
-                    total = base_ref[lines, cols]
-                    inside = (first_col + q >= PIV) & (first_row + p >= PIV)
-                    reduced = total - product[lines, i * BLK : (i + 1) * BLK]
-                    out[lines, cols] = jnp.where(inside, reduced, total)
+        writes = []
+        for which, copies in ((0, own), (1, other)):
+            for copy in copies:
+                copy.wait()
+            side = jnp.abs(sc[SIB] - which)
+            lanes = span(side, rows)
+            product = times_transpose(left, halves(col_factor[which]))
+            for p in range(HALF):
+                lines = slice(p * BLK, (p + 1) * BLK)
+                for i in range(HALF):
+                    cols = slice(i * BLK, (i + 1) * BLK)
+                    here = span(side * HALF + i, BLK)
+                    total = base_ref[lines, here]
+                    inside = (first_col + side * HALF + i >= PIV) & (first_row + p >= PIV)
+                    reduced = total - product[lines, cols]
+                    result[which, lines, cols] = jnp.where(inside, reduced, total)
+            write = pltpu.make_async_copy(
+                result.at[which], out.at[:, lanes], sems.at[2 * count + which]
+            )
+            write.start()
+            writes.append(write)
+        for write in writes:
+            write.wait()
 
     return pl.pallas_call(
         body,
         in_specs=[SMEM] + [ANY] * (2 * count) + [VMEM] * 3,
-        out_specs=VMEM,
+        out_specs=ANY,
         out_shape=f32(rows, width),
         scratch_shapes=[
             pltpu.VMEM((2, rows, PANEL), jnp.float32),
-            pltpu.SemaphoreType.DMA((2 * count,)),
+            pltpu.VMEM((2, rows, rows), jnp.float32),
+            pltpu.SemaphoreType.DMA((2 * count + 2,)),
         ],
         compiler_params=limit_for(BLK, 16),
         name="finish",

time: 160 us -> 155 us (0.969)
  starting transfers between devices: 62.4 us -> 56.3 us
    ppermute x37, waiting for transfers between devices: 45.5 us -> 62.2 us  [swapped(): return lax.ppermute(value, axis, [(i, i ^ mask) for i in range(count)])]
    ppermute x5 -> x4, waiting for transfers between devices: 14.2 us -> 6.48 us  [rotated(): lax.ppermute(value, axis, [(i, (i + steps) % count) for i in range(count)])]
    ppermute x2 -> x1, waiting for transfers between devices: 9.27 us -> 3.57 us  [around_row(): far.append(lax.ppermute(middle, 'row', pairs))]
    ppermute x5 -> x4, starting transfers between devices: 10.1 us -> 6.16 us  [rotated(): lax.ppermute(value, axis, [(i, (i + steps) % count) for i in range(count)])]
    ppermute x37, starting transfers between devices: 33.7 us -> 31 us  [swapped(): return lax.ppermute(value, axis, [(i, i ^ mask) for i in range(count)])]
    ppermute x1, starting transfers between devices: 1.58 us -> 3.5 us  [around_row(): lax.ppermute(value, 'row', [(i, i + d) for i in range(count - d)])]
    ppermute x1, waiting for transfers between devices: 1.71 us -> 0.01 us  [around_row(): lax.ppermute(value, 'row', [(i + d, i) for i in range(count - d)])]
  transfers between devices with their start and end apart: 51 -> 49, of which waited for: 19 -> 15; matrix products, arithmetic and copies ran while one was open for 0% -> 0% of each run, Pallas kernels for 10% -> 11%
where the time goes in v8:
time: 155 us
  waiting for transfers between devices  72.2 us (47%)
  starting transfers between devices  56.3 us (36%)
  Pallas kernels  23 us (15%)
  local copies, waits for them, and re-layouts  3.18 us (2%)
    ppermute x37, waiting for transfers between devices, swapped(): return lax.ppermute(value, axis, [(i, i ^ mask) for i in range(count)])  62.2 us
    ppermute x37, starting transfers between devices, swapped(): return lax.ppermute(value, axis, [(i, i ^ mask) for i in range(count)])  31 us
    ppermute x3, starting transfers between devices, shards(): dealt.append(lax.ppermute(value, 'col', [(0, j)]) if j else value)  7.43 us
    ppermute x4, waiting for transfers between devices, rotated(): lax.ppermute(value, axis, [(i, (i + steps) % count) for i in range(count)])  6.48 us
    ppermute x4, starting transfers between devices, rotated(): lax.ppermute(value, axis, [(i, (i + steps) % count) for i in range(count)])  6.16 us
    ppermute x2, starting transfers between devices, shifted(): return lax.ppermute(value, axis, [(i, i + 1) for i in range(count - 1)])  5.67 us
    pallas_call x1, Pallas kernels, finish(): pl.pallas_call(body, in_specs=[SMEM] + [ANY] * (2 * count) + [VMEM] * 3,...  5.16 us
    pallas_call x1, Pallas kernels, assemble(): pl.pallas_call(body, in_specs=[SMEM, VMEM] + [ANY] * (4 * count) + [VMEM]...  3.62 us
  transfers between devices with their start and end apart: 49, of which 15 were waited for; matrix products, arithmetic and copies ran while one was open for 0% of the time, Pallas kernels for 11%

profile of v8, /device:TPU:0, one launch (start us, length us, event | category | flops | bytes accessed | tf_op | source)
XLA Modules:
  0.0 155.1 jit_solution(8984275607688847696)
XLA Ops:
  0.0 4.1 %collective-permute-start.4 = (f32[128,1024]{1,0:T(8,128)}, f32[128,1024]{1,0:T(8,128)S(1)}, u32[]{:S(2)}, u32[]{:S(2)}) collective-permute-start(f32[128,1024]{1,0:T(8,128)} %bitcast.2), channel_id=1, source_target_pairs={{0,8},{4,12},{8,0},{12,4},{1,9},{5,13},{9,1},{13,5},{2,10},{6,14},... | collective-permute-start | bytes 1572872 | tf_op jit(solution)/shard_map/ppermute | solution.py:56
  4.1 1.5 collective-permute-start
  5.6 0.7 copy-done.5
  6.2 1.3 lookup_table.1.sc.refs_0_
  7.6 1.3 copy-done
  8.9 1.2 copy-done.4
  10.1 0.9 cut_slices.1
  10.9 0.6 collective-permute-start.7
  11.5 1.5 collective-permute-start.8
  13.1 1.4 collective-permute-start.9
  14.5 10.2 %collective-permute-done.7.refs_11_ = f32[512,128]{1,0:T(8,128)S(1)} collective-permute-done((f32[512,128]{1,0:T(8,128)S(1)}, f32[512,128]{1,0:T(8,128)S(1)}, u32[]{:S(2)}, u32[]{:S(2)}) %collective-permute-start.7) | collective-permute-done | bytes 262176 | tf_op jit(solution)/shard_map/ppermute | solution.py:61
  24.7 1.5 collective-permute-start.1
  26.2 1.4 collective-permute-start.2
  27.6 3.7 %collective-permute-done.9.refs_13_ = f32[512,128]{1,0:T(8,128)S(1)} collective-permute-done((f32[512,128]{1,0:T(8,128)S(1)}, f32[512,128]{1,0:T(8,128)S(1)}, u32[]{:S(2)}, u32[]{:S(2)}) %collective-permute-start.9) | collective-permute-done | bytes 262176 | tf_op jit(solution)/shard_map/ppermute | solution.py:61
  31.4 3.5 %collective-permute-start.3 = (f32[128,1024]{1,0:T(8,128)S(1)}, f32[128,1024]{1,0:T(8,128)S(1)}, u32[]{:S(2)}, u32[]{:S(2)}) collective-permute-start(f32[128,1024]{1,0:T(8,128)S(1)} %bitcast.6), channel_id=1, source_target_pairs={{0,4},{4,8},{8,12},{1,5},{5,9},{9,13},{2,6},{6,10},{10,14},{3,7},{... | collective-permute-start | bytes 1572872 | tf_op jit(solution)/shard_map/ppermute | solution.py:184
  34.9 1.3 collective-permute-start.6
  36.2 1.3 collective-permute-start.5
  37.5 14.3 %collective-permute-done.1.refs_3_ = f32[128,1024]{1,0:T(8,128)S(1)} collective-permute-done((f32[128,1024]{1,0:T(8,128)S(1)}, f32[128,1024]{1,0:T(8,128)S(1)}, u32[]{:S(2)}, u32[]{:S(2)}) %collective-permute-start.1) | collective-permute-done | bytes 524320 | tf_op jit(solution)/shard_map/ppermute | solution.py:61
  51.8 3.4 %collective-permute-start.18 = (f32[96,512]{1,0:T(8,128)S(1)}, f32[96,512]{1,0:T(8,128)S(1)}, u32[]{:S(2)}, u32[]{:S(2)}) collective-permute-start(f32[96,512]{1,0:T(8,128)S(1)} %get-tuple-element.48), channel_id=1, source_target_pairs={{0,1},{4,5},{8,9},{12,13},{16,17},{20,21},{24,25},{28,29}} | collective-permute-start | bytes 589832 | tf_op jit(solution)/shard_map/ppermute | solution.py:612
  55.2 3.6 %collective-permute-done.5.refs_8_ = f32[128,1024]{1,0:T(8,128)S(1)} collective-permute-done((f32[128,1024]{1,0:T(8,128)S(1)}, f32[128,1024]{1,0:T(8,128)S(1)}, u32[]{:S(2)}, u32[]{:S(2)}) %collective-permute-start.5) | collective-permute-done | bytes 524320 | tf_op jit(solution)/shard_map/ppermute | solution.py:188
  58.8 3.4 %slice_products.1 = (f32[512,128]{1,0:T(8,128)S(1)}, f32[512,128]{1,0:T(8,128)S(1)}, f32[512,128]{1,0:T(8,128)S(1)}, f32[512,128]{1,0:T(8,128)S(1)}, f32[256,128]{1,0:T(8,128)S(1)}, /*index=5*/f32[3,256,128]{2,1,0:T(8,128)S(1)}) custom-call(s32[35]{0:T(128)S(1)} %lookup_table.1.sc.refs_0_, f32[128,1024]{1,0:T(8,128)S(1)} %bitcast.8, ...), custom_call_target="tpu_custom_call" | custom-call | tf_op jit(solution)/shard_map/slice_products/pallas_call | solution.py:230
  62.2 1.6 %collective-permute-start.10 = (f32[256,128]{1,0:T(8,128)S(1)}, f32[256,128]{1,0:T(8,128)S(1)}, u32[]{:S(2)}, u32[]{:S(2)}) collective-permute-start(f32[256,128]{1,0:T(8,128)S(1)} %get-tuple-element.42), channel_id=1, source_target_pairs={{0,4},{4,8},{8,12},{1,5},{5,9},{9,13},{2,6},{6,10},{10,14},{3,7},{... | collective-permute-start | bytes 393224 | tf_op jit(solution)/shard_map/ppermute | solution.py:66
  63.8 2.4 %collective-permute-start.19 = (f32[96,512]{1,0:T(8,128)S(1)}, f32[96,512]{1,0:T(8,128)S(1)}, u32[]{:S(2)}, u32[]{:S(2)}) collective-permute-start(f32[96,512]{1,0:T(8,128)S(1)} %get-tuple-element.49), channel_id=1, source_target_pairs={{0,2},{4,6},{8,10},{12,14},{16,18},{20,22},{24,26},{28,30}} | collective-permute-start | bytes 589832 | tf_op jit(solution)/shard_map/ppermute | solution.py:612
  66.3 1.6 %collective-permute-start.20 = (f32[96,512]{1,0:T(8,128)S(1)}, f32[96,512]{1,0:T(8,128)S(1)}, u32[]{:S(2)}, u32[]{:S(2)}) collective-permute-start(f32[96,512]{1,0:T(8,128)S(1)} %get-tuple-element.50), channel_id=1, source_target_pairs={{0,3},{4,7},{8,11},{12,15},{16,19},{20,23},{24,27},{28,31}} | collective-permute-start | bytes 589832 | tf_op jit(solution)/shard_map/ppermute | solution.py:612
  67.9 0.8 place_rows.1
  68.8 0.4 collective-permute-start.12
  69.2 3.0 %collective-permute-start.13 = (f32[2,96,128]{2,1,0:T(8,128)S(1)}, f32[2,96,128]{2,1,0:T(8,128)S(1)}, u32[]{:S(2)}, u32[]{:S(2)}) collective-permute-start(f32[2,96,128]{2,1,0:T(8,128)S(1)} %get-tuple-element.46), channel_id=1, source_target_pairs={{0,3},{1,2},{2,1},{3,0},{4,7},{5,6},{6,5},{7,4},{8,11},{9,10},{10,... | collective-permute-start | bytes 294920 | tf_op jit(solution)/shard_map/ppermute | solution.py:61
  72.3 1.1 collective-permute-done.11.refs_2_
  73.5 0.4 collective-permute-start.16
  73.9 1.0 collective-permute-done.13.refs_4_
  74.9 2.1 %collective-permute-start.31 = (f32[512,128]{1,0:T(8,128)S(1)}, f32[512,128]{1,0:T(8,128)S(1)}, u32[]{:S(2)}, u32[]{:S(2)}) collective-permute-start(f32[512,128]{1,0:T(8,128)S(1)} %get-tuple-element.39.refs_2_), channel_id=1, source_target_pairs={{0,1},{1,0},{2,3},{3,2},{4,5},{5,4},{6,7},{7,6},{8,9},{9,8},{10,11... | collective-permute-start | bytes 786440 | tf_op jit(solution)/shard_map/ppermute | solution.py:61
  77.0 1.4 collective-permute-start.32
  78.4 0.2 collective-permute-start.33
  78.6 4.1 %collective-permute-start.34 = (f32[3,256,128]{2,1,0:T(8,128)S(1)}, f32[3,256,128]{2,1,0:T(8,128)S(1)}, u32[]{:S(2)}, u32[]{:S(2)}) collective-permute-start(f32[3,256,128]{2,1,0:T(8,128)S(1)} %get-tuple-element.55), channel_id=1, source_target_pairs={{0,4},{4,8},{8,12},{1,5},{5,9},{9,13},{2,6},{6,10},{10,14},{3,7},{... | collective-permute-start | bytes 1179656 | tf_op jit(solution)/shard_map/ppermute | solution.py:66
  82.7 2.1 %factor_slice.1.refs_1_ = f32[96,512]{1,0:T(8,128)S(1)} custom-call(s32[35]{0:T(128)S(1)} %lookup_table.1.sc.refs_0_, f32[2,96,128]{2,1,0:T(8,128)S(1)} %get-tuple-element.43.refs_1_, f32[2,96,128]{2,1,0:T(8,128)S(1)} %collective-permute-done.11.refs_2_, f32[2,96,128]{2,1,0:T(8,128)S(1)} %collective-permute-done.12.refs_3_, ...), custom_call_target="tpu_custom_call" | custom-call | tf_op jit(solution)/shard_map/factor_slice/pallas_call | solution.py:388
  84.8 1.4 collective-permute-start.46
  86.2 4.5 %collective-permute-done.32.refs_4_ = f32[512,128]{1,0:T(8,128)S(1)} collective-permute-done((f32[512,128]{1,0:T(8,128)S(1)}, f32[512,128]{1,0:T(8,128)S(1)}, u32[]{:S(2)}, u32[]{:S(2)}) %collective-permute-start.32) | collective-permute-done | bytes 262176 | tf_op jit(solution)/shard_map/ppermute | solution.py:61
  90.7 1.7 %collective-permute-start.47 = (f32[96,512]{1,0:T(8,128)S(1)}, f32[96,512]{1,0:T(8,128)S(1)}, u32[]{:S(2)}, u32[]{:S(2)}) collective-permute-start(f32[96,512]{1,0:T(8,128)S(1)} %factor_slice.1.refs_1_), channel_id=1, source_target_pairs={{0,2},{1,3},{2,0},{3,1},{4,6},{5,7},{6,4},{7,5},{8,10},{9,11},{10,... | collective-permute-start | bytes 589832 | tf_op jit(solution)/shard_map/ppermute | solution.py:61
  92.4 1.6 %collective-permute-start.48 = (f32[96,512]{1,0:T(8,128)S(1)}, f32[96,512]{1,0:T(8,128)S(1)}, u32[]{:S(2)}, u32[]{:S(2)}) collective-permute-start(f32[96,512]{1,0:T(8,128)S(1)} %factor_slice.1.refs_1_), channel_id=1, source_target_pairs={{0,3},{1,2},{2,1},{3,0},{4,7},{5,6},{6,5},{7,4},{8,11},{9,10},{10,... | collective-permute-start | bytes 589832 | tf_op jit(solution)/shard_map/ppermute | solution.py:61
  94.1 0.9 collective-permute-start.21
  95.0 0.2 collective-permute-start.22
  95.2 2.2 %pack_halo.1 = (f32[1024,128]{1,0:T(8,128)S(1)}, f32[1024,128]{1,0:T(8,128)S(1)}, f32[1024,128]{1,0:T(8,128)S(1)}, f32[1024,128]{1,0:T(8,128)S(1)}) custom-call(s32[35]{0:T(128)S(1)} %lookup_table.1.sc.refs_0_, f32[512,128]{1,0:T(8,128)S(1)} %get-tuple-element.38.refs_1_.refs_2_, f32[512,128]{1,0:T(8,128)S(1)} %get-tuple-element.39.refs_2_, ...), custom_call_target="tpu_custom_call" | custom-call | tf_op jit(solution)/shard_map/pack_halo/pallas_call | solution.py:277
  97.5 4.7 %collective-permute-done.47.refs_3_ = f32[96,512]{1,0:T(8,128)S(1)} collective-permute-done((f32[96,512]{1,0:T(8,128)S(1)}, f32[96,512]{1,0:T(8,128)S(1)}, u32[]{:S(2)}, u32[]{:S(2)}) %collective-permute-start.47) | collective-permute-done | bytes 196640 | tf_op jit(solution)/shard_map/ppermute | solution.py:61
  102.2 0.6 collective-permute-start.35
  102.8 1.2 collective-permute-start.36
  104.0 0.9 collective-permute-start.23
  104.9 5.0 %collective-permute-done.22.refs_3_ = f32[96,512]{1,0:T(8,128)S(1)} collective-permute-done((f32[96,512]{1,0:T(8,128)S(1)}, f32[96,512]{1,0:T(8,128)S(1)}, u32[]{:S(2)}, u32[]{:S(2)}) %collective-permute-start.22) | collective-permute-done | bytes 196640 | tf_op jit(solution)/shard_map/ppermute | solution.py:56
  109.9 2.6 %collective-permute-start.37 = (f32[1024,128]{1,0:T(8,128)S(1)}, f32[1024,128]{1,0:T(8,128)S(1)}, u32[]{:S(2)}, u32[]{:S(2)}) collective-permute-start(f32[1024,128]{1,0:T(8,128)S(1)} %get-tuple-element.59), channel_id=1, source_target_pairs={{0,3},{1,2},{2,1},{3,0},{4,7},{5,6},{6,5},{7,4},{8,11},{9,10},{10,... | collective-permute-start | bytes 1572872 | tf_op jit(solution)/shard_map/ppermute | solution.py:61
  112.5 1.5 collective-permute-done.23.refs_4_
  114.0 1.7 %pick_for_cols.1 = (f32[96,512]{1,0:T(8,128)S(1)}, f32[96,512]{1,0:T(8,128)S(1)}, f32[96,512]{1,0:T(8,128)S(1)}, f32[96,512]{1,0:T(8,128)S(1)}) custom-call(s32[35]{0:T(128)S(1)} %lookup_table.1.sc.refs_0_, f32[96,512]{1,0:T(8,128)S(1)} %factor_slice.1.refs_1_, f32[96,512]{1,0:T(8,128)S(1)} %collective-permute-done.21.refs_2_, ...), custom_call_target="tpu_custom_call" | custom-call | tf_op jit(solution)/shard_map/pick_for_cols/pallas_call | solution.py:301
  115.7 1.3 collective-permute-start.24
  117.0 0.2 collective-permute-start.42
  117.2 0.3 collective-permute-start.43
  117.5 7.5 %collective-permute-done.36.refs_8_ = f32[1024,128]{1,0:T(8,128)S(1)} collective-permute-done((f32[1024,128]{1,0:T(8,128)S(1)}, f32[1024,128]{1,0:T(8,128)S(1)}, u32[]{:S(2)}, u32[]{:S(2)}) %collective-permute-start.36) | collective-permute-done | bytes 524320 | tf_op jit(solution)/shard_map/ppermute | solution.py:61
  125.0 6.2 %collective-permute-done.24.refs_2_ = f32[96,512]{1,0:T(8,128)S(1)} collective-permute-done((f32[96,512]{1,0:T(8,128)S(1)}, f32[96,512]{1,0:T(8,128)S(1)}, u32[]{:S(2)}, u32[]{:S(2)}) %collective-permute-start.24) | collective-permute-done | bytes 196640 | tf_op jit(solution)/shard_map/ppermute | solution.py:61
  131.2 1.7 %collective-permute-start.25 = (f32[96,512]{1,0:T(8,128)S(1)}, f32[96,512]{1,0:T(8,128)S(1)}, u32[]{:S(2)}, u32[]{:S(2)}) collective-permute-start(f32[96,512]{1,0:T(8,128)S(1)} %get-tuple-element.53), channel_id=1, source_target_pairs={{0,2},{1,3},{2,0},{3,1},{4,6},{5,7},{6,4},{7,5},{8,10},{9,11},{10,... | collective-permute-start | bytes 589832 | tf_op jit(solution)/shard_map/ppermute | solution.py:61
  132.9 4.0 %collective-permute-done.25.refs_3_ = f32[96,512]{1,0:T(8,128)S(1)} collective-permute-done((f32[96,512]{1,0:T(8,128)S(1)}, f32[96,512]{1,0:T(8,128)S(1)}, u32[]{:S(2)}, u32[]{:S(2)}) %collective-permute-start.25) | collective-permute-done | bytes 196640 | tf_op jit(solution)/shard_map/ppermute | solution.py:61
  136.9 1.7 %collective-permute-start.26 = (f32[96,512]{1,0:T(8,128)S(1)}, f32[96,512]{1,0:T(8,128)S(1)}, u32[]{:S(2)}, u32[]{:S(2)}) collective-permute-start(f32[96,512]{1,0:T(8,128)S(1)} %get-tuple-element.54), channel_id=1, source_target_pairs={{0,3},{1,2},{2,1},{3,0},{4,7},{5,6},{6,5},{7,4},{8,11},{9,10},{10,... | collective-permute-start | bytes 589832 | tf_op jit(solution)/shard_map/ppermute | solution.py:61
  138.5 4.9 %collective-permute-done.26.refs_4_ = f32[96,512]{1,0:T(8,128)S(1)} collective-permute-done((f32[96,512]{1,0:T(8,128)S(1)}, f32[96,512]{1,0:T(8,128)S(1)}, u32[]{:S(2)}, u32[]{:S(2)}) %collective-permute-start.26) | collective-permute-done | bytes 196640 | tf_op jit(solution)/shard_map/ppermute | solution.py:61
  143.4 0.5 collective-permute-start.28
  144.0 0.4 collective-permute-start.30
  144.5 1.7 %lay_rows.1 = (f32[384,512]{1,0:T(8,128)S(1)}, bf16[384,512]{1,0:T(8,128)(2,1)S(1)}, bf16[384,512]{1,0:T(8,128)(2,1)S(1)}) custom-call(s32[35]{0:T(128)S(1)} %lookup_table.1.sc.refs_0_, f32[96,512]{1,0:T(8,128)S(1)} %factor_slice.1.refs_1_, f32[96,512]{1,0:T(8,128)S(1)} %collective-permute-done.46.refs_2_, f32[96,512]{1,0:T(8,128)S(1)} %collective-permute-done.47.refs_3_, ...), custom_call_target="tpu_custom_call" | custom-call | tf_op jit(solution)/shard_map/lay_rows/pallas_call | solution.py:417
  146.2 3.6 %assemble.1.refs_9_ = f32[384,768]{1,0:T(8,128)S(1)} custom-call(s32[35]{0:T(128)S(1)} %lookup_table.1.sc.refs_0_, f32[384,768]{1,0:T(8,128)S(1)} %copy-done.1, f32[512,128]{1,0:T(8,128)S(1)} %get-tuple-element.38.refs_1_.refs_2_, f32[512,128]{1,0:T(8,128)S(1)} %collective-permute-done.31.refs_3_, f32[512,128]{1,0:T(8,128)S(1)} %collective-permute-done.32.refs_4_, ...), custom_call_target="tpu_custom_call" | custom-call | tf_op jit(solution)/shard_map/assemble/pallas_call | solution.py:507
  149.9 5.2 %finish.1 = f32[384,768]{1,0:T(8,128)} custom-call(s32[35]{0:T(128)S(1)} %lookup_table.1.sc.refs_0_, f32[96,512]{1,0:T(8,128)S(1)} %get-tuple-element.51.refs_1_, f32[96,512]{1,0:T(8,128)S(1)} %collective-permute-done.24.refs_2_, f32[96,512]{1,0:T(8,128)S(1)} %collective-permute-done.25.refs_3_, f32[96,512]{1,0:T(8,128)S(1)} %collective-permute-done.26.refs_4_, ...), custom_call_target="tpu_custom_call" | custom-call | tf_op jit(solution)/shard_map/finish/pallas_call | solution.py:563
  (56 shorter events, 0.4 us)
Async XLA Ops:
  0.0 34.9 %collective-permute-start.4 = (f32[128,1024]{1,0:T(8,128)}, f32[128,1024]{1,0:T(8,128)S(1)}, u32[]{:S(2)}, u32[]{:S(2)}) collective-permute-start(f32[128,1024]{1,0:T(8,128)} %bitcast.2), channel_id=1, source_target_pairs={{0,8},{4,12},{8,0},{12,4},{1,9},{5,13},{9,1},{13,5},{2,10},{6,14},... | collective-permute-start | bytes 1572872 | tf_op jit(solution)/shard_map/ppermute | solution.py:56
  4.1 32.1 %collective-permute-start = (f32[128,1024]{1,0:T(8,128)}, f32[128,1024]{1,0:T(8,128)S(1)}, u32[]{:S(2)}, u32[]{:S(2)}) collective-permute-start(f32[128,1024]{1,0:T(8,128)} %bitcast.3), channel_id=1, source_target_pairs={{0,1},{1,0},{2,3},{3,2},{4,5},{5,4},{6,7},{7,6},{8,9},{9,8},{10,11... | collective-permute-start | bytes 1572872 | tf_op jit(solution)/shard_map/ppermute | solution.py:61
  5.6 0.7 copy-start.5
  7.6 1.3 copy-start
  8.9 1.2 copy-start.4
  10.1 14.6 %copy-start.2 = (f32[1,128,1024]{2,1,0:T(8,128)S(1)}, f32[1,128,1024]{2,1,0:T(8,128)}, u32[]{:S(2)}) copy-start(f32[1,128,1024]{2,1,0:T(8,128)} %param.6) | copy-start | bytes 1572868
  10.9 13.7 %collective-permute-start.7 = (f32[512,128]{1,0:T(8,128)S(1)}, f32[512,128]{1,0:T(8,128)S(1)}, u32[]{:S(2)}, u32[]{:S(2)}) collective-permute-start(f32[512,128]{1,0:T(8,128)S(1)} %get-tuple-element.35), channel_id=1, source_target_pairs={{0,1},{1,0},{2,3},{3,2},{4,5},{5,4},{6,7},{7,6},{8,9},{9,8},{10,11... | collective-permute-start | bytes 786440 | tf_op jit(solution)/shard_map/ppermute | solution.py:61
  11.5 14.7 %collective-permute-start.8 = (f32[512,128]{1,0:T(8,128)S(1)}, f32[512,128]{1,0:T(8,128)S(1)}, u32[]{:S(2)}, u32[]{:S(2)}) collective-permute-start(f32[512,128]{1,0:T(8,128)S(1)} %get-tuple-element.36), channel_id=1, source_target_pairs={{0,2},{1,3},{2,0},{3,1},{4,6},{5,7},{6,4},{7,5},{8,10},{9,11},{10,... | collective-permute-start | bytes 786440 | tf_op jit(solution)/shard_map/ppermute | solution.py:61
  13.1 18.3 %collective-permute-start.9 = (f32[512,128]{1,0:T(8,128)S(1)}, f32[512,128]{1,0:T(8,128)S(1)}, u32[]{:S(2)}, u32[]{:S(2)}) collective-permute-start(f32[512,128]{1,0:T(8,128)S(1)} %get-tuple-element.37), channel_id=1, source_target_pairs={{0,3},{1,2},{2,1},{3,0},{4,7},{5,6},{6,5},{7,4},{8,11},{9,10},{10,... | collective-permute-start | bytes 786440 | tf_op jit(solution)/shard_map/ppermute | solution.py:61
  24.7 27.1 %collective-permute-start.1 = (f32[128,1024]{1,0:T(8,128)S(1)}, f32[128,1024]{1,0:T(8,128)S(1)}, u32[]{:S(2)}, u32[]{:S(2)}) collective-permute-start(f32[128,1024]{1,0:T(8,128)S(1)} %bitcast.4), channel_id=1, source_target_pairs={{0,2},{1,3},{2,0},{3,1},{4,6},{5,7},{6,4},{7,5},{8,10},{9,11},{10,... | collective-permute-start | bytes 1572872 | tf_op jit(solution)/shard_map/ppermute | solution.py:61
  26.2 29.0 %collective-permute-start.2 = (f32[128,1024]{1,0:T(8,128)S(1)}, f32[128,1024]{1,0:T(8,128)S(1)}, u32[]{:S(2)}, u32[]{:S(2)}) collective-permute-start(f32[128,1024]{1,0:T(8,128)S(1)} %bitcast.5), channel_id=1, source_target_pairs={{0,3},{1,2},{2,1},{3,0},{4,7},{5,6},{6,5},{7,4},{8,11},{9,10},{10,... | collective-permute-start | bytes 1572872 | tf_op jit(solution)/shard_map/ppermute | solution.py:61
  31.4 23.8 %collective-permute-start.3 = (f32[128,1024]{1,0:T(8,128)S(1)}, f32[128,1024]{1,0:T(8,128)S(1)}, u32[]{:S(2)}, u32[]{:S(2)}) collective-permute-start(f32[128,1024]{1,0:T(8,128)S(1)} %bitcast.6), channel_id=1, source_target_pairs={{0,4},{4,8},{8,12},{1,5},{5,9},{9,13},{2,6},{6,10},{10,14},{3,7},{... | collective-permute-start | bytes 1572872 | tf_op jit(solution)/shard_map/ppermute | solution.py:184
  34.9 20.3 %collective-permute-start.6 = (f32[128,1024]{1,0:T(8,128)S(1)}, f32[128,1024]{1,0:T(8,128)S(1)}, u32[]{:S(2)}, u32[]{:S(2)}) collective-permute-start(f32[128,1024]{1,0:T(8,128)S(1)} %bitcast.7), channel_id=1, source_target_pairs={{4,0},{8,4},{12,8},{5,1},{9,5},{13,9},{6,2},{10,6},{14,10},{7,3},{... | collective-permute-start | bytes 1572872 | tf_op jit(solution)/shard_map/ppermute | solution.py:185
  36.2 22.6 %collective-permute-start.5 = (f32[128,1024]{1,0:T(8,128)S(1)}, f32[128,1024]{1,0:T(8,128)S(1)}, u32[]{:S(2)}, u32[]{:S(2)}) collective-permute-start(f32[128,1024]{1,0:T(8,128)S(1)} %collective-permute-done.4.refs_7_), channel_id=1, source_target_pairs={{8,12},{4,0},{9,13},{5,1},{10,14},{6,2},{11,15},{7,3},{24,28},{20,... | collective-permute-start | bytes 1572872 | tf_op jit(solution)/shard_map/ppermute | solution.py:188
  51.8 17.4 %collective-permute-start.18 = (f32[96,512]{1,0:T(8,128)S(1)}, f32[96,512]{1,0:T(8,128)S(1)}, u32[]{:S(2)}, u32[]{:S(2)}) collective-permute-start(f32[96,512]{1,0:T(8,128)S(1)} %get-tuple-element.48), channel_id=1, source_target_pairs={{0,1},{4,5},{8,9},{12,13},{16,17},{20,21},{24,25},{28,29}} | collective-permute-start | bytes 589832 | tf_op jit(solution)/shard_map/ppermute | solution.py:612
  62.2 20.4 %copy-start.3 = (f32[512,512]{1,0:T(8,128)S(1)}, f32[512,512]{1,0:T(8,128)}, u32[]{:S(2)}) copy-start(f32[512,512]{1,0:T(8,128)} %refs_13_.1) | copy-start | bytes 3145732
  62.2 5.6 %collective-permute-start.10 = (f32[256,128]{1,0:T(8,128)S(1)}, f32[256,128]{1,0:T(8,128)S(1)}, u32[]{:S(2)}, u32[]{:S(2)}) collective-permute-start(f32[256,128]{1,0:T(8,128)S(1)} %get-tuple-element.42), channel_id=1, source_target_pairs={{0,4},{4,8},{8,12},{1,5},{5,9},{9,13},{2,6},{6,10},{10,14},{3,7},{... | collective-permute-start | bytes 393224 | tf_op jit(solution)/shard_map/ppermute | solution.py:66
  63.8 8.5 %collective-permute-start.19 = (f32[96,512]{1,0:T(8,128)S(1)}, f32[96,512]{1,0:T(8,128)S(1)}, u32[]{:S(2)}, u32[]{:S(2)}) collective-permute-start(f32[96,512]{1,0:T(8,128)S(1)} %get-tuple-element.49), channel_id=1, source_target_pairs={{0,2},{4,6},{8,10},{12,14},{16,18},{20,22},{24,26},{28,30}} | collective-permute-start | bytes 589832 | tf_op jit(solution)/shard_map/ppermute | solution.py:612
  66.3 8.6 %collective-permute-start.20 = (f32[96,512]{1,0:T(8,128)S(1)}, f32[96,512]{1,0:T(8,128)S(1)}, u32[]{:S(2)}, u32[]{:S(2)}) collective-permute-start(f32[96,512]{1,0:T(8,128)S(1)} %get-tuple-element.50), channel_id=1, source_target_pairs={{0,3},{4,7},{8,11},{12,15},{16,19},{20,23},{24,27},{28,31}} | collective-permute-start | bytes 589832 | tf_op jit(solution)/shard_map/ppermute | solution.py:612
  68.7 4.7 %collective-permute-start.11 = (f32[2,96,128]{2,1,0:T(8,128)S(1)}, f32[2,96,128]{2,1,0:T(8,128)S(1)}, u32[]{:S(2)}, u32[]{:S(2)}) collective-permute-start(f32[2,96,128]{2,1,0:T(8,128)S(1)} %get-tuple-element.44), channel_id=1, source_target_pairs={{0,1},{1,0},{2,3},{3,2},{4,5},{5,4},{6,7},{7,6},{8,9},{9,8},{10,11... | collective-permute-start | bytes 294920 | tf_op jit(solution)/shard_map/ppermute | solution.py:61
  68.8 4.7 %collective-permute-start.12 = (f32[2,96,128]{2,1,0:T(8,128)S(1)}, f32[2,96,128]{2,1,0:T(8,128)S(1)}, u32[]{:S(2)}, u32[]{:S(2)}) collective-permute-start(f32[2,96,128]{2,1,0:T(8,128)S(1)} %get-tuple-element.45), channel_id=1, source_target_pairs={{0,2},{1,3},{2,0},{3,1},{4,6},{5,7},{6,4},{7,5},{8,10},{9,11},{10,... | collective-permute-start | bytes 294920 | tf_op jit(solution)/shard_map/ppermute | solution.py:61
  69.2 5.6 %collective-permute-start.13 = (f32[2,96,128]{2,1,0:T(8,128)S(1)}, f32[2,96,128]{2,1,0:T(8,128)S(1)}, u32[]{:S(2)}, u32[]{:S(2)}) collective-permute-start(f32[2,96,128]{2,1,0:T(8,128)S(1)} %get-tuple-element.46), channel_id=1, source_target_pairs={{0,3},{1,2},{2,1},{3,0},{4,7},{5,6},{6,5},{7,4},{8,11},{9,10},{10,... | collective-permute-start | bytes 294920 | tf_op jit(solution)/shard_map/ppermute | solution.py:61
  72.3 4.7 %collective-permute-start.14 = (f32[2,96,128]{2,1,0:T(8,128)S(1)}, f32[2,96,128]{2,1,0:T(8,128)S(1)}, u32[]{:S(2)}, u32[]{:S(2)}) collective-permute-start(f32[2,96,128]{2,1,0:T(8,128)S(1)} %get-tuple-element.43.refs_1_), channel_id=1, source_target_pairs={{0,16},{16,0},{1,17},{17,1},{2,18},{18,2},{3,19},{19,3},{4,20},{20... | collective-permute-start | bytes 294920 | tf_op jit(solution)/shard_map/ppermute | solution.py:61
  73.4 5.0 %collective-permute-start.15 = (f32[2,96,128]{2,1,0:T(8,128)S(1)}, f32[2,96,128]{2,1,0:T(8,128)S(1)}, u32[]{:S(2)}, u32[]{:S(2)}) collective-permute-start(f32[2,96,128]{2,1,0:T(8,128)S(1)} %collective-permute-done.11.refs_2_), channel_id=1, source_target_pairs={{0,16},{16,0},{1,17},{17,1},{2,18},{18,2},{3,19},{19,3},{4,20},{20... | collective-permute-start | bytes 294920 | tf_op jit(solution)/shard_map/ppermute | solution.py:61
  73.5 5.1 %collective-permute-start.16 = (f32[2,96,128]{2,1,0:T(8,128)S(1)}, f32[2,96,128]{2,1,0:T(8,128)S(1)}, u32[]{:S(2)}, u32[]{:S(2)}) collective-permute-start(f32[2,96,128]{2,1,0:T(8,128)S(1)} %collective-permute-done.12.refs_3_), channel_id=1, source_target_pairs={{0,16},{16,0},{1,17},{17,1},{2,18},{18,2},{3,19},{19,3},{4,20},{20... | collective-permute-start | bytes 294920 | tf_op jit(solution)/shard_map/ppermute | solution.py:61
  74.9 3.7 %collective-permute-start.17 = (f32[2,96,128]{2,1,0:T(8,128)S(1)}, f32[2,96,128]{2,1,0:T(8,128)S(1)}, u32[]{:S(2)}, u32[]{:S(2)}) collective-permute-start(f32[2,96,128]{2,1,0:T(8,128)S(1)} %collective-permute-done.13.refs_4_), channel_id=1, source_target_pairs={{0,16},{16,0},{1,17},{17,1},{2,18},{18,2},{3,19},{19,3},{4,20},{20... | collective-permute-start | bytes 294920 | tf_op jit(solution)/shard_map/ppermute | solution.py:61
  74.9 9.9 %collective-permute-start.31 = (f32[512,128]{1,0:T(8,128)S(1)}, f32[512,128]{1,0:T(8,128)S(1)}, u32[]{:S(2)}, u32[]{:S(2)}) collective-permute-start(f32[512,128]{1,0:T(8,128)S(1)} %get-tuple-element.39.refs_2_), channel_id=1, source_target_pairs={{0,1},{1,0},{2,3},{3,2},{4,5},{5,4},{6,7},{7,6},{8,9},{9,8},{10,11... | collective-permute-start | bytes 786440 | tf_op jit(solution)/shard_map/ppermute | solution.py:61
  77.0 13.7 %collective-permute-start.32 = (f32[512,128]{1,0:T(8,128)S(1)}, f32[512,128]{1,0:T(8,128)S(1)}, u32[]{:S(2)}, u32[]{:S(2)}) collective-permute-start(f32[512,128]{1,0:T(8,128)S(1)} %get-tuple-element.40.refs_3_), channel_id=1, source_target_pairs={{0,2},{1,3},{2,0},{3,1},{4,6},{5,7},{6,4},{7,5},{8,10},{9,11},{10,... | collective-permute-start | bytes 786440 | tf_op jit(solution)/shard_map/ppermute | solution.py:61
  78.4 12.3 %collective-permute-start.33 = (f32[512,128]{1,0:T(8,128)S(1)}, f32[512,128]{1,0:T(8,128)S(1)}, u32[]{:S(2)}, u32[]{:S(2)}) collective-permute-start(f32[512,128]{1,0:T(8,128)S(1)} %get-tuple-element.41.refs_4_), channel_id=1, source_target_pairs={{0,3},{1,2},{2,1},{3,0},{4,7},{5,6},{6,5},{7,4},{8,11},{9,10},{10,... | collective-permute-start | bytes 786440 | tf_op jit(solution)/shard_map/ppermute | solution.py:61
  78.5 13.9 %collective-permute-start.38 = (f32[512,128]{1,0:T(8,128)S(1)}, f32[512,128]{1,0:T(8,128)S(1)}, u32[]{:S(2)}, u32[]{:S(2)}) collective-permute-start(f32[512,128]{1,0:T(8,128)S(1)} %get-tuple-element.38.refs_1_.refs_2_), channel_id=1, source_target_pairs={{0,16},{16,0},{1,17},{17,1},{2,18},{18,2},{3,19},{19,3},{4,20},{20... | collective-permute-start | bytes 786440 | tf_op jit(solution)/shard_map/ppermute | solution.py:61
  78.6 15.5 %collective-permute-start.34 = (f32[3,256,128]{2,1,0:T(8,128)S(1)}, f32[3,256,128]{2,1,0:T(8,128)S(1)}, u32[]{:S(2)}, u32[]{:S(2)}) collective-permute-start(f32[3,256,128]{2,1,0:T(8,128)S(1)} %get-tuple-element.55), channel_id=1, source_target_pairs={{0,4},{4,8},{8,12},{1,5},{5,9},{9,13},{2,6},{6,10},{10,14},{3,7},{... | collective-permute-start | bytes 1179656 | tf_op jit(solution)/shard_map/ppermute | solution.py:66
  84.8 10.2 %collective-permute-start.46 = (f32[96,512]{1,0:T(8,128)S(1)}, f32[96,512]{1,0:T(8,128)S(1)}, u32[]{:S(2)}, u32[]{:S(2)}) collective-permute-start(f32[96,512]{1,0:T(8,128)S(1)} %factor_slice.1.refs_1_), channel_id=1, source_target_pairs={{0,1},{1,0},{2,3},{3,2},{4,5},{5,4},{6,7},{7,6},{8,9},{9,8},{10,11... | collective-permute-start | bytes 589832 | tf_op jit(solution)/shard_map/ppermute | solution.py:61
  90.7 13.3 %collective-permute-start.39 = (f32[512,128]{1,0:T(8,128)S(1)}, f32[512,128]{1,0:T(8,128)S(1)}, u32[]{:S(2)}, u32[]{:S(2)}) collective-permute-start(f32[512,128]{1,0:T(8,128)S(1)} %collective-permute-done.31.refs_3_), channel_id=1, source_target_pairs={{0,16},{16,0},{1,17},{17,1},{2,18},{18,2},{3,19},{19,3},{4,20},{20... | collective-permute-start | bytes 786440 | tf_op jit(solution)/shard_map/ppermute | solution.py:61
  90.7 11.5 %collective-permute-start.47 = (f32[96,512]{1,0:T(8,128)S(1)}, f32[96,512]{1,0:T(8,128)S(1)}, u32[]{:S(2)}, u32[]{:S(2)}) collective-permute-start(f32[96,512]{1,0:T(8,128)S(1)} %factor_slice.1.refs_1_), channel_id=1, source_target_pairs={{0,2},{1,3},{2,0},{3,1},{4,6},{5,7},{6,4},{7,5},{8,10},{9,11},{10,... | collective-permute-start | bytes 589832 | tf_op jit(solution)/shard_map/ppermute | solution.py:61
  92.4 10.4 %collective-permute-start.48 = (f32[96,512]{1,0:T(8,128)S(1)}, f32[96,512]{1,0:T(8,128)S(1)}, u32[]{:S(2)}, u32[]{:S(2)}) collective-permute-start(f32[96,512]{1,0:T(8,128)S(1)} %factor_slice.1.refs_1_), channel_id=1, source_target_pairs={{0,3},{1,2},{2,1},{3,0},{4,7},{5,6},{6,5},{7,4},{8,11},{9,10},{10,... | collective-permute-start | bytes 589832 | tf_op jit(solution)/shard_map/ppermute | solution.py:61
  94.1 10.8 %collective-permute-start.21 = (f32[96,512]{1,0:T(8,128)S(1)}, f32[96,512]{1,0:T(8,128)S(1)}, u32[]{:S(2)}, u32[]{:S(2)}) collective-permute-start(f32[96,512]{1,0:T(8,128)S(1)} %factor_slice.1.refs_1_), channel_id=1, source_target_pairs={{0,4},{4,8},{8,12},{12,0},{1,5},{5,9},{9,13},{13,1},{2,6},{6,10},{... | collective-permute-start | bytes 589832 | tf_op jit(solution)/shard_map/ppermute | solution.py:56
  95.0 14.9 %collective-permute-start.22 = (f32[96,512]{1,0:T(8,128)S(1)}, f32[96,512]{1,0:T(8,128)S(1)}, u32[]{:S(2)}, u32[]{:S(2)}) collective-permute-start(f32[96,512]{1,0:T(8,128)S(1)} %factor_slice.1.refs_1_), channel_id=1, source_target_pairs={{0,8},{4,12},{8,0},{12,4},{1,9},{5,13},{9,1},{13,5},{2,10},{6,14},... | collective-permute-start | bytes 589832 | tf_op jit(solution)/shard_map/ppermute | solution.py:56
  97.5 48.7 %copy-start.1 = (f32[384,768]{1,0:T(8,128)S(1)}, f32[384,768]{1,0:T(8,128)}, u32[]{:S(2)}) copy-start(f32[384,768]{1,0:T(8,128)} %refs_1_.1) | copy-start | bytes 3538948
  102.2 15.0 %collective-permute-start.35 = (f32[1024,128]{1,0:T(8,128)S(1)}, f32[1024,128]{1,0:T(8,128)S(1)}, u32[]{:S(2)}, u32[]{:S(2)}) collective-permute-start(f32[1024,128]{1,0:T(8,128)S(1)} %get-tuple-element.57), channel_id=1, source_target_pairs={{0,1},{1,0},{2,3},{3,2},{4,5},{5,4},{6,7},{7,6},{8,9},{9,8},{10,11... | collective-permute-start | bytes 1572872 | tf_op jit(solution)/shard_map/ppermute | solution.py:61
  102.8 22.2 %collective-permute-start.36 = (f32[1024,128]{1,0:T(8,128)S(1)}, f32[1024,128]{1,0:T(8,128)S(1)}, u32[]{:S(2)}, u32[]{:S(2)}) collective-permute-start(f32[1024,128]{1,0:T(8,128)S(1)} %get-tuple-element.58), channel_id=1, source_target_pairs={{0,2},{1,3},{2,0},{3,1},{4,6},{5,7},{6,4},{7,5},{8,10},{9,11},{10,... | collective-permute-start | bytes 1572872 | tf_op jit(solution)/shard_map/ppermute | solution.py:61
  104.0 10.0 %collective-permute-start.23 = (f32[96,512]{1,0:T(8,128)S(1)}, f32[96,512]{1,0:T(8,128)S(1)}, u32[]{:S(2)}, u32[]{:S(2)}) collective-permute-start(f32[96,512]{1,0:T(8,128)S(1)} %factor_slice.1.refs_1_), channel_id=1, source_target_pairs={{0,12},{4,0},{8,4},{12,8},{1,13},{5,1},{9,5},{13,9},{2,14},{6,2},{... | collective-permute-start | bytes 589832 | tf_op jit(solution)/shard_map/ppermute | solution.py:56
  104.9 10.8 %collective-permute-start.40 = (f32[512,128]{1,0:T(8,128)S(1)}, f32[512,128]{1,0:T(8,128)S(1)}, u32[]{:S(2)}, u32[]{:S(2)}) collective-permute-start(f32[512,128]{1,0:T(8,128)S(1)} %collective-permute-done.32.refs_4_), channel_id=1, source_target_pairs={{0,16},{16,0},{1,17},{17,1},{2,18},{18,2},{3,19},{19,3},{4,20},{20... | collective-permute-start | bytes 786440 | tf_op jit(solution)/shard_map/ppermute | solution.py:61
  109.9 23.0 %collective-permute-start.37 = (f32[1024,128]{1,0:T(8,128)S(1)}, f32[1024,128]{1,0:T(8,128)S(1)}, u32[]{:S(2)}, u32[]{:S(2)}) collective-permute-start(f32[1024,128]{1,0:T(8,128)S(1)} %get-tuple-element.59), channel_id=1, source_target_pairs={{0,3},{1,2},{2,1},{3,0},{4,7},{5,6},{6,5},{7,4},{8,11},{9,10},{10,... | collective-permute-start | bytes 1572872 | tf_op jit(solution)/shard_map/ppermute | solution.py:61
  114.0 3.0 %collective-permute-start.41 = (f32[512,128]{1,0:T(8,128)S(1)}, f32[512,128]{1,0:T(8,128)S(1)}, u32[]{:S(2)}, u32[]{:S(2)}) collective-permute-start(f32[512,128]{1,0:T(8,128)S(1)} %collective-permute-done.33.refs_5_), channel_id=1, source_target_pairs={{0,16},{16,0},{1,17},{17,1},{2,18},{18,2},{3,19},{19,3},{4,20},{20... | collective-permute-start | bytes 786440 | tf_op jit(solution)/shard_map/ppermute | solution.py:61
  115.7 15.5 %collective-permute-start.24 = (f32[96,512]{1,0:T(8,128)S(1)}, f32[96,512]{1,0:T(8,128)S(1)}, u32[]{:S(2)}, u32[]{:S(2)}) collective-permute-start(f32[96,512]{1,0:T(8,128)S(1)} %get-tuple-element.52), channel_id=1, source_target_pairs={{0,1},{1,0},{2,3},{3,2},{4,5},{5,4},{6,7},{7,6},{8,9},{9,8},{10,11... | collective-permute-start | bytes 589832 | tf_op jit(solution)/shard_map/ppermute | solution.py:61
  117.0 26.5 %collective-permute-start.42 = (f32[1024,128]{1,0:T(8,128)S(1)}, f32[1024,128]{1,0:T(8,128)S(1)}, u32[]{:S(2)}, u32[]{:S(2)}) collective-permute-start(f32[1024,128]{1,0:T(8,128)S(1)} %get-tuple-element.56.refs_6_), channel_id=1, source_target_pairs={{0,16},{16,0},{1,17},{17,1},{2,18},{18,2},{3,19},{19,3},{4,20},{20... | collective-permute-start | bytes 1572872 | tf_op jit(solution)/shard_map/ppermute | solution.py:61
  117.2 26.8 %collective-permute-start.43 = (f32[1024,128]{1,0:T(8,128)S(1)}, f32[1024,128]{1,0:T(8,128)S(1)}, u32[]{:S(2)}, u32[]{:S(2)}) collective-permute-start(f32[1024,128]{1,0:T(8,128)S(1)} %collective-permute-done.35.refs_7_), channel_id=1, source_target_pairs={{0,16},{16,0},{1,17},{17,1},{2,18},{18,2},{3,19},{19,3},{4,20},{20... | collective-permute-start | bytes 1572872 | tf_op jit(solution)/shard_map/ppermute | solution.py:61
  125.0 19.0 %collective-permute-start.44 = (f32[1024,128]{1,0:T(8,128)S(1)}, f32[1024,128]{1,0:T(8,128)S(1)}, u32[]{:S(2)}, u32[]{:S(2)}) collective-permute-start(f32[1024,128]{1,0:T(8,128)S(1)} %collective-permute-done.36.refs_8_), channel_id=1, source_target_pairs={{0,16},{16,0},{1,17},{17,1},{2,18},{18,2},{3,19},{19,3},{4,20},{20... | collective-permute-start | bytes 1572872 | tf_op jit(solution)/shard_map/ppermute | solution.py:61
  131.2 5.7 %collective-permute-start.25 = (f32[96,512]{1,0:T(8,128)S(1)}, f32[96,512]{1,0:T(8,128)S(1)}, u32[]{:S(2)}, u32[]{:S(2)}) collective-permute-start(f32[96,512]{1,0:T(8,128)S(1)} %get-tuple-element.53), channel_id=1, source_target_pairs={{0,2},{1,3},{2,0},{3,1},{4,6},{5,7},{6,4},{7,5},{8,10},{9,11},{10,... | collective-permute-start | bytes 589832 | tf_op jit(solution)/shard_map/ppermute | solution.py:61
  132.9 13.3 %collective-permute-start.45 = (f32[1024,128]{1,0:T(8,128)S(1)}, f32[1024,128]{1,0:T(8,128)S(1)}, u32[]{:S(2)}, u32[]{:S(2)}) collective-permute-start(f32[1024,128]{1,0:T(8,128)S(1)} %collective-permute-done.37.refs_9_), channel_id=1, source_target_pairs={{0,16},{16,0},{1,17},{17,1},{2,18},{18,2},{3,19},{19,3},{4,20},{20... | collective-permute-start | bytes 1572872 | tf_op jit(solution)/shard_map/ppermute | solution.py:61
  136.9 6.6 %collective-permute-start.26 = (f32[96,512]{1,0:T(8,128)S(1)}, f32[96,512]{1,0:T(8,128)S(1)}, u32[]{:S(2)}, u32[]{:S(2)}) collective-permute-start(f32[96,512]{1,0:T(8,128)S(1)} %get-tuple-element.54), channel_id=1, source_target_pairs={{0,3},{1,2},{2,1},{3,0},{4,7},{5,6},{6,5},{7,4},{8,11},{9,10},{10,... | collective-permute-start | bytes 589832 | tf_op jit(solution)/shard_map/ppermute | solution.py:61
  143.4 6.4 %collective-permute-start.27 = (f32[96,512]{1,0:T(8,128)S(1)}, f32[96,512]{1,0:T(8,128)S(1)}, u32[]{:S(2)}, u32[]{:S(2)}) collective-permute-start(f32[96,512]{1,0:T(8,128)S(1)} %get-tuple-element.51.refs_1_), channel_id=1, source_target_pairs={{0,16},{16,0},{1,17},{17,1},{2,18},{18,2},{3,19},{19,3},{4,20},{20... | collective-permute-start | bytes 589832 | tf_op jit(solution)/shard_map/ppermute | solution.py:61
  143.4 6.4 %collective-permute-start.28 = (f32[96,512]{1,0:T(8,128)S(1)}, f32[96,512]{1,0:T(8,128)S(1)}, u32[]{:S(2)}, u32[]{:S(2)}) collective-permute-start(f32[96,512]{1,0:T(8,128)S(1)} %collective-permute-done.24.refs_2_), channel_id=1, source_target_pairs={{0,16},{16,0},{1,17},{17,1},{2,18},{18,2},{3,19},{19,3},{4,20},{20... | collective-permute-start | bytes 589832 | tf_op jit(solution)/shard_map/ppermute | solution.py:61
  143.9 5.9 %collective-permute-start.29 = (f32[96,512]{1,0:T(8,128)S(1)}, f32[96,512]{1,0:T(8,128)S(1)}, u32[]{:S(2)}, u32[]{:S(2)}) collective-permute-start(f32[96,512]{1,0:T(8,128)S(1)} %collective-permute-done.25.refs_3_), channel_id=1, source_target_pairs={{0,16},{16,0},{1,17},{17,1},{2,18},{18,2},{3,19},{19,3},{4,20},{20... | collective-permute-start | bytes 589832 | tf_op jit(solution)/shard_map/ppermute | solution.py:61
  144.0 5.9 %collective-permute-start.30 = (f32[96,512]{1,0:T(8,128)S(1)}, f32[96,512]{1,0:T(8,128)S(1)}, u32[]{:S(2)}, u32[]{:S(2)}) collective-permute-start(f32[96,512]{1,0:T(8,128)S(1)} %collective-permute-done.26.refs_4_), channel_id=1, source_target_pairs={{0,16},{16,0},{1,17},{17,1},{2,18},{18,2},{3,19},{19,3},{4,20},{20... | collective-permute-start | bytes 589832 | tf_op jit(solution)/shard_map/ppermute | solution.py:61

commit v9 on v6

--- a/solution.py
+++ b/solution.py
@@ -545,35 +545,47 @@
         sc = refs[0]
         own_refs = refs[1 : 1 + count]
         other_refs = refs[1 + count : 1 + 2 * count]
-        base_ref, high_ref, low_ref, out, col_factor, sems = refs[1 + 2 * count :]
-        own = gather_copies(sc, own_refs, col_factor.at[sc[SIB]], sems, piece_rows)
-        other = gather_copies(
-            sc, other_refs, col_factor.at[1 - sc[SIB]], sems, piece_rows, count
-        )
-        run_copies(own + other)
+        base_ref, high_ref, low_ref, out, col_factor, result, sems = refs[1 + 2 * count :]
+        own = gather_copies(sc, own_refs, col_factor.at[0], sems, piece_rows)
+        other = gather_copies(sc, other_refs, col_factor.at[1], sems, piece_rows, count)
+        for copy in own + other:
+            copy.start()
         left = high_ref[...], low_ref[...]
         first_row = (sc[ROW] * 2 + sc[SIB]) * HALF
         first_col = sc[COL] * PBD
-        for side in range(2):
-            product = times_transpose(left, halves(col_factor[side]))
-            for i in range(HALF):
-                q = side * HALF + i
-                cols = slice(q * BLK, (q + 1) * BLK)
-                for p in range(HALF):
-                    lines = slice(p * BLK, (p + 1) * BLK)
-                    total = base_ref[lines, cols]
-                    inside = (first_col + q >= PIV) & (first_row + p >= PIV)
-                    reduced = total - product[lines, i * BLK : (i + 1) * BLK]
-                    out[lines, cols] = jnp.where(inside, reduced, total)
+        writes = []
+        for which, copies in ((0, own), (1, other)):
+            for copy in copies:
+                copy.wait()
+            side = jnp.abs(sc[SIB] - which)
+            lanes = span(side, rows)
+            product = times_transpose(left, halves(col_factor[which]))
+            for p in range(HALF):
+                lines = slice(p * BLK, (p + 1) * BLK)
+                for i in range(HALF):
+                    cols = slice(i * BLK, (i + 1) * BLK)
+                    here = span(side * HALF + i, BLK)
+                    total = base_ref[lines, here]
+                    inside = (first_col + side * HALF + i >= PIV) & (first_row + p >= PIV)
+                    reduced = total - product[lines, cols]
+                    result[which, lines, cols] = jnp.where(inside, reduced, total)
+            write = pltpu.make_async_copy(
+                result.at[which], out.at[:, lanes], sems.at[2 * count + which]
+            )
+            write.start()
+            writes.append(write)
+        for write in writes:
+            write.wait()
 
     return pl.pallas_call(
         body,
         in_specs=[SMEM] + [ANY] * (2 * count) + [VMEM] * 3,
-        out_specs=VMEM,
+        out_specs=ANY,
         out_shape=f32(rows, width),
         scratch_shapes=[
             pltpu.VMEM((2, rows, PANEL), jnp.float32),
-            pltpu.SemaphoreType.DMA((2 * count,)),
+            pltpu.VMEM((2, rows, rows), jnp.float32),
+            pltpu.SemaphoreType.DMA((2 * count + 2,)),
         ],
         compiler_params=limit_for(BLK, 16),
         name="finish",

time: 161 us -> 161 us (level)
  no operation moved by 1% of the time
where the time goes in v9:
time: 161 us; the launch traced here: 160 us
  starting transfers between devices  70.6 us (44%)
  waiting for transfers between devices  61.8 us (38%)
  Pallas kernels  23.8 us (15%)
  local copies, waits for them, and re-layouts  3.18 us (2%)
    ppermute x41, waiting for transfers between devices, swapped(): return lax.ppermute(value, axis, [(i, i ^ mask) for i in range(count)])  49.2 us
    ppermute x41, starting transfers between devices, swapped(): return lax.ppermute(value, axis, [(i, i ^ mask) for i in range(count)])  38.2 us
    ppermute x4, starting transfers between devices, rotated(): lax.ppermute(value, axis, [(i, (i + steps) % count) for i in range(count)])  7.95 us
    ppermute x4, waiting for transfers between devices, rotated(): lax.ppermute(value, axis, [(i, (i + steps) % count) for i in range(count)])  7.74 us
    ppermute x2, starting transfers between devices, shifted(): return lax.ppermute(value, axis, [(i, i + 1) for i in range(count - 1)])  6.77 us
    ppermute x3, starting transfers between devices, shards(): dealt.append(lax.ppermute(value, 'col', [(0, j)]) if j else value)  6 us
    pallas_call x1, Pallas kernels, finish(): pl.pallas_call(body, in_specs=[SMEM] + [ANY] * (2 * count) + [VMEM] * 3,...  5.16 us
    pallas_call x1, Pallas kernels, slice_products(): pl.pallas_call(body, in_specs=[SMEM] + [ANY] * (count + many) + [VMEM] *...  4.33 us
  transfers between devices with their start and end apart: 56, of which 15 were waited for; matrix products, arithmetic and copies ran while one was open for 0% of the time, Pallas kernels for 12%

profile of v9, /device:TPU:0, one launch (start us, length us, event | category | flops | bytes accessed | tf_op | source)
XLA Modules:
  0.0 159.7 jit_solution(8666889979093961237)
XLA Ops:
  0.0 4.1 %collective-permute-start.4 = (f32[128,1024]{1,0:T(8,128)}, f32[128,1024]{1,0:T(8,128)S(1)}, u32[]{:S(2)}, u32[]{:S(2)}) collective-permute-start(f32[128,1024]{1,0:T(8,128)} %bitcast.2), channel_id=1, source_target_pairs={{0,8},{4,12},{8,0},{12,4},{1,9},{5,13},{9,1},{13,5},{2,10},{6,14},... | collective-permute-start | bytes 1572872 | tf_op jit(solution)/shard_map/ppermute | solution.py:56
  4.1 1.5 collective-permute-start
  5.6 0.7 copy-done.5
  6.2 1.3 lookup_table.1.sc.refs_0_
  7.6 1.3 copy-done
  8.9 1.2 copy-done.4
  10.1 0.9 cut_slices.1
  10.9 0.6 collective-permute-start.7
  11.5 1.5 collective-permute-start.8
  13.1 1.4 collective-permute-start.9
  14.5 10.2 %collective-permute-done.7.refs_11_ = f32[512,128]{1,0:T(8,128)S(1)} collective-permute-done((f32[512,128]{1,0:T(8,128)S(1)}, f32[512,128]{1,0:T(8,128)S(1)}, u32[]{:S(2)}, u32[]{:S(2)}) %collective-permute-start.7) | collective-permute-done | bytes 262176 | tf_op jit(solution)/shard_map/ppermute | solution.py:61
  24.7 1.5 collective-permute-start.1
  26.2 1.4 collective-permute-start.2
  27.6 3.7 %collective-permute-done.9.refs_13_ = f32[512,128]{1,0:T(8,128)S(1)} collective-permute-done((f32[512,128]{1,0:T(8,128)S(1)}, f32[512,128]{1,0:T(8,128)S(1)}, u32[]{:S(2)}, u32[]{:S(2)}) %collective-permute-start.9) | collective-permute-done | bytes 262176 | tf_op jit(solution)/shard_map/ppermute | solution.py:61
  31.4 3.5 %collective-permute-start.3 = (f32[128,1024]{1,0:T(8,128)S(1)}, f32[128,1024]{1,0:T(8,128)S(1)}, u32[]{:S(2)}, u32[]{:S(2)}) collective-permute-start(f32[128,1024]{1,0:T(8,128)S(1)} %bitcast.6), channel_id=1, source_target_pairs={{0,4},{4,8},{8,12},{1,5},{5,9},{9,13},{2,6},{6,10},{10,14},{3,7},{... | collective-permute-start | bytes 1572872 | tf_op jit(solution)/shard_map/ppermute | solution.py:184
  34.9 1.3 collective-permute-start.6
  36.2 1.3 collective-permute-start.5
  37.5 14.3 %collective-permute-done.1.refs_3_ = f32[128,1024]{1,0:T(8,128)S(1)} collective-permute-done((f32[128,1024]{1,0:T(8,128)S(1)}, f32[128,1024]{1,0:T(8,128)S(1)}, u32[]{:S(2)}, u32[]{:S(2)}) %collective-permute-start.1) | collective-permute-done | bytes 524320 | tf_op jit(solution)/shard_map/ppermute | solution.py:61
  51.8 3.4 %collective-permute-start.18 = (f32[96,512]{1,0:T(8,128)S(1)}, f32[96,512]{1,0:T(8,128)S(1)}, u32[]{:S(2)}, u32[]{:S(2)}) collective-permute-start(f32[96,512]{1,0:T(8,128)S(1)} %get-tuple-element.51), channel_id=1, source_target_pairs={{0,1},{4,5},{8,9},{12,13},{16,17},{20,21},{24,25},{28,29}} | collective-permute-start | bytes 589832 | tf_op jit(solution)/shard_map/ppermute | solution.py:629
  55.2 1.3 collective-permute-start.19
  56.5 1.3 collective-permute-start.20
  57.8 1.0 collective-permute-done.5.refs_8_
  58.8 4.3 %slice_products.1 = (f32[512,128]{1,0:T(8,128)S(1)}, f32[512,128]{1,0:T(8,128)S(1)}, f32[512,128]{1,0:T(8,128)S(1)}, f32[512,128]{1,0:T(8,128)S(1)}, f32[512,128...) custom-call(s32[35]{0:T(128)S(1)} %lookup_table.1.sc.refs_0_, ...), custom_call_target="tpu_custom_call" | custom-call | tf_op jit(solution)/shard_map/slice_products/pallas_call | solution.py:237
  63.1 2.7 %collective-permute-start.10 = (f32[256,128]{1,0:T(8,128)S(1)}, f32[256,128]{1,0:T(8,128)S(1)}, u32[]{:S(2)}, u32[]{:S(2)}) collective-permute-start(f32[256,128]{1,0:T(8,128)S(1)} %get-tuple-element.45), channel_id=1, source_target_pairs={{0,4},{4,8},{8,12},{1,5},{5,9},{9,13},{2,6},{6,10},{10,14},{3,7},{... | collective-permute-start | bytes 393224 | tf_op jit(solution)/shard_map/ppermute | solution.py:66
  65.8 2.5 %collective-permute-done.10.refs_5_.edge_ref = f32[256,128]{1,0:T(8,128)S(1)} collective-permute-done((f32[256,128]{1,0:T(8,128)S(1)}, f32[256,128]{1,0:T(8,128)S(1)}, u32[]{:S(2)}, u32[]{:S(2)}) %collective-permute-start.10) | collective-permute-done | bytes 131104 | tf_op jit(solution)/shard_map/ppermute | solution.py:66
  68.3 0.8 place_rows.1
  69.2 0.5 collective-permute-start.11
  69.6 1.3 collective-permute-start.39
  70.9 1.7 %collective-permute-start.31 = (f32[512,128]{1,0:T(8,128)S(1)}, f32[512,128]{1,0:T(8,128)S(1)}, u32[]{:S(2)}, u32[]{:S(2)}) collective-permute-start(f32[512,128]{1,0:T(8,128)S(1)} %get-tuple-element.42.refs_2_), channel_id=1, source_target_pairs={{0,1},{1,0},{2,3},{3,2},{4,5},{5,4},{6,7},{7,6},{8,9},{9,8},{10,11... | collective-permute-start | bytes 786440 | tf_op jit(solution)/shard_map/ppermute | solution.py:61
  72.6 2.7 %collective-permute-start.12 = (f32[2,96,128]{2,1,0:T(8,128)S(1)}, f32[2,96,128]{2,1,0:T(8,128)S(1)}, u32[]{:S(2)}, u32[]{:S(2)}) collective-permute-start(f32[2,96,128]{2,1,0:T(8,128)S(1)} %get-tuple-element.48), channel_id=1, source_target_pairs={{0,2},{1,3},{2,0},{3,1},{4,6},{5,7},{6,4},{7,5},{8,10},{9,11},{10,... | collective-permute-start | bytes 294920 | tf_op jit(solution)/shard_map/ppermute | solution.py:61
  75.4 1.8 %collective-permute-start.13 = (f32[2,96,128]{2,1,0:T(8,128)S(1)}, f32[2,96,128]{2,1,0:T(8,128)S(1)}, u32[]{:S(2)}, u32[]{:S(2)}) collective-permute-start(f32[2,96,128]{2,1,0:T(8,128)S(1)} %get-tuple-element.49), channel_id=1, source_target_pairs={{0,3},{1,2},{2,1},{3,0},{4,7},{5,6},{6,5},{7,4},{8,11},{9,10},{10,... | collective-permute-start | bytes 294920 | tf_op jit(solution)/shard_map/ppermute | solution.py:61
  77.2 7.6 %collective-permute-done.12.refs_3_ = f32[2,96,128]{2,1,0:T(8,128)S(1)} collective-permute-done((f32[2,96,128]{2,1,0:T(8,128)S(1)}, f32[2,96,128]{2,1,0:T(8,128)S(1)}, u32[]{:S(2)}, u32[]{:S(2)}) %collective-permute-start.12) | collective-permute-done | bytes 98336 | tf_op jit(solution)/shard_map/ppermute | solution.py:61
  84.7 0.5 collective-permute-start.15
  85.2 0.8 collective-permute-done.14.refs_5_
  86.0 0.7 collective-permute-start.33
  86.7 4.1 %collective-permute-start.34 = (f32[3,256,128]{2,1,0:T(8,128)S(1)}, f32[3,256,128]{2,1,0:T(8,128)S(1)}, u32[]{:S(2)}, u32[]{:S(2)}) collective-permute-start(f32[3,256,128]{2,1,0:T(8,128)S(1)} %get-tuple-element.58), channel_id=1, source_target_pairs={{0,4},{4,8},{8,12},{1,5},{5,9},{9,13},{2,6},{6,10},{10,14},{3,7},{... | collective-permute-start | bytes 1179656 | tf_op jit(solution)/shard_map/ppermute | solution.py:66
  91.4 0.8 collective-permute-done.16.refs_7_
  92.2 0.7 collective-permute-start.38
  93.2 2.1 %factor_slice.1.refs_1_ = f32[96,512]{1,0:T(8,128)S(1)} custom-call(s32[35]{0:T(128)S(1)} %lookup_table.1.sc.refs_0_, f32[2,96,128]{2,1,0:T(8,128)S(1)} %get-tuple-element.46.refs_1_, f32[2,96,128]{2,1,0:T(8,128)S(1)} %collective-permute-done.11.refs_2_, f32[2,96,128]{2,1,0:T(8,128)S(1)} %collective-permute-done.12.refs_3_, ...), custom_call_target="tpu_custom_call" | custom-call | tf_op jit(solution)/shard_map/factor_slice/pallas_call | solution.py:409
  95.3 1.7 %collective-permute-start.53 = (f32[96,512]{1,0:T(8,128)S(1)}, f32[96,512]{1,0:T(8,128)S(1)}, u32[]{:S(2)}, u32[]{:S(2)}) collective-permute-start(f32[96,512]{1,0:T(8,128)S(1)} %factor_slice.1.refs_1_), channel_id=1, source_target_pairs={{0,1},{1,0},{2,3},{3,2},{4,5},{5,4},{6,7},{7,6},{8,9},{9,8},{10,11... | collective-permute-start | bytes 589832 | tf_op jit(solution)/shard_map/ppermute | solution.py:61
  97.0 3.9 %collective-permute-start.54 = (f32[96,512]{1,0:T(8,128)S(1)}, f32[96,512]{1,0:T(8,128)S(1)}, u32[]{:S(2)}, u32[]{:S(2)}) collective-permute-start(f32[96,512]{1,0:T(8,128)S(1)} %factor_slice.1.refs_1_), channel_id=1, source_target_pairs={{0,2},{1,3},{2,0},{3,1},{4,6},{5,7},{6,4},{7,5},{8,10},{9,11},{10,... | collective-permute-start | bytes 589832 | tf_op jit(solution)/shard_map/ppermute | solution.py:61
  100.9 4.6 %collective-permute-start.55 = (f32[96,512]{1,0:T(8,128)S(1)}, f32[96,512]{1,0:T(8,128)S(1)}, u32[]{:S(2)}, u32[]{:S(2)}) collective-permute-start(f32[96,512]{1,0:T(8,128)S(1)} %factor_slice.1.refs_1_), channel_id=1, source_target_pairs={{0,3},{1,2},{2,1},{3,0},{4,7},{5,6},{6,5},{7,4},{8,11},{9,10},{10,... | collective-permute-start | bytes 589832 | tf_op jit(solution)/shard_map/ppermute | solution.py:61
  105.5 3.6 %collective-permute-start.40 = (f32[512,128]{1,0:T(8,128)S(1)}, f32[512,128]{1,0:T(8,128)S(1)}, u32[]{:S(2)}, u32[]{:S(2)}) collective-permute-start(f32[512,128]{1,0:T(8,128)S(1)} %collective-permute-done.39.refs_12_), channel_id=1, source_target_pairs={{0,1},{4,5},{8,9},{12,13},{16,17},{20,21},{24,25},{28,29}} | collective-permute-start | bytes 786440 | tf_op jit(solution)/shard_map/ppermute | solution.py:301
  109.2 0.5 collective-permute-start.43
  109.8 3.0 %collective-permute-done.55.refs_4_ = f32[96,512]{1,0:T(8,128)S(1)} collective-permute-done((f32[96,512]{1,0:T(8,128)S(1)}, f32[96,512]{1,0:T(8,128)S(1)}, u32[]{:S(2)}, u32[]{:S(2)}) %collective-permute-start.55) | collective-permute-done | bytes 196640 | tf_op jit(solution)/shard_map/ppermute | solution.py:61
  112.9 1.4 collective-permute-done.40.refs_13_
  114.8 3.4 %collective-permute-start.23 = (f32[96,512]{1,0:T(8,128)S(1)}, f32[96,512]{1,0:T(8,128)S(1)}, u32[]{:S(2)}, u32[]{:S(2)}) collective-permute-start(f32[96,512]{1,0:T(8,128)S(1)} %factor_slice.1.refs_1_), channel_id=1, source_target_pairs={{0,12},{4,0},{8,4},{12,8},{1,13},{5,1},{9,5},{13,9},{2,14},{6,2},{... | collective-permute-start | bytes 589832 | tf_op jit(solution)/shard_map/ppermute | solution.py:56
  118.2 2.0 %pack_halo.1 = (f32[512,128]{1,0:T(8,128)S(1)}, f32[512,128]{1,0:T(8,128)S(1)}, f32[512,128]{1,0:T(8,128)S(1)}, f32[512,128]{1,0:T(8,128)S(1)}) custom-call(s32[35]{0:T(128)S(1)} %lookup_table.1.sc.refs_0_, f32[256,128]{1,0:T(8,128)S(1)} %collective-permute-done.10.refs_5_.edge_ref, f32[3,256,128]{2,1,0:T(8,128)S(1)} %collective-permute-done.34.up_ref), custom_call_target="tpu_custom_call" | custom-call | tf_op jit(solution)/shard_map/pack_halo/pallas_call | solution.py:277
  120.3 2.5 %collective-permute-start.35 = (f32[512,128]{1,0:T(8,128)S(1)}, f32[512,128]{1,0:T(8,128)S(1)}, u32[]{:S(2)}, u32[]{:S(2)}) collective-permute-start(f32[512,128]{1,0:T(8,128)S(1)} %get-tuple-element.60), channel_id=1, source_target_pairs={{0,1},{1,0},{2,3},{3,2},{4,5},{5,4},{6,7},{7,6},{8,9},{9,8},{10,11... | collective-permute-start | bytes 786440 | tf_op jit(solution)/shard_map/ppermute | solution.py:61
  122.8 1.2 collective-permute-done.21.refs_2_
  124.0 6.6 %collective-permute-done.22.refs_3_ = f32[96,512]{1,0:T(8,128)S(1)} collective-permute-done((f32[96,512]{1,0:T(8,128)S(1)}, f32[96,512]{1,0:T(8,128)S(1)}, u32[]{:S(2)}, u32[]{:S(2)}) %collective-permute-start.22) | collective-permute-done | bytes 196640 | tf_op jit(solution)/shard_map/ppermute | solution.py:56
  130.6 1.7 %pick_for_cols.1 = (f32[96,512]{1,0:T(8,128)S(1)}, f32[96,512]{1,0:T(8,128)S(1)}, f32[96,512]{1,0:T(8,128)S(1)}, f32[96,512]{1,0:T(8,128)S(1)}) custom-call(s32[35]{0:T(128)S(1)} %lookup_table.1.sc.refs_0_, f32[96,512]{1,0:T(8,128)S(1)} %factor_slice.1.refs_1_, f32[96,512]{1,0:T(8,128)S(1)} %collective-permute-done.21.refs_2_, ...), custom_call_target="tpu_custom_call" | custom-call | tf_op jit(solution)/shard_map/pick_for_cols/pallas_call | solution.py:322
  132.3 2.0 %collective-permute-start.24 = (f32[96,512]{1,0:T(8,128)S(1)}, f32[96,512]{1,0:T(8,128)S(1)}, u32[]{:S(2)}, u32[]{:S(2)}) collective-permute-start(f32[96,512]{1,0:T(8,128)S(1)} %get-tuple-element.55), channel_id=1, source_target_pairs={{0,1},{1,0},{2,3},{3,2},{4,5},{5,4},{6,7},{7,6},{8,9},{9,8},{10,11... | collective-permute-start | bytes 589832 | tf_op jit(solution)/shard_map/ppermute | solution.py:61
  134.4 1.5 collective-permute-start.25
  136.1 1.9 %collective-permute-done.37.refs_9_ = f32[512,128]{1,0:T(8,128)S(1)} collective-permute-done((f32[512,128]{1,0:T(8,128)S(1)}, f32[512,128]{1,0:T(8,128)S(1)}, u32[]{:S(2)}, u32[]{:S(2)}) %collective-permute-start.37) | collective-permute-done | bytes 262176 | tf_op jit(solution)/shard_map/ppermute | solution.py:61
  138.0 0.5 collective-permute-start.47
  138.5 2.9 %collective-permute-done.24.refs_2_ = f32[96,512]{1,0:T(8,128)S(1)} collective-permute-done((f32[96,512]{1,0:T(8,128)S(1)}, f32[96,512]{1,0:T(8,128)S(1)}, u32[]{:S(2)}, u32[]{:S(2)}) %collective-permute-start.24) | collective-permute-done | bytes 196640 | tf_op jit(solution)/shard_map/ppermute | solution.py:61
  141.4 2.7 %collective-permute-start.26 = (f32[96,512]{1,0:T(8,128)S(1)}, f32[96,512]{1,0:T(8,128)S(1)}, u32[]{:S(2)}, u32[]{:S(2)}) collective-permute-start(f32[96,512]{1,0:T(8,128)S(1)} %get-tuple-element.57), channel_id=1, source_target_pairs={{0,3},{1,2},{2,1},{3,0},{4,7},{5,6},{6,5},{7,4},{8,11},{9,10},{10,... | collective-permute-start | bytes 589832 | tf_op jit(solution)/shard_map/ppermute | solution.py:61
  144.1 4.0 %collective-permute-done.26.refs_4_ = f32[96,512]{1,0:T(8,128)S(1)} collective-permute-done((f32[96,512]{1,0:T(8,128)S(1)}, f32[96,512]{1,0:T(8,128)S(1)}, u32[]{:S(2)}, u32[]{:S(2)}) %collective-permute-start.26) | collective-permute-done | bytes 196640 | tf_op jit(solution)/shard_map/ppermute | solution.py:61
  148.0 0.5 collective-permute-start.28
  148.6 0.4 collective-permute-start.30
  149.1 1.7 %lay_rows.1 = (f32[384,512]{1,0:T(8,128)S(1)}, bf16[384,512]{1,0:T(8,128)(2,1)S(1)}, bf16[384,512]{1,0:T(8,128)(2,1)S(1)}) custom-call(s32[35]{0:T(128)S(1)} %lookup_table.1.sc.refs_0_, f32[96,512]{1,0:T(8,128)S(1)} %factor_slice.1.refs_1_, f32[96,512]{1,0:T(8,128)S(1)} %collective-permute-done.53.refs_2_, f32[96,512]{1,0:T(8,128)S(1)} %collective-permute-done.54.refs_3_, ...), custom_call_target="tpu_custom_call" | custom-call | tf_op jit(solution)/shard_map/lay_rows/pallas_call | solution.py:438
  150.8 3.7 %assemble.1.refs_9_ = f32[384,768]{1,0:T(8,128)S(1)} custom-call(s32[35]{0:T(128)S(1)} %lookup_table.1.sc.refs_0_, f32[384,768]{1,0:T(8,128)S(1)} %copy-done.1, f32[512,128]{1,0:T(8,128)S(1)} %get-tuple-element.41.refs_1_.refs_2_, f32[512,128]{1,0:T(8,128)S(1)} %collective-permute-done.31.refs_3_, f32[512,128]{1,0:T(8,128)S(1)} %collective-permute-done.32.refs_4_, ...), custom_call_target="tpu_custom_call" | custom-call | tf_op jit(solution)/shard_map/assemble/pallas_call | solution.py:524
  154.6 5.2 %finish.1 = f32[384,768]{1,0:T(8,128)} custom-call(s32[35]{0:T(128)S(1)} %lookup_table.1.sc.refs_0_, f32[96,512]{1,0:T(8,128)S(1)} %get-tuple-element.54.refs_1_, f32[96,512]{1,0:T(8,128)S(1)} %collective-permute-done.24.refs_2_, f32[96,512]{1,0:T(8,128)S(1)} %collective-permute-done.25.refs_3_, f32[96,512]{1,0:T(8,128)S(1)} %collective-permute-done.26.refs_4_, ...), custom_call_target="tpu_custom_call" | custom-call | tf_op jit(solution)/shard_map/finish/pallas_call | solution.py:580
  (70 shorter events, 2.1 us)
Async XLA Ops:
  0.0 34.9 %collective-permute-start.4 = (f32[128,1024]{1,0:T(8,128)}, f32[128,1024]{1,0:T(8,128)S(1)}, u32[]{:S(2)}, u32[]{:S(2)}) collective-permute-start(f32[128,1024]{1,0:T(8,128)} %bitcast.2), channel_id=1, source_target_pairs={{0,8},{4,12},{8,0},{12,4},{1,9},{5,13},{9,1},{13,5},{2,10},{6,14},... | collective-permute-start | bytes 1572872 | tf_op jit(solution)/shard_map/ppermute | solution.py:56
  4.1 32.1 %collective-permute-start = (f32[128,1024]{1,0:T(8,128)}, f32[128,1024]{1,0:T(8,128)S(1)}, u32[]{:S(2)}, u32[]{:S(2)}) collective-permute-start(f32[128,1024]{1,0:T(8,128)} %bitcast.3), channel_id=1, source_target_pairs={{0,1},{1,0},{2,3},{3,2},{4,5},{5,4},{6,7},{7,6},{8,9},{9,8},{10,11... | collective-permute-start | bytes 1572872 | tf_op jit(solution)/shard_map/ppermute | solution.py:61
  5.6 0.7 copy-start.5
  7.6 1.3 copy-start
  8.9 1.2 copy-start.4
  10.1 14.6 %copy-start.2 = (f32[1,128,1024]{2,1,0:T(8,128)S(1)}, f32[1,128,1024]{2,1,0:T(8,128)}, u32[]{:S(2)}) copy-start(f32[1,128,1024]{2,1,0:T(8,128)} %param.6) | copy-start | bytes 1572868
  10.9 13.7 %collective-permute-start.7 = (f32[512,128]{1,0:T(8,128)S(1)}, f32[512,128]{1,0:T(8,128)S(1)}, u32[]{:S(2)}, u32[]{:S(2)}) collective-permute-start(f32[512,128]{1,0:T(8,128)S(1)} %get-tuple-element.38), channel_id=1, source_target_pairs={{0,1},{1,0},{2,3},{3,2},{4,5},{5,4},{6,7},{7,6},{8,9},{9,8},{10,11... | collective-permute-start | bytes 786440 | tf_op jit(solution)/shard_map/ppermute | solution.py:61
  11.5 14.7 %collective-permute-start.8 = (f32[512,128]{1,0:T(8,128)S(1)}, f32[512,128]{1,0:T(8,128)S(1)}, u32[]{:S(2)}, u32[]{:S(2)}) collective-permute-start(f32[512,128]{1,0:T(8,128)S(1)} %get-tuple-element.39), channel_id=1, source_target_pairs={{0,2},{1,3},{2,0},{3,1},{4,6},{5,7},{6,4},{7,5},{8,10},{9,11},{10,... | collective-permute-start | bytes 786440 | tf_op jit(solution)/shard_map/ppermute | solution.py:61
  13.1 18.3 %collective-permute-start.9 = (f32[512,128]{1,0:T(8,128)S(1)}, f32[512,128]{1,0:T(8,128)S(1)}, u32[]{:S(2)}, u32[]{:S(2)}) collective-permute-start(f32[512,128]{1,0:T(8,128)S(1)} %get-tuple-element.40), channel_id=1, source_target_pairs={{0,3},{1,2},{2,1},{3,0},{4,7},{5,6},{6,5},{7,4},{8,11},{9,10},{10,... | collective-permute-start | bytes 786440 | tf_op jit(solution)/shard_map/ppermute | solution.py:61
  24.7 27.1 %collective-permute-start.1 = (f32[128,1024]{1,0:T(8,128)S(1)}, f32[128,1024]{1,0:T(8,128)S(1)}, u32[]{:S(2)}, u32[]{:S(2)}) collective-permute-start(f32[128,1024]{1,0:T(8,128)S(1)} %bitcast.4), channel_id=1, source_target_pairs={{0,2},{1,3},{2,0},{3,1},{4,6},{5,7},{6,4},{7,5},{8,10},{9,11},{10,... | collective-permute-start | bytes 1572872 | tf_op jit(solution)/shard_map/ppermute | solution.py:61
  26.2 29.0 %collective-permute-start.2 = (f32[128,1024]{1,0:T(8,128)S(1)}, f32[128,1024]{1,0:T(8,128)S(1)}, u32[]{:S(2)}, u32[]{:S(2)}) collective-permute-start(f32[128,1024]{1,0:T(8,128)S(1)} %bitcast.5), channel_id=1, source_target_pairs={{0,3},{1,2},{2,1},{3,0},{4,7},{5,6},{6,5},{7,4},{8,11},{9,10},{10,... | collective-permute-start | bytes 1572872 | tf_op jit(solution)/shard_map/ppermute | solution.py:61
  31.4 25.2 %collective-permute-start.3 = (f32[128,1024]{1,0:T(8,128)S(1)}, f32[128,1024]{1,0:T(8,128)S(1)}, u32[]{:S(2)}, u32[]{:S(2)}) collective-permute-start(f32[128,1024]{1,0:T(8,128)S(1)} %bitcast.6), channel_id=1, source_target_pairs={{0,4},{4,8},{8,12},{1,5},{5,9},{9,13},{2,6},{6,10},{10,14},{3,7},{... | collective-permute-start | bytes 1572872 | tf_op jit(solution)/shard_map/ppermute | solution.py:184
  34.9 23.0 %collective-permute-start.6 = (f32[128,1024]{1,0:T(8,128)S(1)}, f32[128,1024]{1,0:T(8,128)S(1)}, u32[]{:S(2)}, u32[]{:S(2)}) collective-permute-start(f32[128,1024]{1,0:T(8,128)S(1)} %bitcast.7), channel_id=1, source_target_pairs={{4,0},{8,4},{12,8},{5,1},{9,5},{13,9},{6,2},{10,6},{14,10},{7,3},{... | collective-permute-start | bytes 1572872 | tf_op jit(solution)/shard_map/ppermute | solution.py:185
  36.2 22.6 %collective-permute-start.5 = (f32[128,1024]{1,0:T(8,128)S(1)}, f32[128,1024]{1,0:T(8,128)S(1)}, u32[]{:S(2)}, u32[]{:S(2)}) collective-permute-start(f32[128,1024]{1,0:T(8,128)S(1)} %collective-permute-done.4.refs_7_), channel_id=1, source_target_pairs={{8,12},{4,0},{9,13},{5,1},{10,14},{6,2},{11,15},{7,3},{24,28},{20,... | collective-permute-start | bytes 1572872 | tf_op jit(solution)/shard_map/ppermute | solution.py:188
  51.8 19.1 %collective-permute-start.18 = (f32[96,512]{1,0:T(8,128)S(1)}, f32[96,512]{1,0:T(8,128)S(1)}, u32[]{:S(2)}, u32[]{:S(2)}) collective-permute-start(f32[96,512]{1,0:T(8,128)S(1)} %get-tuple-element.51), channel_id=1, source_target_pairs={{0,1},{4,5},{8,9},{12,13},{16,17},{20,21},{24,25},{28,29}} | collective-permute-start | bytes 589832 | tf_op jit(solution)/shard_map/ppermute | solution.py:629
  55.2 17.4 %collective-permute-start.19 = (f32[96,512]{1,0:T(8,128)S(1)}, f32[96,512]{1,0:T(8,128)S(1)}, u32[]{:S(2)}, u32[]{:S(2)}) collective-permute-start(f32[96,512]{1,0:T(8,128)S(1)} %get-tuple-element.52), channel_id=1, source_target_pairs={{0,2},{4,6},{8,10},{12,14},{16,18},{20,22},{24,26},{28,30}} | collective-permute-start | bytes 589832 | tf_op jit(solution)/shard_map/ppermute | solution.py:629
  56.5 18.8 %collective-permute-start.20 = (f32[96,512]{1,0:T(8,128)S(1)}, f32[96,512]{1,0:T(8,128)S(1)}, u32[]{:S(2)}, u32[]{:S(2)}) collective-permute-start(f32[96,512]{1,0:T(8,128)S(1)} %get-tuple-element.53), channel_id=1, source_target_pairs={{0,3},{4,7},{8,11},{12,15},{16,19},{20,23},{24,27},{28,31}} | collective-permute-start | bytes 589832 | tf_op jit(solution)/shard_map/ppermute | solution.py:629
  63.1 30.0 %copy-start.3 = (f32[512,512]{1,0:T(8,128)S(1)}, f32[512,512]{1,0:T(8,128)}, u32[]{:S(2)}) copy-start(f32[512,512]{1,0:T(8,128)} %refs_13_.1) | copy-start | bytes 3145732
  63.1 5.2 %collective-permute-start.10 = (f32[256,128]{1,0:T(8,128)S(1)}, f32[256,128]{1,0:T(8,128)S(1)}, u32[]{:S(2)}, u32[]{:S(2)}) collective-permute-start(f32[256,128]{1,0:T(8,128)S(1)} %get-tuple-element.45), channel_id=1, source_target_pairs={{0,4},{4,8},{8,12},{1,5},{5,9},{9,13},{2,6},{6,10},{10,14},{3,7},{... | collective-permute-start | bytes 393224 | tf_op jit(solution)/shard_map/ppermute | solution.py:66
  69.2 6.2 %collective-permute-start.11 = (f32[2,96,128]{2,1,0:T(8,128)S(1)}, f32[2,96,128]{2,1,0:T(8,128)S(1)}, u32[]{:S(2)}, u32[]{:S(2)}) collective-permute-start(f32[2,96,128]{2,1,0:T(8,128)S(1)} %get-tuple-element.47), channel_id=1, source_target_pairs={{0,1},{1,0},{2,3},{3,2},{4,5},{5,4},{6,7},{7,6},{8,9},{9,8},{10,11... | collective-permute-start | bytes 294920 | tf_op jit(solution)/shard_map/ppermute | solution.py:61
  69.6 17.1 %collective-permute-start.39 = (f32[512,128]{1,0:T(8,128)S(1)}, f32[512,128]{1,0:T(8,128)S(1)}, u32[]{:S(2)}, u32[]{:S(2)}) collective-permute-start(f32[512,128]{1,0:T(8,128)S(1)} %get-tuple-element.65), channel_id=1, source_target_pairs={{2,0},{3,1},{6,4},{7,5},{10,8},{11,9},{14,12},{15,13},{18,16},{19,... | collective-permute-start | bytes 786440 | tf_op jit(solution)/shard_map/ppermute | solution.py:298
  70.9 15.8 %collective-permute-start.31 = (f32[512,128]{1,0:T(8,128)S(1)}, f32[512,128]{1,0:T(8,128)S(1)}, u32[]{:S(2)}, u32[]{:S(2)}) collective-permute-start(f32[512,128]{1,0:T(8,128)S(1)} %get-tuple-element.42.refs_2_), channel_id=1, source_target_pairs={{0,1},{1,0},{2,3},{3,2},{4,5},{5,4},{6,7},{7,6},{8,9},{9,8},{10,11... | collective-permute-start | bytes 786440 | tf_op jit(solution)/shard_map/ppermute | solution.py:61
  72.6 12.1 %collective-permute-start.12 = (f32[2,96,128]{2,1,0:T(8,128)S(1)}, f32[2,96,128]{2,1,0:T(8,128)S(1)}, u32[]{:S(2)}, u32[]{:S(2)}) collective-permute-start(f32[2,96,128]{2,1,0:T(8,128)S(1)} %get-tuple-element.48), channel_id=1, source_target_pairs={{0,2},{1,3},{2,0},{3,1},{4,6},{5,7},{6,4},{7,5},{8,10},{9,11},{10,... | collective-permute-start | bytes 294920 | tf_op jit(solution)/shard_map/ppermute | solution.py:61
  75.3 15.5 %collective-permute-start.32 = (f32[512,128]{1,0:T(8,128)S(1)}, f32[512,128]{1,0:T(8,128)S(1)}, u32[]{:S(2)}, u32[]{:S(2)}) collective-permute-start(f32[512,128]{1,0:T(8,128)S(1)} %get-tuple-element.43.refs_3_), channel_id=1, source_target_pairs={{0,2},{1,3},{2,0},{3,1},{4,6},{5,7},{6,4},{7,5},{8,10},{9,11},{10,... | collective-permute-start | bytes 786440 | tf_op jit(solution)/shard_map/ppermute | solution.py:61
  75.4 9.4 %collective-permute-start.13 = (f32[2,96,128]{2,1,0:T(8,128)S(1)}, f32[2,96,128]{2,1,0:T(8,128)S(1)}, u32[]{:S(2)}, u32[]{:S(2)}) collective-permute-start(f32[2,96,128]{2,1,0:T(8,128)S(1)} %get-tuple-element.49), channel_id=1, source_target_pairs={{0,3},{1,2},{2,1},{3,0},{4,7},{5,6},{6,5},{7,4},{8,11},{9,10},{10,... | collective-permute-start | bytes 294920 | tf_op jit(solution)/shard_map/ppermute | solution.py:61
  84.7 1.3 collective-permute-start.14
  84.7 6.4 %collective-permute-start.15 = (f32[2,96,128]{2,1,0:T(8,128)S(1)}, f32[2,96,128]{2,1,0:T(8,128)S(1)}, u32[]{:S(2)}, u32[]{:S(2)}) collective-permute-start(f32[2,96,128]{2,1,0:T(8,128)S(1)} %collective-permute-done.11.refs_2_), channel_id=1, source_target_pairs={{0,16},{16,0},{1,17},{17,1},{2,18},{18,2},{3,19},{19,3},{4,20},{20... | collective-permute-start | bytes 294920 | tf_op jit(solution)/shard_map/ppermute | solution.py:61
  86.0 9.3 %collective-permute-start.33 = (f32[512,128]{1,0:T(8,128)S(1)}, f32[512,128]{1,0:T(8,128)S(1)}, u32[]{:S(2)}, u32[]{:S(2)}) collective-permute-start(f32[512,128]{1,0:T(8,128)S(1)} %get-tuple-element.44.refs_4_), channel_id=1, source_target_pairs={{0,3},{1,2},{2,1},{3,0},{4,7},{5,6},{6,5},{7,4},{8,11},{9,10},{10,... | collective-permute-start | bytes 786440 | tf_op jit(solution)/shard_map/ppermute | solution.py:61
  86.7 10.3 %collective-permute-start.41 = (f32[512,128]{1,0:T(8,128)S(1)}, f32[512,128]{1,0:T(8,128)S(1)}, u32[]{:S(2)}, u32[]{:S(2)}) collective-permute-start(f32[512,128]{1,0:T(8,128)S(1)} %get-tuple-element.41.refs_1_.refs_2_), channel_id=1, source_target_pairs={{0,16},{16,0},{1,17},{17,1},{2,18},{18,2},{3,19},{19,3},{4,20},{20... | collective-permute-start | bytes 786440 | tf_op jit(solution)/shard_map/ppermute | solution.py:61
  86.7 22.4 %collective-permute-start.34 = (f32[3,256,128]{2,1,0:T(8,128)S(1)}, f32[3,256,128]{2,1,0:T(8,128)S(1)}, u32[]{:S(2)}, u32[]{:S(2)}) collective-permute-start(f32[3,256,128]{2,1,0:T(8,128)S(1)} %get-tuple-element.58), channel_id=1, source_target_pairs={{0,4},{4,8},{8,12},{1,5},{5,9},{9,13},{2,6},{6,10},{10,14},{3,7},{... | collective-permute-start | bytes 1179656 | tf_op jit(solution)/shard_map/ppermute | solution.py:66
  90.8 1.4 collective-permute-start.16
  91.1 1.8 %collective-permute-start.17 = (f32[2,96,128]{2,1,0:T(8,128)S(1)}, f32[2,96,128]{2,1,0:T(8,128)S(1)}, u32[]{:S(2)}, u32[]{:S(2)}) collective-permute-start(f32[2,96,128]{2,1,0:T(8,128)S(1)} %collective-permute-done.13.refs_4_), channel_id=1, source_target_pairs={{0,16},{16,0},{1,17},{17,1},{2,18},{18,2},{3,19},{19,3},{4,20},{20... | collective-permute-start | bytes 294920 | tf_op jit(solution)/shard_map/ppermute | solution.py:61
  92.2 8.7 %collective-permute-start.38 = (f32[512,128]{1,0:T(8,128)S(1)}, f32[512,128]{1,0:T(8,128)S(1)}, u32[]{:S(2)}, u32[]{:S(2)}) collective-permute-start(f32[512,128]{1,0:T(8,128)S(1)} %get-tuple-element.64), channel_id=1, source_target_pairs={{2,3},{3,2},{6,7},{7,6},{10,11},{11,10},{14,15},{15,14},{18,19},{1... | collective-permute-start | bytes 786440 | tf_op jit(solution)/shard_map/ppermute | solution.py:298
  92.9 12.6 %collective-permute-start.49 = (f32[512,128]{1,0:T(8,128)S(1)}, f32[512,128]{1,0:T(8,128)S(1)}, u32[]{:S(2)}, u32[]{:S(2)}) collective-permute-start(f32[512,128]{1,0:T(8,128)S(1)} %get-tuple-element.63.refs_10_), channel_id=1, source_target_pairs={{0,16},{16,0},{1,17},{17,1},{2,18},{18,2},{3,19},{19,3},{4,20},{20... | collective-permute-start | bytes 786440 | tf_op jit(solution)/shard_map/ppermute | solution.py:61
  95.3 55.5 %copy-start.1 = (f32[384,768]{1,0:T(8,128)S(1)}, f32[384,768]{1,0:T(8,128)}, u32[]{:S(2)}) copy-start(f32[384,768]{1,0:T(8,128)} %refs_1_.1) | copy-start | bytes 3538948
  95.3 13.9 %collective-permute-start.53 = (f32[96,512]{1,0:T(8,128)S(1)}, f32[96,512]{1,0:T(8,128)S(1)}, u32[]{:S(2)}, u32[]{:S(2)}) collective-permute-start(f32[96,512]{1,0:T(8,128)S(1)} %factor_slice.1.refs_1_), channel_id=1, source_target_pairs={{0,1},{1,0},{2,3},{3,2},{4,5},{5,4},{6,7},{7,6},{8,9},{9,8},{10,11... | collective-permute-start | bytes 589832 | tf_op jit(solution)/shard_map/ppermute | solution.py:61
  97.0 12.7 %collective-permute-start.54 = (f32[96,512]{1,0:T(8,128)S(1)}, f32[96,512]{1,0:T(8,128)S(1)}, u32[]{:S(2)}, u32[]{:S(2)}) collective-permute-start(f32[96,512]{1,0:T(8,128)S(1)} %factor_slice.1.refs_1_), channel_id=1, source_target_pairs={{0,2},{1,3},{2,0},{3,1},{4,6},{5,7},{6,4},{7,5},{8,10},{9,11},{10,... | collective-permute-start | bytes 589832 | tf_op jit(solution)/shard_map/ppermute | solution.py:61
  100.9 11.9 %collective-permute-start.55 = (f32[96,512]{1,0:T(8,128)S(1)}, f32[96,512]{1,0:T(8,128)S(1)}, u32[]{:S(2)}, u32[]{:S(2)}) collective-permute-start(f32[96,512]{1,0:T(8,128)S(1)} %factor_slice.1.refs_1_), channel_id=1, source_target_pairs={{0,3},{1,2},{2,1},{3,0},{4,7},{5,6},{6,5},{7,4},{8,11},{9,10},{10,... | collective-permute-start | bytes 589832 | tf_op jit(solution)/shard_map/ppermute | solution.py:61
  105.5 8.8 %collective-permute-start.40 = (f32[512,128]{1,0:T(8,128)S(1)}, f32[512,128]{1,0:T(8,128)S(1)}, u32[]{:S(2)}, u32[]{:S(2)}) collective-permute-start(f32[512,128]{1,0:T(8,128)S(1)} %collective-permute-done.39.refs_12_), channel_id=1, source_target_pairs={{0,1},{4,5},{8,9},{12,13},{16,17},{20,21},{24,25},{28,29}} | collective-permute-start | bytes 786440 | tf_op jit(solution)/shard_map/ppermute | solution.py:301
  109.1 5.4 %collective-permute-start.42 = (f32[512,128]{1,0:T(8,128)S(1)}, f32[512,128]{1,0:T(8,128)S(1)}, u32[]{:S(2)}, u32[]{:S(2)}) collective-permute-start(f32[512,128]{1,0:T(8,128)S(1)} %collective-permute-done.31.refs_3_), channel_id=1, source_target_pairs={{0,16},{16,0},{1,17},{17,1},{2,18},{18,2},{3,19},{19,3},{4,20},{20... | collective-permute-start | bytes 786440 | tf_op jit(solution)/shard_map/ppermute | solution.py:61
  109.2 5.5 %collective-permute-start.43 = (f32[512,128]{1,0:T(8,128)S(1)}, f32[512,128]{1,0:T(8,128)S(1)}, u32[]{:S(2)}, u32[]{:S(2)}) collective-permute-start(f32[512,128]{1,0:T(8,128)S(1)} %collective-permute-done.32.refs_4_), channel_id=1, source_target_pairs={{0,16},{16,0},{1,17},{17,1},{2,18},{18,2},{3,19},{19,3},{4,20},{20... | collective-permute-start | bytes 786440 | tf_op jit(solution)/shard_map/ppermute | solution.py:61
  109.7 8.5 %collective-permute-start.44 = (f32[512,128]{1,0:T(8,128)S(1)}, f32[512,128]{1,0:T(8,128)S(1)}, u32[]{:S(2)}, u32[]{:S(2)}) collective-permute-start(f32[512,128]{1,0:T(8,128)S(1)} %collective-permute-done.33.refs_5_), channel_id=1, source_target_pairs={{0,16},{16,0},{1,17},{17,1},{2,18},{18,2},{3,19},{19,3},{4,20},{20... | collective-permute-start | bytes 786440 | tf_op jit(solution)/shard_map/ppermute | solution.py:61
  112.9 7.4 %collective-permute-start.51 = (f32[512,128]{1,0:T(8,128)S(1)}, f32[512,128]{1,0:T(8,128)S(1)}, u32[]{:S(2)}, u32[]{:S(2)}) collective-permute-start(f32[512,128]{1,0:T(8,128)S(1)} %collective-permute-done.39.refs_12_), channel_id=1, source_target_pairs={{0,16},{16,0},{1,17},{17,1},{2,18},{18,2},{3,19},{19,3},{4,20},{20... | collective-permute-start | bytes 786440 | tf_op jit(solution)/shard_map/ppermute | solution.py:61
  114.3 9.7 %collective-permute-start.21 = (f32[96,512]{1,0:T(8,128)S(1)}, f32[96,512]{1,0:T(8,128)S(1)}, u32[]{:S(2)}, u32[]{:S(2)}) collective-permute-start(f32[96,512]{1,0:T(8,128)S(1)} %factor_slice.1.refs_1_), channel_id=1, source_target_pairs={{0,4},{4,8},{8,12},{12,0},{1,5},{5,9},{9,13},{13,1},{2,6},{6,10},{... | collective-permute-start | bytes 589832 | tf_op jit(solution)/shard_map/ppermute | solution.py:56
  114.6 16.0 %collective-permute-start.22 = (f32[96,512]{1,0:T(8,128)S(1)}, f32[96,512]{1,0:T(8,128)S(1)}, u32[]{:S(2)}, u32[]{:S(2)}) collective-permute-start(f32[96,512]{1,0:T(8,128)S(1)} %factor_slice.1.refs_1_), channel_id=1, source_target_pairs={{0,8},{4,12},{8,0},{12,4},{1,9},{5,13},{9,1},{13,5},{2,10},{6,14},... | collective-permute-start | bytes 589832 | tf_op jit(solution)/shard_map/ppermute | solution.py:56
  114.8 15.9 %collective-permute-start.23 = (f32[96,512]{1,0:T(8,128)S(1)}, f32[96,512]{1,0:T(8,128)S(1)}, u32[]{:S(2)}, u32[]{:S(2)}) collective-permute-start(f32[96,512]{1,0:T(8,128)S(1)} %factor_slice.1.refs_1_), channel_id=1, source_target_pairs={{0,12},{4,0},{8,4},{12,8},{1,13},{5,1},{9,5},{13,9},{2,14},{6,2},{... | collective-permute-start | bytes 589832 | tf_op jit(solution)/shard_map/ppermute | solution.py:56
  118.2 14.1 %collective-permute-start.50 = (f32[512,128]{1,0:T(8,128)S(1)}, f32[512,128]{1,0:T(8,128)S(1)}, u32[]{:S(2)}, u32[]{:S(2)}) collective-permute-start(f32[512,128]{1,0:T(8,128)S(1)} %collective-permute-done.38.refs_11_), channel_id=1, source_target_pairs={{0,16},{16,0},{1,17},{17,1},{2,18},{18,2},{3,19},{19,3},{4,20},{20... | collective-permute-start | bytes 786440 | tf_op jit(solution)/shard_map/ppermute | solution.py:61
  120.3 14.1 %collective-permute-start.35 = (f32[512,128]{1,0:T(8,128)S(1)}, f32[512,128]{1,0:T(8,128)S(1)}, u32[]{:S(2)}, u32[]{:S(2)}) collective-permute-start(f32[512,128]{1,0:T(8,128)S(1)} %get-tuple-element.60), channel_id=1, source_target_pairs={{0,1},{1,0},{2,3},{3,2},{4,5},{5,4},{6,7},{7,6},{8,9},{9,8},{10,11... | collective-permute-start | bytes 786440 | tf_op jit(solution)/shard_map/ppermute | solution.py:61
  124.0 11.9 %collective-permute-start.36 = (f32[512,128]{1,0:T(8,128)S(1)}, f32[512,128]{1,0:T(8,128)S(1)}, u32[]{:S(2)}, u32[]{:S(2)}) collective-permute-start(f32[512,128]{1,0:T(8,128)S(1)} %get-tuple-element.61), channel_id=1, source_target_pairs={{0,2},{1,3},{2,0},{3,1},{4,6},{5,7},{6,4},{7,5},{8,10},{9,11},{10,... | collective-permute-start | bytes 786440 | tf_op jit(solution)/shard_map/ppermute | solution.py:61
  130.5 7.4 %collective-permute-start.37 = (f32[512,128]{1,0:T(8,128)S(1)}, f32[512,128]{1,0:T(8,128)S(1)}, u32[]{:S(2)}, u32[]{:S(2)}) collective-permute-start(f32[512,128]{1,0:T(8,128)S(1)} %get-tuple-element.62), channel_id=1, source_target_pairs={{0,3},{1,2},{2,1},{3,0},{4,7},{5,6},{6,5},{7,4},{8,11},{9,10},{10,... | collective-permute-start | bytes 786440 | tf_op jit(solution)/shard_map/ppermute | solution.py:61
  130.6 7.4 %collective-permute-start.45 = (f32[512,128]{1,0:T(8,128)S(1)}, f32[512,128]{1,0:T(8,128)S(1)}, u32[]{:S(2)}, u32[]{:S(2)}) collective-permute-start(f32[512,128]{1,0:T(8,128)S(1)} %get-tuple-element.59.refs_6_), channel_id=1, source_target_pairs={{0,16},{16,0},{1,17},{17,1},{2,18},{18,2},{3,19},{19,3},{4,20},{20... | collective-permute-start | bytes 786440 | tf_op jit(solution)/shard_map/ppermute | solution.py:61
  132.3 9.0 %collective-permute-start.24 = (f32[96,512]{1,0:T(8,128)S(1)}, f32[96,512]{1,0:T(8,128)S(1)}, u32[]{:S(2)}, u32[]{:S(2)}) collective-permute-start(f32[96,512]{1,0:T(8,128)S(1)} %get-tuple-element.55), channel_id=1, source_target_pairs={{0,1},{1,0},{2,3},{3,2},{4,5},{5,4},{6,7},{7,6},{8,9},{9,8},{10,11... | collective-permute-start | bytes 589832 | tf_op jit(solution)/shard_map/ppermute | solution.py:61
  134.4 9.7 %collective-permute-start.25 = (f32[96,512]{1,0:T(8,128)S(1)}, f32[96,512]{1,0:T(8,128)S(1)}, u32[]{:S(2)}, u32[]{:S(2)}) collective-permute-start(f32[96,512]{1,0:T(8,128)S(1)} %get-tuple-element.56), channel_id=1, source_target_pairs={{0,2},{1,3},{2,0},{3,1},{4,6},{5,7},{6,4},{7,5},{8,10},{9,11},{10,... | collective-permute-start | bytes 589832 | tf_op jit(solution)/shard_map/ppermute | solution.py:61
  135.9 12.1 %collective-permute-start.52 = (f32[512,128]{1,0:T(8,128)S(1)}, f32[512,128]{1,0:T(8,128)S(1)}, u32[]{:S(2)}, u32[]{:S(2)}) collective-permute-start(f32[512,128]{1,0:T(8,128)S(1)} %collective-permute-done.40.refs_13_), channel_id=1, source_target_pairs={{0,16},{16,0},{1,17},{17,1},{2,18},{18,2},{3,19},{19,3},{4,20},{20... | collective-permute-start | bytes 786440 | tf_op jit(solution)/shard_map/ppermute | solution.py:61
  138.0 10.5 %collective-permute-start.46 = (f32[512,128]{1,0:T(8,128)S(1)}, f32[512,128]{1,0:T(8,128)S(1)}, u32[]{:S(2)}, u32[]{:S(2)}) collective-permute-start(f32[512,128]{1,0:T(8,128)S(1)} %collective-permute-done.35.refs_7_), channel_id=1, source_target_pairs={{0,16},{16,0},{1,17},{17,1},{2,18},{18,2},{3,19},{19,3},{4,20},{20... | collective-permute-start | bytes 786440 | tf_op jit(solution)/shard_map/ppermute | solution.py:61
  138.0 10.6 %collective-permute-start.47 = (f32[512,128]{1,0:T(8,128)S(1)}, f32[512,128]{1,0:T(8,128)S(1)}, u32[]{:S(2)}, u32[]{:S(2)}) collective-permute-start(f32[512,128]{1,0:T(8,128)S(1)} %collective-permute-done.36.refs_8_), channel_id=1, source_target_pairs={{0,16},{16,0},{1,17},{17,1},{2,18},{18,2},{3,19},{19,3},{4,20},{20... | collective-permute-start | bytes 786440 | tf_op jit(solution)/shard_map/ppermute | solution.py:61
  141.4 6.6 %collective-permute-start.26 = (f32[96,512]{1,0:T(8,128)S(1)}, f32[96,512]{1,0:T(8,128)S(1)}, u32[]{:S(2)}, u32[]{:S(2)}) collective-permute-start(f32[96,512]{1,0:T(8,128)S(1)} %get-tuple-element.57), channel_id=1, source_target_pairs={{0,3},{1,2},{2,1},{3,0},{4,7},{5,6},{6,5},{7,4},{8,11},{9,10},{10,... | collective-permute-start | bytes 589832 | tf_op jit(solution)/shard_map/ppermute | solution.py:61
  144.1 6.8 %collective-permute-start.48 = (f32[512,128]{1,0:T(8,128)S(1)}, f32[512,128]{1,0:T(8,128)S(1)}, u32[]{:S(2)}, u32[]{:S(2)}) collective-permute-start(f32[512,128]{1,0:T(8,128)S(1)} %collective-permute-done.37.refs_9_), channel_id=1, source_target_pairs={{0,16},{16,0},{1,17},{17,1},{2,18},{18,2},{3,19},{19,3},{4,20},{20... | collective-permute-start | bytes 786440 | tf_op jit(solution)/shard_map/ppermute | solution.py:61
  148.0 6.5 %collective-permute-start.27 = (f32[96,512]{1,0:T(8,128)S(1)}, f32[96,512]{1,0:T(8,128)S(1)}, u32[]{:S(2)}, u32[]{:S(2)}) collective-permute-start(f32[96,512]{1,0:T(8,128)S(1)} %get-tuple-element.54.refs_1_), channel_id=1, source_target_pairs={{0,16},{16,0},{1,17},{17,1},{2,18},{18,2},{3,19},{19,3},{4,20},{20... | collective-permute-start | bytes 589832 | tf_op jit(solution)/shard_map/ppermute | solution.py:61
  148.0 6.5 %collective-permute-start.28 = (f32[96,512]{1,0:T(8,128)S(1)}, f32[96,512]{1,0:T(8,128)S(1)}, u32[]{:S(2)}, u32[]{:S(2)}) collective-permute-start(f32[96,512]{1,0:T(8,128)S(1)} %collective-permute-done.24.refs_2_), channel_id=1, source_target_pairs={{0,16},{16,0},{1,17},{17,1},{2,18},{18,2},{3,19},{19,3},{4,20},{20... | collective-permute-start | bytes 589832 | tf_op jit(solution)/shard_map/ppermute | solution.py:61
  148.5 6.0 %collective-permute-start.29 = (f32[96,512]{1,0:T(8,128)S(1)}, f32[96,512]{1,0:T(8,128)S(1)}, u32[]{:S(2)}, u32[]{:S(2)}) collective-permute-start(f32[96,512]{1,0:T(8,128)S(1)} %collective-permute-done.25.refs_3_), channel_id=1, source_target_pairs={{0,16},{16,0},{1,17},{17,1},{2,18},{18,2},{3,19},{19,3},{4,20},{20... | collective-permute-start | bytes 589832 | tf_op jit(solution)/shard_map/ppermute | solution.py:61
  148.6 5.9 %collective-permute-start.30 = (f32[96,512]{1,0:T(8,128)S(1)}, f32[96,512]{1,0:T(8,128)S(1)}, u32[]{:S(2)}, u32[]{:S(2)}) collective-permute-start(f32[96,512]{1,0:T(8,128)S(1)} %collective-permute-done.26.refs_4_), channel_id=1, source_target_pairs={{0,16},{16,0},{1,17},{17,1},{2,18},{18,2},{3,19},{19,3},{4,20},{20... | collective-permute-start | bytes 589832 | tf_op jit(solution)/shard_map/ppermute | solution.py:61
